TPU v7x, 32 devices: a whole 2x2x4 slice. The times are simulated.
32 devices in a mesh: kpt: 2 (over y), dom: 8 (over z, x), band: 2 (over core).
Axes of the slice: x: 2, y: 2, z: 4, core: 2. Of those that a mesh axis runs over, the one named last changes fastest.
Arguments:
- wavefunctions: bfloat16 [65536, 256], P(('kpt', 'dom'), 'band'), parts along dimension 0, may hold values from -40 to 40
- bounds: float32 [4], P('kpt'), parts along dimension 0, may hold values from 0.5 to 23, as said below
- cell_matrix: bfloat16 [512, 512], replicated, may hold values from -1 to 4, as said below
- cell_scale: float32 [128], P('dom'), may hold values from 0.5 to 6
- potential: float32 [32768], P('dom'), may hold values from 0.5 to 3
- cell_nodes: int32 [128, 512], P('dom'), may hold values from 0 to 5119, as said below
- face_nodes: int32 [32, 256], P('dom'), may hold values from -1 to 4095, as said below
Outputs:
- rotated: float32 [65536, 256], P(('kpt', 'dom'), 'band'), parts along dimension 0
There are 2 independent parts, one for each index of `kpt`. A program takes and returns all parts, laid end to end along the dimension named above; an argument that names none is the same for every part. Nothing has to cross between parts.
Inputs may be any that keep to these rules, and one draw needn't show every extreme that they name: `face_nodes`: row 4 d + o lists in its first slots the own nodes (0 to 4095 of block d) sent to block d + (1, -1, 2, -2)[o]; the remaining slots hold -1; at least one row whose neighbour block exists is full. `cell_nodes`: entries below 4096 are own nodes of the cell's block, the others ghost rows of its extended block. bounds[1] exceeds bounds[0] by 8 or more. `cell_matrix`: symmetric.
All inputs are finite; a program needn't handle non-finite values.
Results may differ from a plain program's by a relative error of at most 0.0054.
Values may be sent and summed in bfloat16 or wider, within the bound.
No kernel may reach another device: no remote copies, remote signals or barrier semaphores. Data moves between devices by JAX's collectives and lax.ppermute only.
A program may use at most 64 MiB of HBM per device.

v0:
```python
import jax
import jax.numpy as jnp
from jax import lax
from jax.sharding import PartitionSpec as P

peer_offsets = (1, -1, 2, -2)


def passed_along(value, axis, by):
    size = lax.axis_size(axis)
    pairs = [(i, i + by) for i in range(size) if 0 <= i + by < size]
    return lax.ppermute(value, axis, pairs)


def on_device(wavefunctions, bounds, cell_matrix, cell_scale, potential, cell_nodes, face_nodes):
    node_dev, columns = wavefunctions.shape
    slot_count = face_nodes.shape[1]
    ext_count = node_dev + 4 * slot_count
    filled = face_nodes >= 0
    safe_index = jnp.maximum(face_nodes, 0)
    targets = jnp.where(filled, face_nodes, node_dev).reshape(-1)
    flat_maps = cell_nodes.reshape(-1)

    def apply_operator(vectors):
        outgoing = jnp.where(filled[:, :, None], vectors[safe_index], jnp.zeros((), vectors.dtype))
        ghosts = [None, None, None, None]
        for offset_idx in range(4):
            ghosts[offset_idx] = passed_along(outgoing[offset_idx], "dom", peer_offsets[offset_idx])
        extended = jnp.concatenate([vectors] + ghosts, 0)
        gathered = extended[cell_nodes]
        products = jnp.einsum(
            "ij,cjk->cik", cell_matrix, gathered, preferred_element_type=jnp.float32
        )
        products = products * cell_scale[:, None, None]
        summed = jax.ops.segment_sum(
            products.reshape(-1, columns), flat_maps, num_segments=ext_count
        )
        ghost_acc = summed[node_dev:].reshape(4, slot_count, columns)
        returned = [None, None, None, None]
        for offset_idx in range(4):
            returned[offset_idx] = passed_along(
                ghost_acc[offset_idx], "dom", -peer_offsets[offset_idx]
            )
        returned_sum = jax.ops.segment_sum(
            jnp.stack(returned).reshape(-1, columns), targets, num_segments=node_dev + 1
        )
        return (
            summed[:node_dev]
            + returned_sum[:node_dev]
            + potential[:, None] * vectors.astype(jnp.float32)
        )

    center = (bounds[0] + bounds[1]) / 2.0
    half_width = (bounds[1] - bounds[0]) / 2.0
    wave_wide = wavefunctions.astype(jnp.float32)
    image_one = apply_operator(wavefunctions)
    degree_one = ((image_one - center * wave_wide) / half_width).astype(jnp.bfloat16)
    image_two = apply_operator(degree_one)
    degree_two = (
        2.0 * (image_two - center * degree_one.astype(jnp.float32)) / half_width - wave_wide
    ).astype(jnp.bfloat16)
    panel_all = lax.all_gather(degree_two, "band", axis=1, tiled=True)
    band_count = panel_all.shape[1]
    node_count = node_dev * lax.axis_size("dom")
    col_start = lax.axis_index("band") * columns
    margin_part = jnp.einsum("nc,nd->cd", degree_two, panel_all, preferred_element_type=jnp.float32)
    margin_part = lax.psum(margin_part, "dom")
    margin = lax.all_gather(margin_part, "band", axis=0, tiled=True)
    margin = margin / node_count
    factor = jnp.linalg.cholesky(margin)
    inverse = lax.linalg.triangular_solve(
        factor, jnp.eye(band_count, dtype=factor.dtype), left_side=True, lower=True
    )
    own_rows = lax.dynamic_slice_in_dim(inverse, col_start, columns, 0)
    return jnp.dot(panel_all.astype(jnp.float32), own_rows.T, precision=lax.Precision.HIGHEST)


def solution(mesh):
    return jax.shard_map(
        on_device,
        mesh=mesh,
        in_specs=(
            P(("kpt", "dom"), "band"),
            P("kpt"),
            P(),
            P("dom"),
            P("dom"),
            P("dom", None),
            P("dom", None),
        ),
        out_specs=P(("kpt", "dom"), "band"),
        check_vma=False,
    )
```

profile of v0, /device:TPU:0, one launch (start us, length us, event | category | flops | bytes accessed | tf_op | source)
XLA Modules:
  0.0 440.4 jit_solution(5676288269677081462)
XLA Ops:
  12.5 4.8 %collective-permute-start = (bf16[256,128]{1,0:T(8,128)(2,1)S(1)}, bf16[256,128]{1,0:T(8,128)(2,1)S(1)}, u32[]{:S(2)}, u32[]{:S(2)}) collective-permute-start(bf16[256,128]{1,0:T(8,128)(2,1)S(1)} %get-tuple-element.40), channel_id=1, source_target_pairs={{0,2},{2,4},{4,6},{6,8},{8,10},{10,12},{12,14},{1,3},{3,5},{5,7},{... | collective-permute-start | bytes 196616 | tf_op jit(solution)/shard_map/ppermute | solution.py:12
  18.7 5.5 %collective-permute-start.2 = (bf16[256,128]{1,0:T(8,128)(2,1)S(1)}, bf16[256,128]{1,0:T(8,128)(2,1)S(1)}, u32[]{:S(2)}, u32[]{:S(2)}) collective-permute-start(bf16[256,128]{1,0:T(8,128)(2,1)S(1)} %get-tuple-element.38), channel_id=1, source_target_pairs={{0,4},{2,6},{4,8},{6,10},{8,12},{10,14},{1,5},{3,7},{5,9},{7,11},{... | collective-permute-start | bytes 196616 | tf_op jit(solution)/shard_map/ppermute | solution.py:12
  30.4 29.5 %gather_fusion.1 = bf16[8192,128]{1,0:T(8,128)(2,1)} fusion(bf16[5120,128]{1,0:T(8,128)(2,1)S(1)} %constant_dynamic-update-slice_fusion, s32[8192]{0:T(1024)S(1)} %broadcast_clamp_fusion), kind=kCustom, calls=%fused_computation.1 | custom fusion | bytes 4227072 | tf_op jit(solution)/shard_map/gather | solution.py:30
  59.9 5.2 %multiply_bitcast_fusion.1 = f32[16,512,128]{1,2,0:T(8,128)} fusion(bf16[16,512,128]{2,1,0:T(8,128)(2,1)} %bitcast.91, f32[16]{0:T(128)S(1)} %copy-done.6, bf16[512,512]{1,0:T(8,128)(2,1)S(1)} %copy-done), kind=kOutput, calls=%fused_computation.11 | convolution fusion | flops 1074790400 | bytes 6815808 | tf_op jit(solution)/shard_map/ij,cjk->cik/dot_general | solution.py:31
  65.1 5.4 %copy.13 = f32[16,512,128]{2,1,0:T(8,128)} copy(f32[16,512,128]{1,2,0:T(8,128)} %multiply_bitcast_fusion.1) | data formatting | bytes 8388608 | tf_op jit(solution)/shard_map/mul | solution.py:34
  70.5 46.0 %scatter_custom_fusion = f32[5120,128]{1,0:T(8,128)} fusion(s32[8192]{0:T(1024)S(1)} %bitcast.108, f32[8192,128]{1,0:T(8,128)} %bitcast.93, f32[]{:T(128)} %constant.94.clone.1), kind=kCustom, calls=%fused_computation.30 | custom fusion | flops 1048576 | bytes 2621952 | tf_op jit(solution)/shard_map/scatter-add | solution.py:35
  121.4 4.6 %collective-permute-start.7 = (f32[256,128]{1,0:T(8,128)S(1)}, f32[256,128]{1,0:T(8,128)S(1)}, u32[]{:S(2)}, u32[]{:S(2)}) collective-permute-start(f32[256,128]{1,0:T(8,128)S(1)} %get-tuple-element.30), channel_id=1, source_target_pairs={{0,4},{2,6},{4,8},{6,10},{8,12},{10,14},{1,5},{3,7},{5,9},{7,11},{... | collective-permute-start | bytes 393224 | tf_op jit(solution)/shard_map/ppermute | solution.py:12
  133.3 8.2 %scatter_custom_fusion.1 = f32[4097,128]{1,0:T(8,128)} fusion(s32[1024]{0:T(1024)S(1)} %bitcast.111, f32[1024,128]{1,0:T(8,128)S(1)} %bitcast.97, f32[]{:T(128)} %constant.94.clone.1), kind=kCustom, calls=%fused_computation.36 | custom fusion | flops 131072 | bytes 2097668 | tf_op jit(solution)/shard_map/scatter-add | solution.py:44
  149.3 4.5 %collective-permute-start.8 = (bf16[256,128]{1,0:T(8,128)(2,1)S(1)}, bf16[256,128]{1,0:T(8,128)(2,1)S(1)}, u32[]{:S(2)}, u32[]{:S(2)}) collective-permute-start(bf16[256,128]{1,0:T(8,128)(2,1)S(1)} %get-tuple-element.36), channel_id=1, source_target_pairs={{0,2},{2,4},{4,6},{6,8},{8,10},{10,12},{12,14},{1,3},{3,5},{5,7},{... | collective-permute-start | bytes 196616 | tf_op jit(solution)/shard_map/ppermute | solution.py:12
  155.1 4.4 collective-permute-start.10
  165.7 29.5 %gather_fusion.3 = bf16[8192,128]{1,0:T(8,128)(2,1)} fusion(bf16[5120,128]{1,0:T(8,128)(2,1)S(1)} %constant_dynamic-update-slice_fusion.5, s32[8192]{0:T(1024)S(1)} %broadcast_clamp_fusion), kind=kCustom, calls=%fused_computation.3 | custom fusion | bytes 4227072 | tf_op jit(solution)/shard_map/gather | solution.py:30
  195.2 5.2 %multiply_bitcast_fusion = f32[16,512,128]{1,2,0:T(8,128)} fusion(bf16[16,512,128]{2,1,0:T(8,128)(2,1)} %bitcast.90, f32[16]{0:T(128)S(1)} %copy-done.6, bf16[512,512]{1,0:T(8,128)(2,1)S(1)} %copy-done), kind=kOutput, calls=%fused_computation.10 | convolution fusion | flops 1074790400 | bytes 6815808 | tf_op jit(solution)/shard_map/ij,cjk->cik/dot_general | solution.py:31
  200.4 5.4 %copy.15 = f32[16,512,128]{2,1,0:T(8,128)} copy(f32[16,512,128]{1,2,0:T(8,128)} %multiply_bitcast_fusion) | data formatting | bytes 8388608 | tf_op jit(solution)/shard_map/mul | solution.py:34
  205.8 46.0 %scatter_custom_fusion.2 = f32[5120,128]{1,0:T(8,128)} fusion(s32[8192]{0:T(1024)S(1)} %bitcast.109, f32[8192,128]{1,0:T(8,128)} %bitcast.92, f32[]{:T(128)} %constant.94.clone.1), kind=kCustom, calls=%fused_computation.28 | custom fusion | flops 1048576 | bytes 2621952 | tf_op jit(solution)/shard_map/scatter-add | solution.py:35
  254.3 4.6 %collective-permute-start.13 = (f32[256,128]{1,0:T(8,128)S(1)}, f32[256,128]{1,0:T(8,128)S(1)}, u32[]{:S(2)}, u32[]{:S(2)}) collective-permute-start(f32[256,128]{1,0:T(8,128)S(1)} %get-tuple-element.28), channel_id=1, source_target_pairs={{0,2},{2,4},{4,6},{6,8},{8,10},{10,12},{12,14},{1,3},{3,5},{5,7},{... | collective-permute-start | bytes 393224 | tf_op jit(solution)/shard_map/ppermute | solution.py:12
  260.1 4.6 %collective-permute-start.15 = (f32[256,128]{1,0:T(8,128)S(1)}, f32[256,128]{1,0:T(8,128)S(1)}, u32[]{:S(2)}, u32[]{:S(2)}) collective-permute-start(f32[256,128]{1,0:T(8,128)S(1)} %get-tuple-element.26), channel_id=1, source_target_pairs={{0,4},{2,6},{4,8},{6,10},{8,12},{10,14},{1,5},{3,7},{5,9},{7,11},{... | collective-permute-start | bytes 393224 | tf_op jit(solution)/shard_map/ppermute | solution.py:12
  267.2 8.2 %scatter_custom_fusion.3 = f32[4097,128]{1,0:T(8,128)} fusion(s32[1024]{0:T(1024)S(1)} %bitcast.112, f32[1024,128]{1,0:T(8,128)S(1)} %bitcast.96, f32[]{:T(128)} %constant.94.clone.1), kind=kCustom, calls=%fused_computation.34 | custom fusion | flops 131072 | bytes 2097668 | tf_op jit(solution)/shard_map/scatter-add | solution.py:44
  278.9 11.4 %all-gather.2.cloned.1.call-done = bf16[4096,256]{1,0:T(8,128)(2,1)} async-done(((bf16[4096,128]{1,0:T(8,128)(2,1)}), bf16[4096,256]{1,0:T(8,128)(2,1)}) %all-gather.2.cloned.1.call-update) | async-done | bytes 2097168 | tf_op jit(solution)/shard_map/all_gather | solution.py:62
  293.9 71.0 %all-reduce.3.cloned.1.call-done = f32[128,256]{0,1:T(8,128)} async-done(((f32[128,256]{0,1:T(8,128)}), f32[128,256]{0,1:T(8,128)}) %all-reduce.3.cloned.1.call-update) | async-done | bytes 131088 | tf_op jit(solution)/shard_map/psum | solution.py:67
  367.6 11.7 %cholesky.50 = f32[128,128]{1,0:T(8,128)S(1)} custom-call(f32[128,128]{1,0:T(8,128)S(1)} %cholesky.118), custom_call_target="Cholesky" | custom-call | tf_op jit(solution)/shard_map/jit(cholesky)/cholesky | solution.py:70
  379.4 9.8 %custom-call.14 = f32[1,128,128]{1,2,0:T(8,128)S(1)} custom-call(f32[1,128,128]{2,1,0:T(8,128)S(1)} %get-tuple-element.44), custom_call_target="InvertDiagBlocksLowerTriangular" | custom-call | tf_op jit(solution)/shard_map/jit(cholesky)/cholesky | solution.py:70
  389.7 11.7 %cholesky.105 = f32[128,128]{1,0:T(8,128)S(1)} custom-call(f32[128,128]{1,0:T(8,128)S(1)} %convolution_subtract_fusion.1), custom_call_target="Cholesky" | custom-call | tf_op jit(solution)/shard_map/jit(cholesky)/cholesky | solution.py:70
  403.6 5.5 %while.1 = (s32[]{:T(128)}, f32[256,256]{1,0:T(8,128)S(1)}, s32[2,2]{1,0:T(2,128)S(1)}, f32[2,128,128]{2,1,0:T(8,128)}, s32[]{:T(128)}) while((s32[]{:T(128)}, f32[256,256]{1,0:T(8,128)S(1)}, s32[2,2]{1,0:T(2,128)S(1)}, f32[2,128,128]{2,1,0:T(8,128)}, s32[]{:T(128)}) %tuple.38), condition=%wide.while_cond, body=%wide.while_body.sunk | while | flops 2 | bytes 132705 | solution.py:71
  409.1 20.5 %custom-call.15 = f32[2,128,128]{1,2,0:T(8,128)S(1)} custom-call(f32[2,128,128]{2,1,0:T(8,128)} %get-tuple-element.12), custom_call_target="InvertDiagBlocksLowerTriangular" | custom-call | tf_op jit(solution)/shard_map/triangular_solve | solution.py:71
  (103 shorter events, 65.0 us)
Async XLA Ops:
  6.5 53.4 %copy-start = (bf16[512,512]{1,0:T(8,128)(2,1)S(1)}, bf16[512,512]{1,0:T(8,128)(2,1)}, u32[]{:S(2)}) copy-start(bf16[512,512]{1,0:T(8,128)(2,1)} %param.9) | copy-start | bytes 1572868
  6.5 283.8 %all-gather.2.cloned.1.call-start = ((), (), s32[]{:S(2)}) async-start(), calls=%async_computation | async-start | bytes 3145728 | tf_op jit(solution)/shard_map/all_gather | solution.py:62
  12.5 13.2 %collective-permute-start = (bf16[256,128]{1,0:T(8,128)(2,1)S(1)}, bf16[256,128]{1,0:T(8,128)(2,1)S(1)}, u32[]{:S(2)}, u32[]{:S(2)}) collective-permute-start(bf16[256,128]{1,0:T(8,128)(2,1)S(1)} %get-tuple-element.40), channel_id=1, source_target_pairs={{0,2},{2,4},{4,6},{6,8},{8,10},{10,12},{12,14},{1,3},{3,5},{5,7},{... | collective-permute-start | bytes 196616 | tf_op jit(solution)/shard_map/ppermute | solution.py:12
  17.4 8.3 %collective-permute-start.1 = (bf16[256,128]{1,0:T(8,128)(2,1)S(1)}, bf16[256,128]{1,0:T(8,128)(2,1)S(1)}, u32[]{:S(2)}, u32[]{:S(2)}) collective-permute-start(bf16[256,128]{1,0:T(8,128)(2,1)S(1)} %get-tuple-element.39), channel_id=1, source_target_pairs={{2,0},{4,2},{6,4},{8,6},{10,8},{12,10},{14,12},{3,1},{5,3},{7,5},{... | collective-permute-start | bytes 196616 | tf_op jit(solution)/shard_map/ppermute | solution.py:12
  18.7 7.4 %collective-permute-start.2 = (bf16[256,128]{1,0:T(8,128)(2,1)S(1)}, bf16[256,128]{1,0:T(8,128)(2,1)S(1)}, u32[]{:S(2)}, u32[]{:S(2)}) collective-permute-start(bf16[256,128]{1,0:T(8,128)(2,1)S(1)} %get-tuple-element.38), channel_id=1, source_target_pairs={{0,4},{2,6},{4,8},{6,10},{8,12},{10,14},{1,5},{3,7},{5,9},{7,11},{... | collective-permute-start | bytes 196616 | tf_op jit(solution)/shard_map/ppermute | solution.py:12
  24.2 6.2 %collective-permute-start.3 = (bf16[256,128]{1,0:T(8,128)(2,1)S(1)}, bf16[256,128]{1,0:T(8,128)(2,1)S(1)}, u32[]{:S(2)}, u32[]{:S(2)}) collective-permute-start(bf16[256,128]{1,0:T(8,128)(2,1)S(1)} %get-tuple-element.37), channel_id=1, source_target_pairs={{4,0},{6,2},{8,4},{10,6},{12,8},{14,10},{5,1},{7,3},{9,5},{11,7},{... | collective-permute-start | bytes 196616 | tf_op jit(solution)/shard_map/ppermute | solution.py:12
  30.4 29.5 %copy-start.6 = (f32[16]{0:T(128)S(1)}, f32[16]{0:T(128)}, u32[]{:S(2)}) copy-start(f32[16]{0:T(128)} %param.10) | copy-start | bytes 196
  70.5 56.8 %copy-start.7 = (f32[2]{0:T(128)S(1)}, f32[2]{0:T(128)}, u32[]{:S(2)}) copy-start(f32[2]{0:T(128)} %param.8) | copy-start | bytes 28
  116.5 25.0 %copy-start.5 = (f32[4096]{0:T(1024)S(1)}, f32[4096]{0:T(1024)}, u32[]{:S(2)}) copy-start(f32[4096]{0:T(1024)} %param.11) | copy-start | bytes 49156
  117.6 12.9 %collective-permute-start.5 = (f32[256,128]{1,0:T(8,128)S(1)}, f32[256,128]{1,0:T(8,128)S(1)}, u32[]{:S(2)}, u32[]{:S(2)}) collective-permute-start(f32[256,128]{1,0:T(8,128)S(1)} %get-tuple-element.32), channel_id=1, source_target_pairs={{0,2},{2,4},{4,6},{6,8},{8,10},{10,12},{12,14},{1,3},{3,5},{5,7},{... | collective-permute-start | bytes 393224 | tf_op jit(solution)/shard_map/ppermute | solution.py:12
  120.1 10.4 %collective-permute-start.6 = (f32[256,128]{1,0:T(8,128)S(1)}, f32[256,128]{1,0:T(8,128)S(1)}, u32[]{:S(2)}, u32[]{:S(2)}) collective-permute-start(f32[256,128]{1,0:T(8,128)S(1)} %get-tuple-element.31), channel_id=1, source_target_pairs={{4,0},{6,2},{8,4},{10,6},{12,8},{14,10},{5,1},{7,3},{9,5},{11,7},{... | collective-permute-start | bytes 393224 | tf_op jit(solution)/shard_map/ppermute | solution.py:12
  121.4 9.1 %collective-permute-start.7 = (f32[256,128]{1,0:T(8,128)S(1)}, f32[256,128]{1,0:T(8,128)S(1)}, u32[]{:S(2)}, u32[]{:S(2)}) collective-permute-start(f32[256,128]{1,0:T(8,128)S(1)} %get-tuple-element.30), channel_id=1, source_target_pairs={{0,4},{2,6},{4,8},{6,10},{8,12},{10,14},{1,5},{3,7},{5,9},{7,11},{... | collective-permute-start | bytes 393224 | tf_op jit(solution)/shard_map/ppermute | solution.py:12
  126.0 7.3 %collective-permute-start.4 = (f32[256,128]{1,0:T(8,128)S(1)}, f32[256,128]{1,0:T(8,128)S(1)}, u32[]{:S(2)}, u32[]{:S(2)}) collective-permute-start(f32[256,128]{1,0:T(8,128)S(1)} %get-tuple-element.29), channel_id=1, source_target_pairs={{2,0},{4,2},{6,4},{8,6},{10,8},{12,10},{14,12},{3,1},{5,3},{7,5},{... | collective-permute-start | bytes 393224 | tf_op jit(solution)/shard_map/ppermute | solution.py:12
  149.3 11.7 %collective-permute-start.8 = (bf16[256,128]{1,0:T(8,128)(2,1)S(1)}, bf16[256,128]{1,0:T(8,128)(2,1)S(1)}, u32[]{:S(2)}, u32[]{:S(2)}) collective-permute-start(bf16[256,128]{1,0:T(8,128)(2,1)S(1)} %get-tuple-element.36), channel_id=1, source_target_pairs={{0,2},{2,4},{4,6},{6,8},{8,10},{10,12},{12,14},{1,3},{3,5},{5,7},{... | collective-permute-start | bytes 196616 | tf_op jit(solution)/shard_map/ppermute | solution.py:12
  153.8 7.2 %collective-permute-start.9 = (bf16[256,128]{1,0:T(8,128)(2,1)S(1)}, bf16[256,128]{1,0:T(8,128)(2,1)S(1)}, u32[]{:S(2)}, u32[]{:S(2)}) collective-permute-start(bf16[256,128]{1,0:T(8,128)(2,1)S(1)} %get-tuple-element.35), channel_id=1, source_target_pairs={{2,0},{4,2},{6,4},{8,6},{10,8},{12,10},{14,12},{3,1},{5,3},{7,5},{... | collective-permute-start | bytes 196616 | tf_op jit(solution)/shard_map/ppermute | solution.py:12
  155.1 6.3 %collective-permute-start.10 = (bf16[256,128]{1,0:T(8,128)(2,1)S(1)}, bf16[256,128]{1,0:T(8,128)(2,1)S(1)}, u32[]{:S(2)}, u32[]{:S(2)}) collective-permute-start(bf16[256,128]{1,0:T(8,128)(2,1)S(1)} %get-tuple-element.34), channel_id=1, source_target_pairs={{0,4},{2,6},{4,8},{6,10},{8,12},{10,14},{1,5},{3,7},{5,9},{7,11},{... | collective-permute-start | bytes 196616 | tf_op jit(solution)/shard_map/ppermute | solution.py:12
  159.5 6.2 %collective-permute-start.11 = (bf16[256,128]{1,0:T(8,128)(2,1)S(1)}, bf16[256,128]{1,0:T(8,128)(2,1)S(1)}, u32[]{:S(2)}, u32[]{:S(2)}) collective-permute-start(bf16[256,128]{1,0:T(8,128)(2,1)S(1)} %get-tuple-element.33), channel_id=1, source_target_pairs={{4,0},{6,2},{8,4},{10,6},{12,8},{14,10},{5,1},{7,3},{9,5},{11,7},{... | collective-permute-start | bytes 196616 | tf_op jit(solution)/shard_map/ppermute | solution.py:12
  251.7 23.6 %copy-start.2 = (bf16[4096,128]{1,0:T(8,128)(2,1)S(1)}, bf16[4096,128]{1,0:T(8,128)(2,1)}, u32[]{:S(2)}) copy-start(bf16[4096,128]{1,0:T(8,128)(2,1)} %get-tuple-element.22) | copy-start | bytes 3145732
  253.0 11.7 %collective-permute-start.12 = (f32[256,128]{1,0:T(8,128)S(1)}, f32[256,128]{1,0:T(8,128)S(1)}, u32[]{:S(2)}, u32[]{:S(2)}) collective-permute-start(f32[256,128]{1,0:T(8,128)S(1)} %get-tuple-element.25), channel_id=1, source_target_pairs={{2,0},{4,2},{6,4},{8,6},{10,8},{12,10},{14,12},{3,1},{5,3},{7,5},{... | collective-permute-start | bytes 393224 | tf_op jit(solution)/shard_map/ppermute | solution.py:12
  254.3 10.4 %collective-permute-start.13 = (f32[256,128]{1,0:T(8,128)S(1)}, f32[256,128]{1,0:T(8,128)S(1)}, u32[]{:S(2)}, u32[]{:S(2)}) collective-permute-start(f32[256,128]{1,0:T(8,128)S(1)} %get-tuple-element.28), channel_id=1, source_target_pairs={{0,2},{2,4},{4,6},{6,8},{8,10},{10,12},{12,14},{1,3},{3,5},{5,7},{... | collective-permute-start | bytes 393224 | tf_op jit(solution)/shard_map/ppermute | solution.py:12
  258.8 6.9 %collective-permute-start.14 = (f32[256,128]{1,0:T(8,128)S(1)}, f32[256,128]{1,0:T(8,128)S(1)}, u32[]{:S(2)}, u32[]{:S(2)}) collective-permute-start(f32[256,128]{1,0:T(8,128)S(1)} %get-tuple-element.27), channel_id=1, source_target_pairs={{4,0},{6,2},{8,4},{10,6},{12,8},{14,10},{5,1},{7,3},{9,5},{11,7},{... | collective-permute-start | bytes 393224 | tf_op jit(solution)/shard_map/ppermute | solution.py:12
  260.1 7.1 %collective-permute-start.15 = (f32[256,128]{1,0:T(8,128)S(1)}, f32[256,128]{1,0:T(8,128)S(1)}, u32[]{:S(2)}, u32[]{:S(2)}) collective-permute-start(f32[256,128]{1,0:T(8,128)S(1)} %get-tuple-element.26), channel_id=1, source_target_pairs={{0,4},{2,6},{4,8},{6,10},{8,12},{10,14},{1,5},{3,7},{5,9},{7,11},{... | collective-permute-start | bytes 393224 | tf_op jit(solution)/shard_map/ppermute | solution.py:12
  278.8 86.1 %all-reduce.3.cloned.1.call-start = ((), (), s32[]{:S(2)}) async-start(), calls=%async_computation.1 | async-start | bytes 262144 | tf_op jit(solution)/shard_map/psum | solution.py:67
  367.6 62.9 %copy-start.3 = (bf16[4096,256]{1,0:T(8,128)(2,1)S(1)}, bf16[4096,256]{1,0:T(8,128)(2,1)}, u32[]{:S(2)}) copy-start(bf16[4096,256]{1,0:T(8,128)(2,1)} %all-gather.2.cloned.1.call-done) | copy-start | bytes 6291460
  (2 other events, 32.3 us)
Sparse Core Ops, SparseCore 0:
  279.0 11.2 all-gather.1
  294.0 70.8 all-reduce.2
where the time goes:
time: 442 us; the launch traced here: 440 us
  other arithmetic  172 us (39%)
  waiting for transfers between devices  96.9 us (22%)
  local copies, waits for them, and re-layouts  86.9 us (20%)
  starting transfers between devices  46 us (10%)
  matrix products  18.4 us (4%)
  between operations  17.8 us (4%)
    scatter-add x2, other arithmetic, apply_operator(): jax.ops.segment_sum(products.reshape(-1, columns), flat_maps, num_segment...  91.9 us
    psum x1, waiting for transfers between devices, on_device(): margin_part = lax.psum(margin_part, 'dom')  71 us
    gather x2, local copies, waits for them, and re-layouts, apply_operator(): gathered = extended[cell_nodes]  59 us
    ppermute x16, starting transfers between devices, passed_along(): return lax.ppermute(value, axis, pairs)  46 us
    another operation x6, other arithmetic, on_device(): factor = jnp.linalg.cholesky(margin)  34 us
    another operation x3, other arithmetic, on_device(): lax.linalg.triangular_solve(factor, jnp.eye(band_count, dtype=factor.dtyp...  20.5 us
    scatter-add x2, other arithmetic, apply_operator(): jax.ops.segment_sum(jnp.stack(returned).reshape(-1, columns), targets, nu...  16.3 us
    ppermute x16, waiting for transfers between devices, passed_along(): return lax.ppermute(value, axis, pairs)  14.5 us
  transfers between devices with their start and end apart: 18, of which 9 were waited for; matrix products, arithmetic and copies ran while one was open for 0% of the time, Pallas kernels for 0%

commit v1 on v0

v1 whole, which is shorter than its diff:
```python
import functools

import jax
import jax.numpy as jnp
from jax import lax
from jax.experimental import pallas as pl
from jax.experimental.pallas import tpu as pltpu
from jax.sharding import PartitionSpec as P

peer_offsets = (1, -1, 2, -2)
f32, bf16 = jnp.float32, jnp.bfloat16
LANES, GROUP, PANEL = 128, 8, 8
vmem = pl.BlockSpec(memory_space=pltpu.VMEM)
smem = pl.BlockSpec(memory_space=pltpu.SMEM)
params = pltpu.CompilerParams(vmem_limit_bytes=58 * 2**20)


def passed_along(value, axis, by):
    size = lax.axis_size(axis)
    pairs = [(i, i + by) for i in range(size) if 0 <= i + by < size]
    return lax.ppermute(value, axis, pairs)


def gather_faces(faces_ref, table_ref, rows_ref, out_refs):
    spare = table_ref.shape[0] - 8
    slots = out_refs[0].shape[0]

    def body(step, _):
        base = step * 16
        for u in range(16):
            face = faces_ref[base + u]
            face = jnp.where(face < 0, spare, face)
            rows_ref[pl.ds(base + u, 1), :] = table_ref[pl.ds(face, 1), :]
        return 0

    lax.fori_loop(0, 4 * slots // 16, body, 0)
    for o in range(4):
        out_refs[o][...] = rows_ref[o * slots : (o + 1) * slots, :].astype(bf16)


def face_kernel(faces_ref, vec_ref, o0, o1, o2, o3, table_ref, rows_ref):
    nodes = vec_ref.shape[0]
    table_ref[0:nodes, :] = vec_ref[...].astype(f32)
    table_ref[nodes : nodes + 8, :] = jnp.zeros((8, LANES), f32)
    gather_faces(faces_ref, table_ref, rows_ref, (o0, o1, o2, o3))


def send_faces(faces, vectors):
    nodes, slots = vectors.shape[0], faces.shape[0] // 4
    return pl.pallas_call(
        face_kernel,
        out_shape=[jax.ShapeDtypeStruct((slots, LANES), bf16)] * 4,
        in_specs=[smem, vmem],
        out_specs=[vmem] * 4,
        scratch_shapes=[
            pltpu.VMEM((nodes + 8, LANES), f32),
            pltpu.VMEM((4 * slots, LANES), f32),
        ],
        compiler_params=params,
    )(faces, vectors)


def cells_kernel(
    maps_ref, scale_ref, matrix_ref, vec_ref, h0, h1, h2, h3, own_ref, g0, g1, g2, g3,
    ext_ref, in_ref, out_ref, *acc
):
    nodes, slots = vec_ref.shape[0], h0.shape[0]
    size = matrix_ref.shape[0]
    ext = nodes + 4 * slots
    ext_ref[0:nodes, :] = vec_ref[...].astype(f32)
    for o, ghost in enumerate((h0, h1, h2, h3)):
        ext_ref[nodes + o * slots : nodes + (o + 1) * slots, :] = ghost[...].astype(f32)

    def clear(step, _):
        rows = pl.ds(pl.multiple_of(step * 64, 64), 64)
        for a in acc:
            a[rows, :] = jnp.zeros((64, LANES), f32)
        return 0

    lax.fori_loop(0, ext // 64, clear, 0)
    cells = scale_ref.shape[0]
    for first in range(0, cells, GROUP):

        def gather(step, _):
            base = step * 8
            for u in range(8):
                for k in range(GROUP):
                    row = maps_ref[(first + k) * size + base + u]
                    in_ref[k, pl.ds(base + u, 1), :] = ext_ref[pl.ds(row, 1), :]
            return 0

        lax.fori_loop(0, size // 8, gather, 0)
        for k in range(0, GROUP, 2):
            pair = jnp.concatenate([in_ref[k].astype(bf16), in_ref[k + 1].astype(bf16)], 1)
            product = jnp.dot(matrix_ref[...], pair, preferred_element_type=f32)
            out_ref[k] = product[:, :LANES] * scale_ref[first + k]
            out_ref[k + 1] = product[:, LANES:] * scale_ref[first + k + 1]

        def scatter(step, _):
            base = step * 8
            for u in range(8):
                rows = [maps_ref[(first + k) * size + base + u] for k in range(GROUP)]
                sums = [
                    acc[k][pl.ds(rows[k], 1), :] + out_ref[k, pl.ds(base + u, 1), :]
                    for k in range(GROUP)
                ]
                for k in range(GROUP):
                    acc[k][pl.ds(rows[k], 1), :] = sums[k]
            return 0

        lax.fori_loop(0, size // 8, scatter, 0)

    def total(start):
        rows = pl.ds(start, 64)
        parts = [a[rows, :] for a in acc]
        while len(parts) > 1:
            parts = [parts[i] + parts[i + 1] for i in range(0, len(parts), 2)]
        return parts[0]

    def reduce_own(step, _):
        start = pl.multiple_of(step * 64, 64)
        own_ref[pl.ds(start, 64), :] = total(start)
        return 0

    lax.fori_loop(0, nodes // 64, reduce_own, 0)
    for o, ghost in enumerate((g0, g1, g2, g3)):
        for r in range(0, slots, 64):
            ghost[r : r + 64, :] = total(nodes + o * slots + r)


def apply_cells(maps, scale, matrix, vectors, ghosts):
    nodes, slots, size = vectors.shape[0], ghosts[0].shape[0], matrix.shape[0]
    ext = nodes + 4 * slots
    return pl.pallas_call(
        cells_kernel,
        out_shape=[jax.ShapeDtypeStruct((nodes, LANES), f32)]
        + [jax.ShapeDtypeStruct((slots, LANES), f32)] * 4,
        in_specs=[smem, smem] + [vmem] * 6,
        out_specs=[vmem] * 5,
        scratch_shapes=[
            pltpu.VMEM((ext, LANES), f32),
            pltpu.VMEM((GROUP, size, LANES), f32),
            pltpu.VMEM((GROUP, size, LANES), f32),
        ]
        + [pltpu.VMEM((ext, LANES), f32)] * GROUP,
        compiler_params=params,
    )(maps, scale, matrix, vectors, *ghosts)


def add_returned(faces_ref, returned, acc):
    spare = acc[0].shape[0] - 8
    slots = returned[0].shape[0]
    for a in acc:
        a[...] = jnp.zeros(a.shape, f32)

    def body(step, _):
        base = step * 4
        for u in range(4):
            rows = [faces_ref[o * slots + base + u] for o in range(4)]
            rows = [jnp.where(row < 0, spare, row) for row in rows]
            sums = [
                acc[o][pl.ds(rows[o], 1), :] + returned[o][pl.ds(base + u, 1), :]
                for o in range(4)
            ]
            for o in range(4):
                acc[o][pl.ds(rows[o], 1), :] = sums[o]
        return 0

    lax.fori_loop(0, slots // 4, body, 0)


def first_kernel(
    faces_ref, inv_ref, own_ref, coef_ref, vec_ref, r0, r1, r2, r3,
    out_ref, o0, o1, o2, o3, table_ref, rows_ref, *acc
):
    nodes = vec_ref.shape[0]
    add_returned(faces_ref, (r0, r1, r2, r3), acc)

    def combine(step, _):
        rows = pl.ds(pl.multiple_of(step * 64, 64), 64)
        image = own_ref[rows, :] + (
            (acc[0][rows, :] + acc[1][rows, :]) + (acc[2][rows, :] + acc[3][rows, :])
        )
        value = image * inv_ref[0] + coef_ref[rows, :] * vec_ref[rows, :].astype(f32)
        value = value.astype(bf16)
        out_ref[rows, :] = value
        table_ref[rows, :] = value.astype(f32)
        return 0

    lax.fori_loop(0, nodes // 64, combine, 0)
    table_ref[nodes : nodes + 8, :] = jnp.zeros((8, LANES), f32)
    gather_faces(faces_ref, table_ref, rows_ref, (o0, o1, o2, o3))


def second_kernel(
    faces_ref, inv_ref, own_ref, coef_ref, vec_ref, old_ref, r0, r1, r2, r3, out_ref, *acc
):
    nodes = vec_ref.shape[0]
    add_returned(faces_ref, (r0, r1, r2, r3), acc)

    def combine(step, _):
        rows = pl.ds(pl.multiple_of(step * 64, 64), 64)
        image = own_ref[rows, :] + (
            (acc[0][rows, :] + acc[1][rows, :]) + (acc[2][rows, :] + acc[3][rows, :])
        )
        value = image * inv_ref[0] + coef_ref[rows, :] * vec_ref[rows, :].astype(f32)
        out_ref[rows, :] = (2.0 * value - old_ref[rows, :].astype(f32)).astype(bf16)
        return 0

    lax.fori_loop(0, nodes // 64, combine, 0)


def finish_first(faces, inv, own, coef, vectors, returned):
    nodes, slots = vectors.shape[0], faces.shape[0] // 4
    return pl.pallas_call(
        first_kernel,
        out_shape=[jax.ShapeDtypeStruct((nodes, LANES), bf16)]
        + [jax.ShapeDtypeStruct((slots, LANES), bf16)] * 4,
        in_specs=[smem, smem] + [vmem] * 7,
        out_specs=[vmem] * 5,
        scratch_shapes=[
            pltpu.VMEM((nodes + 8, LANES), f32),
            pltpu.VMEM((4 * slots, LANES), f32),
        ]
        + [pltpu.VMEM((nodes + 8, LANES), f32)] * 4,
        compiler_params=params,
    )(faces, inv, own, coef, vectors, *returned)


def finish_second(faces, inv, own, coef, vectors, old, returned):
    nodes = vectors.shape[0]
    return pl.pallas_call(
        second_kernel,
        out_shape=jax.ShapeDtypeStruct((nodes, LANES), bf16),
        in_specs=[smem, smem] + [vmem] * 8,
        out_specs=vmem,
        scratch_shapes=[pltpu.VMEM((nodes + 8, LANES), f32)] * 4,
        compiler_params=params,
    )(faces, inv, own, coef, vectors, old, *returned)


def margin_kernel(band_ref, own_ref, other_ref, out_ref):
    half = LANES // 2
    nt = functools.partial(
        lax.dot_general,
        dimension_numbers=(((0,), (0,)), ((), ())),
        preferred_element_type=f32,
    )

    def write(low, high, band):
        low_rows = low[:, band * half : (band + 1) * half]
        high_rows = high[:, band * half : (band + 1) * half]
        block = nt(low_rows, low)
        cross = nt(low_rows, high)
        tail = nt(high_rows, high)
        row = lax.broadcasted_iota(jnp.int32, (half, LANES), 0) + band * half
        col = lax.broadcasted_iota(jnp.int32, (half, LANES), 1)
        out_ref[0:half, :] = jnp.where(col >= row, block, tail)
        out_ref[half : 2 * half, :] = cross
        diag = jnp.sum(jnp.where(col == row, tail, 0.0), 0, keepdims=True)
        out_ref[2 * half : 2 * half + 8, :] = jnp.broadcast_to(diag, (8, LANES))

    @pl.when(band_ref[0] == 0)
    def _():
        write(own_ref[...], other_ref[...], 0)

    @pl.when(band_ref[0] != 0)
    def _():
        write(other_ref[...], own_ref[...], 1)


def margin_rows(band, own, other):
    return pl.pallas_call(
        margin_kernel,
        out_shape=jax.ShapeDtypeStruct((LANES + 8, LANES), f32),
        in_specs=[smem, vmem, vmem],
        out_specs=vmem,
        compiler_params=params,
    )(band, own, other)


def split_three(x):
    high = x.astype(bf16)
    rest = x - high.astype(f32)
    mid = rest.astype(bf16)
    return high, mid, (rest - mid.astype(f32)).astype(bf16)


def invert_factor(work_ref, panel_ref):
    total = work_ref.shape[0]
    col = lax.broadcasted_iota(jnp.int32, (PANEL, total), 1)
    row = lax.broadcasted_iota(jnp.int32, (PANEL, total), 0)

    def step(p, start_row):
        first = pl.multiple_of(p * PANEL, PANEL)
        rows = work_ref[pl.ds(first, PANEL), :]
        halves = [rows[:, h * LANES : (h + 1) * LANES] for h in range(total // LANES)]
        block = halves[start_row // LANES]
        block = pltpu.roll(block, lax.rem(total - first, LANES), 1)
        columns = [
            jnp.broadcast_to(block[:, k : k + 1], (PANEL, LANES)) for k in range(PANEL)
        ]
        entry = {
            (i, k): columns[k][i : i + 1, :] for i in range(PANEL) for k in range(i + 1)
        }
        panel = jnp.where((col >= first) & (col < first + PANEL), 0.0, rows)
        panel = jnp.where(col == row + first, 1.0, panel)
        done = []
        for k in range(PANEL):
            pivot = entry[k, k]
            scale = lax.rsqrt(pivot)
            scale = scale * (1.5 - 0.5 * pivot * scale * scale)
            for i in range(k + 1, PANEL):
                entry[i, k] = entry[i, k] * scale
            for i in range(k + 1, PANEL):
                for m in range(k + 1, i + 1):
                    entry[i, m] = entry[i, m] - entry[i, k] * entry[m, k]
            line = panel[k : k + 1, :]
            wide = lambda x: jnp.concatenate([x] * (total // LANES), 1)
            for m in range(k):
                line = line - wide(entry[k, m]) * done[m]
            line = line * wide(scale)
            done.append(line)
            panel_ref[k : k + 1, :] = line
        panel = panel_ref[...]
        right = jnp.where(col >= first + PANEL, panel, 0.0)
        ah, am, al = split_three(right)
        bh, bm, bl = split_three(panel)
        lhs = jnp.concatenate([x.astype(f32) for x in (ah, ah, am, am, ah, al)], 0).astype(bf16)
        rhs = jnp.concatenate([x.astype(f32) for x in (bh, bm, bh, bm, bl, bh)], 0).astype(bf16)
        update = lax.dot_general(
            lhs[:, start_row:], rhs, (((0,), (0,)), ((), ())), preferred_element_type=f32
        )
        below = work_ref[start_row:, :]
        big = lax.broadcasted_iota(jnp.int32, below.shape, 1)
        inside = (big >= first) & (big < first + PANEL)
        work_ref[start_row:, :] = jnp.where(inside, 0.0, below) - update
        work_ref[pl.ds(first, PANEL), :] = panel

    per = LANES // PANEL
    for h in range(total // LANES):
        lax.fori_loop(h * per, (h + 1) * per, lambda p, _: (step(p, h * LANES), 0)[1], 0)


def rotate_kernel(
    band_ref, count_ref, mine_ref, theirs_ref, own_ref, other_ref, out_ref, work_ref, panel_ref
):
    half = LANES // 2
    band = band_ref[0]
    mine, theirs = mine_ref[...] * count_ref[0], theirs_ref[...] * count_ref[0]
    top = jnp.where(band == 0, mine, theirs)
    bottom = jnp.where(band == 0, theirs, mine)
    packed = jnp.concatenate([top[0:half], bottom[0:half]], 0)
    cross = jnp.concatenate([top[half:LANES], bottom[half:LANES]], 0)
    diag = top[LANES : LANES + 1] + bottom[LANES : LANES + 1]
    flipped = packed.T
    row = lax.broadcasted_iota(jnp.int32, (LANES, LANES), 0)
    col = lax.broadcasted_iota(jnp.int32, (LANES, LANES), 1)
    work_ref[0:LANES, 0:LANES] = jnp.where(col >= row, packed, flipped)
    work_ref[0:LANES, LANES:] = cross
    work_ref[LANES:, 0:LANES] = cross.T
    tail = jnp.where(col < row, packed, flipped)
    work_ref[LANES:, LANES:] = jnp.where(col == row, jnp.broadcast_to(diag, tail.shape), tail)
    invert_factor(work_ref, panel_ref)
    lower = jnp.where(col <= row, 1.0, 0.0)
    first = work_ref[0:LANES, 0:LANES] * lower
    last = work_ref[LANES:, LANES:] * lower
    corner = work_ref[LANES:, 0:LANES]
    from_own = jnp.where(band == 0, first, last)
    from_other = jnp.where(band == 0, jnp.zeros_like(corner), corner)
    weights = jnp.concatenate([from_own, from_other], 1)
    high = weights.astype(bf16)
    low = (weights - high.astype(f32)).astype(bf16)
    weights = jnp.concatenate([high, low], 0)
    chunk = 512

    def body(step, _):
        rows = pl.ds(pl.multiple_of(step * chunk, chunk), chunk)
        both = jnp.concatenate([own_ref[rows, :], other_ref[rows, :]], 1)
        product = lax.dot_general(
            both, weights, (((1,), (1,)), ((), ())), preferred_element_type=f32
        )
        out_ref[rows, :] = product[:, :LANES] + product[:, LANES:]
        return 0

    lax.fori_loop(0, own_ref.shape[0] // chunk, body, 0)


def rotate(band, inv_count, mine, theirs, own, other):
    return pl.pallas_call(
        rotate_kernel,
        out_shape=jax.ShapeDtypeStruct(own.shape, f32),
        in_specs=[smem, smem] + [vmem] * 4,
        out_specs=vmem,
        scratch_shapes=[pltpu.VMEM((2 * LANES, 2 * LANES), f32), pltpu.VMEM((PANEL, 2 * LANES), f32)],
        compiler_params=params,
    )(band, inv_count, mine, theirs, own, other)


def summed_over(value, axis):
    size = lax.axis_size(axis)
    if size & (size - 1):
        return lax.psum(value, axis)
    stride = 1
    while stride < size:
        value = value + lax.ppermute(value, axis, [(i, i ^ stride) for i in range(size)])
        stride *= 2
    return value


def swapped(value):
    return lax.ppermute(value, "band", [(0, 1), (1, 0)])


def on_device(wavefunctions, bounds, cell_matrix, cell_scale, potential, cell_nodes, face_nodes):
    nodes, columns = wavefunctions.shape
    maps = cell_nodes.reshape(-1)
    faces = face_nodes.reshape(-1)
    center = (bounds[0] + bounds[1]) / 2.0
    half_width = (bounds[1] - bounds[0]) / 2.0
    inv = (1.0 / half_width).reshape(1)
    coef = jnp.broadcast_to(((potential - center) / half_width)[:, None], (nodes, columns))

    def forward(blocks):
        return [passed_along(blocks[o], "dom", peer_offsets[o]) for o in range(4)]

    def backward(blocks):
        return [passed_along(blocks[o], "dom", -peer_offsets[o]) for o in range(4)]

    ghosts = forward(send_faces(faces, wavefunctions))
    own, *sums = apply_cells(maps, cell_scale, cell_matrix, wavefunctions, ghosts)
    degree_one, *blocks = finish_first(faces, inv, own, coef, wavefunctions, backward(sums))
    own, *sums = apply_cells(maps, cell_scale, cell_matrix, degree_one, forward(blocks))
    degree_two = finish_second(
        faces, inv, own, coef, degree_one, wavefunctions, backward(sums)
    )
    other = swapped(degree_two)
    band = lax.axis_index("band").astype(jnp.int32).reshape(1)
    mine = summed_over(margin_rows(band, degree_two, other), "dom")
    inv_count = jnp.full((1,), 1.0 / (nodes * lax.axis_size("dom")), f32)
    return rotate(band, inv_count, mine, swapped(mine), degree_two, other)


def solution(mesh):
    return jax.shard_map(
        on_device,
        mesh=mesh,
        in_specs=(
            P(("kpt", "dom"), "band"),
            P("kpt"),
            P(),
            P("dom"),
            P("dom"),
            P("dom", None),
            P("dom", None),
        ),
        out_specs=P(("kpt", "dom"), "band"),
        check_vma=False,
    )
```

time: 442 us -> 181 us (0.41)
  other arithmetic: 172 us -> 0.92 us
  Pallas kernels: 0 us -> 86.6 us
  local copies, waits for them, and re-layouts: 86.9 us -> 9.52 us
  waiting for transfers between devices: 96.9 us -> 23.3 us
  matrix products: 18.4 us -> 0 us
  between operations: 17.8 us -> 2.91 us
  starting transfers between devices: 46 us -> 56.8 us
    scatter-add x4 -> x0, other arithmetic: 108 us -> none  [the longest x2 91.9 us: apply_operator(): jax.ops.segment_sum(products.reshape(-1, columns), flat_maps, num_segment...]
    pallas_call x0 -> x7, Pallas kernels: none -> 86.6 us  [the longest x2 42.8 us: apply_cells(): pl.pallas_call(cells_kernel, out_shape=[jax.ShapeDtypeStruct((nodes, LANE...]
    psum x1 -> x0, waiting for transfers between devices: 71 us -> none  [on_device(): margin_part = lax.psum(margin_part, 'dom')]
    gather x4 -> x0, local copies, waits for them, and re-layouts: 67.4 us -> none  [the longest x2 59 us: apply_operator(): gathered = extended[cell_nodes]]
    another operation x11 -> x0, other arithmetic: 54.6 us -> none  [the longest x6 34 us: on_device(): factor = jnp.linalg.cholesky(margin)]
    dot_general x4 -> x0, matrix products: 17.1 us -> none  [the longest x2 10.5 us: apply_operator(): jnp.einsum('ij,cjk->cik', cell_matrix, gathered, preferred_element_type=j...]
    ppermute x0 -> x5, waiting for transfers between devices: none -> 12.1 us  [the longest x3 8 us: summed_over(): lax.ppermute(value, axis, [(i, i ^ stride) for i in range(size)])]
    all_gather x1 -> x0, waiting for transfers between devices: 11.4 us -> none  [on_device(): panel_all = lax.all_gather(degree_two, 'band', axis=1, tiled=True)]
  transfers between devices with their start and end apart: 18 -> 21, of which waited for: 9 -> 12; matrix products, arithmetic and copies ran while one was open for 0% -> 2% of each run, Pallas kernels for 0% -> 0%
where the time goes in v1:
time: 181 us; the launch traced here: 180 us
  Pallas kernels  86.6 us (48%)
  starting transfers between devices  56.8 us (31%)
  waiting for transfers between devices  23.3 us (13%)
  local copies, waits for them, and re-layouts  9.52 us (5%)
  between operations  2.91 us (2%)
    ppermute x16, starting transfers between devices, passed_along(): return lax.ppermute(value, axis, pairs)  48 us
    pallas_call x2, Pallas kernels, apply_cells(): pl.pallas_call(cells_kernel, out_shape=[jax.ShapeDtypeStruct((nodes, LANE...  42.8 us
    pallas_call x1, Pallas kernels, rotate(): pl.pallas_call(rotate_kernel, out_shape=jax.ShapeDtypeStruct(own.shape, f...  20.4 us
    ppermute x16, waiting for transfers between devices, passed_along(): return lax.ppermute(value, axis, pairs)  11.2 us
    pallas_call x1, Pallas kernels, finish_first(): pl.pallas_call(first_kernel, out_shape=[jax.ShapeDtypeStruct((nodes, LANE...  9.03 us
    ppermute x3, starting transfers between devices, summed_over(): lax.ppermute(value, axis, [(i, i ^ stride) for i in range(size)])  8.69 us
    ppermute x3, waiting for transfers between devices, summed_over(): lax.ppermute(value, axis, [(i, i ^ stride) for i in range(size)])  8 us
    pallas_call x1, Pallas kernels, finish_second(): pl.pallas_call(second_kernel, out_shape=jax.ShapeDtypeStruct((nodes, LANE...  7.76 us
  transfers between devices with their start and end apart: 21, of which 12 were waited for; matrix products, arithmetic and copies ran while one was open for 2% of the time, Pallas kernels for 0%

profile of v1, /device:TPU:0, one launch (start us, length us, event | category | flops | bytes accessed | tf_op | source)
XLA Modules:
  0.0 180.1 jit_solution(8880217331433421190)
XLA Ops:
  1.3 3.7 %shard_map.73 = (bf16[256,128]{1,0:T(8,128)(2,1)}, bf16[256,128]{1,0:T(8,128)(2,1)}, bf16[256,128]{1,0:T(8,128)(2,1)}, bf16[256,128]{1,0:T(8,128)(2,1)}) custom-call(s32[1024]{0:T(1024)} %bitcast.10, bf16[4096,128]{1,0:T(8,128)(2,1)} %old_ref.1), custom_call_target="tpu_custom_call" | custom-call | tf_op jit(solution)/shard_map/pallas_call | solution.py:50
  5.0 4.8 %collective-permute-start = (bf16[256,128]{1,0:T(8,128)(2,1)}, bf16[256,128]{1,0:T(8,128)(2,1)S(1)}, u32[]{:S(2)}, u32[]{:S(2)}) collective-permute-start(bf16[256,128]{1,0:T(8,128)(2,1)} %get-tuple-element.24), channel_id=1, source_target_pairs={{0,2},{2,4},{4,6},{6,8},{8,10},{10,12},{12,14},{1,3},{3,5},{5,7},{... | collective-permute-start | bytes 196616 | tf_op jit(solution)/shard_map/ppermute | solution.py:21
  11.2 5.5 %collective-permute-start.2 = (bf16[256,128]{1,0:T(8,128)(2,1)}, bf16[256,128]{1,0:T(8,128)(2,1)S(1)}, u32[]{:S(2)}, u32[]{:S(2)}) collective-permute-start(bf16[256,128]{1,0:T(8,128)(2,1)} %get-tuple-element.26), channel_id=1, source_target_pairs={{0,4},{2,6},{4,8},{6,10},{8,12},{10,14},{1,5},{3,7},{5,9},{7,11},{... | collective-permute-start | bytes 196616 | tf_op jit(solution)/shard_map/ppermute | solution.py:21
  24.0 21.4 %shard_map.74 = (f32[4096,128]{1,0:T(8,128)}, f32[256,128]{1,0:T(8,128)}, f32[256,128]{1,0:T(8,128)}, f32[256,128]{1,0:T(8,128)}, f32[256,128]{1,0:T(8,128)}) custom-call(s32[8192]{0:T(1024)} %bitcast.8, f32[16]{0:T(128)} %scale_ref.3, bf16[512,512]{1,0:T(8,128)(2,1)} %matrix_ref.3, bf16[4096,128]{1,0:T(8,128)(2,1)} %old_ref.1, bf16[256,128]{1,0:T(8,128)(2,1)} %copy-done.11, ...), custom_call_target="tpu_custom_call" | custom-call | tf_op jit(solution)/shard_map/pallas_call | solution.py:134
  46.7 4.6 %collective-permute-start.5 = (f32[256,128]{1,0:T(8,128)}, f32[256,128]{1,0:T(8,128)S(1)}, u32[]{:S(2)}, u32[]{:S(2)}) collective-permute-start(f32[256,128]{1,0:T(8,128)} %get-tuple-element.30), channel_id=1, source_target_pairs={{0,2},{2,4},{4,6},{6,8},{8,10},{10,12},{12,14},{1,3},{3,5},{5,7},{... | collective-permute-start | bytes 393224 | tf_op jit(solution)/shard_map/ppermute | solution.py:21
  52.6 5.2 %collective-permute-start.7 = (f32[256,128]{1,0:T(8,128)}, f32[256,128]{1,0:T(8,128)S(1)}, u32[]{:S(2)}, u32[]{:S(2)}) collective-permute-start(f32[256,128]{1,0:T(8,128)} %get-tuple-element.32), channel_id=1, source_target_pairs={{0,4},{2,6},{4,8},{6,10},{8,12},{10,14},{1,5},{3,7},{5,9},{7,11},{... | collective-permute-start | bytes 393224 | tf_op jit(solution)/shard_map/ppermute | solution.py:21
  60.6 2.0 %broadcast_in_dim.2.coef_ref = f32[4096,128]{1,0:T(8,128)} broadcast(f32[4096]{0:T(1024)S(1)} %subtract_divide_fusion), dimensions={0} | broadcast | bytes 2113536 | tf_op jit(solution)/shard_map/broadcast_in_dim | solution.py:422
  62.5 9.0 %shard_map.75 = (bf16[4096,128]{1,0:T(8,128)(2,1)}, bf16[256,128]{1,0:T(8,128)(2,1)}, bf16[256,128]{1,0:T(8,128)(2,1)}, bf16[256,128]{1,0:T(8,128)(2,1)}, bf16[256,128]{1,0:T(8,128)(2,1)}) custom-call(s32[1024]{0:T(1024)} %bitcast.11, f32[1]{0:T(128)} %bitcast.2.inv_ref, f32[4096,128]{1,0:T(8,128)} %get-tuple-element.28.own_ref, ...), custom_call_target="tpu_custom_call" | custom-call | tf_op jit(solution)/shard_map/pallas_call | solution.py:215
  71.6 4.2 %collective-permute-start.10 = (bf16[256,128]{1,0:T(8,128)(2,1)}, bf16[256,128]{1,0:T(8,128)(2,1)S(1)}, u32[]{:S(2)}, u32[]{:S(2)}) collective-permute-start(bf16[256,128]{1,0:T(8,128)(2,1)} %get-tuple-element.36), channel_id=1, source_target_pairs={{0,4},{2,6},{4,8},{6,10},{8,12},{10,14},{1,5},{3,7},{5,9},{7,11},{... | collective-permute-start | bytes 196616 | tf_op jit(solution)/shard_map/ppermute | solution.py:21
  77.1 3.4 %collective-permute-start.8 = (bf16[256,128]{1,0:T(8,128)(2,1)}, bf16[256,128]{1,0:T(8,128)(2,1)S(1)}, u32[]{:S(2)}, u32[]{:S(2)}) collective-permute-start(bf16[256,128]{1,0:T(8,128)(2,1)} %get-tuple-element.34), channel_id=1, source_target_pairs={{0,2},{2,4},{4,6},{6,8},{8,10},{10,12},{12,14},{1,3},{3,5},{5,7},{... | collective-permute-start | bytes 196616 | tf_op jit(solution)/shard_map/ppermute | solution.py:21
  82.7 4.8 %collective-permute-done.9.h1 = bf16[256,128]{1,0:T(8,128)(2,1)S(1)} collective-permute-done((bf16[256,128]{1,0:T(8,128)(2,1)}, bf16[256,128]{1,0:T(8,128)(2,1)S(1)}, u32[]{:S(2)}, u32[]{:S(2)}) %collective-permute-start.9) | collective-permute-done | bytes 65568 | tf_op jit(solution)/shard_map/ppermute | solution.py:21
  88.1 21.4 %shard_map.76 = (f32[4096,128]{1,0:T(8,128)}, f32[256,128]{1,0:T(8,128)}, f32[256,128]{1,0:T(8,128)}, f32[256,128]{1,0:T(8,128)}, f32[256,128]{1,0:T(8,128)}) custom-call(s32[8192]{0:T(1024)} %bitcast.9, f32[16]{0:T(128)} %scale_ref.3, bf16[512,512]{1,0:T(8,128)(2,1)} %matrix_ref.3, bf16[4096,128]{1,0:T(8,128)(2,1)} %get-tuple-element.33.vec_ref, ...), custom_call_target="tpu_custom_call" | custom-call | tf_op jit(solution)/shard_map/pallas_call | solution.py:134
  110.8 5.5 %collective-permute-start.13 = (f32[256,128]{1,0:T(8,128)}, f32[256,128]{1,0:T(8,128)S(1)}, u32[]{:S(2)}, u32[]{:S(2)}) collective-permute-start(f32[256,128]{1,0:T(8,128)} %get-tuple-element.40), channel_id=1, source_target_pairs={{0,2},{2,4},{4,6},{6,8},{8,10},{10,12},{12,14},{1,3},{3,5},{5,7},{... | collective-permute-start | bytes 393224 | tf_op jit(solution)/shard_map/ppermute | solution.py:21
  117.6 4.6 %collective-permute-start.15 = (f32[256,128]{1,0:T(8,128)}, f32[256,128]{1,0:T(8,128)S(1)}, u32[]{:S(2)}, u32[]{:S(2)}) collective-permute-start(f32[256,128]{1,0:T(8,128)} %get-tuple-element.42), channel_id=1, source_target_pairs={{0,4},{2,6},{4,8},{6,10},{8,12},{10,14},{1,5},{3,7},{5,9},{7,11},{... | collective-permute-start | bytes 393224 | tf_op jit(solution)/shard_map/ppermute | solution.py:21
  125.6 7.8 %shard_map.77.own_ref = bf16[4096,128]{1,0:T(8,128)(2,1)} custom-call(s32[1024]{0:T(1024)} %bitcast.12, f32[1]{0:T(128)} %bitcast.2.inv_ref, f32[4096,128]{1,0:T(8,128)} %get-tuple-element.38.own_ref, f32[4096,128]{1,0:T(8,128)} %broadcast_in_dim.2.coef_ref, bf16[4096,128]{1,0:T(8,128)(2,1)} %get-tuple-element.33.vec_ref, bf16[4096,128]{1,0:T(8,128)(2,1)} %old_ref.1, ...), custom_call_target="tpu_custom_call" | custom-call | tf_op jit(solution)/shard_map/pallas_call | solution.py:232
  133.4 2.9 %collective-permute-done.16.other_ref = bf16[4096,128]{1,0:T(8,128)(2,1)S(1)} collective-permute-done((bf16[4096,128]{1,0:T(8,128)(2,1)}, bf16[4096,128]{1,0:T(8,128)(2,1)S(1)}, u32[]{:S(2)}, u32[]{:S(2)}) %collective-permute-start.16) | collective-permute-done | bytes 1048608 | tf_op jit(solution)/shard_map/ppermute | solution.py:412
  137.2 2.9 %shard_map.78 = f32[136,128]{1,0:T(8,128)} custom-call(s32[1]{0:T(128)} %bitcast.band_ref, bf16[4096,128]{1,0:T(8,128)(2,1)} %shard_map.77.own_ref, bf16[4096,128]{1,0:T(8,128)(2,1)} %copy-done), custom_call_target="tpu_custom_call" | custom-call | tf_op jit(solution)/shard_map/pallas_call | solution.py:273
  140.1 2.9 %collective-permute-start.17 = (f32[136,128]{1,0:T(8,128)}, f32[136,128]{1,0:T(8,128)S(1)}, u32[]{:S(2)}, u32[]{:S(2)}) collective-permute-start(f32[136,128]{1,0:T(8,128)} %shard_map.78), channel_id=1, source_target_pairs={{0,2},{2,0},{4,6},{6,4},{8,10},{10,8},{12,14},{14,12},{1,3},{3,1},... | collective-permute-start | bytes 208904 | tf_op jit(solution)/shard_map/ppermute | solution.py:406
  143.1 3.2 %collective-permute-done.17 = f32[136,128]{1,0:T(8,128)S(1)} collective-permute-done((f32[136,128]{1,0:T(8,128)}, f32[136,128]{1,0:T(8,128)S(1)}, u32[]{:S(2)}, u32[]{:S(2)}) %collective-permute-start.17) | collective-permute-done | bytes 69664 | tf_op jit(solution)/shard_map/ppermute | solution.py:406
  147.2 2.4 %collective-permute-start.18 = (f32[136,128]{1,0:T(8,128)S(1)}, f32[136,128]{1,0:T(8,128)S(1)}, u32[]{:S(2)}, u32[]{:S(2)}) collective-permute-start(f32[136,128]{1,0:T(8,128)S(1)} %add.14), channel_id=1, source_target_pairs={{0,4},{2,6},{4,0},{6,2},{8,12},{10,14},{12,8},{14,10},{1,5},{3,7},... | collective-permute-start | bytes 208904 | tf_op jit(solution)/shard_map/ppermute | solution.py:406
  149.6 2.5 %collective-permute-done.18 = f32[136,128]{1,0:T(8,128)S(1)} collective-permute-done((f32[136,128]{1,0:T(8,128)S(1)}, f32[136,128]{1,0:T(8,128)S(1)}, u32[]{:S(2)}, u32[]{:S(2)}) %collective-permute-start.18) | collective-permute-done | bytes 69664 | tf_op jit(solution)/shard_map/ppermute | solution.py:406
  152.0 3.4 %collective-permute-start.19 = (f32[136,128]{1,0:T(8,128)S(1)}, f32[136,128]{1,0:T(8,128)S(1)}, u32[]{:S(2)}, u32[]{:S(2)}) collective-permute-start(f32[136,128]{1,0:T(8,128)S(1)} %add.15), channel_id=1, source_target_pairs={{0,8},{2,10},{4,12},{6,14},{8,0},{10,2},{12,4},{14,6},{1,9},{3,11}... | collective-permute-start | bytes 208904 | tf_op jit(solution)/shard_map/ppermute | solution.py:406
  155.4 2.3 %collective-permute-done.19 = f32[136,128]{1,0:T(8,128)S(1)} collective-permute-done((f32[136,128]{1,0:T(8,128)S(1)}, f32[136,128]{1,0:T(8,128)S(1)}, u32[]{:S(2)}, u32[]{:S(2)}) %collective-permute-start.19) | collective-permute-done | bytes 69664 | tf_op jit(solution)/shard_map/ppermute | solution.py:406
  159.7 20.4 %shard_map.79 = f32[4096,128]{1,0:T(8,128)} custom-call(s32[1]{0:T(128)} %bitcast.band_ref, f32[1]{0:T(128)} %constant.11.clone.1.count_ref, f32[136,128]{1,0:T(8,128)} %copy-done.1, f32[136,128]{1,0:T(8,128)} %copy-done.10, bf16[4096,128]{1,0:T(8,128)(2,1)} %shard_map.77.own_ref, bf16[4096,128]{1,0:T(8,128)(2,1)} %copy-done), custom_call_target="tpu_custom_call" | custom-call | tf_op jit(solution)/shard_map/pallas_call | solution.py:390
  (73 shorter events, 26.5 us)
Async XLA Ops:
  0.0 57.8 %copy-start.19 = (f32[4096]{0:T(1024)S(1)}, f32[4096]{0:T(1024)}, u32[]{:S(2)}) copy-start(f32[4096]{0:T(1024)} %param.11) | copy-start | bytes 49156
  5.0 18.3 %collective-permute-start = (bf16[256,128]{1,0:T(8,128)(2,1)}, bf16[256,128]{1,0:T(8,128)(2,1)S(1)}, u32[]{:S(2)}, u32[]{:S(2)}) collective-permute-start(bf16[256,128]{1,0:T(8,128)(2,1)} %get-tuple-element.24), channel_id=1, source_target_pairs={{0,2},{2,4},{4,6},{6,8},{8,10},{10,12},{12,14},{1,3},{3,5},{5,7},{... | collective-permute-start | bytes 196616 | tf_op jit(solution)/shard_map/ppermute | solution.py:21
  9.9 13.4 %collective-permute-start.1 = (bf16[256,128]{1,0:T(8,128)(2,1)}, bf16[256,128]{1,0:T(8,128)(2,1)S(1)}, u32[]{:S(2)}, u32[]{:S(2)}) collective-permute-start(bf16[256,128]{1,0:T(8,128)(2,1)} %get-tuple-element.25), channel_id=1, source_target_pairs={{2,0},{4,2},{6,4},{8,6},{10,8},{12,10},{14,12},{3,1},{5,3},{7,5},{... | collective-permute-start | bytes 196616 | tf_op jit(solution)/shard_map/ppermute | solution.py:21
  11.2 12.2 %collective-permute-start.2 = (bf16[256,128]{1,0:T(8,128)(2,1)}, bf16[256,128]{1,0:T(8,128)(2,1)S(1)}, u32[]{:S(2)}, u32[]{:S(2)}) collective-permute-start(bf16[256,128]{1,0:T(8,128)(2,1)} %get-tuple-element.26), channel_id=1, source_target_pairs={{0,4},{2,6},{4,8},{6,10},{8,12},{10,14},{1,5},{3,7},{5,9},{7,11},{... | collective-permute-start | bytes 196616 | tf_op jit(solution)/shard_map/ppermute | solution.py:21
  16.7 6.6 %collective-permute-start.3 = (bf16[256,128]{1,0:T(8,128)(2,1)}, bf16[256,128]{1,0:T(8,128)(2,1)S(1)}, u32[]{:S(2)}, u32[]{:S(2)}) collective-permute-start(bf16[256,128]{1,0:T(8,128)(2,1)} %get-tuple-element.27), channel_id=1, source_target_pairs={{4,0},{6,2},{8,4},{10,6},{12,8},{14,10},{5,1},{7,3},{9,5},{11,7},{... | collective-permute-start | bytes 196616 | tf_op jit(solution)/shard_map/ppermute | solution.py:21
  45.4 12.4 %collective-permute-start.4 = (f32[256,128]{1,0:T(8,128)}, f32[256,128]{1,0:T(8,128)S(1)}, u32[]{:S(2)}, u32[]{:S(2)}) collective-permute-start(f32[256,128]{1,0:T(8,128)} %get-tuple-element.29), channel_id=1, source_target_pairs={{2,0},{4,2},{6,4},{8,6},{10,8},{12,10},{14,12},{3,1},{5,3},{7,5},{... | collective-permute-start | bytes 393224 | tf_op jit(solution)/shard_map/ppermute | solution.py:21
  46.7 11.1 %collective-permute-start.5 = (f32[256,128]{1,0:T(8,128)}, f32[256,128]{1,0:T(8,128)S(1)}, u32[]{:S(2)}, u32[]{:S(2)}) collective-permute-start(f32[256,128]{1,0:T(8,128)} %get-tuple-element.30), channel_id=1, source_target_pairs={{0,2},{2,4},{4,6},{6,8},{8,10},{10,12},{12,14},{1,3},{3,5},{5,7},{... | collective-permute-start | bytes 393224 | tf_op jit(solution)/shard_map/ppermute | solution.py:21
  51.3 7.7 %collective-permute-start.6 = (f32[256,128]{1,0:T(8,128)}, f32[256,128]{1,0:T(8,128)S(1)}, u32[]{:S(2)}, u32[]{:S(2)}) collective-permute-start(f32[256,128]{1,0:T(8,128)} %get-tuple-element.31), channel_id=1, source_target_pairs={{4,0},{6,2},{8,4},{10,6},{12,8},{14,10},{5,1},{7,3},{9,5},{11,7},{... | collective-permute-start | bytes 393224 | tf_op jit(solution)/shard_map/ppermute | solution.py:21
  52.6 8.0 %collective-permute-start.7 = (f32[256,128]{1,0:T(8,128)}, f32[256,128]{1,0:T(8,128)S(1)}, u32[]{:S(2)}, u32[]{:S(2)}) collective-permute-start(f32[256,128]{1,0:T(8,128)} %get-tuple-element.32), channel_id=1, source_target_pairs={{0,4},{2,6},{4,8},{6,10},{8,12},{10,14},{1,5},{3,7},{5,9},{7,11},{... | collective-permute-start | bytes 393224 | tf_op jit(solution)/shard_map/ppermute | solution.py:21
  71.6 10.3 %collective-permute-start.10 = (bf16[256,128]{1,0:T(8,128)(2,1)}, bf16[256,128]{1,0:T(8,128)(2,1)S(1)}, u32[]{:S(2)}, u32[]{:S(2)}) collective-permute-start(bf16[256,128]{1,0:T(8,128)(2,1)} %get-tuple-element.36), channel_id=1, source_target_pairs={{0,4},{2,6},{4,8},{6,10},{8,12},{10,14},{1,5},{3,7},{5,9},{7,11},{... | collective-permute-start | bytes 196616 | tf_op jit(solution)/shard_map/ppermute | solution.py:21
  75.8 6.4 %collective-permute-start.11 = (bf16[256,128]{1,0:T(8,128)(2,1)}, bf16[256,128]{1,0:T(8,128)(2,1)S(1)}, u32[]{:S(2)}, u32[]{:S(2)}) collective-permute-start(bf16[256,128]{1,0:T(8,128)(2,1)} %get-tuple-element.37), channel_id=1, source_target_pairs={{4,0},{6,2},{8,4},{10,6},{12,8},{14,10},{5,1},{7,3},{9,5},{11,7},{... | collective-permute-start | bytes 196616 | tf_op jit(solution)/shard_map/ppermute | solution.py:21
  77.1 5.6 %collective-permute-start.8 = (bf16[256,128]{1,0:T(8,128)(2,1)}, bf16[256,128]{1,0:T(8,128)(2,1)S(1)}, u32[]{:S(2)}, u32[]{:S(2)}) collective-permute-start(bf16[256,128]{1,0:T(8,128)(2,1)} %get-tuple-element.34), channel_id=1, source_target_pairs={{0,2},{2,4},{4,6},{6,8},{8,10},{10,12},{12,14},{1,3},{3,5},{5,7},{... | collective-permute-start | bytes 196616 | tf_op jit(solution)/shard_map/ppermute | solution.py:21
  80.5 7.0 %collective-permute-start.9 = (bf16[256,128]{1,0:T(8,128)(2,1)}, bf16[256,128]{1,0:T(8,128)(2,1)S(1)}, u32[]{:S(2)}, u32[]{:S(2)}) collective-permute-start(bf16[256,128]{1,0:T(8,128)(2,1)} %get-tuple-element.35), channel_id=1, source_target_pairs={{2,0},{4,2},{6,4},{8,6},{10,8},{12,10},{14,12},{3,1},{5,3},{7,5},{... | collective-permute-start | bytes 196616 | tf_op jit(solution)/shard_map/ppermute | solution.py:21
  81.8 5.7 %copy-start.15 = (bf16[256,128]{1,0:T(8,128)(2,1)}, bf16[256,128]{1,0:T(8,128)(2,1)S(1)}, u32[]{:S(2)}) copy-start(bf16[256,128]{1,0:T(8,128)(2,1)S(1)} %collective-permute-done.10.h2) | copy-start | bytes 196612
  82.2 5.3 %copy-start.16 = (bf16[256,128]{1,0:T(8,128)(2,1)}, bf16[256,128]{1,0:T(8,128)(2,1)S(1)}, u32[]{:S(2)}) copy-start(bf16[256,128]{1,0:T(8,128)(2,1)S(1)} %collective-permute-done.11.h3) | copy-start | bytes 196612
  109.5 12.6 %collective-permute-start.12 = (f32[256,128]{1,0:T(8,128)}, f32[256,128]{1,0:T(8,128)S(1)}, u32[]{:S(2)}, u32[]{:S(2)}) collective-permute-start(f32[256,128]{1,0:T(8,128)} %get-tuple-element.39), channel_id=1, source_target_pairs={{2,0},{4,2},{6,4},{8,6},{10,8},{12,10},{14,12},{3,1},{5,3},{7,5},{... | collective-permute-start | bytes 393224 | tf_op jit(solution)/shard_map/ppermute | solution.py:21
  110.8 11.3 %collective-permute-start.13 = (f32[256,128]{1,0:T(8,128)}, f32[256,128]{1,0:T(8,128)S(1)}, u32[]{:S(2)}, u32[]{:S(2)}) collective-permute-start(f32[256,128]{1,0:T(8,128)} %get-tuple-element.40), channel_id=1, source_target_pairs={{0,2},{2,4},{4,6},{6,8},{8,10},{10,12},{12,14},{1,3},{3,5},{5,7},{... | collective-permute-start | bytes 393224 | tf_op jit(solution)/shard_map/ppermute | solution.py:21
  116.3 7.1 %collective-permute-start.14 = (f32[256,128]{1,0:T(8,128)}, f32[256,128]{1,0:T(8,128)S(1)}, u32[]{:S(2)}, u32[]{:S(2)}) collective-permute-start(f32[256,128]{1,0:T(8,128)} %get-tuple-element.41), channel_id=1, source_target_pairs={{4,0},{6,2},{8,4},{10,6},{12,8},{14,10},{5,1},{7,3},{9,5},{11,7},{... | collective-permute-start | bytes 393224 | tf_op jit(solution)/shard_map/ppermute | solution.py:21
  117.6 7.4 %collective-permute-start.15 = (f32[256,128]{1,0:T(8,128)}, f32[256,128]{1,0:T(8,128)S(1)}, u32[]{:S(2)}, u32[]{:S(2)}) collective-permute-start(f32[256,128]{1,0:T(8,128)} %get-tuple-element.42), channel_id=1, source_target_pairs={{0,4},{2,6},{4,8},{6,10},{8,12},{10,14},{1,5},{3,7},{5,9},{7,11},{... | collective-permute-start | bytes 393224 | tf_op jit(solution)/shard_map/ppermute | solution.py:21
  133.3 2.9 %collective-permute-start.16 = (bf16[4096,128]{1,0:T(8,128)(2,1)}, bf16[4096,128]{1,0:T(8,128)(2,1)S(1)}, u32[]{:S(2)}, u32[]{:S(2)}) collective-permute-start(bf16[4096,128]{1,0:T(8,128)(2,1)} %shard_map.77.own_ref), channel_id=1, source_target_pairs={{0,1},{1,0},{2,3},{3,2},{4,5},{5,4},{6,7},{7,6},{8,9},{9,8},{10,11... | collective-permute-start | bytes 3145736 | tf_op jit(solution)/shard_map/ppermute | solution.py:412
  140.1 6.2 %collective-permute-start.17 = (f32[136,128]{1,0:T(8,128)}, f32[136,128]{1,0:T(8,128)S(1)}, u32[]{:S(2)}, u32[]{:S(2)}) collective-permute-start(f32[136,128]{1,0:T(8,128)} %shard_map.78), channel_id=1, source_target_pairs={{0,2},{2,0},{4,6},{6,4},{8,10},{10,8},{12,14},{14,12},{1,3},{3,1},... | collective-permute-start | bytes 208904 | tf_op jit(solution)/shard_map/ppermute | solution.py:406
  147.2 4.8 %collective-permute-start.18 = (f32[136,128]{1,0:T(8,128)S(1)}, f32[136,128]{1,0:T(8,128)S(1)}, u32[]{:S(2)}, u32[]{:S(2)}) collective-permute-start(f32[136,128]{1,0:T(8,128)S(1)} %add.14), channel_id=1, source_target_pairs={{0,4},{2,6},{4,0},{6,2},{8,12},{10,14},{12,8},{14,10},{1,5},{3,7},... | collective-permute-start | bytes 208904 | tf_op jit(solution)/shard_map/ppermute | solution.py:406
  152.0 5.7 %collective-permute-start.19 = (f32[136,128]{1,0:T(8,128)S(1)}, f32[136,128]{1,0:T(8,128)S(1)}, u32[]{:S(2)}, u32[]{:S(2)}) collective-permute-start(f32[136,128]{1,0:T(8,128)S(1)} %add.15), channel_id=1, source_target_pairs={{0,8},{2,10},{4,12},{6,14},{8,0},{10,2},{12,4},{14,6},{1,9},{3,11}... | collective-permute-start | bytes 208904 | tf_op jit(solution)/shard_map/ppermute | solution.py:406
  157.8 1.3 collective-permute-start.20
  (17 other events, 33.8 us)

commit v2 on v1

v2 whole, which is shorter than its diff:
```python
import functools

import jax
import jax.numpy as jnp
from jax import lax
from jax.experimental import pallas as pl
from jax.experimental.pallas import tpu as pltpu
from jax.sharding import PartitionSpec as P

peer_offsets = (1, -1, 2, -2)
f32, bf16 = jnp.float32, jnp.bfloat16
LANES, GROUP, PANEL = 128, 8, 16
vmem = pl.BlockSpec(memory_space=pltpu.VMEM)
smem = pl.BlockSpec(memory_space=pltpu.SMEM)
hbm = pl.BlockSpec(memory_space=pltpu.HBM)


def grant(mib):
    return pltpu.CompilerParams(vmem_limit_bytes=mib * 2**20)


def exchange_pairs(size):
    first = ([i for i in range(size) if i % 2 == 0], 1)
    second = ([i for i in range(size) if i % 2 == 1], 1)
    third = ([i for i in range(size) if i % 4 < 2], 2)
    fourth = ([i for i in range(size) if i % 4 >= 2], 2)
    return [
        [pair for i in starts if i + by < size for pair in ((i, i + by), (i + by, i))]
        for starts, by in (first, second, third, fourth)
    ]


def face_of(side_ref, q):
    side = side_ref[q // 2]
    return (q // 2) * 2 + (side if q % 2 == 0 else 1 - side)


def gather_faces(side_ref, faces_ref, table_ref, rows_ref, out_refs):
    slots = out_refs[0].shape[0]
    for q in range(4):
        offset = face_of(side_ref, q) * slots

        def body(step, _):
            base = step * 64
            for u in range(64):
                face = faces_ref[offset + base + u]
                rows_ref[pl.ds(base + u, 1), :] = table_ref[pl.ds(face, 1), :]
            return 0

        lax.fori_loop(0, slots // 64, body, 0)
        out_refs[q][...] = rows_ref[...].astype(bf16)


def face_kernel(side_ref, faces_ref, vec_ref, o0, o1, o2, o3, table_ref, rows_ref):
    nodes = vec_ref.shape[0]
    table_ref[0:nodes, :] = vec_ref[...].astype(f32)
    table_ref[nodes : nodes + 8, :] = jnp.zeros((8, LANES), f32)
    gather_faces(side_ref, faces_ref, table_ref, rows_ref, (o0, o1, o2, o3))


def send_faces(side, faces, vectors):
    nodes, slots = vectors.shape[0], faces.shape[0] // 4
    return pl.pallas_call(
        face_kernel,
        out_shape=[jax.ShapeDtypeStruct((slots, LANES), bf16)] * 4,
        in_specs=[smem, smem, vmem],
        out_specs=[vmem] * 4,
        scratch_shapes=[
            pltpu.VMEM((nodes + 8, LANES), f32),
            pltpu.VMEM((slots, LANES), f32),
        ],
        compiler_params=grant(8),
    )(side, faces, vectors)


def cells_kernel(
    outer, side_ref, maps_ref, scale_ref, whole_ref, given_ref, h0, h1, h2, h3,
    own_ref, g0, g1, g2, g3, matrix_ref, ext_ref, in_ref, out_ref, sems, *rest
):
    acc = rest[:GROUP]
    nodes, slots = given_ref.shape[0], h0.shape[0]
    size = matrix_ref.shape[0]
    ext = nodes + 4 * slots
    fetch = pltpu.make_async_copy(whole_ref, matrix_ref, sems.at[0])
    if outer:
        vec_ref = rest[GROUP]
        load = pltpu.make_async_copy(given_ref, vec_ref, sems.at[1])
        load.start()
    else:
        vec_ref = given_ref
    fetch.start()
    for q, ghost in enumerate((h0, h1, h2, h3)):
        start = pl.multiple_of(nodes + (face_of(side_ref, q) ^ 1) * slots, slots)
        ext_ref[pl.ds(start, slots), :] = ghost[...].astype(f32)

    def clear(step, _):
        rows = pl.ds(pl.multiple_of(step * 64, 64), 64)
        for a in acc:
            a[rows, :] = jnp.zeros((64, LANES), f32)
        return 0

    lax.fori_loop(0, ext // 64, clear, 0)
    if outer:
        load.wait()
    ext_ref[0:nodes, :] = vec_ref[...].astype(f32)
    cells = scale_ref.shape[0]
    for first in range(0, cells, GROUP):

        def gather(step, _):
            base = step * 8
            for u in range(8):
                for k in range(GROUP):
                    row = maps_ref[(first + k) * size + base + u]
                    in_ref[k, pl.ds(base + u, 1), :] = ext_ref[pl.ds(row, 1), :]
            return 0

        lax.fori_loop(0, size // 8, gather, 0)
        if first == 0:
            fetch.wait()
        for k in range(0, GROUP, 2):
            pair = jnp.concatenate([in_ref[k].astype(bf16), in_ref[k + 1].astype(bf16)], 1)
            product = jnp.dot(matrix_ref[...], pair, preferred_element_type=f32)
            out_ref[k] = product[:, :LANES] * scale_ref[first + k]
            out_ref[k + 1] = product[:, LANES:] * scale_ref[first + k + 1]

        def scatter(step, _):
            base = step * 8
            for u in range(8):
                rows = [maps_ref[(first + k) * size + base + u] for k in range(GROUP)]
                sums = [
                    acc[k][pl.ds(rows[k], 1), :] + out_ref[k, pl.ds(base + u, 1), :]
                    for k in range(GROUP)
                ]
                for k in range(GROUP):
                    acc[k][pl.ds(rows[k], 1), :] = sums[k]
            return 0

        lax.fori_loop(0, size // 8, scatter, 0)

    def total(start):
        rows = pl.ds(start, 64)
        parts = [a[rows, :] for a in acc]
        while len(parts) > 1:
            parts = [parts[i] + parts[i + 1] for i in range(0, len(parts), 2)]
        return parts[0]

    def reduce_own(step, _):
        start = pl.multiple_of(step * 64, 64)
        own_ref[pl.ds(start, 64), :] = total(start)
        return 0

    lax.fori_loop(0, nodes // 64, reduce_own, 0)
    for q, ghost in enumerate((g0, g1, g2, g3)):
        start = pl.multiple_of(nodes + (face_of(side_ref, q) ^ 1) * slots, slots)
        for r in range(0, slots, 64):
            ghost[r : r + 64, :] = total(pl.multiple_of(start + r, 64))


def apply_cells(side, maps, scale, matrix, vectors, ghosts, outer):
    nodes, slots, size = vectors.shape[0], ghosts[0].shape[0], matrix.shape[0]
    ext = nodes + 4 * slots
    return pl.pallas_call(
        functools.partial(cells_kernel, outer),
        out_shape=[jax.ShapeDtypeStruct((nodes, LANES), f32)]
        + [jax.ShapeDtypeStruct((slots, LANES), f32)] * 4,
        in_specs=[smem, smem, smem, hbm, hbm if outer else vmem] + [vmem] * 4,
        out_specs=[vmem] * 5,
        scratch_shapes=[
            pltpu.VMEM((size, size), bf16),
            pltpu.VMEM((ext, LANES), f32),
            pltpu.VMEM((GROUP, size, LANES), f32),
            pltpu.VMEM((GROUP, size, LANES), f32),
            pltpu.SemaphoreType.DMA((2,)),
        ]
        + [pltpu.VMEM((ext, LANES), f32)] * GROUP
        + [pltpu.VMEM((nodes, LANES), bf16)] * outer,
        compiler_params=grant(36),
    )(side, maps, scale, matrix, vectors, *ghosts)


def add_returned(side_ref, faces_ref, returned, acc):
    slots = returned[0].shape[0]
    for a in acc:
        a[...] = jnp.zeros(a.shape, f32)
    offsets = [face_of(side_ref, q) * slots for q in range(4)]

    def body(step, _):
        base = step * 16
        for u in range(16):
            rows = [faces_ref[offsets[q] + base + u] for q in range(4)]
            sums = [
                acc[q][pl.ds(rows[q], 1), :] + returned[q][pl.ds(base + u, 1), :]
                for q in range(4)
            ]
            for q in range(4):
                acc[q][pl.ds(rows[q], 1), :] = sums[q]
        return 0

    lax.fori_loop(0, slots // 16, body, 0)


def filtered(interval_ref, own_ref, pot_ref, vec_ref, acc, write):
    low = jnp.full((1, LANES), interval_ref[0])
    high = jnp.full((1, LANES), interval_ref[1])
    center, half_width = (low + high) / 2.0, (high - low) / 2.0
    inverse = 1.0 / half_width
    shifts = ((pot_ref[...] - center) * inverse).T
    for step in range(shifts.shape[1]):
        rows = slice(step * LANES, (step + 1) * LANES)
        image = own_ref[rows, :] + (
            (acc[0][rows, :] + acc[1][rows, :]) + (acc[2][rows, :] + acc[3][rows, :])
        )
        shift = jnp.broadcast_to(shifts[:, step : step + 1], (LANES, LANES))
        write(rows, image * inverse + shift * vec_ref[rows, :].astype(f32))


def first_kernel(
    side_ref, faces_ref, interval_ref, own_ref, pot_ref, vec_ref, r0, r1, r2, r3,
    out_ref, o0, o1, o2, o3, table_ref, rows_ref, *acc
):
    nodes = vec_ref.shape[0]
    add_returned(side_ref, faces_ref, (r0, r1, r2, r3), acc)

    def write(rows, value):
        value = value.astype(bf16)
        out_ref[rows, :] = value
        table_ref[rows, :] = value.astype(f32)

    filtered(interval_ref, own_ref, pot_ref, vec_ref, acc, write)
    table_ref[nodes : nodes + 8, :] = jnp.zeros((8, LANES), f32)
    gather_faces(side_ref, faces_ref, table_ref, rows_ref, (o0, o1, o2, o3))


def second_kernel(
    side_ref, faces_ref, interval_ref, own_ref, pot_ref, vec_ref, r0, r1, r2, r3, old_ref,
    out_ref, *acc
):
    add_returned(side_ref, faces_ref, (r0, r1, r2, r3), acc)

    def write(rows, value):
        out_ref[rows, :] = (2.0 * value - old_ref[rows, :].astype(f32)).astype(bf16)

    filtered(interval_ref, own_ref, pot_ref, vec_ref, acc, write)


def finish_first(side, faces, interval, own, potential, vectors, returned):
    nodes, slots = vectors.shape[0], returned[0].shape[0]
    return pl.pallas_call(
        first_kernel,
        out_shape=[jax.ShapeDtypeStruct((nodes, LANES), bf16)]
        + [jax.ShapeDtypeStruct((slots, LANES), bf16)] * 4,
        in_specs=[smem] * 3 + [vmem] * 7,
        out_specs=[vmem] * 5,
        scratch_shapes=[
            pltpu.VMEM((nodes + 8, LANES), f32),
            pltpu.VMEM((slots, LANES), f32),
        ]
        + [pltpu.VMEM((nodes + 8, LANES), f32)] * 4,
        compiler_params=grant(20),
    )(side, faces, interval, own, potential, vectors, *returned)


def finish_second(side, faces, interval, own, potential, vectors, returned, old):
    nodes = vectors.shape[0]
    return pl.pallas_call(
        second_kernel,
        out_shape=jax.ShapeDtypeStruct((nodes, LANES), bf16),
        in_specs=[smem] * 3 + [vmem] * 8,
        out_specs=vmem,
        scratch_shapes=[pltpu.VMEM((nodes + 8, LANES), f32)] * 4,
        compiler_params=grant(20),
    )(side, faces, interval, own, potential, vectors, *returned, old)


def margin_kernel(band_ref, own_ref, other_ref, out_ref):
    half = LANES // 2
    nt = functools.partial(
        lax.dot_general,
        dimension_numbers=(((0,), (0,)), ((), ())),
        preferred_element_type=f32,
    )

    def write(low, high, band):
        low_rows = low[:, band * half : (band + 1) * half]
        high_rows = high[:, band * half : (band + 1) * half]
        block = nt(low_rows, low)
        cross = nt(low_rows, high)
        tail = nt(high_rows, high)
        row = lax.broadcasted_iota(jnp.int32, (half, LANES), 0) + band * half
        col = lax.broadcasted_iota(jnp.int32, (half, LANES), 1)
        out_ref[0:half, :] = jnp.where(col >= row, block, tail)
        out_ref[half : 2 * half, :] = cross
        diag = jnp.sum(jnp.where(col == row, tail, 0.0), 0, keepdims=True)
        out_ref[2 * half : 2 * half + 8, :] = jnp.broadcast_to(diag, (8, LANES))

    @pl.when(band_ref[0] == 0)
    def _():
        write(own_ref[...], other_ref[...], 0)

    @pl.when(band_ref[0] != 0)
    def _():
        write(other_ref[...], own_ref[...], 1)


def margin_rows(band, own, other):
    return pl.pallas_call(
        margin_kernel,
        out_shape=jax.ShapeDtypeStruct((LANES + 8, LANES), f32),
        in_specs=[smem, vmem, vmem],
        out_specs=vmem,
        compiler_params=grant(12),
    )(band, own, other)


def split_three(x):
    high = x.astype(bf16)
    rest = x - high.astype(f32)
    mid = rest.astype(bf16)
    return high, mid, (rest - mid.astype(f32)).astype(bf16)


def invert_factor(work_ref, block_ref, panel_ref):
    total = work_ref.shape[0]
    halves = total // LANES
    col = lax.broadcasted_iota(jnp.int32, (PANEL, total), 1)
    row = lax.broadcasted_iota(jnp.int32, (PANEL, total), 0)

    def step(p, start_row):
        first = pl.multiple_of(p * PANEL, PANEL)
        rows = work_ref[pl.ds(first, PANEL), :]
        block = rows[:, start_row : start_row + LANES]
        block = pltpu.roll(block, lax.rem(total - first, LANES), 1)
        for k in range(PANEL):
            block_ref[k] = jnp.broadcast_to(block[:, k : k + 1], (PANEL, LANES))
        panel = jnp.where((col >= first) & (col < first + PANEL), 0.0, rows)
        panel = jnp.where(col == row + first, 1.0, panel)
        for h in range(halves):
            panel_ref[h] = panel[:, h * LANES : (h + 1) * LANES]
        entry = {
            (i, k): block_ref[k, pl.ds(i, 8, stride=0), :]
            for k in range(PANEL)
            for i in range(k, PANEL)
        }
        done = []
        for k in range(PANEL):
            scale = lax.rsqrt(entry[k, k])
            lines = [panel_ref[h, pl.ds(k, 8, stride=0), :] for h in range(halves)]
            for i in range(k + 1, PANEL):
                entry[i, k] = entry[i, k] * scale
            for i in range(k + 1, PANEL):
                for m in range(k + 1, i + 1):
                    entry[i, m] = entry[i, m] - entry[i, k] * entry[m, k]
            for m in range(k):
                lines = [line - entry[k, m] * old for line, old in zip(lines, done[m])]
            lines = [line * scale for line in lines]
            done.append(lines)
            for h in range(halves):
                panel_ref[h, k : k + 1, :] = lines[h][k % 8 : k % 8 + 1, :]
        panel = jnp.concatenate([panel_ref[h] for h in range(halves)], 1)
        right = jnp.where(col >= first + PANEL, panel, 0.0)
        ah, am, al = split_three(right)
        bh, bm, bl = split_three(panel)
        lhs = jnp.concatenate([ah, ah, am, am, ah, al], 0)
        rhs = jnp.concatenate([bh, bm, bh, bm, bl, bh], 0)
        update = lax.dot_general(
            lhs[:, start_row:], rhs, (((0,), (0,)), ((), ())), preferred_element_type=f32
        )
        below = work_ref[start_row:, :]
        big = lax.broadcasted_iota(jnp.int32, below.shape, 1)
        inside = (big >= first) & (big < first + PANEL)
        work_ref[start_row:, :] = jnp.where(inside, 0.0, below) - update
        work_ref[pl.ds(first, PANEL), :] = panel

    per = LANES // PANEL
    for h in range(halves):
        lax.fori_loop(h * per, (h + 1) * per, lambda p, _: (step(p, h * LANES), 0)[1], 0)


def rotate_kernel(
    band_ref, count_ref, mine_ref, theirs_ref, own_ref, other_ref, out_ref, work_ref,
    block_ref, panel_ref
):
    half = LANES // 2
    band = band_ref[0]
    mine, theirs = mine_ref[...] * count_ref[0], theirs_ref[...] * count_ref[0]
    top = jnp.where(band == 0, mine, theirs)
    bottom = jnp.where(band == 0, theirs, mine)
    packed = jnp.concatenate([top[0:half], bottom[0:half]], 0)
    cross = jnp.concatenate([top[half:LANES], bottom[half:LANES]], 0)
    diag = top[LANES : LANES + 1] + bottom[LANES : LANES + 1]
    flipped = packed.T
    row = lax.broadcasted_iota(jnp.int32, (LANES, LANES), 0)
    col = lax.broadcasted_iota(jnp.int32, (LANES, LANES), 1)
    work_ref[0:LANES, 0:LANES] = jnp.where(col >= row, packed, flipped)
    work_ref[0:LANES, LANES:] = cross
    work_ref[LANES:, 0:LANES] = cross.T
    tail = jnp.where(col < row, packed, flipped)
    work_ref[LANES:, LANES:] = jnp.where(col == row, jnp.broadcast_to(diag, tail.shape), tail)
    invert_factor(work_ref, block_ref, panel_ref)
    lower = jnp.where(col <= row, 1.0, 0.0)
    first = work_ref[0:LANES, 0:LANES] * lower
    last = work_ref[LANES:, LANES:] * lower
    corner = work_ref[LANES:, 0:LANES]
    from_own = jnp.where(band == 0, first, last)
    from_other = jnp.where(band == 0, jnp.zeros_like(corner), corner)
    weights = jnp.concatenate([from_own, from_other], 1)
    high = weights.astype(bf16)
    low = (weights - high.astype(f32)).astype(bf16)
    weights = jnp.concatenate([high, low], 0)
    chunk = 512

    def body(step, _):
        rows = pl.ds(pl.multiple_of(step * chunk, chunk), chunk)
        both = jnp.concatenate([own_ref[rows, :], other_ref[rows, :]], 1)
        product = lax.dot_general(
            both, weights, (((1,), (1,)), ((), ())), preferred_element_type=f32
        )
        out_ref[rows, :] = product[:, :LANES] + product[:, LANES:]
        return 0

    lax.fori_loop(0, own_ref.shape[0] // chunk, body, 0)


def rotate(band, inv_count, mine, theirs, own, other):
    return pl.pallas_call(
        rotate_kernel,
        out_shape=jax.ShapeDtypeStruct(own.shape, f32),
        in_specs=[smem, smem] + [vmem] * 4,
        out_specs=vmem,
        scratch_shapes=[
            pltpu.VMEM((2 * LANES, 2 * LANES), f32),
            pltpu.VMEM((PANEL, PANEL, LANES), f32),
            pltpu.VMEM((2, PANEL, LANES), f32),
        ],
        compiler_params=grant(12),
    )(band, inv_count, mine, theirs, own, other)


def summed_over(value, axis):
    size = lax.axis_size(axis)
    if size & (size - 1):
        return lax.psum(value, axis)
    stride = 1
    while stride < size:
        count = min(4, size // stride)
        parts = [
            lax.ppermute(value, axis, [(i, i ^ (k * stride)) for i in range(size)])
            for k in range(1, count)
        ]
        value = value + sum(parts[1:], parts[0])
        stride *= count
    return value


def swapped(value):
    return lax.ppermute(value, "band", [(0, 1), (1, 0)])


def on_device(wavefunctions, bounds, cell_matrix, cell_scale, potential, cell_nodes, face_nodes):
    nodes = wavefunctions.shape[0]
    faces = jnp.where(face_nodes < 0, nodes, face_nodes).reshape(-1)
    potential = potential.reshape(-1, LANES)
    at = lax.axis_index("dom").astype(jnp.int32)
    side = jnp.stack([at % 2, at // 2 % 2])
    pairs = exchange_pairs(lax.axis_size("dom"))

    def exchanged(blocks):
        return [lax.ppermute(block, "dom", pair) for block, pair in zip(blocks, pairs)]

    cells = functools.partial(apply_cells, side, cell_nodes.reshape(-1), cell_scale, cell_matrix)
    ghosts = exchanged(send_faces(side, faces, wavefunctions))
    own, *sums = cells(wavefunctions, ghosts, True)
    degree_one, *blocks = finish_first(
        side, faces, bounds, own, potential, wavefunctions, exchanged(sums)
    )
    own, *sums = cells(degree_one, exchanged(blocks), False)
    degree_two = finish_second(
        side, faces, bounds, own, potential, degree_one, exchanged(sums), wavefunctions
    )
    other = swapped(degree_two)
    band = lax.axis_index("band").astype(jnp.int32).reshape(1)
    mine = summed_over(margin_rows(band, degree_two, other), "dom")
    inv_count = jnp.full((1,), 1.0 / (nodes * lax.axis_size("dom")), f32)
    return rotate(band, inv_count, mine, swapped(mine), degree_two, other)


def solution(mesh):
    return jax.shard_map(
        on_device,
        mesh=mesh,
        in_specs=(
            P(("kpt", "dom"), "band"),
            P("kpt"),
            P(),
            P("dom"),
            P("dom"),
            P("dom", None),
            P("dom", None),
        ),
        out_specs=P(("kpt", "dom"), "band"),
        check_vma=False,
    )
```

time: 181 us -> 138 us (0.76)
  Pallas kernels: 86.6 us -> 65.2 us
  starting transfers between devices: 56.8 us -> 43.7 us
  local copies, waits for them, and re-layouts: 9.52 us -> 4.93 us
  between operations: 2.91 us -> 0.23 us
    ppermute x19 -> x20, starting transfers between devices: 56.7 us -> 43.6 us  [the longest x16 34.5 us: exchanged(): lax.ppermute(block, 'dom', pair)]
    pallas_call x1, Pallas kernels: 20.4 us -> 14.5 us  [rotate(): pl.pallas_call(rotate_kernel, out_shape=jax.ShapeDtypeStruct(own.shape, f...]
    pallas_call x1, Pallas kernels: 9.03 us -> 4.76 us  [finish_first(): pl.pallas_call(first_kernel, out_shape=[jax.ShapeDtypeStruct((nodes, LANE...]
    pallas_call x1, Pallas kernels: 7.76 us -> 3.98 us  [finish_second(): pl.pallas_call(second_kernel, out_shape=jax.ShapeDtypeStruct((nodes, LANE...]
    pallas_call x2, Pallas kernels: 42.8 us -> 39.5 us  [apply_cells(): pl.pallas_call(functools.partial(cells_kernel, outer), out_shape=[jax.Sha...]
    pallas_call x1, Pallas kernels: 2.91 us -> 0.74 us  [margin_rows(): pl.pallas_call(margin_kernel, out_shape=jax.ShapeDtypeStruct((LANES + 8,...]
    pallas_call x1, Pallas kernels: 3.74 us -> 1.65 us  [send_faces(): pl.pallas_call(face_kernel, out_shape=[jax.ShapeDtypeStruct((slots, LANES...]
    broadcast_in_dim x1 -> x0, local copies, waits for them, and re-layouts: 1.96 us -> none  [on_device(): jnp.broadcast_to(((potential - center) / half_width)[:, None], (nodes, co...]
  transfers between devices with their start and end apart: 21 -> 22, of which waited for: 12 -> 9; matrix products, arithmetic and copies ran while one was open for 2% -> 1% of each run, Pallas kernels for 0% -> 0%
where the time goes in v2:
time: 138 us
  Pallas kernels  65.2 us (47%)
  starting transfers between devices  43.7 us (32%)
  waiting for transfers between devices  22.7 us (16%)
  local copies, waits for them, and re-layouts  4.93 us (4%)
    pallas_call x2, Pallas kernels, apply_cells(): pl.pallas_call(functools.partial(cells_kernel, outer), out_shape=[jax.Sha...  39.5 us
    ppermute x16, starting transfers between devices, exchanged(): lax.ppermute(block, 'dom', pair)  34.5 us
    pallas_call x1, Pallas kernels, rotate(): pl.pallas_call(rotate_kernel, out_shape=jax.ShapeDtypeStruct(own.shape, f...  14.5 us
    ppermute x16, waiting for transfers between devices, exchanged(): lax.ppermute(block, 'dom', pair)  11 us
    ppermute x4, starting transfers between devices, summed_over(): lax.ppermute(value, axis, [(i, i ^ k * stride) for i in range(size)])  9.12 us
    ppermute x4, waiting for transfers between devices, summed_over(): lax.ppermute(value, axis, [(i, i ^ k * stride) for i in range(size)])  7.79 us
    unnamed x16, local copies, waits for them, and re-layouts  4.93 us
    pallas_call x1, Pallas kernels, finish_first(): pl.pallas_call(first_kernel, out_shape=[jax.ShapeDtypeStruct((nodes, LANE...  4.76 us
  transfers between devices with their start and end apart: 22, of which 9 were waited for; matrix products, arithmetic and copies ran while one was open for 1% of the time, Pallas kernels for 0%

profile of v2, /device:TPU:0, one launch (start us, length us, event | category | flops | bytes accessed | tf_op | source)
XLA Modules:
  0.0 137.6 jit_solution(2253077167774876174)
XLA Ops:
  2.0 1.6 %shard_map.73 = (bf16[256,128]{1,0:T(8,128)(2,1)S(1)}, bf16[256,128]{1,0:T(8,128)(2,1)S(1)}, bf16[256,128]{1,0:T(8,128)(2,1)S(1)}, bf16[256,128]{1,0:T(8,128)(2,1)S(1)}) custom-call(s32[2]{0:T(128)S(1)} %pad_add_fusion.side_ref, s32[1024]{0:T(1024)S(1)} %bitcast.13, bf16[4096,128]{1,0:T(8,128)(2,1)S(1)} %copy-done), custom_call_target="tpu_custom_call" | custom-call | tf_op jit(solution)/shard_map/pallas_call | solution.py:63
  3.7 3.0 %collective-permute-start = (bf16[256,128]{1,0:T(8,128)(2,1)S(1)}, bf16[256,128]{1,0:T(8,128)(2,1)S(1)}, u32[]{:S(2)}, u32[]{:S(2)}) collective-permute-start(bf16[256,128]{1,0:T(8,128)(2,1)S(1)} %get-tuple-element.24), channel_id=1, source_target_pairs={{0,2},{2,0},{4,6},{6,4},{8,10},{10,8},{12,14},{14,12},{1,3},{3,1},... | collective-permute-start | bytes 196616 | tf_op jit(solution)/shard_map/ppermute | solution.py:468
  7.3 2.9 %collective-permute-start.2 = (bf16[256,128]{1,0:T(8,128)(2,1)S(1)}, bf16[256,128]{1,0:T(8,128)(2,1)S(1)}, u32[]{:S(2)}, u32[]{:S(2)}) collective-permute-start(bf16[256,128]{1,0:T(8,128)(2,1)S(1)} %get-tuple-element.26), channel_id=1, source_target_pairs={{0,4},{4,0},{2,6},{6,2},{8,12},{12,8},{10,14},{14,10},{1,5},{5,1},... | collective-permute-start | bytes 196616 | tf_op jit(solution)/shard_map/ppermute | solution.py:468
  11.7 1.7 %collective-permute-done.2.h2 = bf16[256,128]{1,0:T(8,128)(2,1)S(1)} collective-permute-done((bf16[256,128]{1,0:T(8,128)(2,1)S(1)}, bf16[256,128]{1,0:T(8,128)(2,1)S(1)}, u32[]{:S(2)}, u32[]{:S(2)}) %collective-permute-start.2) | collective-permute-done | bytes 65568 | tf_op jit(solution)/shard_map/ppermute | solution.py:468
  16.3 19.8 %shard_map.74 = (f32[4096,128]{1,0:T(8,128)S(1)}, f32[256,128]{1,0:T(8,128)S(1)}, f32[256,128]{1,0:T(8,128)S(1)}, f32[256,128]{1,0:T(8,128)S(1)}, f32[256,128]{1,0:T(8,128)S(1)}) custom-call(s32[2]{0:T(128)S(1)} %pad_add_fusion.side_ref, s32[8192]{0:T(1024)S(1)} %bitcast.9, f32[16]{0:T(128)S(1)} %copy-done.5, bf16[512,512]{1,0:T(8,128)(2,1)S(1)} %copy-done.3, ...), custom_call_target="tpu_custom_call" | custom-call | tf_op jit(solution)/shard_map/pallas_call | solution.py:162
  36.1 2.7 %collective-permute-start.4 = (f32[256,128]{1,0:T(8,128)S(1)}, f32[256,128]{1,0:T(8,128)S(1)}, u32[]{:S(2)}, u32[]{:S(2)}) collective-permute-start(f32[256,128]{1,0:T(8,128)S(1)} %get-tuple-element.29), channel_id=1, source_target_pairs={{0,2},{2,0},{4,6},{6,4},{8,10},{10,8},{12,14},{14,12},{1,3},{3,1},... | collective-permute-start | bytes 393224 | tf_op jit(solution)/shard_map/ppermute | solution.py:468
  39.4 5.2 %collective-permute-start.6 = (f32[256,128]{1,0:T(8,128)S(1)}, f32[256,128]{1,0:T(8,128)S(1)}, u32[]{:S(2)}, u32[]{:S(2)}) collective-permute-start(f32[256,128]{1,0:T(8,128)S(1)} %get-tuple-element.31), channel_id=1, source_target_pairs={{0,4},{4,0},{2,6},{6,2},{8,12},{12,8},{10,14},{14,10},{1,5},{5,1},... | collective-permute-start | bytes 393224 | tf_op jit(solution)/shard_map/ppermute | solution.py:468
  45.3 3.6 %collective-permute-done.6.r2 = f32[256,128]{1,0:T(8,128)S(1)} collective-permute-done((f32[256,128]{1,0:T(8,128)S(1)}, f32[256,128]{1,0:T(8,128)S(1)}, u32[]{:S(2)}, u32[]{:S(2)}) %collective-permute-start.6) | collective-permute-done | bytes 131104 | tf_op jit(solution)/shard_map/ppermute | solution.py:468
  48.9 4.8 %shard_map.75 = (bf16[4096,128]{1,0:T(8,128)(2,1)S(1)}, bf16[256,128]{1,0:T(8,128)(2,1)S(1)}, bf16[256,128]{1,0:T(8,128)(2,1)S(1)}, bf16[256,128]{1,0:T(8,128)(2,1)S(1)}, bf16[256,128]{1,0:T(8,128)(2,1)S(1)}) custom-call(s32[2]{0:T(128)S(1)} %pad_add_fusion.side_ref, s32[1024]{0:T(1024)S(1)} %bitcast.14, f32[2]{0:T(128)S(1)} %copy-done.6, ...), custom_call_target="tpu_custom_call" | custom-call | tf_op jit(solution)/shard_map/pallas_call | solution.py:248
  53.7 2.2 %collective-permute-start.8 = (bf16[256,128]{1,0:T(8,128)(2,1)S(1)}, bf16[256,128]{1,0:T(8,128)(2,1)S(1)}, u32[]{:S(2)}, u32[]{:S(2)}) collective-permute-start(bf16[256,128]{1,0:T(8,128)(2,1)S(1)} %get-tuple-element.34), channel_id=1, source_target_pairs={{0,2},{2,0},{4,6},{6,4},{8,10},{10,8},{12,14},{14,12},{1,3},{3,1},... | collective-permute-start | bytes 196616 | tf_op jit(solution)/shard_map/ppermute | solution.py:468
  56.6 5.1 %collective-permute-start.10 = (bf16[256,128]{1,0:T(8,128)(2,1)S(1)}, bf16[256,128]{1,0:T(8,128)(2,1)S(1)}, u32[]{:S(2)}, u32[]{:S(2)}) collective-permute-start(bf16[256,128]{1,0:T(8,128)(2,1)S(1)} %get-tuple-element.36), channel_id=1, source_target_pairs={{0,4},{4,0},{2,6},{6,2},{8,12},{12,8},{10,14},{14,10},{1,5},{5,1},... | collective-permute-start | bytes 196616 | tf_op jit(solution)/shard_map/ppermute | solution.py:468
  62.4 2.2 %collective-permute-done.10.h2 = bf16[256,128]{1,0:T(8,128)(2,1)S(1)} collective-permute-done((bf16[256,128]{1,0:T(8,128)(2,1)S(1)}, bf16[256,128]{1,0:T(8,128)(2,1)S(1)}, u32[]{:S(2)}, u32[]{:S(2)}) %collective-permute-start.10) | collective-permute-done | bytes 65568 | tf_op jit(solution)/shard_map/ppermute | solution.py:468
  64.5 19.7 %shard_map.76 = (f32[4096,128]{1,0:T(8,128)S(1)}, f32[256,128]{1,0:T(8,128)S(1)}, f32[256,128]{1,0:T(8,128)S(1)}, f32[256,128]{1,0:T(8,128)S(1)}, f32[256,128]{1,0:T(8,128)S(1)}) custom-call(s32[2]{0:T(128)S(1)} %pad_add_fusion.side_ref, s32[8192]{0:T(1024)S(1)} %bitcast.10, f32[16]{0:T(128)S(1)} %copy-done.5, bf16[512,512]{1,0:T(8,128)(2,1)S(1)} %copy-done.3, ...), custom_call_target="tpu_custom_call" | custom-call | tf_op jit(solution)/shard_map/pallas_call | solution.py:162
  84.3 2.9 %collective-permute-start.12 = (f32[256,128]{1,0:T(8,128)S(1)}, f32[256,128]{1,0:T(8,128)S(1)}, u32[]{:S(2)}, u32[]{:S(2)}) collective-permute-start(f32[256,128]{1,0:T(8,128)S(1)} %get-tuple-element.39), channel_id=1, source_target_pairs={{0,2},{2,0},{4,6},{6,4},{8,10},{10,8},{12,14},{14,12},{1,3},{3,1},... | collective-permute-start | bytes 393224 | tf_op jit(solution)/shard_map/ppermute | solution.py:468
  87.9 5.2 %collective-permute-start.14 = (f32[256,128]{1,0:T(8,128)S(1)}, f32[256,128]{1,0:T(8,128)S(1)}, u32[]{:S(2)}, u32[]{:S(2)}) collective-permute-start(f32[256,128]{1,0:T(8,128)S(1)} %get-tuple-element.41), channel_id=1, source_target_pairs={{0,4},{4,0},{2,6},{6,2},{8,12},{12,8},{10,14},{14,10},{1,5},{5,1},... | collective-permute-start | bytes 393224 | tf_op jit(solution)/shard_map/ppermute | solution.py:468
  93.8 3.6 %collective-permute-done.14.r2 = f32[256,128]{1,0:T(8,128)S(1)} collective-permute-done((f32[256,128]{1,0:T(8,128)S(1)}, f32[256,128]{1,0:T(8,128)S(1)}, u32[]{:S(2)}, u32[]{:S(2)}) %collective-permute-start.14) | collective-permute-done | bytes 131104 | tf_op jit(solution)/shard_map/ppermute | solution.py:468
  97.4 4.0 %shard_map.77.own_ref = bf16[4096,128]{1,0:T(8,128)(2,1)S(1)} custom-call(s32[2]{0:T(128)S(1)} %pad_add_fusion.side_ref, s32[1024]{0:T(1024)S(1)} %bitcast.15, f32[2]{0:T(128)S(1)} %copy-done.6, f32[4096,128]{1,0:T(8,128)S(1)} %get-tuple-element.38.own_ref, f32[32,128]{1,0:T(8,128)S(1)} %bitcast.12, ...), custom_call_target="tpu_custom_call" | custom-call | tf_op jit(solution)/shard_map/pallas_call | solution.py:265
  101.4 2.6 %collective-permute-done.16.other_ref = bf16[4096,128]{1,0:T(8,128)(2,1)S(1)} collective-permute-done((bf16[4096,128]{1,0:T(8,128)(2,1)S(1)}, bf16[4096,128]{1,0:T(8,128)(2,1)S(1)}, u32[]{:S(2)}, u32[]{:S(2)}) %collective-permute-start.16) | collective-permute-done | bytes 1048608 | tf_op jit(solution)/shard_map/ppermute | solution.py:456
  104.8 5.4 %collective-permute-start.19 = (f32[136,128]{1,0:T(8,128)S(1)}, f32[136,128]{1,0:T(8,128)S(1)}, u32[]{:S(2)}, u32[]{:S(2)}) collective-permute-start(f32[136,128]{1,0:T(8,128)S(1)} %shard_map.78), channel_id=1, source_target_pairs={{0,6},{2,4},{4,2},{6,0},{8,14},{10,12},{12,10},{14,8},{1,7},{3,5},... | collective-permute-start | bytes 208904 | tf_op jit(solution)/shard_map/ppermute | solution.py:447
  110.9 2.4 %collective-permute-done.19 = f32[136,128]{1,0:T(8,128)S(1)} collective-permute-done((f32[136,128]{1,0:T(8,128)S(1)}, f32[136,128]{1,0:T(8,128)S(1)}, u32[]{:S(2)}, u32[]{:S(2)}) %collective-permute-start.19) | collective-permute-done | bytes 69664 | tf_op jit(solution)/shard_map/ppermute | solution.py:447
  113.3 1.5 %collective-permute-done.18 = f32[136,128]{1,0:T(8,128)S(1)} collective-permute-done((f32[136,128]{1,0:T(8,128)S(1)}, f32[136,128]{1,0:T(8,128)S(1)}, u32[]{:S(2)}, u32[]{:S(2)}) %collective-permute-start.18) | collective-permute-done | bytes 69664 | tf_op jit(solution)/shard_map/ppermute | solution.py:447
  114.8 3.0 %collective-permute-start.20 = (f32[136,128]{1,0:T(8,128)S(1)}, f32[136,128]{1,0:T(8,128)S(1)}, u32[]{:S(2)}, u32[]{:S(2)}) collective-permute-start(f32[136,128]{1,0:T(8,128)S(1)} %add_add_fusion), channel_id=1, source_target_pairs={{0,8},{2,10},{4,12},{6,14},{8,0},{10,2},{12,4},{14,6},{1,9},{3,11}... | collective-permute-start | bytes 208904 | tf_op jit(solution)/shard_map/ppermute | solution.py:447
  117.8 3.9 %collective-permute-done.20 = f32[136,128]{1,0:T(8,128)S(1)} collective-permute-done((f32[136,128]{1,0:T(8,128)S(1)}, f32[136,128]{1,0:T(8,128)S(1)}, u32[]{:S(2)}, u32[]{:S(2)}) %collective-permute-start.20) | collective-permute-done | bytes 69664 | tf_op jit(solution)/shard_map/ppermute | solution.py:447
  123.1 14.5 %shard_map.79 = f32[4096,128]{1,0:T(8,128)} custom-call(s32[1]{0:T(128)} %bitcast.band_ref, f32[1]{0:T(128)} %constant.34.clone.1.count_ref, f32[136,128]{1,0:T(8,128)S(1)} %add.25.mine_ref, f32[136,128]{1,0:T(8,128)S(1)} %collective-permute-done.21.theirs_ref, bf16[4096,128]{1,0:T(8,128)(2,1)S(1)} %shard_map.77.own_ref, ...), custom_call_target="tpu_custom_call" | custom-call | tf_op jit(solution)/shard_map/pallas_call | solution.py:425
  (47 shorter events, 13.8 us)
Async XLA Ops:
  0.0 48.9 %copy-start.6 = (f32[2]{0:T(128)S(1)}, f32[2]{0:T(128)}, u32[]{:S(2)}) copy-start(f32[2]{0:T(128)} %interval_ref.3) | copy-start | bytes 28
  0.0 48.9 %copy-start.4 = (f32[4096]{0:T(1024)S(1)}, f32[4096]{0:T(1024)}, u32[]{:S(2)}) copy-start(f32[4096]{0:T(1024)} %param.11) | copy-start | bytes 49156
  3.7 8.0 %collective-permute-start = (bf16[256,128]{1,0:T(8,128)(2,1)S(1)}, bf16[256,128]{1,0:T(8,128)(2,1)S(1)}, u32[]{:S(2)}, u32[]{:S(2)}) collective-permute-start(bf16[256,128]{1,0:T(8,128)(2,1)S(1)} %get-tuple-element.24), channel_id=1, source_target_pairs={{0,2},{2,0},{4,6},{6,4},{8,10},{10,8},{12,14},{14,12},{1,3},{3,1},... | collective-permute-start | bytes 196616 | tf_op jit(solution)/shard_map/ppermute | solution.py:468
  6.7 5.0 %collective-permute-start.1 = (bf16[256,128]{1,0:T(8,128)(2,1)S(1)}, bf16[256,128]{1,0:T(8,128)(2,1)S(1)}, u32[]{:S(2)}, u32[]{:S(2)}) collective-permute-start(bf16[256,128]{1,0:T(8,128)(2,1)S(1)} %get-tuple-element.25), channel_id=1, source_target_pairs={{2,4},{4,2},{6,8},{8,6},{10,12},{12,10},{3,5},{5,3},{7,9},{9,7},{1... | collective-permute-start | bytes 196616 | tf_op jit(solution)/shard_map/ppermute | solution.py:468
  7.3 6.0 %collective-permute-start.2 = (bf16[256,128]{1,0:T(8,128)(2,1)S(1)}, bf16[256,128]{1,0:T(8,128)(2,1)S(1)}, u32[]{:S(2)}, u32[]{:S(2)}) collective-permute-start(bf16[256,128]{1,0:T(8,128)(2,1)S(1)} %get-tuple-element.26), channel_id=1, source_target_pairs={{0,4},{4,0},{2,6},{6,2},{8,12},{12,8},{10,14},{14,10},{1,5},{5,1},... | collective-permute-start | bytes 196616 | tf_op jit(solution)/shard_map/ppermute | solution.py:468
  10.2 3.1 %collective-permute-start.3 = (bf16[256,128]{1,0:T(8,128)(2,1)S(1)}, bf16[256,128]{1,0:T(8,128)(2,1)S(1)}, u32[]{:S(2)}, u32[]{:S(2)}) collective-permute-start(bf16[256,128]{1,0:T(8,128)(2,1)S(1)} %get-tuple-element.27), channel_id=1, source_target_pairs={{4,8},{8,4},{6,10},{10,6},{5,9},{9,5},{7,11},{11,7},{20,24},{24,20... | collective-permute-start | bytes 196616 | tf_op jit(solution)/shard_map/ppermute | solution.py:468
  36.1 9.2 %collective-permute-start.4 = (f32[256,128]{1,0:T(8,128)S(1)}, f32[256,128]{1,0:T(8,128)S(1)}, u32[]{:S(2)}, u32[]{:S(2)}) collective-permute-start(f32[256,128]{1,0:T(8,128)S(1)} %get-tuple-element.29), channel_id=1, source_target_pairs={{0,2},{2,0},{4,6},{6,4},{8,10},{10,8},{12,14},{14,12},{1,3},{3,1},... | collective-permute-start | bytes 393224 | tf_op jit(solution)/shard_map/ppermute | solution.py:468
  38.8 6.6 %collective-permute-start.5 = (f32[256,128]{1,0:T(8,128)S(1)}, f32[256,128]{1,0:T(8,128)S(1)}, u32[]{:S(2)}, u32[]{:S(2)}) collective-permute-start(f32[256,128]{1,0:T(8,128)S(1)} %get-tuple-element.30), channel_id=1, source_target_pairs={{2,4},{4,2},{6,8},{8,6},{10,12},{12,10},{3,5},{5,3},{7,9},{9,7},{1... | collective-permute-start | bytes 393224 | tf_op jit(solution)/shard_map/ppermute | solution.py:468
  39.4 9.5 %collective-permute-start.6 = (f32[256,128]{1,0:T(8,128)S(1)}, f32[256,128]{1,0:T(8,128)S(1)}, u32[]{:S(2)}, u32[]{:S(2)}) collective-permute-start(f32[256,128]{1,0:T(8,128)S(1)} %get-tuple-element.31), channel_id=1, source_target_pairs={{0,4},{4,0},{2,6},{6,2},{8,12},{12,8},{10,14},{14,10},{1,5},{5,1},... | collective-permute-start | bytes 393224 | tf_op jit(solution)/shard_map/ppermute | solution.py:468
  44.7 4.3 %collective-permute-start.7 = (f32[256,128]{1,0:T(8,128)S(1)}, f32[256,128]{1,0:T(8,128)S(1)}, u32[]{:S(2)}, u32[]{:S(2)}) collective-permute-start(f32[256,128]{1,0:T(8,128)S(1)} %get-tuple-element.32), channel_id=1, source_target_pairs={{4,8},{8,4},{6,10},{10,6},{5,9},{9,5},{7,11},{11,7},{20,24},{24,20... | collective-permute-start | bytes 393224 | tf_op jit(solution)/shard_map/ppermute | solution.py:468
  53.7 8.6 %collective-permute-start.8 = (bf16[256,128]{1,0:T(8,128)(2,1)S(1)}, bf16[256,128]{1,0:T(8,128)(2,1)S(1)}, u32[]{:S(2)}, u32[]{:S(2)}) collective-permute-start(bf16[256,128]{1,0:T(8,128)(2,1)S(1)} %get-tuple-element.34), channel_id=1, source_target_pairs={{0,2},{2,0},{4,6},{6,4},{8,10},{10,8},{12,14},{14,12},{1,3},{3,1},... | collective-permute-start | bytes 196616 | tf_op jit(solution)/shard_map/ppermute | solution.py:468
  55.9 6.4 %collective-permute-start.9 = (bf16[256,128]{1,0:T(8,128)(2,1)S(1)}, bf16[256,128]{1,0:T(8,128)(2,1)S(1)}, u32[]{:S(2)}, u32[]{:S(2)}) collective-permute-start(bf16[256,128]{1,0:T(8,128)(2,1)S(1)} %get-tuple-element.35), channel_id=1, source_target_pairs={{2,4},{4,2},{6,8},{8,6},{10,12},{12,10},{3,5},{5,3},{7,9},{9,7},{1... | collective-permute-start | bytes 196616 | tf_op jit(solution)/shard_map/ppermute | solution.py:468
  56.6 8.0 %collective-permute-start.10 = (bf16[256,128]{1,0:T(8,128)(2,1)S(1)}, bf16[256,128]{1,0:T(8,128)(2,1)S(1)}, u32[]{:S(2)}, u32[]{:S(2)}) collective-permute-start(bf16[256,128]{1,0:T(8,128)(2,1)S(1)} %get-tuple-element.36), channel_id=1, source_target_pairs={{0,4},{4,0},{2,6},{6,2},{8,12},{12,8},{10,14},{14,10},{1,5},{5,1},... | collective-permute-start | bytes 196616 | tf_op jit(solution)/shard_map/ppermute | solution.py:468
  61.7 2.9 %collective-permute-start.11 = (bf16[256,128]{1,0:T(8,128)(2,1)S(1)}, bf16[256,128]{1,0:T(8,128)(2,1)S(1)}, u32[]{:S(2)}, u32[]{:S(2)}) collective-permute-start(bf16[256,128]{1,0:T(8,128)(2,1)S(1)} %get-tuple-element.37), channel_id=1, source_target_pairs={{4,8},{8,4},{6,10},{10,6},{5,9},{9,5},{7,11},{11,7},{20,24},{24,20... | collective-permute-start | bytes 196616 | tf_op jit(solution)/shard_map/ppermute | solution.py:468
  84.3 9.5 %collective-permute-start.12 = (f32[256,128]{1,0:T(8,128)S(1)}, f32[256,128]{1,0:T(8,128)S(1)}, u32[]{:S(2)}, u32[]{:S(2)}) collective-permute-start(f32[256,128]{1,0:T(8,128)S(1)} %get-tuple-element.39), channel_id=1, source_target_pairs={{0,2},{2,0},{4,6},{6,4},{8,10},{10,8},{12,14},{14,12},{1,3},{3,1},... | collective-permute-start | bytes 393224 | tf_op jit(solution)/shard_map/ppermute | solution.py:468
  87.2 6.6 %collective-permute-start.13 = (f32[256,128]{1,0:T(8,128)S(1)}, f32[256,128]{1,0:T(8,128)S(1)}, u32[]{:S(2)}, u32[]{:S(2)}) collective-permute-start(f32[256,128]{1,0:T(8,128)S(1)} %get-tuple-element.40), channel_id=1, source_target_pairs={{2,4},{4,2},{6,8},{8,6},{10,12},{12,10},{3,5},{5,3},{7,9},{9,7},{1... | collective-permute-start | bytes 393224 | tf_op jit(solution)/shard_map/ppermute | solution.py:468
  87.9 9.5 %collective-permute-start.14 = (f32[256,128]{1,0:T(8,128)S(1)}, f32[256,128]{1,0:T(8,128)S(1)}, u32[]{:S(2)}, u32[]{:S(2)}) collective-permute-start(f32[256,128]{1,0:T(8,128)S(1)} %get-tuple-element.41), channel_id=1, source_target_pairs={{0,4},{4,0},{2,6},{6,2},{8,12},{12,8},{10,14},{14,10},{1,5},{5,1},... | collective-permute-start | bytes 393224 | tf_op jit(solution)/shard_map/ppermute | solution.py:468
  93.1 4.3 %collective-permute-start.15 = (f32[256,128]{1,0:T(8,128)S(1)}, f32[256,128]{1,0:T(8,128)S(1)}, u32[]{:S(2)}, u32[]{:S(2)}) collective-permute-start(f32[256,128]{1,0:T(8,128)S(1)} %get-tuple-element.42), channel_id=1, source_target_pairs={{4,8},{8,4},{6,10},{10,6},{5,9},{9,5},{7,11},{11,7},{20,24},{24,20... | collective-permute-start | bytes 393224 | tf_op jit(solution)/shard_map/ppermute | solution.py:468
  101.3 2.7 %collective-permute-start.16 = (bf16[4096,128]{1,0:T(8,128)(2,1)S(1)}, bf16[4096,128]{1,0:T(8,128)(2,1)S(1)}, u32[]{:S(2)}, u32[]{:S(2)}) collective-permute-start(bf16[4096,128]{1,0:T(8,128)(2,1)S(1)} %shard_map.77.own_ref), channel_id=1, source_target_pairs={{0,1},{1,0},{2,3},{3,2},{4,5},{5,4},{6,7},{7,6},{8,9},{9,8},{10,11... | collective-permute-start | bytes 3145736 | tf_op jit(solution)/shard_map/ppermute | solution.py:456
  104.8 8.5 %collective-permute-start.19 = (f32[136,128]{1,0:T(8,128)S(1)}, f32[136,128]{1,0:T(8,128)S(1)}, u32[]{:S(2)}, u32[]{:S(2)}) collective-permute-start(f32[136,128]{1,0:T(8,128)S(1)} %shard_map.78), channel_id=1, source_target_pairs={{0,6},{2,4},{4,2},{6,0},{8,14},{10,12},{12,10},{14,8},{1,7},{3,5},... | collective-permute-start | bytes 208904 | tf_op jit(solution)/shard_map/ppermute | solution.py:447
  110.3 4.5 %collective-permute-start.18 = (f32[136,128]{1,0:T(8,128)S(1)}, f32[136,128]{1,0:T(8,128)S(1)}, u32[]{:S(2)}, u32[]{:S(2)}) collective-permute-start(f32[136,128]{1,0:T(8,128)S(1)} %shard_map.78), channel_id=1, source_target_pairs={{0,4},{2,6},{4,0},{6,2},{8,12},{10,14},{12,8},{14,10},{1,5},{3,7},... | collective-permute-start | bytes 208904 | tf_op jit(solution)/shard_map/ppermute | solution.py:447
  110.3 4.5 %collective-permute-start.17 = (f32[136,128]{1,0:T(8,128)S(1)}, f32[136,128]{1,0:T(8,128)S(1)}, u32[]{:S(2)}, u32[]{:S(2)}) collective-permute-start(f32[136,128]{1,0:T(8,128)S(1)} %shard_map.78), channel_id=1, source_target_pairs={{0,2},{2,0},{4,6},{6,4},{8,10},{10,8},{12,14},{14,12},{1,3},{3,1},... | collective-permute-start | bytes 208904 | tf_op jit(solution)/shard_map/ppermute | solution.py:447
  114.8 6.9 %collective-permute-start.20 = (f32[136,128]{1,0:T(8,128)S(1)}, f32[136,128]{1,0:T(8,128)S(1)}, u32[]{:S(2)}, u32[]{:S(2)}) collective-permute-start(f32[136,128]{1,0:T(8,128)S(1)} %add_add_fusion), channel_id=1, source_target_pairs={{0,8},{2,10},{4,12},{6,14},{8,0},{10,2},{12,4},{14,6},{1,9},{3,11}... | collective-permute-start | bytes 208904 | tf_op jit(solution)/shard_map/ppermute | solution.py:447
  121.8 1.3 collective-permute-start.21
  (5 other events, 52.6 us)

commit v3 on v2

--- a/solution.py
+++ b/solution.py
@@ -30,15 +30,10 @@
     ]
 
 
-def face_of(side_ref, q):
-    side = side_ref[q // 2]
-    return (q // 2) * 2 + (side if q % 2 == 0 else 1 - side)
-
-
-def gather_faces(side_ref, faces_ref, table_ref, rows_ref, out_refs):
+def gather_faces(order_ref, faces_ref, table_ref, rows_ref, out_refs):
     slots = out_refs[0].shape[0]
     for q in range(4):
-        offset = face_of(side_ref, q) * slots
+        offset = order_ref[q] * slots
 
         def body(step, _):
             base = step * 64
@@ -51,11 +46,11 @@
         out_refs[q][...] = rows_ref[...].astype(bf16)
 
 
-def face_kernel(side_ref, faces_ref, vec_ref, o0, o1, o2, o3, table_ref, rows_ref):
+def face_kernel(order_ref, faces_ref, vec_ref, o0, o1, o2, o3, table_ref, rows_ref):
     nodes = vec_ref.shape[0]
     table_ref[0:nodes, :] = vec_ref[...].astype(f32)
     table_ref[nodes : nodes + 8, :] = jnp.zeros((8, LANES), f32)
-    gather_faces(side_ref, faces_ref, table_ref, rows_ref, (o0, o1, o2, o3))
+    gather_faces(order_ref, faces_ref, table_ref, rows_ref, (o0, o1, o2, o3))
 
 
 def send_faces(side, faces, vectors):
@@ -74,7 +69,7 @@
 
 
 def cells_kernel(
-    outer, side_ref, maps_ref, scale_ref, whole_ref, given_ref, h0, h1, h2, h3,
+    outer, order_ref, maps_ref, scale_ref, whole_ref, given_ref, h0, h1, h2, h3,
     own_ref, g0, g1, g2, g3, matrix_ref, ext_ref, in_ref, out_ref, sems, *rest
 ):
     acc = rest[:GROUP]
@@ -90,7 +85,7 @@
         vec_ref = given_ref
     fetch.start()
     for q, ghost in enumerate((h0, h1, h2, h3)):
-        start = pl.multiple_of(nodes + (face_of(side_ref, q) ^ 1) * slots, slots)
+        start = pl.multiple_of(nodes + (order_ref[q] ^ 1) * slots, slots)
         ext_ref[pl.ds(start, slots), :] = ghost[...].astype(f32)
 
     def clear(step, _):
@@ -151,7 +146,7 @@
 
     lax.fori_loop(0, nodes // 64, reduce_own, 0)
     for q, ghost in enumerate((g0, g1, g2, g3)):
-        start = pl.multiple_of(nodes + (face_of(side_ref, q) ^ 1) * slots, slots)
+        start = pl.multiple_of(nodes + (order_ref[q] ^ 1) * slots, slots)
         for r in range(0, slots, 64):
             ghost[r : r + 64, :] = total(pl.multiple_of(start + r, 64))
 
@@ -178,11 +173,11 @@
     )(side, maps, scale, matrix, vectors, *ghosts)
 
 
-def add_returned(side_ref, faces_ref, returned, acc):
+def add_returned(order_ref, faces_ref, returned, acc):
     slots = returned[0].shape[0]
     for a in acc:
         a[...] = jnp.zeros(a.shape, f32)
-    offsets = [face_of(side_ref, q) * slots for q in range(4)]
+    offsets = [order_ref[q] * slots for q in range(4)]
 
     def body(step, _):
         base = step * 16
@@ -215,11 +210,11 @@
 
 
 def first_kernel(
-    side_ref, faces_ref, interval_ref, own_ref, pot_ref, vec_ref, r0, r1, r2, r3,
+    order_ref, faces_ref, interval_ref, own_ref, pot_ref, vec_ref, r0, r1, r2, r3,
     out_ref, o0, o1, o2, o3, table_ref, rows_ref, *acc
 ):
     nodes = vec_ref.shape[0]
-    add_returned(side_ref, faces_ref, (r0, r1, r2, r3), acc)
+    add_returned(order_ref, faces_ref, (r0, r1, r2, r3), acc)
 
     def write(rows, value):
         value = value.astype(bf16)
@@ -228,14 +223,14 @@
 
     filtered(interval_ref, own_ref, pot_ref, vec_ref, acc, write)
     table_ref[nodes : nodes + 8, :] = jnp.zeros((8, LANES), f32)
-    gather_faces(side_ref, faces_ref, table_ref, rows_ref, (o0, o1, o2, o3))
+    gather_faces(order_ref, faces_ref, table_ref, rows_ref, (o0, o1, o2, o3))
 
 
 def second_kernel(
-    side_ref, faces_ref, interval_ref, own_ref, pot_ref, vec_ref, r0, r1, r2, r3, old_ref,
+    order_ref, faces_ref, interval_ref, own_ref, pot_ref, vec_ref, r0, r1, r2, r3, old_ref,
     out_ref, *acc
 ):
-    add_returned(side_ref, faces_ref, (r0, r1, r2, r3), acc)
+    add_returned(order_ref, faces_ref, (r0, r1, r2, r3), acc)
 
     def write(rows, value):
         out_ref[rows, :] = (2.0 * value - old_ref[rows, :].astype(f32)).astype(bf16)
@@ -461,11 +456,21 @@
     faces = jnp.where(face_nodes < 0, nodes, face_nodes).reshape(-1)
     potential = potential.reshape(-1, LANES)
     at = lax.axis_index("dom").astype(jnp.int32)
-    side = jnp.stack([at % 2, at // 2 % 2])
+    band = lax.axis_index("band").astype(jnp.int32)
+    kind = jnp.arange(4, dtype=jnp.int32) ^ (2 * band)
+    flip = jnp.where(kind < 2, at % 2, at // 2 % 2)
+    side = kind // 2 * 2 + ((kind % 2) ^ flip)
     pairs = exchange_pairs(lax.axis_size("dom"))
 
     def exchanged(blocks):
-        return [lax.ppermute(block, "dom", pair) for block, pair in zip(blocks, pairs)]
+        return [
+            lax.ppermute(
+                block,
+                ("dom", "band"),
+                [(2 * i + b, 2 * j + b) for b in range(2) for i, j in pairs[q ^ (2 * b)]],
+            )
+            for q, block in enumerate(blocks)
+        ]
 
     cells = functools.partial(apply_cells, side, cell_nodes.reshape(-1), cell_scale, cell_matrix)
     ghosts = exchanged(send_faces(side, faces, wavefunctions))
@@ -478,7 +483,7 @@
         side, faces, bounds, own, potential, degree_one, exchanged(sums), wavefunctions
     )
     other = swapped(degree_two)
-    band = lax.axis_index("band").astype(jnp.int32).reshape(1)
+    band = band.reshape(1)
     mine = summed_over(margin_rows(band, degree_two, other), "dom")
     inv_count = jnp.full((1,), 1.0 / (nodes * lax.axis_size("dom")), f32)
     return rotate(band, inv_count, mine, swapped(mine), degree_two, other)

time: 138 us -> 138 us (level)
  waiting for transfers between devices: 22.7 us -> 24.8 us
  starting transfers between devices: 43.7 us -> 41.7 us
    ppermute x16, waiting for transfers between devices: 11 us -> 13.1 us  [exchanged(): lax.ppermute(block, ('dom', 'band'), [(2 * i + b, 2 * j + b) for b in ran...]
    ppermute x16, starting transfers between devices: 34.5 us -> 32.7 us  [exchanged(): lax.ppermute(block, ('dom', 'band'), [(2 * i + b, 2 * j + b) for b in ran...]
where the time goes in v3:
time: 138 us
  Pallas kernels  65.1 us (47%)
  starting transfers between devices  41.7 us (30%)
  waiting for transfers between devices  24.8 us (18%)
  local copies, waits for them, and re-layouts  4.93 us (4%)
    pallas_call x2, Pallas kernels, apply_cells(): pl.pallas_call(functools.partial(cells_kernel, outer), out_shape=[jax.Sha...  39.5 us
    ppermute x16, starting transfers between devices, exchanged(): lax.ppermute(block, ('dom', 'band'), [(2 * i + b, 2 * j + b) for b in ran...  32.7 us
    pallas_call x1, Pallas kernels, rotate(): pl.pallas_call(rotate_kernel, out_shape=jax.ShapeDtypeStruct(own.shape, f...  14.5 us
    ppermute x16, waiting for transfers between devices, exchanged(): lax.ppermute(block, ('dom', 'band'), [(2 * i + b, 2 * j + b) for b in ran...  13.1 us
    ppermute x4, starting transfers between devices, summed_over(): lax.ppermute(value, axis, [(i, i ^ k * stride) for i in range(size)])  8.84 us
    ppermute x4, waiting for transfers between devices, summed_over(): lax.ppermute(value, axis, [(i, i ^ k * stride) for i in range(size)])  7.8 us
    unnamed x16, local copies, waits for them, and re-layouts  4.93 us
    pallas_call x1, Pallas kernels, finish_first(): pl.pallas_call(first_kernel, out_shape=[jax.ShapeDtypeStruct((nodes, LANE...  4.75 us
  transfers between devices with their start and end apart: 22, of which 9 were waited for; matrix products, arithmetic and copies ran while one was open for 1% of the time, Pallas kernels for 0%

profile of v3, /device:TPU:0, one launch (start us, length us, event | category | flops | bytes accessed | tf_op | source)
XLA Modules:
  0.0 137.6 jit_solution(11659111096227414001)
XLA Ops:
  2.0 1.6 %shard_map.73 = (bf16[256,128]{1,0:T(8,128)(2,1)S(1)}, bf16[256,128]{1,0:T(8,128)(2,1)S(1)}, bf16[256,128]{1,0:T(8,128)(2,1)S(1)}, bf16[256,128]{1,0:T(8,128)(2,1)S(1)}) custom-call(s32[4]{0:T(128)S(1)} %fusion.2.order_ref, s32[1024]{0:T(1024)S(1)} %bitcast.11, bf16[4096,128]{1,0:T(8,128)(2,1)S(1)} %copy-done), custom_call_target="tpu_custom_call" | custom-call | tf_op jit(solution)/shard_map/pallas_call | solution.py:58
  3.6 3.0 %collective-permute-start = (bf16[256,128]{1,0:T(8,128)(2,1)S(1)}, bf16[256,128]{1,0:T(8,128)(2,1)S(1)}, u32[]{:S(2)}, u32[]{:S(2)}) collective-permute-start(bf16[256,128]{1,0:T(8,128)(2,1)S(1)} %get-tuple-element.24), channel_id=1, source_target_pairs={{0,2},{2,0},{4,6},{6,4},{8,10},{10,8},{12,14},{14,12},{1,5},{5,1},... | collective-permute-start | bytes 196616 | tf_op jit(solution)/shard_map/ppermute | solution.py:467
  7.3 2.9 %collective-permute-start.2 = (bf16[256,128]{1,0:T(8,128)(2,1)S(1)}, bf16[256,128]{1,0:T(8,128)(2,1)S(1)}, u32[]{:S(2)}, u32[]{:S(2)}) collective-permute-start(bf16[256,128]{1,0:T(8,128)(2,1)S(1)} %get-tuple-element.26), channel_id=1, source_target_pairs={{0,4},{4,0},{2,6},{6,2},{8,12},{12,8},{10,14},{14,10},{1,3},{3,1},... | collective-permute-start | bytes 196616 | tf_op jit(solution)/shard_map/ppermute | solution.py:467
  11.6 1.4 %collective-permute-done.2.h2 = bf16[256,128]{1,0:T(8,128)(2,1)S(1)} collective-permute-done((bf16[256,128]{1,0:T(8,128)(2,1)S(1)}, bf16[256,128]{1,0:T(8,128)(2,1)S(1)}, u32[]{:S(2)}, u32[]{:S(2)}) %collective-permute-start.2) | collective-permute-done | bytes 65568 | tf_op jit(solution)/shard_map/ppermute | solution.py:467
  16.0 19.8 %shard_map.74 = (f32[4096,128]{1,0:T(8,128)S(1)}, f32[256,128]{1,0:T(8,128)S(1)}, f32[256,128]{1,0:T(8,128)S(1)}, f32[256,128]{1,0:T(8,128)S(1)}, f32[256,128]{1,0:T(8,128)S(1)}) custom-call(s32[4]{0:T(128)S(1)} %fusion.2.order_ref, s32[8192]{0:T(1024)S(1)} %bitcast.7, f32[16]{0:T(128)S(1)} %copy-done.5, bf16[512,512]{1,0:T(8,128)(2,1)S(1)} %copy-done.3, ...), custom_call_target="tpu_custom_call" | custom-call | tf_op jit(solution)/shard_map/pallas_call | solution.py:157
  35.8 2.9 %collective-permute-start.4 = (f32[256,128]{1,0:T(8,128)S(1)}, f32[256,128]{1,0:T(8,128)S(1)}, u32[]{:S(2)}, u32[]{:S(2)}) collective-permute-start(f32[256,128]{1,0:T(8,128)S(1)} %get-tuple-element.29), channel_id=1, source_target_pairs={{0,2},{2,0},{4,6},{6,4},{8,10},{10,8},{12,14},{14,12},{1,5},{5,1},... | collective-permute-start | bytes 393224 | tf_op jit(solution)/shard_map/ppermute | solution.py:467
  39.4 5.2 %collective-permute-start.6 = (f32[256,128]{1,0:T(8,128)S(1)}, f32[256,128]{1,0:T(8,128)S(1)}, u32[]{:S(2)}, u32[]{:S(2)}) collective-permute-start(f32[256,128]{1,0:T(8,128)S(1)} %get-tuple-element.31), channel_id=1, source_target_pairs={{0,4},{4,0},{2,6},{6,2},{8,12},{12,8},{10,14},{14,10},{1,3},{3,1},... | collective-permute-start | bytes 393224 | tf_op jit(solution)/shard_map/ppermute | solution.py:467
  45.3 5.0 %collective-permute-done.6.r2 = f32[256,128]{1,0:T(8,128)S(1)} collective-permute-done((f32[256,128]{1,0:T(8,128)S(1)}, f32[256,128]{1,0:T(8,128)S(1)}, u32[]{:S(2)}, u32[]{:S(2)}) %collective-permute-start.6) | collective-permute-done | bytes 131104 | tf_op jit(solution)/shard_map/ppermute | solution.py:467
  50.3 4.7 %shard_map.75 = (bf16[4096,128]{1,0:T(8,128)(2,1)S(1)}, bf16[256,128]{1,0:T(8,128)(2,1)S(1)}, bf16[256,128]{1,0:T(8,128)(2,1)S(1)}, bf16[256,128]{1,0:T(8,128)(2,1)S(1)}, bf16[256,128]{1,0:T(8,128)(2,1)S(1)}) custom-call(s32[4]{0:T(128)S(1)} %fusion.2.order_ref, s32[1024]{0:T(1024)S(1)} %bitcast.12, f32[2]{0:T(128)S(1)} %copy-done.6, ...), custom_call_target="tpu_custom_call" | custom-call | tf_op jit(solution)/shard_map/pallas_call | solution.py:243
  56.6 5.1 %collective-permute-start.10 = (bf16[256,128]{1,0:T(8,128)(2,1)S(1)}, bf16[256,128]{1,0:T(8,128)(2,1)S(1)}, u32[]{:S(2)}, u32[]{:S(2)}) collective-permute-start(bf16[256,128]{1,0:T(8,128)(2,1)S(1)} %get-tuple-element.36), channel_id=1, source_target_pairs={{0,4},{4,0},{2,6},{6,2},{8,12},{12,8},{10,14},{14,10},{1,3},{3,1},... | collective-permute-start | bytes 196616 | tf_op jit(solution)/shard_map/ppermute | solution.py:467
  62.3 2.9 %collective-permute-done.10.h2 = bf16[256,128]{1,0:T(8,128)(2,1)S(1)} collective-permute-done((bf16[256,128]{1,0:T(8,128)(2,1)S(1)}, bf16[256,128]{1,0:T(8,128)(2,1)S(1)}, u32[]{:S(2)}, u32[]{:S(2)}) %collective-permute-start.10) | collective-permute-done | bytes 65568 | tf_op jit(solution)/shard_map/ppermute | solution.py:467
  65.2 19.7 %shard_map.76 = (f32[4096,128]{1,0:T(8,128)S(1)}, f32[256,128]{1,0:T(8,128)S(1)}, f32[256,128]{1,0:T(8,128)S(1)}, f32[256,128]{1,0:T(8,128)S(1)}, f32[256,128]{1,0:T(8,128)S(1)}) custom-call(s32[4]{0:T(128)S(1)} %fusion.2.order_ref, s32[8192]{0:T(1024)S(1)} %bitcast.8, f32[16]{0:T(128)S(1)} %copy-done.5, bf16[512,512]{1,0:T(8,128)(2,1)S(1)} %copy-done.3, ...), custom_call_target="tpu_custom_call" | custom-call | tf_op jit(solution)/shard_map/pallas_call | solution.py:157
  85.0 2.3 %collective-permute-start.12 = (f32[256,128]{1,0:T(8,128)S(1)}, f32[256,128]{1,0:T(8,128)S(1)}, u32[]{:S(2)}, u32[]{:S(2)}) collective-permute-start(f32[256,128]{1,0:T(8,128)S(1)} %get-tuple-element.39), channel_id=1, source_target_pairs={{0,2},{2,0},{4,6},{6,4},{8,10},{10,8},{12,14},{14,12},{1,5},{5,1},... | collective-permute-start | bytes 393224 | tf_op jit(solution)/shard_map/ppermute | solution.py:467
  87.9 5.2 %collective-permute-start.14 = (f32[256,128]{1,0:T(8,128)S(1)}, f32[256,128]{1,0:T(8,128)S(1)}, u32[]{:S(2)}, u32[]{:S(2)}) collective-permute-start(f32[256,128]{1,0:T(8,128)S(1)} %get-tuple-element.41), channel_id=1, source_target_pairs={{0,4},{4,0},{2,6},{6,2},{8,12},{12,8},{10,14},{14,10},{1,3},{3,1},... | collective-permute-start | bytes 393224 | tf_op jit(solution)/shard_map/ppermute | solution.py:467
  93.8 3.8 %collective-permute-done.14.r2 = f32[256,128]{1,0:T(8,128)S(1)} collective-permute-done((f32[256,128]{1,0:T(8,128)S(1)}, f32[256,128]{1,0:T(8,128)S(1)}, u32[]{:S(2)}, u32[]{:S(2)}) %collective-permute-start.14) | collective-permute-done | bytes 131104 | tf_op jit(solution)/shard_map/ppermute | solution.py:467
  97.6 4.0 %shard_map.77.own_ref = bf16[4096,128]{1,0:T(8,128)(2,1)S(1)} custom-call(s32[4]{0:T(128)S(1)} %fusion.2.order_ref, s32[1024]{0:T(1024)S(1)} %bitcast.13, f32[2]{0:T(128)S(1)} %copy-done.6, f32[4096,128]{1,0:T(8,128)S(1)} %get-tuple-element.38.own_ref, f32[32,128]{1,0:T(8,128)S(1)} %bitcast.10, bf16[4096,128]{1,0:T(8,128)(2,1)S(1)} %get-tuple-element.33.given_ref.vec_ref, ...), custom_call_target="tpu_custom_call" | custom-call | tf_op jit(solution)/shard_map/pallas_call | solution.py:260
  101.7 2.6 %collective-permute-done.16.other_ref = bf16[4096,128]{1,0:T(8,128)(2,1)S(1)} collective-permute-done((bf16[4096,128]{1,0:T(8,128)(2,1)S(1)}, bf16[4096,128]{1,0:T(8,128)(2,1)S(1)}, u32[]{:S(2)}, u32[]{:S(2)}) %collective-permute-start.16) | collective-permute-done | bytes 1048608 | tf_op jit(solution)/shard_map/ppermute | solution.py:451
  105.0 5.2 %collective-permute-start.19 = (f32[136,128]{1,0:T(8,128)S(1)}, f32[136,128]{1,0:T(8,128)S(1)}, u32[]{:S(2)}, u32[]{:S(2)}) collective-permute-start(f32[136,128]{1,0:T(8,128)S(1)} %shard_map.78), channel_id=1, source_target_pairs={{0,6},{2,4},{4,2},{6,0},{8,14},{10,12},{12,10},{14,8},{1,7},{3,5},... | collective-permute-start | bytes 208904 | tf_op jit(solution)/shard_map/ppermute | solution.py:442
  110.9 2.3 %collective-permute-done.19 = f32[136,128]{1,0:T(8,128)S(1)} collective-permute-done((f32[136,128]{1,0:T(8,128)S(1)}, f32[136,128]{1,0:T(8,128)S(1)}, u32[]{:S(2)}, u32[]{:S(2)}) %collective-permute-start.19) | collective-permute-done | bytes 69664 | tf_op jit(solution)/shard_map/ppermute | solution.py:442
  113.3 1.6 %collective-permute-done.18 = f32[136,128]{1,0:T(8,128)S(1)} collective-permute-done((f32[136,128]{1,0:T(8,128)S(1)}, f32[136,128]{1,0:T(8,128)S(1)}, u32[]{:S(2)}, u32[]{:S(2)}) %collective-permute-start.18) | collective-permute-done | bytes 69664 | tf_op jit(solution)/shard_map/ppermute | solution.py:442
  114.8 3.0 %collective-permute-start.20 = (f32[136,128]{1,0:T(8,128)S(1)}, f32[136,128]{1,0:T(8,128)S(1)}, u32[]{:S(2)}, u32[]{:S(2)}) collective-permute-start(f32[136,128]{1,0:T(8,128)S(1)} %add_add_fusion), channel_id=1, source_target_pairs={{0,8},{2,10},{4,12},{6,14},{8,0},{10,2},{12,4},{14,6},{1,9},{3,11}... | collective-permute-start | bytes 208904 | tf_op jit(solution)/shard_map/ppermute | solution.py:442
  117.8 3.9 %collective-permute-done.20 = f32[136,128]{1,0:T(8,128)S(1)} collective-permute-done((f32[136,128]{1,0:T(8,128)S(1)}, f32[136,128]{1,0:T(8,128)S(1)}, u32[]{:S(2)}, u32[]{:S(2)}) %collective-permute-start.20) | collective-permute-done | bytes 69664 | tf_op jit(solution)/shard_map/ppermute | solution.py:442
  121.8 1.2 collective-permute-done.21.theirs_ref
  123.1 14.5 %shard_map.79 = f32[4096,128]{1,0:T(8,128)} custom-call(s32[1]{0:T(128)} %bitcast.band_ref, f32[1]{0:T(128)} %constant.52.clone.1.count_ref, f32[136,128]{1,0:T(8,128)S(1)} %add.37.mine_ref, f32[136,128]{1,0:T(8,128)S(1)} %collective-permute-done.21.theirs_ref, bf16[4096,128]{1,0:T(8,128)(2,1)S(1)} %shard_map.77.own_ref, ...), custom_call_target="tpu_custom_call" | custom-call | tf_op jit(solution)/shard_map/pallas_call | solution.py:420
  (47 shorter events, 13.4 us)
Async XLA Ops:
  0.0 50.3 %copy-start.6 = (f32[2]{0:T(128)S(1)}, f32[2]{0:T(128)}, u32[]{:S(2)}) copy-start(f32[2]{0:T(128)} %interval_ref.3) | copy-start | bytes 28
  0.0 50.3 %copy-start.4 = (f32[4096]{0:T(1024)S(1)}, f32[4096]{0:T(1024)}, u32[]{:S(2)}) copy-start(f32[4096]{0:T(1024)} %param.11) | copy-start | bytes 49156
  3.6 8.0 %collective-permute-start = (bf16[256,128]{1,0:T(8,128)(2,1)S(1)}, bf16[256,128]{1,0:T(8,128)(2,1)S(1)}, u32[]{:S(2)}, u32[]{:S(2)}) collective-permute-start(bf16[256,128]{1,0:T(8,128)(2,1)S(1)} %get-tuple-element.24), channel_id=1, source_target_pairs={{0,2},{2,0},{4,6},{6,4},{8,10},{10,8},{12,14},{14,12},{1,5},{5,1},... | collective-permute-start | bytes 196616 | tf_op jit(solution)/shard_map/ppermute | solution.py:467
  6.6 5.0 %collective-permute-start.1 = (bf16[256,128]{1,0:T(8,128)(2,1)S(1)}, bf16[256,128]{1,0:T(8,128)(2,1)S(1)}, u32[]{:S(2)}, u32[]{:S(2)}) collective-permute-start(bf16[256,128]{1,0:T(8,128)(2,1)S(1)} %get-tuple-element.25), channel_id=1, source_target_pairs={{2,4},{4,2},{6,8},{8,6},{10,12},{12,10},{5,9},{9,5},{7,11},{11,7},... | collective-permute-start | bytes 196616 | tf_op jit(solution)/shard_map/ppermute | solution.py:467
  7.3 5.8 %collective-permute-start.2 = (bf16[256,128]{1,0:T(8,128)(2,1)S(1)}, bf16[256,128]{1,0:T(8,128)(2,1)S(1)}, u32[]{:S(2)}, u32[]{:S(2)}) collective-permute-start(bf16[256,128]{1,0:T(8,128)(2,1)S(1)} %get-tuple-element.26), channel_id=1, source_target_pairs={{0,4},{4,0},{2,6},{6,2},{8,12},{12,8},{10,14},{14,10},{1,3},{3,1},... | collective-permute-start | bytes 196616 | tf_op jit(solution)/shard_map/ppermute | solution.py:467
  10.2 2.9 %collective-permute-start.3 = (bf16[256,128]{1,0:T(8,128)(2,1)S(1)}, bf16[256,128]{1,0:T(8,128)(2,1)S(1)}, u32[]{:S(2)}, u32[]{:S(2)}) collective-permute-start(bf16[256,128]{1,0:T(8,128)(2,1)S(1)} %get-tuple-element.27), channel_id=1, source_target_pairs={{4,8},{8,4},{6,10},{10,6},{3,5},{5,3},{7,9},{9,7},{11,13},{13,11},... | collective-permute-start | bytes 196616 | tf_op jit(solution)/shard_map/ppermute | solution.py:467
  35.8 9.5 %collective-permute-start.4 = (f32[256,128]{1,0:T(8,128)S(1)}, f32[256,128]{1,0:T(8,128)S(1)}, u32[]{:S(2)}, u32[]{:S(2)}) collective-permute-start(f32[256,128]{1,0:T(8,128)S(1)} %get-tuple-element.29), channel_id=1, source_target_pairs={{0,2},{2,0},{4,6},{6,4},{8,10},{10,8},{12,14},{14,12},{1,5},{5,1},... | collective-permute-start | bytes 393224 | tf_op jit(solution)/shard_map/ppermute | solution.py:467
  38.7 6.6 %collective-permute-start.5 = (f32[256,128]{1,0:T(8,128)S(1)}, f32[256,128]{1,0:T(8,128)S(1)}, u32[]{:S(2)}, u32[]{:S(2)}) collective-permute-start(f32[256,128]{1,0:T(8,128)S(1)} %get-tuple-element.30), channel_id=1, source_target_pairs={{2,4},{4,2},{6,8},{8,6},{10,12},{12,10},{5,9},{9,5},{7,11},{11,7},... | collective-permute-start | bytes 393224 | tf_op jit(solution)/shard_map/ppermute | solution.py:467
  39.4 10.9 %collective-permute-start.6 = (f32[256,128]{1,0:T(8,128)S(1)}, f32[256,128]{1,0:T(8,128)S(1)}, u32[]{:S(2)}, u32[]{:S(2)}) collective-permute-start(f32[256,128]{1,0:T(8,128)S(1)} %get-tuple-element.31), channel_id=1, source_target_pairs={{0,4},{4,0},{2,6},{6,2},{8,12},{12,8},{10,14},{14,10},{1,3},{3,1},... | collective-permute-start | bytes 393224 | tf_op jit(solution)/shard_map/ppermute | solution.py:467
  44.6 5.7 %collective-permute-start.7 = (f32[256,128]{1,0:T(8,128)S(1)}, f32[256,128]{1,0:T(8,128)S(1)}, u32[]{:S(2)}, u32[]{:S(2)}) collective-permute-start(f32[256,128]{1,0:T(8,128)S(1)} %get-tuple-element.32), channel_id=1, source_target_pairs={{4,8},{8,4},{6,10},{10,6},{3,5},{5,3},{7,9},{9,7},{11,13},{13,11},... | collective-permute-start | bytes 393224 | tf_op jit(solution)/shard_map/ppermute | solution.py:467
  55.0 7.3 %collective-permute-start.8 = (bf16[256,128]{1,0:T(8,128)(2,1)S(1)}, bf16[256,128]{1,0:T(8,128)(2,1)S(1)}, u32[]{:S(2)}, u32[]{:S(2)}) collective-permute-start(bf16[256,128]{1,0:T(8,128)(2,1)S(1)} %get-tuple-element.34), channel_id=1, source_target_pairs={{0,2},{2,0},{4,6},{6,4},{8,10},{10,8},{12,14},{14,12},{1,5},{5,1},... | collective-permute-start | bytes 196616 | tf_op jit(solution)/shard_map/ppermute | solution.py:467
  55.9 6.4 %collective-permute-start.9 = (bf16[256,128]{1,0:T(8,128)(2,1)S(1)}, bf16[256,128]{1,0:T(8,128)(2,1)S(1)}, u32[]{:S(2)}, u32[]{:S(2)}) collective-permute-start(bf16[256,128]{1,0:T(8,128)(2,1)S(1)} %get-tuple-element.35), channel_id=1, source_target_pairs={{2,4},{4,2},{6,8},{8,6},{10,12},{12,10},{5,9},{9,5},{7,11},{11,7},... | collective-permute-start | bytes 196616 | tf_op jit(solution)/shard_map/ppermute | solution.py:467
  56.6 8.6 %collective-permute-start.10 = (bf16[256,128]{1,0:T(8,128)(2,1)S(1)}, bf16[256,128]{1,0:T(8,128)(2,1)S(1)}, u32[]{:S(2)}, u32[]{:S(2)}) collective-permute-start(bf16[256,128]{1,0:T(8,128)(2,1)S(1)} %get-tuple-element.36), channel_id=1, source_target_pairs={{0,4},{4,0},{2,6},{6,2},{8,12},{12,8},{10,14},{14,10},{1,3},{3,1},... | collective-permute-start | bytes 196616 | tf_op jit(solution)/shard_map/ppermute | solution.py:467
  61.7 3.6 %collective-permute-start.11 = (bf16[256,128]{1,0:T(8,128)(2,1)S(1)}, bf16[256,128]{1,0:T(8,128)(2,1)S(1)}, u32[]{:S(2)}, u32[]{:S(2)}) collective-permute-start(bf16[256,128]{1,0:T(8,128)(2,1)S(1)} %get-tuple-element.37), channel_id=1, source_target_pairs={{4,8},{8,4},{6,10},{10,6},{3,5},{5,3},{7,9},{9,7},{11,13},{13,11},... | collective-permute-start | bytes 196616 | tf_op jit(solution)/shard_map/ppermute | solution.py:467
  85.0 8.8 %collective-permute-start.12 = (f32[256,128]{1,0:T(8,128)S(1)}, f32[256,128]{1,0:T(8,128)S(1)}, u32[]{:S(2)}, u32[]{:S(2)}) collective-permute-start(f32[256,128]{1,0:T(8,128)S(1)} %get-tuple-element.39), channel_id=1, source_target_pairs={{0,2},{2,0},{4,6},{6,4},{8,10},{10,8},{12,14},{14,12},{1,5},{5,1},... | collective-permute-start | bytes 393224 | tf_op jit(solution)/shard_map/ppermute | solution.py:467
  87.2 6.5 %collective-permute-start.13 = (f32[256,128]{1,0:T(8,128)S(1)}, f32[256,128]{1,0:T(8,128)S(1)}, u32[]{:S(2)}, u32[]{:S(2)}) collective-permute-start(f32[256,128]{1,0:T(8,128)S(1)} %get-tuple-element.40), channel_id=1, source_target_pairs={{2,4},{4,2},{6,8},{8,6},{10,12},{12,10},{5,9},{9,5},{7,11},{11,7},... | collective-permute-start | bytes 393224 | tf_op jit(solution)/shard_map/ppermute | solution.py:467
  87.9 9.7 %collective-permute-start.14 = (f32[256,128]{1,0:T(8,128)S(1)}, f32[256,128]{1,0:T(8,128)S(1)}, u32[]{:S(2)}, u32[]{:S(2)}) collective-permute-start(f32[256,128]{1,0:T(8,128)S(1)} %get-tuple-element.41), channel_id=1, source_target_pairs={{0,4},{4,0},{2,6},{6,2},{8,12},{12,8},{10,14},{14,10},{1,3},{3,1},... | collective-permute-start | bytes 393224 | tf_op jit(solution)/shard_map/ppermute | solution.py:467
  93.1 4.5 %collective-permute-start.15 = (f32[256,128]{1,0:T(8,128)S(1)}, f32[256,128]{1,0:T(8,128)S(1)}, u32[]{:S(2)}, u32[]{:S(2)}) collective-permute-start(f32[256,128]{1,0:T(8,128)S(1)} %get-tuple-element.42), channel_id=1, source_target_pairs={{4,8},{8,4},{6,10},{10,6},{3,5},{5,3},{7,9},{9,7},{11,13},{13,11},... | collective-permute-start | bytes 393224 | tf_op jit(solution)/shard_map/ppermute | solution.py:467
  101.6 2.7 %collective-permute-start.16 = (bf16[4096,128]{1,0:T(8,128)(2,1)S(1)}, bf16[4096,128]{1,0:T(8,128)(2,1)S(1)}, u32[]{:S(2)}, u32[]{:S(2)}) collective-permute-start(bf16[4096,128]{1,0:T(8,128)(2,1)S(1)} %shard_map.77.own_ref), channel_id=1, source_target_pairs={{0,1},{1,0},{2,3},{3,2},{4,5},{5,4},{6,7},{7,6},{8,9},{9,8},{10,11... | collective-permute-start | bytes 3145736 | tf_op jit(solution)/shard_map/ppermute | solution.py:451
  105.0 8.2 %collective-permute-start.19 = (f32[136,128]{1,0:T(8,128)S(1)}, f32[136,128]{1,0:T(8,128)S(1)}, u32[]{:S(2)}, u32[]{:S(2)}) collective-permute-start(f32[136,128]{1,0:T(8,128)S(1)} %shard_map.78), channel_id=1, source_target_pairs={{0,6},{2,4},{4,2},{6,0},{8,14},{10,12},{12,10},{14,8},{1,7},{3,5},... | collective-permute-start | bytes 208904 | tf_op jit(solution)/shard_map/ppermute | solution.py:442
  110.3 4.5 %collective-permute-start.18 = (f32[136,128]{1,0:T(8,128)S(1)}, f32[136,128]{1,0:T(8,128)S(1)}, u32[]{:S(2)}, u32[]{:S(2)}) collective-permute-start(f32[136,128]{1,0:T(8,128)S(1)} %shard_map.78), channel_id=1, source_target_pairs={{0,4},{2,6},{4,0},{6,2},{8,12},{10,14},{12,8},{14,10},{1,5},{3,7},... | collective-permute-start | bytes 208904 | tf_op jit(solution)/shard_map/ppermute | solution.py:442
  110.3 4.5 %collective-permute-start.17 = (f32[136,128]{1,0:T(8,128)S(1)}, f32[136,128]{1,0:T(8,128)S(1)}, u32[]{:S(2)}, u32[]{:S(2)}) collective-permute-start(f32[136,128]{1,0:T(8,128)S(1)} %shard_map.78), channel_id=1, source_target_pairs={{0,2},{2,0},{4,6},{6,4},{8,10},{10,8},{12,14},{14,12},{1,3},{3,1},... | collective-permute-start | bytes 208904 | tf_op jit(solution)/shard_map/ppermute | solution.py:442
  114.8 6.9 %collective-permute-start.20 = (f32[136,128]{1,0:T(8,128)S(1)}, f32[136,128]{1,0:T(8,128)S(1)}, u32[]{:S(2)}, u32[]{:S(2)}) collective-permute-start(f32[136,128]{1,0:T(8,128)S(1)} %add_add_fusion), channel_id=1, source_target_pairs={{0,8},{2,10},{4,12},{6,14},{8,0},{10,2},{12,4},{14,6},{1,9},{3,11}... | collective-permute-start | bytes 208904 | tf_op jit(solution)/shard_map/ppermute | solution.py:442
  121.7 1.3 collective-permute-start.21
  (5 other events, 51.5 us)

commit v4 on v3

--- a/solution.py
+++ b/solution.py
@@ -46,63 +46,70 @@
         out_refs[q][...] = rows_ref[...].astype(bf16)
 
 
-def face_kernel(order_ref, faces_ref, vec_ref, o0, o1, o2, o3, table_ref, rows_ref):
-    nodes = vec_ref.shape[0]
-    table_ref[0:nodes, :] = vec_ref[...].astype(f32)
+def face_kernel(
+    order_ref, faces_ref, given_ref, o0, o1, o2, o3, vec_ref, table_ref, rows_ref, sems
+):
+    nodes, chunk = vec_ref.shape[0], vec_ref.shape[0] // sems.shape[0]
+    copies = []
+    for c in range(sems.shape[0]):
+        rows = pl.ds(c * chunk, chunk)
+        copies.append(pltpu.make_async_copy(given_ref.at[rows], vec_ref.at[rows], sems.at[c]))
+        copies[-1].start()
     table_ref[nodes : nodes + 8, :] = jnp.zeros((8, LANES), f32)
+    for c, copy in enumerate(copies):
+        rows = pl.ds(c * chunk, chunk)
+        copy.wait()
+        table_ref[rows, :] = vec_ref[rows, :].astype(f32)
     gather_faces(order_ref, faces_ref, table_ref, rows_ref, (o0, o1, o2, o3))
 
 
 def send_faces(side, faces, vectors):
     nodes, slots = vectors.shape[0], faces.shape[0] // 4
-    return pl.pallas_call(
+    *blocks, vectors = pl.pallas_call(
         face_kernel,
-        out_shape=[jax.ShapeDtypeStruct((slots, LANES), bf16)] * 4,
-        in_specs=[smem, smem, vmem],
-        out_specs=[vmem] * 4,
+        out_shape=[jax.ShapeDtypeStruct((slots, LANES), bf16)] * 4
+        + [jax.ShapeDtypeStruct((nodes, LANES), bf16)],
+        in_specs=[smem, smem, hbm],
+        out_specs=[vmem] * 5,
         scratch_shapes=[
             pltpu.VMEM((nodes + 8, LANES), f32),
             pltpu.VMEM((slots, LANES), f32),
+            pltpu.SemaphoreType.DMA((4,)),
         ],
         compiler_params=grant(8),
     )(side, faces, vectors)
+    return blocks, vectors
 
 
 def cells_kernel(
-    outer, order_ref, maps_ref, scale_ref, whole_ref, given_ref, h0, h1, h2, h3,
-    own_ref, g0, g1, g2, g3, matrix_ref, ext_ref, in_ref, out_ref, sems, *rest
+    order_ref, names_ref, scales_ref, whole_ref, vec_ref, h0, h1, h2, h3,
+    own_ref, g0, g1, g2, g3, maps_ref, scale_ref, matrix_ref, ext_ref, in_ref, out_ref, sems, *acc
 ):
-    acc = rest[:GROUP]
-    nodes, slots = given_ref.shape[0], h0.shape[0]
+    nodes, slots = vec_ref.shape[0], h0.shape[0]
     size = matrix_ref.shape[0]
     ext = nodes + 4 * slots
     fetch = pltpu.make_async_copy(whole_ref, matrix_ref, sems.at[0])
-    if outer:
-        vec_ref = rest[GROUP]
-        load = pltpu.make_async_copy(given_ref, vec_ref, sems.at[1])
-        load.start()
-    else:
-        vec_ref = given_ref
+    name = pltpu.make_async_copy(names_ref, maps_ref, sems.at[1])
+    scale = pltpu.make_async_copy(scales_ref, scale_ref, sems.at[2])
+    name.start()
+    scale.start()
     fetch.start()
     for q, ghost in enumerate((h0, h1, h2, h3)):
         start = pl.multiple_of(nodes + (order_ref[q] ^ 1) * slots, slots)
         ext_ref[pl.ds(start, slots), :] = ghost[...].astype(f32)
-
-    def clear(step, _):
-        rows = pl.ds(pl.multiple_of(step * 64, 64), 64)
-        for a in acc:
-            a[rows, :] = jnp.zeros((64, LANES), f32)
-        return 0
-
-    lax.fori_loop(0, ext // 64, clear, 0)
-    if outer:
-        load.wait()
+    share = ext // (size // 8)
     ext_ref[0:nodes, :] = vec_ref[...].astype(f32)
+    name.wait()
+    scale.wait()
     cells = scale_ref.shape[0]
     for first in range(0, cells, GROUP):
 
         def gather(step, _):
             base = step * 8
+            if first == 0:
+                cleared = pl.ds(pl.multiple_of(step * share, 8), share)
+                for a in acc:
+                    a[cleared, :] = jnp.zeros((share, LANES), f32)
             for u in range(8):
                 for k in range(GROUP):
                     row = maps_ref[(first + k) * size + base + u]
@@ -151,24 +158,25 @@
             ghost[r : r + 64, :] = total(pl.multiple_of(start + r, 64))
 
 
-def apply_cells(side, maps, scale, matrix, vectors, ghosts, outer):
+def apply_cells(side, maps, scale, matrix, vectors, ghosts):
     nodes, slots, size = vectors.shape[0], ghosts[0].shape[0], matrix.shape[0]
     ext = nodes + 4 * slots
     return pl.pallas_call(
-        functools.partial(cells_kernel, outer),
+        cells_kernel,
         out_shape=[jax.ShapeDtypeStruct((nodes, LANES), f32)]
         + [jax.ShapeDtypeStruct((slots, LANES), f32)] * 4,
-        in_specs=[smem, smem, smem, hbm, hbm if outer else vmem] + [vmem] * 4,
+        in_specs=[smem, hbm, hbm, hbm] + [vmem] * 5,
         out_specs=[vmem] * 5,
         scratch_shapes=[
+            pltpu.SMEM(maps.shape, jnp.int32),
+            pltpu.SMEM(scale.shape, f32),
             pltpu.VMEM((size, size), bf16),
             pltpu.VMEM((ext, LANES), f32),
             pltpu.VMEM((GROUP, size, LANES), f32),
             pltpu.VMEM((GROUP, size, LANES), f32),
-            pltpu.SemaphoreType.DMA((2,)),
+            pltpu.SemaphoreType.DMA((3,)),
         ]
-        + [pltpu.VMEM((ext, LANES), f32)] * GROUP
-        + [pltpu.VMEM((nodes, LANES), bf16)] * outer,
+        + [pltpu.VMEM((ext, LANES), f32)] * GROUP,
         compiler_params=grant(36),
     )(side, maps, scale, matrix, vectors, *ghosts)
 
@@ -373,7 +381,7 @@
 
 def rotate_kernel(
     band_ref, count_ref, mine_ref, theirs_ref, own_ref, other_ref, out_ref, work_ref,
-    block_ref, panel_ref
+    block_ref, panel_ref, result_ref, sems
 ):
     half = LANES // 2
     band = band_ref[0]
@@ -402,18 +410,19 @@
     high = weights.astype(bf16)
     low = (weights - high.astype(f32)).astype(bf16)
     weights = jnp.concatenate([high, low], 0)
-    chunk = 512
-
-    def body(step, _):
-        rows = pl.ds(pl.multiple_of(step * chunk, chunk), chunk)
+    chunk = own_ref.shape[0] // sems.shape[0]
+    copies = []
+    for c in range(sems.shape[0]):
+        rows = pl.ds(c * chunk, chunk)
         both = jnp.concatenate([own_ref[rows, :], other_ref[rows, :]], 1)
         product = lax.dot_general(
             both, weights, (((1,), (1,)), ((), ())), preferred_element_type=f32
         )
-        out_ref[rows, :] = product[:, :LANES] + product[:, LANES:]
-        return 0
-
-    lax.fori_loop(0, own_ref.shape[0] // chunk, body, 0)
+        result_ref[rows, :] = product[:, :LANES] + product[:, LANES:]
+        copies.append(pltpu.make_async_copy(result_ref.at[rows], out_ref.at[rows], sems.at[c]))
+        copies[-1].start()
+    for copy in copies:
+        copy.wait()
 
 
 def rotate(band, inv_count, mine, theirs, own, other):
@@ -421,11 +430,13 @@
         rotate_kernel,
         out_shape=jax.ShapeDtypeStruct(own.shape, f32),
         in_specs=[smem, smem] + [vmem] * 4,
-        out_specs=vmem,
+        out_specs=hbm,
         scratch_shapes=[
             pltpu.VMEM((2 * LANES, 2 * LANES), f32),
             pltpu.VMEM((PANEL, PANEL, LANES), f32),
             pltpu.VMEM((2, PANEL, LANES), f32),
+            pltpu.VMEM(own.shape, f32),
+            pltpu.SemaphoreType.DMA((8,)),
         ],
         compiler_params=grant(12),
     )(band, inv_count, mine, theirs, own, other)
@@ -453,6 +464,9 @@
 
 def on_device(wavefunctions, bounds, cell_matrix, cell_scale, potential, cell_nodes, face_nodes):
     nodes = wavefunctions.shape[0]
+    cell_matrix = pltpu.with_memory_space_constraint(cell_matrix, pltpu.HBM)
+    cell_scale = pltpu.with_memory_space_constraint(cell_scale, pltpu.HBM)
+    held = pltpu.with_memory_space_constraint(wavefunctions, pltpu.HBM)
     faces = jnp.where(face_nodes < 0, nodes, face_nodes).reshape(-1)
     potential = potential.reshape(-1, LANES)
     at = lax.axis_index("dom").astype(jnp.int32)
@@ -473,12 +487,12 @@
         ]
 
     cells = functools.partial(apply_cells, side, cell_nodes.reshape(-1), cell_scale, cell_matrix)
-    ghosts = exchanged(send_faces(side, faces, wavefunctions))
-    own, *sums = cells(wavefunctions, ghosts, True)
+    blocks, vectors = send_faces(side, faces, held)
+    own, *sums = cells(vectors, exchanged(blocks))
     degree_one, *blocks = finish_first(
-        side, faces, bounds, own, potential, wavefunctions, exchanged(sums)
+        side, faces, bounds, own, potential, vectors, exchanged(sums)
     )
-    own, *sums = cells(degree_one, exchanged(blocks), False)
+    own, *sums = cells(degree_one, exchanged(blocks))
     degree_two = finish_second(
         side, faces, bounds, own, potential, degree_one, exchanged(sums), wavefunctions
     )

time: 138 us -> 132 us (0.957)
  local copies, waits for them, and re-layouts: 4.93 us -> 0.79 us
  Pallas kernels: 65.1 us -> 63.5 us
    unnamed x16 -> x8, local copies, waits for them, and re-layouts: 4.93 us -> 0.79 us
    pallas_call x1, Pallas kernels: 14.5 us -> 12.8 us  [rotate(): pl.pallas_call(rotate_kernel, out_shape=jax.ShapeDtypeStruct(own.shape, f...]
where the time goes in v4:
time: 132 us
  Pallas kernels  63.5 us (48%)
  starting transfers between devices  41.3 us (31%)
  waiting for transfers between devices  25.2 us (19%)
    pallas_call x2, Pallas kernels, apply_cells(): pl.pallas_call(cells_kernel, out_shape=[jax.ShapeDtypeStruct((nodes, LANE...  38.5 us
    ppermute x16, starting transfers between devices, exchanged(): lax.ppermute(block, ('dom', 'band'), [(2 * i + b, 2 * j + b) for b in ran...  32.8 us
    ppermute x16, waiting for transfers between devices, exchanged(): lax.ppermute(block, ('dom', 'band'), [(2 * i + b, 2 * j + b) for b in ran...  13.2 us
    pallas_call x1, Pallas kernels, rotate(): pl.pallas_call(rotate_kernel, out_shape=jax.ShapeDtypeStruct(own.shape, f...  12.8 us
    ppermute x4, starting transfers between devices, summed_over(): lax.ppermute(value, axis, [(i, i ^ k * stride) for i in range(size)])  8.45 us
    ppermute x4, waiting for transfers between devices, summed_over(): lax.ppermute(value, axis, [(i, i ^ k * stride) for i in range(size)])  8.1 us
    pallas_call x1, Pallas kernels, finish_first(): pl.pallas_call(first_kernel, out_shape=[jax.ShapeDtypeStruct((nodes, LANE...  4.77 us
    pallas_call x1, Pallas kernels, finish_second(): pl.pallas_call(second_kernel, out_shape=jax.ShapeDtypeStruct((nodes, LANE...  4 us
  transfers between devices with their start and end apart: 22, of which 9 were waited for; matrix products, arithmetic and copies ran while one was open for 1% of the time, Pallas kernels for 0%

profile of v4, /device:TPU:0, one launch (start us, length us, event | category | flops | bytes accessed | tf_op | source)
XLA Modules:
  0.0 131.8 jit_solution(6400183240815978127)
XLA Ops:
  0.7 2.8 %shard_map.73 = (bf16[256,128]{1,0:T(8,128)(2,1)S(1)}, bf16[256,128]{1,0:T(8,128)(2,1)S(1)}, bf16[256,128]{1,0:T(8,128)(2,1)S(1)}, bf16[256,128]{1,0:T(8,128)(2,1)S(1)}, bf16[4096,128]{1,0:T(8,128)(2,1)S(1)}) custom-call(s32[4]{0:T(128)S(1)} %fusion.2.order_ref, s32[1024]{0:T(1024)S(1)} %bitcast.11, bf16[4096,128]{1,0:T(8,128)(2,1)} %old_ref.1), custom_call_target="tpu_custom_call" | custom-call | tf_op jit(solution)/shard_map/pallas_call | solution.py:68
  3.5 3.0 %collective-permute-start = (bf16[256,128]{1,0:T(8,128)(2,1)S(1)}, bf16[256,128]{1,0:T(8,128)(2,1)S(1)}, u32[]{:S(2)}, u32[]{:S(2)}) collective-permute-start(bf16[256,128]{1,0:T(8,128)(2,1)S(1)} %get-tuple-element.26), channel_id=1, source_target_pairs={{0,2},{2,0},{4,6},{6,4},{8,10},{10,8},{12,14},{14,12},{1,5},{5,1},... | collective-permute-start | bytes 196616 | tf_op jit(solution)/shard_map/ppermute | solution.py:481
  7.2 2.9 %collective-permute-start.2 = (bf16[256,128]{1,0:T(8,128)(2,1)S(1)}, bf16[256,128]{1,0:T(8,128)(2,1)S(1)}, u32[]{:S(2)}, u32[]{:S(2)}) collective-permute-start(bf16[256,128]{1,0:T(8,128)(2,1)S(1)} %get-tuple-element.28), channel_id=1, source_target_pairs={{0,4},{4,0},{2,6},{6,2},{8,12},{12,8},{10,14},{14,10},{1,3},{3,1},... | collective-permute-start | bytes 196616 | tf_op jit(solution)/shard_map/ppermute | solution.py:481
  11.5 1.4 %collective-permute-done.2.h2 = bf16[256,128]{1,0:T(8,128)(2,1)S(1)} collective-permute-done((bf16[256,128]{1,0:T(8,128)(2,1)S(1)}, bf16[256,128]{1,0:T(8,128)(2,1)S(1)}, u32[]{:S(2)}, u32[]{:S(2)}) %collective-permute-start.2) | collective-permute-done | bytes 65568 | tf_op jit(solution)/shard_map/ppermute | solution.py:481
  12.9 19.2 %shard_map.74 = (f32[4096,128]{1,0:T(8,128)S(1)}, f32[256,128]{1,0:T(8,128)S(1)}, f32[256,128]{1,0:T(8,128)S(1)}, f32[256,128]{1,0:T(8,128)S(1)}, f32[256,128]{1,0:T(8,128)S(1)}) custom-call(s32[4]{0:T(128)S(1)} %fusion.2.order_ref, s32[8192]{0:T(1024)S(1)} %bitcast.7, f32[16]{0:T(128)} %scales_ref.3, bf16[512,512]{1,0:T(8,128)(2,1)} %whole_ref.3, ...), custom_call_target="tpu_custom_call" | custom-call | tf_op jit(solution)/shard_map/pallas_call | solution.py:164
  32.2 2.9 %collective-permute-start.4 = (f32[256,128]{1,0:T(8,128)S(1)}, f32[256,128]{1,0:T(8,128)S(1)}, u32[]{:S(2)}, u32[]{:S(2)}) collective-permute-start(f32[256,128]{1,0:T(8,128)S(1)} %get-tuple-element.31), channel_id=1, source_target_pairs={{0,2},{2,0},{4,6},{6,4},{8,10},{10,8},{12,14},{14,12},{1,5},{5,1},... | collective-permute-start | bytes 393224 | tf_op jit(solution)/shard_map/ppermute | solution.py:481
  35.8 5.2 %collective-permute-start.6 = (f32[256,128]{1,0:T(8,128)S(1)}, f32[256,128]{1,0:T(8,128)S(1)}, u32[]{:S(2)}, u32[]{:S(2)}) collective-permute-start(f32[256,128]{1,0:T(8,128)S(1)} %get-tuple-element.33), channel_id=1, source_target_pairs={{0,4},{4,0},{2,6},{6,2},{8,12},{12,8},{10,14},{14,10},{1,3},{3,1},... | collective-permute-start | bytes 393224 | tf_op jit(solution)/shard_map/ppermute | solution.py:481
  41.7 5.0 %collective-permute-done.6.r2 = f32[256,128]{1,0:T(8,128)S(1)} collective-permute-done((f32[256,128]{1,0:T(8,128)S(1)}, f32[256,128]{1,0:T(8,128)S(1)}, u32[]{:S(2)}, u32[]{:S(2)}) %collective-permute-start.6) | collective-permute-done | bytes 131104 | tf_op jit(solution)/shard_map/ppermute | solution.py:481
  46.7 4.8 %shard_map.75 = (bf16[4096,128]{1,0:T(8,128)(2,1)S(1)}, bf16[256,128]{1,0:T(8,128)(2,1)S(1)}, bf16[256,128]{1,0:T(8,128)(2,1)S(1)}, bf16[256,128]{1,0:T(8,128)(2,1)S(1)}, bf16[256,128]{1,0:T(8,128)(2,1)S(1)}) custom-call(s32[4]{0:T(128)S(1)} %fusion.2.order_ref, s32[1024]{0:T(1024)S(1)} %bitcast.12, f32[2]{0:T(128)S(1)} %copy-done.2, ...), custom_call_target="tpu_custom_call" | custom-call | tf_op jit(solution)/shard_map/pallas_call | solution.py:251
  53.1 5.0 %collective-permute-start.10 = (bf16[256,128]{1,0:T(8,128)(2,1)S(1)}, bf16[256,128]{1,0:T(8,128)(2,1)S(1)}, u32[]{:S(2)}, u32[]{:S(2)}) collective-permute-start(bf16[256,128]{1,0:T(8,128)(2,1)S(1)} %get-tuple-element.38), channel_id=1, source_target_pairs={{0,4},{4,0},{2,6},{6,2},{8,12},{12,8},{10,14},{14,10},{1,3},{3,1},... | collective-permute-start | bytes 196616 | tf_op jit(solution)/shard_map/ppermute | solution.py:481
  58.8 2.9 %collective-permute-done.10.h2 = bf16[256,128]{1,0:T(8,128)(2,1)S(1)} collective-permute-done((bf16[256,128]{1,0:T(8,128)(2,1)S(1)}, bf16[256,128]{1,0:T(8,128)(2,1)S(1)}, u32[]{:S(2)}, u32[]{:S(2)}) %collective-permute-start.10) | collective-permute-done | bytes 65568 | tf_op jit(solution)/shard_map/ppermute | solution.py:481
  61.7 19.2 %shard_map.76 = (f32[4096,128]{1,0:T(8,128)S(1)}, f32[256,128]{1,0:T(8,128)S(1)}, f32[256,128]{1,0:T(8,128)S(1)}, f32[256,128]{1,0:T(8,128)S(1)}, f32[256,128]{1,0:T(8,128)S(1)}) custom-call(s32[4]{0:T(128)S(1)} %fusion.2.order_ref, s32[8192]{0:T(1024)S(1)} %bitcast.8, f32[16]{0:T(128)} %scales_ref.3, bf16[512,512]{1,0:T(8,128)(2,1)} %whole_ref.3, ...), custom_call_target="tpu_custom_call" | custom-call | tf_op jit(solution)/shard_map/pallas_call | solution.py:164
  80.9 2.2 %collective-permute-start.12 = (f32[256,128]{1,0:T(8,128)S(1)}, f32[256,128]{1,0:T(8,128)S(1)}, u32[]{:S(2)}, u32[]{:S(2)}) collective-permute-start(f32[256,128]{1,0:T(8,128)S(1)} %get-tuple-element.41), channel_id=1, source_target_pairs={{0,2},{2,0},{4,6},{6,4},{8,10},{10,8},{12,14},{14,12},{1,5},{5,1},... | collective-permute-start | bytes 393224 | tf_op jit(solution)/shard_map/ppermute | solution.py:481
  83.8 5.2 %collective-permute-start.14 = (f32[256,128]{1,0:T(8,128)S(1)}, f32[256,128]{1,0:T(8,128)S(1)}, u32[]{:S(2)}, u32[]{:S(2)}) collective-permute-start(f32[256,128]{1,0:T(8,128)S(1)} %get-tuple-element.43), channel_id=1, source_target_pairs={{0,4},{4,0},{2,6},{6,2},{8,12},{12,8},{10,14},{14,10},{1,3},{3,1},... | collective-permute-start | bytes 393224 | tf_op jit(solution)/shard_map/ppermute | solution.py:481
  89.7 3.9 %collective-permute-done.14.r2 = f32[256,128]{1,0:T(8,128)S(1)} collective-permute-done((f32[256,128]{1,0:T(8,128)S(1)}, f32[256,128]{1,0:T(8,128)S(1)}, u32[]{:S(2)}, u32[]{:S(2)}) %collective-permute-start.14) | collective-permute-done | bytes 131104 | tf_op jit(solution)/shard_map/ppermute | solution.py:481
  93.6 4.0 %shard_map.77.own_ref = bf16[4096,128]{1,0:T(8,128)(2,1)S(1)} custom-call(s32[4]{0:T(128)S(1)} %fusion.2.order_ref, s32[1024]{0:T(1024)S(1)} %bitcast.13, f32[2]{0:T(128)S(1)} %copy-done.2, f32[4096,128]{1,0:T(8,128)S(1)} %get-tuple-element.40.own_ref, f32[32,128]{1,0:T(8,128)S(1)} %bitcast.10, bf16[4096,128]{1,0:T(8,128)(2,1)S(1)} %get-tuple-element.35.vec_ref, ...), custom_call_target="tpu_custom_call" | custom-call | tf_op jit(solution)/shard_map/pallas_call | solution.py:268
  97.7 2.6 %collective-permute-done.16.other_ref = bf16[4096,128]{1,0:T(8,128)(2,1)S(1)} collective-permute-done((bf16[4096,128]{1,0:T(8,128)(2,1)S(1)}, bf16[4096,128]{1,0:T(8,128)(2,1)S(1)}, u32[]{:S(2)}, u32[]{:S(2)}) %collective-permute-start.16) | collective-permute-done | bytes 1048608 | tf_op jit(solution)/shard_map/ppermute | solution.py:462
  101.1 5.2 %collective-permute-start.19 = (f32[136,128]{1,0:T(8,128)S(1)}, f32[136,128]{1,0:T(8,128)S(1)}, u32[]{:S(2)}, u32[]{:S(2)}) collective-permute-start(f32[136,128]{1,0:T(8,128)S(1)} %shard_map.78), channel_id=1, source_target_pairs={{0,6},{2,4},{4,2},{6,0},{8,14},{10,12},{12,10},{14,8},{1,7},{3,5},... | collective-permute-start | bytes 208904 | tf_op jit(solution)/shard_map/ppermute | solution.py:453
  107.0 2.3 %collective-permute-done.19 = f32[136,128]{1,0:T(8,128)S(1)} collective-permute-done((f32[136,128]{1,0:T(8,128)S(1)}, f32[136,128]{1,0:T(8,128)S(1)}, u32[]{:S(2)}, u32[]{:S(2)}) %collective-permute-start.19) | collective-permute-done | bytes 69664 | tf_op jit(solution)/shard_map/ppermute | solution.py:453
  109.3 1.6 %collective-permute-done.18 = f32[136,128]{1,0:T(8,128)S(1)} collective-permute-done((f32[136,128]{1,0:T(8,128)S(1)}, f32[136,128]{1,0:T(8,128)S(1)}, u32[]{:S(2)}, u32[]{:S(2)}) %collective-permute-start.18) | collective-permute-done | bytes 69664 | tf_op jit(solution)/shard_map/ppermute | solution.py:453
  110.9 2.6 %collective-permute-start.20 = (f32[136,128]{1,0:T(8,128)S(1)}, f32[136,128]{1,0:T(8,128)S(1)}, u32[]{:S(2)}, u32[]{:S(2)}) collective-permute-start(f32[136,128]{1,0:T(8,128)S(1)} %add_add_fusion), channel_id=1, source_target_pairs={{0,8},{2,10},{4,12},{6,14},{8,0},{10,2},{12,4},{14,6},{1,9},{3,11}... | collective-permute-start | bytes 208904 | tf_op jit(solution)/shard_map/ppermute | solution.py:453
  113.5 4.2 %collective-permute-done.20 = f32[136,128]{1,0:T(8,128)S(1)} collective-permute-done((f32[136,128]{1,0:T(8,128)S(1)}, f32[136,128]{1,0:T(8,128)S(1)}, u32[]{:S(2)}, u32[]{:S(2)}) %collective-permute-start.20) | collective-permute-done | bytes 69664 | tf_op jit(solution)/shard_map/ppermute | solution.py:453
  117.8 1.2 collective-permute-done.21.theirs_ref
  119.0 12.8 %shard_map.79 = f32[4096,128]{1,0:T(8,128)} custom-call(s32[1]{0:T(128)} %bitcast.band_ref, f32[1]{0:T(128)} %constant.52.clone.1.count_ref, f32[136,128]{1,0:T(8,128)S(1)} %add.37.mine_ref, f32[136,128]{1,0:T(8,128)S(1)} %collective-permute-done.21.theirs_ref, bf16[4096,128]{1,0:T(8,128)(2,1)S(1)} %shard_map.77.own_ref, ...), custom_call_target="tpu_custom_call" | custom-call | tf_op jit(solution)/shard_map/pallas_call | solution.py:429
  (39 shorter events, 9.4 us)
Async XLA Ops:
  0.0 46.7 %copy-start.1 = (f32[4096]{0:T(1024)S(1)}, f32[4096]{0:T(1024)}, u32[]{:S(2)}) copy-start(f32[4096]{0:T(1024)} %param.11) | copy-start | bytes 49156
  3.5 8.0 %collective-permute-start = (bf16[256,128]{1,0:T(8,128)(2,1)S(1)}, bf16[256,128]{1,0:T(8,128)(2,1)S(1)}, u32[]{:S(2)}, u32[]{:S(2)}) collective-permute-start(bf16[256,128]{1,0:T(8,128)(2,1)S(1)} %get-tuple-element.26), channel_id=1, source_target_pairs={{0,2},{2,0},{4,6},{6,4},{8,10},{10,8},{12,14},{14,12},{1,5},{5,1},... | collective-permute-start | bytes 196616 | tf_op jit(solution)/shard_map/ppermute | solution.py:481
  6.5 5.0 %collective-permute-start.1 = (bf16[256,128]{1,0:T(8,128)(2,1)S(1)}, bf16[256,128]{1,0:T(8,128)(2,1)S(1)}, u32[]{:S(2)}, u32[]{:S(2)}) collective-permute-start(bf16[256,128]{1,0:T(8,128)(2,1)S(1)} %get-tuple-element.27), channel_id=1, source_target_pairs={{2,4},{4,2},{6,8},{8,6},{10,12},{12,10},{5,9},{9,5},{7,11},{11,7},... | collective-permute-start | bytes 196616 | tf_op jit(solution)/shard_map/ppermute | solution.py:481
  7.2 5.8 %collective-permute-start.2 = (bf16[256,128]{1,0:T(8,128)(2,1)S(1)}, bf16[256,128]{1,0:T(8,128)(2,1)S(1)}, u32[]{:S(2)}, u32[]{:S(2)}) collective-permute-start(bf16[256,128]{1,0:T(8,128)(2,1)S(1)} %get-tuple-element.28), channel_id=1, source_target_pairs={{0,4},{4,0},{2,6},{6,2},{8,12},{12,8},{10,14},{14,10},{1,3},{3,1},... | collective-permute-start | bytes 196616 | tf_op jit(solution)/shard_map/ppermute | solution.py:481
  10.1 2.9 %collective-permute-start.3 = (bf16[256,128]{1,0:T(8,128)(2,1)S(1)}, bf16[256,128]{1,0:T(8,128)(2,1)S(1)}, u32[]{:S(2)}, u32[]{:S(2)}) collective-permute-start(bf16[256,128]{1,0:T(8,128)(2,1)S(1)} %get-tuple-element.29), channel_id=1, source_target_pairs={{4,8},{8,4},{6,10},{10,6},{3,5},{5,3},{7,9},{9,7},{11,13},{13,11},... | collective-permute-start | bytes 196616 | tf_op jit(solution)/shard_map/ppermute | solution.py:481
  32.2 9.5 %collective-permute-start.4 = (f32[256,128]{1,0:T(8,128)S(1)}, f32[256,128]{1,0:T(8,128)S(1)}, u32[]{:S(2)}, u32[]{:S(2)}) collective-permute-start(f32[256,128]{1,0:T(8,128)S(1)} %get-tuple-element.31), channel_id=1, source_target_pairs={{0,2},{2,0},{4,6},{6,4},{8,10},{10,8},{12,14},{14,12},{1,5},{5,1},... | collective-permute-start | bytes 393224 | tf_op jit(solution)/shard_map/ppermute | solution.py:481
  35.1 6.6 %collective-permute-start.5 = (f32[256,128]{1,0:T(8,128)S(1)}, f32[256,128]{1,0:T(8,128)S(1)}, u32[]{:S(2)}, u32[]{:S(2)}) collective-permute-start(f32[256,128]{1,0:T(8,128)S(1)} %get-tuple-element.32), channel_id=1, source_target_pairs={{2,4},{4,2},{6,8},{8,6},{10,12},{12,10},{5,9},{9,5},{7,11},{11,7},... | collective-permute-start | bytes 393224 | tf_op jit(solution)/shard_map/ppermute | solution.py:481
  35.8 10.9 %collective-permute-start.6 = (f32[256,128]{1,0:T(8,128)S(1)}, f32[256,128]{1,0:T(8,128)S(1)}, u32[]{:S(2)}, u32[]{:S(2)}) collective-permute-start(f32[256,128]{1,0:T(8,128)S(1)} %get-tuple-element.33), channel_id=1, source_target_pairs={{0,4},{4,0},{2,6},{6,2},{8,12},{12,8},{10,14},{14,10},{1,3},{3,1},... | collective-permute-start | bytes 393224 | tf_op jit(solution)/shard_map/ppermute | solution.py:481
  41.0 5.7 %collective-permute-start.7 = (f32[256,128]{1,0:T(8,128)S(1)}, f32[256,128]{1,0:T(8,128)S(1)}, u32[]{:S(2)}, u32[]{:S(2)}) collective-permute-start(f32[256,128]{1,0:T(8,128)S(1)} %get-tuple-element.34), channel_id=1, source_target_pairs={{4,8},{8,4},{6,10},{10,6},{3,5},{5,3},{7,9},{9,7},{11,13},{13,11},... | collective-permute-start | bytes 393224 | tf_op jit(solution)/shard_map/ppermute | solution.py:481
  46.7 47.0 %copy-start = (bf16[4096,128]{1,0:T(8,128)(2,1)S(1)}, bf16[4096,128]{1,0:T(8,128)(2,1)}, u32[]{:S(2)}) copy-start(bf16[4096,128]{1,0:T(8,128)(2,1)} %old_ref.1) | copy-start | bytes 3145732
  51.5 7.3 %collective-permute-start.8 = (bf16[256,128]{1,0:T(8,128)(2,1)S(1)}, bf16[256,128]{1,0:T(8,128)(2,1)S(1)}, u32[]{:S(2)}, u32[]{:S(2)}) collective-permute-start(bf16[256,128]{1,0:T(8,128)(2,1)S(1)} %get-tuple-element.36), channel_id=1, source_target_pairs={{0,2},{2,0},{4,6},{6,4},{8,10},{10,8},{12,14},{14,12},{1,5},{5,1},... | collective-permute-start | bytes 196616 | tf_op jit(solution)/shard_map/ppermute | solution.py:481
  52.5 6.3 %collective-permute-start.9 = (bf16[256,128]{1,0:T(8,128)(2,1)S(1)}, bf16[256,128]{1,0:T(8,128)(2,1)S(1)}, u32[]{:S(2)}, u32[]{:S(2)}) collective-permute-start(bf16[256,128]{1,0:T(8,128)(2,1)S(1)} %get-tuple-element.37), channel_id=1, source_target_pairs={{2,4},{4,2},{6,8},{8,6},{10,12},{12,10},{5,9},{9,5},{7,11},{11,7},... | collective-permute-start | bytes 196616 | tf_op jit(solution)/shard_map/ppermute | solution.py:481
  53.1 8.6 %collective-permute-start.10 = (bf16[256,128]{1,0:T(8,128)(2,1)S(1)}, bf16[256,128]{1,0:T(8,128)(2,1)S(1)}, u32[]{:S(2)}, u32[]{:S(2)}) collective-permute-start(bf16[256,128]{1,0:T(8,128)(2,1)S(1)} %get-tuple-element.38), channel_id=1, source_target_pairs={{0,4},{4,0},{2,6},{6,2},{8,12},{12,8},{10,14},{14,10},{1,3},{3,1},... | collective-permute-start | bytes 196616 | tf_op jit(solution)/shard_map/ppermute | solution.py:481
  58.1 3.6 %collective-permute-start.11 = (bf16[256,128]{1,0:T(8,128)(2,1)S(1)}, bf16[256,128]{1,0:T(8,128)(2,1)S(1)}, u32[]{:S(2)}, u32[]{:S(2)}) collective-permute-start(bf16[256,128]{1,0:T(8,128)(2,1)S(1)} %get-tuple-element.39), channel_id=1, source_target_pairs={{4,8},{8,4},{6,10},{10,6},{3,5},{5,3},{7,9},{9,7},{11,13},{13,11},... | collective-permute-start | bytes 196616 | tf_op jit(solution)/shard_map/ppermute | solution.py:481
  80.9 8.8 %collective-permute-start.12 = (f32[256,128]{1,0:T(8,128)S(1)}, f32[256,128]{1,0:T(8,128)S(1)}, u32[]{:S(2)}, u32[]{:S(2)}) collective-permute-start(f32[256,128]{1,0:T(8,128)S(1)} %get-tuple-element.41), channel_id=1, source_target_pairs={{0,2},{2,0},{4,6},{6,4},{8,10},{10,8},{12,14},{14,12},{1,5},{5,1},... | collective-permute-start | bytes 393224 | tf_op jit(solution)/shard_map/ppermute | solution.py:481
  83.2 6.6 %collective-permute-start.13 = (f32[256,128]{1,0:T(8,128)S(1)}, f32[256,128]{1,0:T(8,128)S(1)}, u32[]{:S(2)}, u32[]{:S(2)}) collective-permute-start(f32[256,128]{1,0:T(8,128)S(1)} %get-tuple-element.42), channel_id=1, source_target_pairs={{2,4},{4,2},{6,8},{8,6},{10,12},{12,10},{5,9},{9,5},{7,11},{11,7},... | collective-permute-start | bytes 393224 | tf_op jit(solution)/shard_map/ppermute | solution.py:481
  83.8 9.8 %collective-permute-start.14 = (f32[256,128]{1,0:T(8,128)S(1)}, f32[256,128]{1,0:T(8,128)S(1)}, u32[]{:S(2)}, u32[]{:S(2)}) collective-permute-start(f32[256,128]{1,0:T(8,128)S(1)} %get-tuple-element.43), channel_id=1, source_target_pairs={{0,4},{4,0},{2,6},{6,2},{8,12},{12,8},{10,14},{14,10},{1,3},{3,1},... | collective-permute-start | bytes 393224 | tf_op jit(solution)/shard_map/ppermute | solution.py:481
  89.0 4.6 %collective-permute-start.15 = (f32[256,128]{1,0:T(8,128)S(1)}, f32[256,128]{1,0:T(8,128)S(1)}, u32[]{:S(2)}, u32[]{:S(2)}) collective-permute-start(f32[256,128]{1,0:T(8,128)S(1)} %get-tuple-element.44), channel_id=1, source_target_pairs={{4,8},{8,4},{6,10},{10,6},{3,5},{5,3},{7,9},{9,7},{11,13},{13,11},... | collective-permute-start | bytes 393224 | tf_op jit(solution)/shard_map/ppermute | solution.py:481
  97.7 2.7 %collective-permute-start.16 = (bf16[4096,128]{1,0:T(8,128)(2,1)S(1)}, bf16[4096,128]{1,0:T(8,128)(2,1)S(1)}, u32[]{:S(2)}, u32[]{:S(2)}) collective-permute-start(bf16[4096,128]{1,0:T(8,128)(2,1)S(1)} %shard_map.77.own_ref), channel_id=1, source_target_pairs={{0,1},{1,0},{2,3},{3,2},{4,5},{5,4},{6,7},{7,6},{8,9},{9,8},{10,11... | collective-permute-start | bytes 3145736 | tf_op jit(solution)/shard_map/ppermute | solution.py:462
  101.1 8.2 %collective-permute-start.19 = (f32[136,128]{1,0:T(8,128)S(1)}, f32[136,128]{1,0:T(8,128)S(1)}, u32[]{:S(2)}, u32[]{:S(2)}) collective-permute-start(f32[136,128]{1,0:T(8,128)S(1)} %shard_map.78), channel_id=1, source_target_pairs={{0,6},{2,4},{4,2},{6,0},{8,14},{10,12},{12,10},{14,8},{1,7},{3,5},... | collective-permute-start | bytes 208904 | tf_op jit(solution)/shard_map/ppermute | solution.py:453
  106.3 4.6 %collective-permute-start.18 = (f32[136,128]{1,0:T(8,128)S(1)}, f32[136,128]{1,0:T(8,128)S(1)}, u32[]{:S(2)}, u32[]{:S(2)}) collective-permute-start(f32[136,128]{1,0:T(8,128)S(1)} %shard_map.78), channel_id=1, source_target_pairs={{0,4},{2,6},{4,0},{6,2},{8,12},{10,14},{12,8},{14,10},{1,5},{3,7},... | collective-permute-start | bytes 208904 | tf_op jit(solution)/shard_map/ppermute | solution.py:453
  106.3 4.6 %collective-permute-start.17 = (f32[136,128]{1,0:T(8,128)S(1)}, f32[136,128]{1,0:T(8,128)S(1)}, u32[]{:S(2)}, u32[]{:S(2)}) collective-permute-start(f32[136,128]{1,0:T(8,128)S(1)} %shard_map.78), channel_id=1, source_target_pairs={{0,2},{2,0},{4,6},{6,4},{8,10},{10,8},{12,14},{14,12},{1,3},{3,1},... | collective-permute-start | bytes 208904 | tf_op jit(solution)/shard_map/ppermute | solution.py:453
  110.9 6.8 %collective-permute-start.20 = (f32[136,128]{1,0:T(8,128)S(1)}, f32[136,128]{1,0:T(8,128)S(1)}, u32[]{:S(2)}, u32[]{:S(2)}) collective-permute-start(f32[136,128]{1,0:T(8,128)S(1)} %add_add_fusion), channel_id=1, source_target_pairs={{0,8},{2,10},{4,12},{6,14},{8,0},{10,2},{12,4},{14,6},{1,9},{3,11}... | collective-permute-start | bytes 208904 | tf_op jit(solution)/shard_map/ppermute | solution.py:453
  117.7 1.3 %collective-permute-start.21 = (f32[136,128]{1,0:T(8,128)S(1)}, f32[136,128]{1,0:T(8,128)S(1)}, u32[]{:S(2)}, u32[]{:S(2)}) collective-permute-start(f32[136,128]{1,0:T(8,128)S(1)} %add.37.mine_ref), channel_id=1, source_target_pairs={{0,1},{1,0},{2,3},{3,2},{4,5},{5,4},{6,7},{7,6},{8,9},{9,8},{10,11... | collective-permute-start | bytes 208904 | tf_op jit(solution)/shard_map/ppermute | solution.py:462
  (1 other events, 46.7 us)

commit v5 on v4

--- a/solution.py
+++ b/solution.py
@@ -9,7 +9,7 @@
 
 peer_offsets = (1, -1, 2, -2)
 f32, bf16 = jnp.float32, jnp.bfloat16
-LANES, GROUP, PANEL = 128, 8, 16
+LANES, GROUP, PANEL, HALF = 128, 8, 16, 8
 vmem = pl.BlockSpec(memory_space=pltpu.VMEM)
 smem = pl.BlockSpec(memory_space=pltpu.SMEM)
 hbm = pl.BlockSpec(memory_space=pltpu.HBM)
@@ -89,9 +89,15 @@
     size = matrix_ref.shape[0]
     ext = nodes + 4 * slots
     fetch = pltpu.make_async_copy(whole_ref, matrix_ref, sems.at[0])
-    name = pltpu.make_async_copy(names_ref, maps_ref, sems.at[1])
-    scale = pltpu.make_async_copy(scales_ref, scale_ref, sems.at[2])
-    name.start()
+    cells = scale_ref.shape[0]
+    scale = pltpu.make_async_copy(scales_ref, scale_ref, sems.at[1])
+    names = []
+    for batch in range(cells // GROUP):
+        part = pl.ds(batch * GROUP * size, GROUP * size)
+        names.append(
+            pltpu.make_async_copy(names_ref.at[part], maps_ref.at[part], sems.at[2 + batch])
+        )
+        names[-1].start()
     scale.start()
     fetch.start()
     for q, ghost in enumerate((h0, h1, h2, h3)):
@@ -99,10 +105,8 @@
         ext_ref[pl.ds(start, slots), :] = ghost[...].astype(f32)
     share = ext // (size // 8)
     ext_ref[0:nodes, :] = vec_ref[...].astype(f32)
-    name.wait()
-    scale.wait()
-    cells = scale_ref.shape[0]
     for first in range(0, cells, GROUP):
+        names[first // GROUP].wait()
 
         def gather(step, _):
             base = step * 8
@@ -119,6 +123,7 @@
         lax.fori_loop(0, size // 8, gather, 0)
         if first == 0:
             fetch.wait()
+            scale.wait()
         for k in range(0, GROUP, 2):
             pair = jnp.concatenate([in_ref[k].astype(bf16), in_ref[k + 1].astype(bf16)], 1)
             product = jnp.dot(matrix_ref[...], pair, preferred_element_type=f32)
@@ -174,7 +179,7 @@
             pltpu.VMEM((ext, LANES), f32),
             pltpu.VMEM((GROUP, size, LANES), f32),
             pltpu.VMEM((GROUP, size, LANES), f32),
-            pltpu.SemaphoreType.DMA((3,)),
+            pltpu.SemaphoreType.DMA((2 + scale.shape[0] // GROUP,)),
         ]
         + [pltpu.VMEM((ext, LANES), f32)] * GROUP,
         compiler_params=grant(36),
@@ -322,7 +327,7 @@
     return high, mid, (rest - mid.astype(f32)).astype(bf16)
 
 
-def invert_factor(work_ref, block_ref, panel_ref):
+def invert_factor(work_ref, block_ref, panel_ref, lower_ref, second_ref):
     total = work_ref.shape[0]
     halves = total // LANES
     col = lax.broadcasted_iota(jnp.int32, (PANEL, total), 1)
@@ -339,26 +344,58 @@
         panel = jnp.where(col == row + first, 1.0, panel)
         for h in range(halves):
             panel_ref[h] = panel[:, h * LANES : (h + 1) * LANES]
-        entry = {
-            (i, k): block_ref[k, pl.ds(i, 8, stride=0), :]
-            for k in range(PANEL)
-            for i in range(k, PANEL)
-        }
+
+        def repeated(ref, k, i):
+            return ref[k, pl.ds(i, HALF, stride=0), :]
+
+        def factor(entry, below):
+            scales = []
+            for k in range(HALF):
+                scale = lax.rsqrt(entry[k, k])
+                scales.append(scale)
+                for i in range(k + 1, HALF):
+                    entry[i, k] = entry[i, k] * scale
+                for i in range(k + 1, HALF):
+                    for m in range(k + 1, i + 1):
+                        entry[i, m] = entry[i, m] - entry[i, k] * entry[m, k]
+                if below:
+                    below[k] = below[k] * scale
+                    for m in range(k + 1, HALF):
+                        below[m] = below[m] - below[k] * entry[m, k]
+            return scales
+
+        def corner(ref):
+            return {(i, k): repeated(ref, k, i) for k in range(HALF) for i in range(k, HALF)}
+
         done = []
-        for k in range(PANEL):
-            scale = lax.rsqrt(entry[k, k])
-            lines = [panel_ref[h, pl.ds(k, 8, stride=0), :] for h in range(halves)]
-            for i in range(k + 1, PANEL):
-                entry[i, k] = entry[i, k] * scale
-            for i in range(k + 1, PANEL):
-                for m in range(k + 1, i + 1):
-                    entry[i, m] = entry[i, m] - entry[i, k] * entry[m, k]
-            for m in range(k):
-                lines = [line - entry[k, m] * old for line, old in zip(lines, done[m])]
+
+        def write_lines(k, weights, scale):
+            lines = [panel_ref[h, pl.ds(k, HALF, stride=0), :] for h in range(halves)]
+            for m, weight in enumerate(weights):
+                lines = [line - weight * old for line, old in zip(lines, done[m])]
             lines = [line * scale for line in lines]
             done.append(lines)
+            at = k % HALF
             for h in range(halves):
-                panel_ref[h, k : k + 1, :] = lines[h][k % 8 : k % 8 + 1, :]
+                panel_ref[h, k : k + 1, :] = lines[h][at : at + 1, :]
+
+        entry = corner(block_ref)
+        below = [block_ref[k, HALF:PANEL, :] for k in range(HALF)]
+        scales = factor(entry, below)
+        for k in range(HALF):
+            write_lines(k, [entry[k, m] for m in range(k)], scales[k])
+            lower_ref[k] = below[k]
+        cross = {(m, k): repeated(lower_ref, k, m) for k in range(HALF) for m in range(HALF)}
+        for m in range(HALF):
+            column = block_ref[HALF + m, HALF:PANEL, :]
+            for k in range(HALF):
+                column = column - below[k] * cross[m, k]
+            second_ref[m] = column
+        entry = corner(second_ref)
+        scales = factor(entry, None)
+        for k in range(HALF):
+            weights = [cross[k, m] for m in range(HALF)] + [entry[k, m] for m in range(k)]
+            write_lines(HALF + k, weights, scales[k])
         panel = jnp.concatenate([panel_ref[h] for h in range(halves)], 1)
         right = jnp.where(col >= first + PANEL, panel, 0.0)
         ah, am, al = split_three(right)
@@ -381,7 +418,7 @@
 
 def rotate_kernel(
     band_ref, count_ref, mine_ref, theirs_ref, own_ref, other_ref, out_ref, work_ref,
-    block_ref, panel_ref, result_ref, sems
+    block_ref, panel_ref, lower_ref, second_ref, result_ref, sems
 ):
     half = LANES // 2
     band = band_ref[0]
@@ -399,7 +436,7 @@
     work_ref[LANES:, 0:LANES] = cross.T
     tail = jnp.where(col < row, packed, flipped)
     work_ref[LANES:, LANES:] = jnp.where(col == row, jnp.broadcast_to(diag, tail.shape), tail)
-    invert_factor(work_ref, block_ref, panel_ref)
+    invert_factor(work_ref, block_ref, panel_ref, lower_ref, second_ref)
     lower = jnp.where(col <= row, 1.0, 0.0)
     first = work_ref[0:LANES, 0:LANES] * lower
     last = work_ref[LANES:, LANES:] * lower
@@ -435,6 +472,8 @@
             pltpu.VMEM((2 * LANES, 2 * LANES), f32),
             pltpu.VMEM((PANEL, PANEL, LANES), f32),
             pltpu.VMEM((2, PANEL, LANES), f32),
+            pltpu.VMEM((HALF, HALF, LANES), f32),
+            pltpu.VMEM((HALF, HALF, LANES), f32),
             pltpu.VMEM(own.shape, f32),
             pltpu.SemaphoreType.DMA((8,)),
         ],

time: 132 us -> 129 us (0.977)
  Pallas kernels: 63.5 us -> 60.8 us
    pallas_call x1, Pallas kernels: 12.8 us -> 10.9 us  [rotate(): pl.pallas_call(rotate_kernel, out_shape=jax.ShapeDtypeStruct(own.shape, f...]
where the time goes in v5:
time: 129 us
  Pallas kernels  60.8 us (47%)
  starting transfers between devices  41.7 us (32%)
  waiting for transfers between devices  24.9 us (19%)
    pallas_call x2, Pallas kernels, apply_cells(): pl.pallas_call(cells_kernel, out_shape=[jax.ShapeDtypeStruct((nodes, LANE...  37.7 us
    ppermute x16, starting transfers between devices, exchanged(): lax.ppermute(block, ('dom', 'band'), [(2 * i + b, 2 * j + b) for b in ran...  32.8 us
    ppermute x16, waiting for transfers between devices, exchanged(): lax.ppermute(block, ('dom', 'band'), [(2 * i + b, 2 * j + b) for b in ran...  13.1 us
    pallas_call x1, Pallas kernels, rotate(): pl.pallas_call(rotate_kernel, out_shape=jax.ShapeDtypeStruct(own.shape, f...  10.9 us
    ppermute x4, starting transfers between devices, summed_over(): lax.ppermute(value, axis, [(i, i ^ k * stride) for i in range(size)])  8.77 us
    ppermute x4, waiting for transfers between devices, summed_over(): lax.ppermute(value, axis, [(i, i ^ k * stride) for i in range(size)])  7.88 us
    pallas_call x1, Pallas kernels, finish_first(): pl.pallas_call(first_kernel, out_shape=[jax.ShapeDtypeStruct((nodes, LANE...  4.75 us
    pallas_call x1, Pallas kernels, finish_second(): pl.pallas_call(second_kernel, out_shape=jax.ShapeDtypeStruct((nodes, LANE...  3.99 us
  transfers between devices with their start and end apart: 22, of which 9 were waited for; matrix products, arithmetic and copies ran while one was open for 1% of the time, Pallas kernels for 0%

profile of v5, /device:TPU:0, one launch (start us, length us, event | category | flops | bytes accessed | tf_op | source)
XLA Modules:
  0.0 129.1 jit_solution(10248075245992228912)
XLA Ops:
  0.7 2.8 %shard_map.73 = (bf16[256,128]{1,0:T(8,128)(2,1)S(1)}, bf16[256,128]{1,0:T(8,128)(2,1)S(1)}, bf16[256,128]{1,0:T(8,128)(2,1)S(1)}, bf16[256,128]{1,0:T(8,128)(2,1)S(1)}, bf16[4096,128]{1,0:T(8,128)(2,1)S(1)}) custom-call(s32[4]{0:T(128)S(1)} %fusion.2.order_ref, s32[1024]{0:T(1024)S(1)} %bitcast.11, bf16[4096,128]{1,0:T(8,128)(2,1)} %old_ref.1), custom_call_target="tpu_custom_call" | custom-call | tf_op jit(solution)/shard_map/pallas_call | solution.py:68
  3.5 3.0 %collective-permute-start = (bf16[256,128]{1,0:T(8,128)(2,1)S(1)}, bf16[256,128]{1,0:T(8,128)(2,1)S(1)}, u32[]{:S(2)}, u32[]{:S(2)}) collective-permute-start(bf16[256,128]{1,0:T(8,128)(2,1)S(1)} %get-tuple-element.26), channel_id=1, source_target_pairs={{0,2},{2,0},{4,6},{6,4},{8,10},{10,8},{12,14},{14,12},{1,5},{5,1},... | collective-permute-start | bytes 196616 | tf_op jit(solution)/shard_map/ppermute | solution.py:520
  7.2 2.9 %collective-permute-start.2 = (bf16[256,128]{1,0:T(8,128)(2,1)S(1)}, bf16[256,128]{1,0:T(8,128)(2,1)S(1)}, u32[]{:S(2)}, u32[]{:S(2)}) collective-permute-start(bf16[256,128]{1,0:T(8,128)(2,1)S(1)} %get-tuple-element.28), channel_id=1, source_target_pairs={{0,4},{4,0},{2,6},{6,2},{8,12},{12,8},{10,14},{14,10},{1,3},{3,1},... | collective-permute-start | bytes 196616 | tf_op jit(solution)/shard_map/ppermute | solution.py:520
  11.5 1.4 %collective-permute-done.2.h2 = bf16[256,128]{1,0:T(8,128)(2,1)S(1)} collective-permute-done((bf16[256,128]{1,0:T(8,128)(2,1)S(1)}, bf16[256,128]{1,0:T(8,128)(2,1)S(1)}, u32[]{:S(2)}, u32[]{:S(2)}) %collective-permute-start.2) | collective-permute-done | bytes 65568 | tf_op jit(solution)/shard_map/ppermute | solution.py:520
  12.9 18.8 %shard_map.74 = (f32[4096,128]{1,0:T(8,128)S(1)}, f32[256,128]{1,0:T(8,128)S(1)}, f32[256,128]{1,0:T(8,128)S(1)}, f32[256,128]{1,0:T(8,128)S(1)}, f32[256,128]{1,0:T(8,128)S(1)}) custom-call(s32[4]{0:T(128)S(1)} %fusion.2.order_ref, s32[8192]{0:T(1024)S(1)} %bitcast.7, f32[16]{0:T(128)} %scales_ref.3, bf16[512,512]{1,0:T(8,128)(2,1)} %whole_ref.3, ...), custom_call_target="tpu_custom_call" | custom-call | tf_op jit(solution)/shard_map/pallas_call | solution.py:169
  31.8 2.9 %collective-permute-start.4 = (f32[256,128]{1,0:T(8,128)S(1)}, f32[256,128]{1,0:T(8,128)S(1)}, u32[]{:S(2)}, u32[]{:S(2)}) collective-permute-start(f32[256,128]{1,0:T(8,128)S(1)} %get-tuple-element.31), channel_id=1, source_target_pairs={{0,2},{2,0},{4,6},{6,4},{8,10},{10,8},{12,14},{14,12},{1,5},{5,1},... | collective-permute-start | bytes 393224 | tf_op jit(solution)/shard_map/ppermute | solution.py:520
  35.4 5.2 %collective-permute-start.6 = (f32[256,128]{1,0:T(8,128)S(1)}, f32[256,128]{1,0:T(8,128)S(1)}, u32[]{:S(2)}, u32[]{:S(2)}) collective-permute-start(f32[256,128]{1,0:T(8,128)S(1)} %get-tuple-element.33), channel_id=1, source_target_pairs={{0,4},{4,0},{2,6},{6,2},{8,12},{12,8},{10,14},{14,10},{1,3},{3,1},... | collective-permute-start | bytes 393224 | tf_op jit(solution)/shard_map/ppermute | solution.py:520
  41.3 5.0 %collective-permute-done.6.r2 = f32[256,128]{1,0:T(8,128)S(1)} collective-permute-done((f32[256,128]{1,0:T(8,128)S(1)}, f32[256,128]{1,0:T(8,128)S(1)}, u32[]{:S(2)}, u32[]{:S(2)}) %collective-permute-start.6) | collective-permute-done | bytes 131104 | tf_op jit(solution)/shard_map/ppermute | solution.py:520
  46.3 4.8 %shard_map.75 = (bf16[4096,128]{1,0:T(8,128)(2,1)S(1)}, bf16[256,128]{1,0:T(8,128)(2,1)S(1)}, bf16[256,128]{1,0:T(8,128)(2,1)S(1)}, bf16[256,128]{1,0:T(8,128)(2,1)S(1)}, bf16[256,128]{1,0:T(8,128)(2,1)S(1)}) custom-call(s32[4]{0:T(128)S(1)} %fusion.2.order_ref, s32[1024]{0:T(1024)S(1)} %bitcast.12, f32[2]{0:T(128)S(1)} %copy-done.2, ...), custom_call_target="tpu_custom_call" | custom-call | tf_op jit(solution)/shard_map/pallas_call | solution.py:256
  52.7 5.0 %collective-permute-start.10 = (bf16[256,128]{1,0:T(8,128)(2,1)S(1)}, bf16[256,128]{1,0:T(8,128)(2,1)S(1)}, u32[]{:S(2)}, u32[]{:S(2)}) collective-permute-start(bf16[256,128]{1,0:T(8,128)(2,1)S(1)} %get-tuple-element.38), channel_id=1, source_target_pairs={{0,4},{4,0},{2,6},{6,2},{8,12},{12,8},{10,14},{14,10},{1,3},{3,1},... | collective-permute-start | bytes 196616 | tf_op jit(solution)/shard_map/ppermute | solution.py:520
  58.4 2.9 %collective-permute-done.10.h2 = bf16[256,128]{1,0:T(8,128)(2,1)S(1)} collective-permute-done((bf16[256,128]{1,0:T(8,128)(2,1)S(1)}, bf16[256,128]{1,0:T(8,128)(2,1)S(1)}, u32[]{:S(2)}, u32[]{:S(2)}) %collective-permute-start.10) | collective-permute-done | bytes 65568 | tf_op jit(solution)/shard_map/ppermute | solution.py:520
  61.3 18.8 %shard_map.76 = (f32[4096,128]{1,0:T(8,128)S(1)}, f32[256,128]{1,0:T(8,128)S(1)}, f32[256,128]{1,0:T(8,128)S(1)}, f32[256,128]{1,0:T(8,128)S(1)}, f32[256,128]{1,0:T(8,128)S(1)}) custom-call(s32[4]{0:T(128)S(1)} %fusion.2.order_ref, s32[8192]{0:T(1024)S(1)} %bitcast.8, f32[16]{0:T(128)} %scales_ref.3, bf16[512,512]{1,0:T(8,128)(2,1)} %whole_ref.3, ...), custom_call_target="tpu_custom_call" | custom-call | tf_op jit(solution)/shard_map/pallas_call | solution.py:169
  80.1 2.3 %collective-permute-start.12 = (f32[256,128]{1,0:T(8,128)S(1)}, f32[256,128]{1,0:T(8,128)S(1)}, u32[]{:S(2)}, u32[]{:S(2)}) collective-permute-start(f32[256,128]{1,0:T(8,128)S(1)} %get-tuple-element.41), channel_id=1, source_target_pairs={{0,2},{2,0},{4,6},{6,4},{8,10},{10,8},{12,14},{14,12},{1,5},{5,1},... | collective-permute-start | bytes 393224 | tf_op jit(solution)/shard_map/ppermute | solution.py:520
  83.1 5.2 %collective-permute-start.14 = (f32[256,128]{1,0:T(8,128)S(1)}, f32[256,128]{1,0:T(8,128)S(1)}, u32[]{:S(2)}, u32[]{:S(2)}) collective-permute-start(f32[256,128]{1,0:T(8,128)S(1)} %get-tuple-element.43), channel_id=1, source_target_pairs={{0,4},{4,0},{2,6},{6,2},{8,12},{12,8},{10,14},{14,10},{1,3},{3,1},... | collective-permute-start | bytes 393224 | tf_op jit(solution)/shard_map/ppermute | solution.py:520
  88.9 3.8 %collective-permute-done.14.r2 = f32[256,128]{1,0:T(8,128)S(1)} collective-permute-done((f32[256,128]{1,0:T(8,128)S(1)}, f32[256,128]{1,0:T(8,128)S(1)}, u32[]{:S(2)}, u32[]{:S(2)}) %collective-permute-start.14) | collective-permute-done | bytes 131104 | tf_op jit(solution)/shard_map/ppermute | solution.py:520
  92.8 4.0 %shard_map.77.own_ref = bf16[4096,128]{1,0:T(8,128)(2,1)S(1)} custom-call(s32[4]{0:T(128)S(1)} %fusion.2.order_ref, s32[1024]{0:T(1024)S(1)} %bitcast.13, f32[2]{0:T(128)S(1)} %copy-done.2, f32[4096,128]{1,0:T(8,128)S(1)} %get-tuple-element.40.own_ref, f32[32,128]{1,0:T(8,128)S(1)} %bitcast.10, bf16[4096,128]{1,0:T(8,128)(2,1)S(1)} %get-tuple-element.35.vec_ref, ...), custom_call_target="tpu_custom_call" | custom-call | tf_op jit(solution)/shard_map/pallas_call | solution.py:273
  96.8 2.6 %collective-permute-done.16.other_ref = bf16[4096,128]{1,0:T(8,128)(2,1)S(1)} collective-permute-done((bf16[4096,128]{1,0:T(8,128)(2,1)S(1)}, bf16[4096,128]{1,0:T(8,128)(2,1)S(1)}, u32[]{:S(2)}, u32[]{:S(2)}) %collective-permute-start.16) | collective-permute-done | bytes 1048608 | tf_op jit(solution)/shard_map/ppermute | solution.py:501
  100.2 5.3 %collective-permute-start.19 = (f32[136,128]{1,0:T(8,128)S(1)}, f32[136,128]{1,0:T(8,128)S(1)}, u32[]{:S(2)}, u32[]{:S(2)}) collective-permute-start(f32[136,128]{1,0:T(8,128)S(1)} %shard_map.78), channel_id=1, source_target_pairs={{0,6},{2,4},{4,2},{6,0},{8,14},{10,12},{12,10},{14,8},{1,7},{3,5},... | collective-permute-start | bytes 208904 | tf_op jit(solution)/shard_map/ppermute | solution.py:492
  106.2 2.3 %collective-permute-done.19 = f32[136,128]{1,0:T(8,128)S(1)} collective-permute-done((f32[136,128]{1,0:T(8,128)S(1)}, f32[136,128]{1,0:T(8,128)S(1)}, u32[]{:S(2)}, u32[]{:S(2)}) %collective-permute-start.19) | collective-permute-done | bytes 69664 | tf_op jit(solution)/shard_map/ppermute | solution.py:492
  108.5 1.6 %collective-permute-done.18 = f32[136,128]{1,0:T(8,128)S(1)} collective-permute-done((f32[136,128]{1,0:T(8,128)S(1)}, f32[136,128]{1,0:T(8,128)S(1)}, u32[]{:S(2)}, u32[]{:S(2)}) %collective-permute-start.18) | collective-permute-done | bytes 69664 | tf_op jit(solution)/shard_map/ppermute | solution.py:492
  110.1 2.8 %collective-permute-start.20 = (f32[136,128]{1,0:T(8,128)S(1)}, f32[136,128]{1,0:T(8,128)S(1)}, u32[]{:S(2)}, u32[]{:S(2)}) collective-permute-start(f32[136,128]{1,0:T(8,128)S(1)} %add_add_fusion), channel_id=1, source_target_pairs={{0,8},{2,10},{4,12},{6,14},{8,0},{10,2},{12,4},{14,6},{1,9},{3,11}... | collective-permute-start | bytes 208904 | tf_op jit(solution)/shard_map/ppermute | solution.py:492
  112.9 4.0 %collective-permute-done.20 = f32[136,128]{1,0:T(8,128)S(1)} collective-permute-done((f32[136,128]{1,0:T(8,128)S(1)}, f32[136,128]{1,0:T(8,128)S(1)}, u32[]{:S(2)}, u32[]{:S(2)}) %collective-permute-start.20) | collective-permute-done | bytes 69664 | tf_op jit(solution)/shard_map/ppermute | solution.py:492
  117.0 1.2 collective-permute-done.21.theirs_ref
  118.2 10.9 %shard_map.79 = f32[4096,128]{1,0:T(8,128)} custom-call(s32[1]{0:T(128)} %bitcast.band_ref, f32[1]{0:T(128)} %constant.52.clone.1.count_ref, f32[136,128]{1,0:T(8,128)S(1)} %add.37.mine_ref, f32[136,128]{1,0:T(8,128)S(1)} %collective-permute-done.21.theirs_ref, bf16[4096,128]{1,0:T(8,128)(2,1)S(1)} %shard_map.77.own_ref, ...), custom_call_target="tpu_custom_call" | custom-call | tf_op jit(solution)/shard_map/pallas_call | solution.py:466
  (39 shorter events, 9.3 us)
Async XLA Ops:
  0.0 46.2 %copy-start.1 = (f32[4096]{0:T(1024)S(1)}, f32[4096]{0:T(1024)}, u32[]{:S(2)}) copy-start(f32[4096]{0:T(1024)} %param.11) | copy-start | bytes 49156
  3.5 8.0 %collective-permute-start = (bf16[256,128]{1,0:T(8,128)(2,1)S(1)}, bf16[256,128]{1,0:T(8,128)(2,1)S(1)}, u32[]{:S(2)}, u32[]{:S(2)}) collective-permute-start(bf16[256,128]{1,0:T(8,128)(2,1)S(1)} %get-tuple-element.26), channel_id=1, source_target_pairs={{0,2},{2,0},{4,6},{6,4},{8,10},{10,8},{12,14},{14,12},{1,5},{5,1},... | collective-permute-start | bytes 196616 | tf_op jit(solution)/shard_map/ppermute | solution.py:520
  6.5 5.0 %collective-permute-start.1 = (bf16[256,128]{1,0:T(8,128)(2,1)S(1)}, bf16[256,128]{1,0:T(8,128)(2,1)S(1)}, u32[]{:S(2)}, u32[]{:S(2)}) collective-permute-start(bf16[256,128]{1,0:T(8,128)(2,1)S(1)} %get-tuple-element.27), channel_id=1, source_target_pairs={{2,4},{4,2},{6,8},{8,6},{10,12},{12,10},{5,9},{9,5},{7,11},{11,7},... | collective-permute-start | bytes 196616 | tf_op jit(solution)/shard_map/ppermute | solution.py:520
  7.2 5.8 %collective-permute-start.2 = (bf16[256,128]{1,0:T(8,128)(2,1)S(1)}, bf16[256,128]{1,0:T(8,128)(2,1)S(1)}, u32[]{:S(2)}, u32[]{:S(2)}) collective-permute-start(bf16[256,128]{1,0:T(8,128)(2,1)S(1)} %get-tuple-element.28), channel_id=1, source_target_pairs={{0,4},{4,0},{2,6},{6,2},{8,12},{12,8},{10,14},{14,10},{1,3},{3,1},... | collective-permute-start | bytes 196616 | tf_op jit(solution)/shard_map/ppermute | solution.py:520
  10.1 2.9 %collective-permute-start.3 = (bf16[256,128]{1,0:T(8,128)(2,1)S(1)}, bf16[256,128]{1,0:T(8,128)(2,1)S(1)}, u32[]{:S(2)}, u32[]{:S(2)}) collective-permute-start(bf16[256,128]{1,0:T(8,128)(2,1)S(1)} %get-tuple-element.29), channel_id=1, source_target_pairs={{4,8},{8,4},{6,10},{10,6},{3,5},{5,3},{7,9},{9,7},{11,13},{13,11},... | collective-permute-start | bytes 196616 | tf_op jit(solution)/shard_map/ppermute | solution.py:520
  31.8 9.5 %collective-permute-start.4 = (f32[256,128]{1,0:T(8,128)S(1)}, f32[256,128]{1,0:T(8,128)S(1)}, u32[]{:S(2)}, u32[]{:S(2)}) collective-permute-start(f32[256,128]{1,0:T(8,128)S(1)} %get-tuple-element.31), channel_id=1, source_target_pairs={{0,2},{2,0},{4,6},{6,4},{8,10},{10,8},{12,14},{14,12},{1,5},{5,1},... | collective-permute-start | bytes 393224 | tf_op jit(solution)/shard_map/ppermute | solution.py:520
  34.7 6.6 %collective-permute-start.5 = (f32[256,128]{1,0:T(8,128)S(1)}, f32[256,128]{1,0:T(8,128)S(1)}, u32[]{:S(2)}, u32[]{:S(2)}) collective-permute-start(f32[256,128]{1,0:T(8,128)S(1)} %get-tuple-element.32), channel_id=1, source_target_pairs={{2,4},{4,2},{6,8},{8,6},{10,12},{12,10},{5,9},{9,5},{7,11},{11,7},... | collective-permute-start | bytes 393224 | tf_op jit(solution)/shard_map/ppermute | solution.py:520
  35.4 10.9 %collective-permute-start.6 = (f32[256,128]{1,0:T(8,128)S(1)}, f32[256,128]{1,0:T(8,128)S(1)}, u32[]{:S(2)}, u32[]{:S(2)}) collective-permute-start(f32[256,128]{1,0:T(8,128)S(1)} %get-tuple-element.33), channel_id=1, source_target_pairs={{0,4},{4,0},{2,6},{6,2},{8,12},{12,8},{10,14},{14,10},{1,3},{3,1},... | collective-permute-start | bytes 393224 | tf_op jit(solution)/shard_map/ppermute | solution.py:520
  40.6 5.7 %collective-permute-start.7 = (f32[256,128]{1,0:T(8,128)S(1)}, f32[256,128]{1,0:T(8,128)S(1)}, u32[]{:S(2)}, u32[]{:S(2)}) collective-permute-start(f32[256,128]{1,0:T(8,128)S(1)} %get-tuple-element.34), channel_id=1, source_target_pairs={{4,8},{8,4},{6,10},{10,6},{3,5},{5,3},{7,9},{9,7},{11,13},{13,11},... | collective-permute-start | bytes 393224 | tf_op jit(solution)/shard_map/ppermute | solution.py:520
  46.3 46.5 %copy-start = (bf16[4096,128]{1,0:T(8,128)(2,1)S(1)}, bf16[4096,128]{1,0:T(8,128)(2,1)}, u32[]{:S(2)}) copy-start(bf16[4096,128]{1,0:T(8,128)(2,1)} %old_ref.1) | copy-start | bytes 3145732
  51.0 7.4 %collective-permute-start.8 = (bf16[256,128]{1,0:T(8,128)(2,1)S(1)}, bf16[256,128]{1,0:T(8,128)(2,1)S(1)}, u32[]{:S(2)}, u32[]{:S(2)}) collective-permute-start(bf16[256,128]{1,0:T(8,128)(2,1)S(1)} %get-tuple-element.36), channel_id=1, source_target_pairs={{0,2},{2,0},{4,6},{6,4},{8,10},{10,8},{12,14},{14,12},{1,5},{5,1},... | collective-permute-start | bytes 196616 | tf_op jit(solution)/shard_map/ppermute | solution.py:520
  52.0 6.4 %collective-permute-start.9 = (bf16[256,128]{1,0:T(8,128)(2,1)S(1)}, bf16[256,128]{1,0:T(8,128)(2,1)S(1)}, u32[]{:S(2)}, u32[]{:S(2)}) collective-permute-start(bf16[256,128]{1,0:T(8,128)(2,1)S(1)} %get-tuple-element.37), channel_id=1, source_target_pairs={{2,4},{4,2},{6,8},{8,6},{10,12},{12,10},{5,9},{9,5},{7,11},{11,7},... | collective-permute-start | bytes 196616 | tf_op jit(solution)/shard_map/ppermute | solution.py:520
  52.7 8.6 %collective-permute-start.10 = (bf16[256,128]{1,0:T(8,128)(2,1)S(1)}, bf16[256,128]{1,0:T(8,128)(2,1)S(1)}, u32[]{:S(2)}, u32[]{:S(2)}) collective-permute-start(bf16[256,128]{1,0:T(8,128)(2,1)S(1)} %get-tuple-element.38), channel_id=1, source_target_pairs={{0,4},{4,0},{2,6},{6,2},{8,12},{12,8},{10,14},{14,10},{1,3},{3,1},... | collective-permute-start | bytes 196616 | tf_op jit(solution)/shard_map/ppermute | solution.py:520
  57.7 3.6 %collective-permute-start.11 = (bf16[256,128]{1,0:T(8,128)(2,1)S(1)}, bf16[256,128]{1,0:T(8,128)(2,1)S(1)}, u32[]{:S(2)}, u32[]{:S(2)}) collective-permute-start(bf16[256,128]{1,0:T(8,128)(2,1)S(1)} %get-tuple-element.39), channel_id=1, source_target_pairs={{4,8},{8,4},{6,10},{10,6},{3,5},{5,3},{7,9},{9,7},{11,13},{13,11},... | collective-permute-start | bytes 196616 | tf_op jit(solution)/shard_map/ppermute | solution.py:520
  80.1 8.8 %collective-permute-start.12 = (f32[256,128]{1,0:T(8,128)S(1)}, f32[256,128]{1,0:T(8,128)S(1)}, u32[]{:S(2)}, u32[]{:S(2)}) collective-permute-start(f32[256,128]{1,0:T(8,128)S(1)} %get-tuple-element.41), channel_id=1, source_target_pairs={{0,2},{2,0},{4,6},{6,4},{8,10},{10,8},{12,14},{14,12},{1,5},{5,1},... | collective-permute-start | bytes 393224 | tf_op jit(solution)/shard_map/ppermute | solution.py:520
  82.4 6.5 %collective-permute-start.13 = (f32[256,128]{1,0:T(8,128)S(1)}, f32[256,128]{1,0:T(8,128)S(1)}, u32[]{:S(2)}, u32[]{:S(2)}) collective-permute-start(f32[256,128]{1,0:T(8,128)S(1)} %get-tuple-element.42), channel_id=1, source_target_pairs={{2,4},{4,2},{6,8},{8,6},{10,12},{12,10},{5,9},{9,5},{7,11},{11,7},... | collective-permute-start | bytes 393224 | tf_op jit(solution)/shard_map/ppermute | solution.py:520
  83.1 9.7 %collective-permute-start.14 = (f32[256,128]{1,0:T(8,128)S(1)}, f32[256,128]{1,0:T(8,128)S(1)}, u32[]{:S(2)}, u32[]{:S(2)}) collective-permute-start(f32[256,128]{1,0:T(8,128)S(1)} %get-tuple-element.43), channel_id=1, source_target_pairs={{0,4},{4,0},{2,6},{6,2},{8,12},{12,8},{10,14},{14,10},{1,3},{3,1},... | collective-permute-start | bytes 393224 | tf_op jit(solution)/shard_map/ppermute | solution.py:520
  88.2 4.5 %collective-permute-start.15 = (f32[256,128]{1,0:T(8,128)S(1)}, f32[256,128]{1,0:T(8,128)S(1)}, u32[]{:S(2)}, u32[]{:S(2)}) collective-permute-start(f32[256,128]{1,0:T(8,128)S(1)} %get-tuple-element.44), channel_id=1, source_target_pairs={{4,8},{8,4},{6,10},{10,6},{3,5},{5,3},{7,9},{9,7},{11,13},{13,11},... | collective-permute-start | bytes 393224 | tf_op jit(solution)/shard_map/ppermute | solution.py:520
  96.8 2.7 %collective-permute-start.16 = (bf16[4096,128]{1,0:T(8,128)(2,1)S(1)}, bf16[4096,128]{1,0:T(8,128)(2,1)S(1)}, u32[]{:S(2)}, u32[]{:S(2)}) collective-permute-start(bf16[4096,128]{1,0:T(8,128)(2,1)S(1)} %shard_map.77.own_ref), channel_id=1, source_target_pairs={{0,1},{1,0},{2,3},{3,2},{4,5},{5,4},{6,7},{7,6},{8,9},{9,8},{10,11... | collective-permute-start | bytes 3145736 | tf_op jit(solution)/shard_map/ppermute | solution.py:501
  100.2 8.3 %collective-permute-start.19 = (f32[136,128]{1,0:T(8,128)S(1)}, f32[136,128]{1,0:T(8,128)S(1)}, u32[]{:S(2)}, u32[]{:S(2)}) collective-permute-start(f32[136,128]{1,0:T(8,128)S(1)} %shard_map.78), channel_id=1, source_target_pairs={{0,6},{2,4},{4,2},{6,0},{8,14},{10,12},{12,10},{14,8},{1,7},{3,5},... | collective-permute-start | bytes 208904 | tf_op jit(solution)/shard_map/ppermute | solution.py:492
  105.6 4.6 %collective-permute-start.18 = (f32[136,128]{1,0:T(8,128)S(1)}, f32[136,128]{1,0:T(8,128)S(1)}, u32[]{:S(2)}, u32[]{:S(2)}) collective-permute-start(f32[136,128]{1,0:T(8,128)S(1)} %shard_map.78), channel_id=1, source_target_pairs={{0,4},{2,6},{4,0},{6,2},{8,12},{10,14},{12,8},{14,10},{1,5},{3,7},... | collective-permute-start | bytes 208904 | tf_op jit(solution)/shard_map/ppermute | solution.py:492
  105.6 4.6 %collective-permute-start.17 = (f32[136,128]{1,0:T(8,128)S(1)}, f32[136,128]{1,0:T(8,128)S(1)}, u32[]{:S(2)}, u32[]{:S(2)}) collective-permute-start(f32[136,128]{1,0:T(8,128)S(1)} %shard_map.78), channel_id=1, source_target_pairs={{0,2},{2,0},{4,6},{6,4},{8,10},{10,8},{12,14},{14,12},{1,3},{3,1},... | collective-permute-start | bytes 208904 | tf_op jit(solution)/shard_map/ppermute | solution.py:492
  110.1 6.8 %collective-permute-start.20 = (f32[136,128]{1,0:T(8,128)S(1)}, f32[136,128]{1,0:T(8,128)S(1)}, u32[]{:S(2)}, u32[]{:S(2)}) collective-permute-start(f32[136,128]{1,0:T(8,128)S(1)} %add_add_fusion), channel_id=1, source_target_pairs={{0,8},{2,10},{4,12},{6,14},{8,0},{10,2},{12,4},{14,6},{1,9},{3,11}... | collective-permute-start | bytes 208904 | tf_op jit(solution)/shard_map/ppermute | solution.py:492
  116.9 1.3 %collective-permute-start.21 = (f32[136,128]{1,0:T(8,128)S(1)}, f32[136,128]{1,0:T(8,128)S(1)}, u32[]{:S(2)}, u32[]{:S(2)}) collective-permute-start(f32[136,128]{1,0:T(8,128)S(1)} %add.37.mine_ref), channel_id=1, source_target_pairs={{0,1},{1,0},{2,3},{3,2},{4,5},{5,4},{6,7},{7,6},{8,9},{9,8},{10,11... | collective-permute-start | bytes 208904 | tf_op jit(solution)/shard_map/ppermute | solution.py:501
  (1 other events, 46.2 us)

commit v6 on v5

--- a/solution.py
+++ b/solution.py
@@ -30,16 +30,15 @@
     ]
 
 
-def gather_faces(order_ref, faces_ref, table_ref, rows_ref, out_refs):
+def gather_faces(named, table_ref, rows_ref, out_refs):
     slots = out_refs[0].shape[0]
     for q in range(4):
-        offset = order_ref[q] * slots
+        row_of = named(q)
 
         def body(step, _):
             base = step * 64
             for u in range(64):
-                face = faces_ref[offset + base + u]
-                rows_ref[pl.ds(base + u, 1), :] = table_ref[pl.ds(face, 1), :]
+                rows_ref[pl.ds(base + u, 1), :] = table_ref[pl.ds(row_of(base + u), 1), :]
             return 0
 
         lax.fori_loop(0, slots // 64, body, 0)
@@ -55,16 +54,20 @@
         rows = pl.ds(c * chunk, chunk)
         copies.append(pltpu.make_async_copy(given_ref.at[rows], vec_ref.at[rows], sems.at[c]))
         copies[-1].start()
-    table_ref[nodes : nodes + 8, :] = jnp.zeros((8, LANES), f32)
+    table_ref[0:8, :] = jnp.zeros((8, LANES), f32)
     for c, copy in enumerate(copies):
-        rows = pl.ds(c * chunk, chunk)
         copy.wait()
-        table_ref[rows, :] = vec_ref[rows, :].astype(f32)
-    gather_faces(order_ref, faces_ref, table_ref, rows_ref, (o0, o1, o2, o3))
-
-
-def send_faces(side, faces, vectors):
-    nodes, slots = vectors.shape[0], faces.shape[0] // 4
+        table_ref[pl.ds(8 + c * chunk, chunk), :] = vec_ref[pl.ds(c * chunk, chunk), :].astype(f32)
+
+    def named(q):
+        face = order_ref[q]
+        return lambda slot: faces_ref[face, slot] + 8
+
+    gather_faces(named, table_ref, rows_ref, (o0, o1, o2, o3))
+
+
+def send_faces(side, face_nodes, vectors):
+    nodes, slots = vectors.shape[0], face_nodes.shape[1]
     *blocks, vectors = pl.pallas_call(
         face_kernel,
         out_shape=[jax.ShapeDtypeStruct((slots, LANES), bf16)] * 4
@@ -77,7 +80,7 @@
             pltpu.SemaphoreType.DMA((4,)),
         ],
         compiler_params=grant(8),
-    )(side, faces, vectors)
+    )(side, face_nodes, vectors)
     return blocks, vectors
 
 
@@ -103,24 +106,24 @@
     for q, ghost in enumerate((h0, h1, h2, h3)):
         start = pl.multiple_of(nodes + (order_ref[q] ^ 1) * slots, slots)
         ext_ref[pl.ds(start, slots), :] = ghost[...].astype(f32)
-    share = ext // (size // 8)
+    share = ext // (size // 32)
     ext_ref[0:nodes, :] = vec_ref[...].astype(f32)
     for first in range(0, cells, GROUP):
         names[first // GROUP].wait()
 
         def gather(step, _):
-            base = step * 8
+            base = step * 32
             if first == 0:
                 cleared = pl.ds(pl.multiple_of(step * share, 8), share)
                 for a in acc:
                     a[cleared, :] = jnp.zeros((share, LANES), f32)
-            for u in range(8):
+            for u in range(32):
                 for k in range(GROUP):
                     row = maps_ref[(first + k) * size + base + u]
                     in_ref[k, pl.ds(base + u, 1), :] = ext_ref[pl.ds(row, 1), :]
             return 0
 
-        lax.fori_loop(0, size // 8, gather, 0)
+        lax.fori_loop(0, size // 32, gather, 0)
         if first == 0:
             fetch.wait()
             scale.wait()
@@ -131,8 +134,8 @@
             out_ref[k + 1] = product[:, LANES:] * scale_ref[first + k + 1]
 
         def scatter(step, _):
-            base = step * 8
-            for u in range(8):
+            base = step * 32
+            for u in range(32):
                 rows = [maps_ref[(first + k) * size + base + u] for k in range(GROUP)]
                 sums = [
                     acc[k][pl.ds(rows[k], 1), :] + out_ref[k, pl.ds(base + u, 1), :]
@@ -142,7 +145,7 @@
                     acc[k][pl.ds(rows[k], 1), :] = sums[k]
             return 0
 
-        lax.fori_loop(0, size // 8, scatter, 0)
+        lax.fori_loop(0, size // 32, scatter, 0)
 
     def total(start):
         rows = pl.ds(start, 64)
@@ -186,25 +189,49 @@
     )(side, maps, scale, matrix, vectors, *ghosts)
 
 
-def add_returned(order_ref, faces_ref, returned, acc):
+def add_returned(order_ref, faces_ref, at, returned, acc):
     slots = returned[0].shape[0]
     for a in acc:
         a[...] = jnp.zeros(a.shape, f32)
-    offsets = [order_ref[q] * slots for q in range(4)]
+    offsets = [order_ref[at + q] * slots for q in range(2)]
 
     def body(step, _):
-        base = step * 16
-        for u in range(16):
-            rows = [faces_ref[offsets[q] + base + u] for q in range(4)]
+        base = step * 32
+        for u in range(32):
+            rows = [faces_ref[offsets[q] + base + u] for q in range(2)]
             sums = [
                 acc[q][pl.ds(rows[q], 1), :] + returned[q][pl.ds(base + u, 1), :]
-                for q in range(4)
+                for q in range(2)
             ]
-            for q in range(4):
+            for q in range(2):
                 acc[q][pl.ds(rows[q], 1), :] = sums[q]
         return 0
 
-    lax.fori_loop(0, slots // 16, body, 0)
+    lax.fori_loop(0, slots // 32, body, 0)
+
+
+def early_kernel(order_ref, faces_ref, own_ref, r0, r1, out_ref, *acc):
+    add_returned(order_ref, faces_ref, 0, (r0, r1), acc)
+
+    def combine(step, _):
+        rows = pl.ds(pl.multiple_of(step * 64, 64), 64)
+        out_ref[rows, :] = own_ref[rows, :] + (acc[0][rows, :] + acc[1][rows, :])
+        return 0
+
+    lax.fori_loop(0, own_ref.shape[0] // 64, combine, 0)
+
+
+def add_early(side, faces, own, returned):
+    nodes = own.shape[0]
+    return pl.pallas_call(
+        early_kernel,
+        out_shape=jax.ShapeDtypeStruct((nodes, LANES), f32),
+        in_specs=[smem] * 2 + [vmem] * 3,
+        out_specs=vmem,
+        scratch_shapes=[pltpu.VMEM((nodes + 8, LANES), f32)] * 2,
+        compiler_params=grant(12),
+        cost_estimate=pl.CostEstimate(flops=10**6, bytes_accessed=4 * 10**6, transcendentals=0),
+    )(side, faces, own, *returned)
 
 
 def filtered(interval_ref, own_ref, pot_ref, vec_ref, acc, write):
@@ -215,19 +242,17 @@
     shifts = ((pot_ref[...] - center) * inverse).T
     for step in range(shifts.shape[1]):
         rows = slice(step * LANES, (step + 1) * LANES)
-        image = own_ref[rows, :] + (
-            (acc[0][rows, :] + acc[1][rows, :]) + (acc[2][rows, :] + acc[3][rows, :])
-        )
+        image = own_ref[rows, :] + (acc[0][rows, :] + acc[1][rows, :])
         shift = jnp.broadcast_to(shifts[:, step : step + 1], (LANES, LANES))
         write(rows, image * inverse + shift * vec_ref[rows, :].astype(f32))
 
 
 def first_kernel(
-    order_ref, faces_ref, interval_ref, own_ref, pot_ref, vec_ref, r0, r1, r2, r3,
+    order_ref, faces_ref, interval_ref, own_ref, pot_ref, vec_ref, r2, r3,
     out_ref, o0, o1, o2, o3, table_ref, rows_ref, *acc
 ):
     nodes = vec_ref.shape[0]
-    add_returned(order_ref, faces_ref, (r0, r1, r2, r3), acc)
+    add_returned(order_ref, faces_ref, 2, (r2, r3), acc)
 
     def write(rows, value):
         value = value.astype(bf16)
@@ -236,14 +261,19 @@
 
     filtered(interval_ref, own_ref, pot_ref, vec_ref, acc, write)
     table_ref[nodes : nodes + 8, :] = jnp.zeros((8, LANES), f32)
-    gather_faces(order_ref, faces_ref, table_ref, rows_ref, (o0, o1, o2, o3))
+
+    def named(q):
+        offset = order_ref[q] * rows_ref.shape[0]
+        return lambda slot: faces_ref[offset + slot]
+
+    gather_faces(named, table_ref, rows_ref, (o0, o1, o2, o3))
 
 
 def second_kernel(
-    order_ref, faces_ref, interval_ref, own_ref, pot_ref, vec_ref, r0, r1, r2, r3, old_ref,
+    order_ref, faces_ref, interval_ref, own_ref, pot_ref, vec_ref, r2, r3, old_ref,
     out_ref, *acc
 ):
-    add_returned(order_ref, faces_ref, (r0, r1, r2, r3), acc)
+    add_returned(order_ref, faces_ref, 2, (r2, r3), acc)
 
     def write(rows, value):
         out_ref[rows, :] = (2.0 * value - old_ref[rows, :].astype(f32)).astype(bf16)
@@ -253,31 +283,33 @@
 
 def finish_first(side, faces, interval, own, potential, vectors, returned):
     nodes, slots = vectors.shape[0], returned[0].shape[0]
+    own = add_early(side, faces, own, returned[:2])
     return pl.pallas_call(
         first_kernel,
         out_shape=[jax.ShapeDtypeStruct((nodes, LANES), bf16)]
         + [jax.ShapeDtypeStruct((slots, LANES), bf16)] * 4,
-        in_specs=[smem] * 3 + [vmem] * 7,
+        in_specs=[smem] * 3 + [vmem] * 5,
         out_specs=[vmem] * 5,
         scratch_shapes=[
             pltpu.VMEM((nodes + 8, LANES), f32),
             pltpu.VMEM((slots, LANES), f32),
         ]
-        + [pltpu.VMEM((nodes + 8, LANES), f32)] * 4,
+        + [pltpu.VMEM((nodes + 8, LANES), f32)] * 2,
         compiler_params=grant(20),
-    )(side, faces, interval, own, potential, vectors, *returned)
+    )(side, faces, interval, own, potential, vectors, *returned[2:])
 
 
 def finish_second(side, faces, interval, own, potential, vectors, returned, old):
     nodes = vectors.shape[0]
+    own = add_early(side, faces, own, returned[:2])
     return pl.pallas_call(
         second_kernel,
         out_shape=jax.ShapeDtypeStruct((nodes, LANES), bf16),
-        in_specs=[smem] * 3 + [vmem] * 8,
+        in_specs=[smem] * 3 + [vmem] * 6,
         out_specs=vmem,
-        scratch_shapes=[pltpu.VMEM((nodes + 8, LANES), f32)] * 4,
+        scratch_shapes=[pltpu.VMEM((nodes + 8, LANES), f32)] * 2,
         compiler_params=grant(20),
-    )(side, faces, interval, own, potential, vectors, *returned, old)
+    )(side, faces, interval, own, potential, vectors, *returned[2:], old)
 
 
 def margin_kernel(band_ref, own_ref, other_ref, out_ref):
@@ -526,7 +558,7 @@
         ]
 
     cells = functools.partial(apply_cells, side, cell_nodes.reshape(-1), cell_scale, cell_matrix)
-    blocks, vectors = send_faces(side, faces, held)
+    blocks, vectors = send_faces(side, face_nodes, held)
     own, *sums = cells(vectors, exchanged(blocks))
     degree_one, *blocks = finish_first(
         side, faces, bounds, own, potential, vectors, exchanged(sums)

time: 129 us -> 130 us (level)
  waiting for transfers between devices: 24.9 us -> 19.2 us
  Pallas kernels: 60.8 us -> 66.2 us
    ppermute x16, waiting for transfers between devices: 13.1 us -> 7.45 us  [exchanged(): lax.ppermute(block, ('dom', 'band'), [(2 * i + b, 2 * j + b) for b in ran...]
    pallas_call x0 -> x2, Pallas kernels: none -> 5.46 us  [add_early(): pl.pallas_call(early_kernel, out_shape=jax.ShapeDtypeStruct((nodes, LANES...]
    pallas_call x1, Pallas kernels: 2.76 us -> 4.41 us  [send_faces(): pl.pallas_call(face_kernel, out_shape=[jax.ShapeDtypeStruct((slots, LANES...]
  transfers between devices with their start and end apart: 22 -> 22, of which waited for: 9 -> 10; matrix products, arithmetic and copies ran while one was open for 1% -> 1% of each run, Pallas kernels for 0% -> 4%
where the time goes in v6:
time: 130 us
  Pallas kernels  66.2 us (51%)
  starting transfers between devices  42.1 us (32%)
  waiting for transfers between devices  19.2 us (15%)
  local copies, waits for them, and re-layouts  1.53 us (1%)
    pallas_call x2, Pallas kernels, apply_cells(): pl.pallas_call(cells_kernel, out_shape=[jax.ShapeDtypeStruct((nodes, LANE...  36.9 us
    ppermute x16, starting transfers between devices, exchanged(): lax.ppermute(block, ('dom', 'band'), [(2 * i + b, 2 * j + b) for b in ran...  33 us
    pallas_call x1, Pallas kernels, rotate(): pl.pallas_call(rotate_kernel, out_shape=jax.ShapeDtypeStruct(own.shape, f...  10.9 us
    ppermute x4, starting transfers between devices, summed_over(): lax.ppermute(value, axis, [(i, i ^ k * stride) for i in range(size)])  8.95 us
    ppermute x4, waiting for transfers between devices, summed_over(): lax.ppermute(value, axis, [(i, i ^ k * stride) for i in range(size)])  7.85 us
    ppermute x16, waiting for transfers between devices, exchanged(): lax.ppermute(block, ('dom', 'band'), [(2 * i + b, 2 * j + b) for b in ran...  7.45 us
    pallas_call x2, Pallas kernels, add_early(): pl.pallas_call(early_kernel, out_shape=jax.ShapeDtypeStruct((nodes, LANES...  5.46 us
    pallas_call x1, Pallas kernels, send_faces(): pl.pallas_call(face_kernel, out_shape=[jax.ShapeDtypeStruct((slots, LANES...  4.41 us
  transfers between devices with their start and end apart: 22, of which 10 were waited for; matrix products, arithmetic and copies ran while one was open for 1% of the time, Pallas kernels for 4%

profile of v6, /device:TPU:0, one launch (start us, length us, event | category | flops | bytes accessed | tf_op | source)
XLA Modules:
  0.0 129.5 jit_solution(1851591606774291227)
XLA Ops:
  0.8 4.4 %shard_map.73 = (bf16[256,128]{1,0:T(8,128)(2,1)S(1)}, bf16[256,128]{1,0:T(8,128)(2,1)S(1)}, bf16[256,128]{1,0:T(8,128)(2,1)S(1)}, bf16[256,128]{1,0:T(8,128)(2,1)S(1)}, bf16[4096,128]{1,0:T(8,128)(2,1)S(1)}) custom-call(s32[4]{0:T(128)S(1)} %fusion.2.order_ref, s32[4,256]{1,0:T(4,128)S(1)} %copy-done.2, bf16[4096,128]{1,0:T(8,128)(2,1)} %old_ref.1), custom_call_target="tpu_custom_call" | custom-call | tf_op jit(solution)/shard_map/pallas_call | solution.py:71
  5.2 3.0 %collective-permute-start = (bf16[256,128]{1,0:T(8,128)(2,1)S(1)}, bf16[256,128]{1,0:T(8,128)(2,1)S(1)}, u32[]{:S(2)}, u32[]{:S(2)}) collective-permute-start(bf16[256,128]{1,0:T(8,128)(2,1)S(1)} %get-tuple-element.26), channel_id=1, source_target_pairs={{0,2},{2,0},{4,6},{6,4},{8,10},{10,8},{12,14},{14,12},{1,5},{5,1},... | collective-permute-start | bytes 196616 | tf_op jit(solution)/shard_map/ppermute | solution.py:552
  8.8 2.9 %collective-permute-start.2 = (bf16[256,128]{1,0:T(8,128)(2,1)S(1)}, bf16[256,128]{1,0:T(8,128)(2,1)S(1)}, u32[]{:S(2)}, u32[]{:S(2)}) collective-permute-start(bf16[256,128]{1,0:T(8,128)(2,1)S(1)} %get-tuple-element.28), channel_id=1, source_target_pairs={{0,4},{4,0},{2,6},{6,2},{8,12},{12,8},{10,14},{14,10},{1,3},{3,1},... | collective-permute-start | bytes 196616 | tf_op jit(solution)/shard_map/ppermute | solution.py:552
  13.2 1.4 %collective-permute-done.2.h2 = bf16[256,128]{1,0:T(8,128)(2,1)S(1)} collective-permute-done((bf16[256,128]{1,0:T(8,128)(2,1)S(1)}, bf16[256,128]{1,0:T(8,128)(2,1)S(1)}, u32[]{:S(2)}, u32[]{:S(2)}) %collective-permute-start.2) | collective-permute-done | bytes 65568 | tf_op jit(solution)/shard_map/ppermute | solution.py:552
  14.6 18.5 %shard_map.74 = (f32[4096,128]{1,0:T(8,128)S(1)}, f32[256,128]{1,0:T(8,128)S(1)}, f32[256,128]{1,0:T(8,128)S(1)}, f32[256,128]{1,0:T(8,128)S(1)}, f32[256,128]{1,0:T(8,128)S(1)}) custom-call(s32[4]{0:T(128)S(1)} %fusion.2.order_ref, s32[8192]{0:T(1024)S(1)} %bitcast.7, f32[16]{0:T(128)} %scales_ref.3, bf16[512,512]{1,0:T(8,128)(2,1)} %whole_ref.3, ...), custom_call_target="tpu_custom_call" | custom-call | tf_op jit(solution)/shard_map/pallas_call | solution.py:172
  33.1 2.9 %collective-permute-start.4 = (f32[256,128]{1,0:T(8,128)S(1)}, f32[256,128]{1,0:T(8,128)S(1)}, u32[]{:S(2)}, u32[]{:S(2)}) collective-permute-start(f32[256,128]{1,0:T(8,128)S(1)} %get-tuple-element.31), channel_id=1, source_target_pairs={{0,2},{2,0},{4,6},{6,4},{8,10},{10,8},{12,14},{14,12},{1,5},{5,1},... | collective-permute-start | bytes 393224 | tf_op jit(solution)/shard_map/ppermute | solution.py:552
  36.7 5.2 %collective-permute-start.6 = (f32[256,128]{1,0:T(8,128)S(1)}, f32[256,128]{1,0:T(8,128)S(1)}, u32[]{:S(2)}, u32[]{:S(2)}) collective-permute-start(f32[256,128]{1,0:T(8,128)S(1)} %get-tuple-element.33), channel_id=1, source_target_pairs={{0,4},{4,0},{2,6},{6,2},{8,12},{12,8},{10,14},{14,10},{1,3},{3,1},... | collective-permute-start | bytes 393224 | tf_op jit(solution)/shard_map/ppermute | solution.py:552
  42.6 2.7 %shard_map.75.own_ref = f32[4096,128]{1,0:T(8,128)S(1)} custom-call(s32[4]{0:T(128)S(1)} %fusion.2.order_ref, s32[1024]{0:T(1024)S(1)} %bitcast.9, f32[4096,128]{1,0:T(8,128)S(1)} %get-tuple-element.30.own_ref, f32[256,128]{1,0:T(8,128)S(1)} %collective-permute-done.4.r0, f32[256,128]{1,0:T(8,128)S(1)} %collective-permute-done.5.r1), custom_call_target="tpu_custom_call" | custom-call | flops 1000000 | bytes 4000000 | tf_op jit(solution)/shard_map/pallas_call | solution.py:226
  45.4 2.2 %collective-permute-done.6.r2 = f32[256,128]{1,0:T(8,128)S(1)} collective-permute-done((f32[256,128]{1,0:T(8,128)S(1)}, f32[256,128]{1,0:T(8,128)S(1)}, u32[]{:S(2)}, u32[]{:S(2)}) %collective-permute-start.6) | collective-permute-done | bytes 131104 | tf_op jit(solution)/shard_map/ppermute | solution.py:552
  47.5 4.3 %shard_map.76 = (bf16[4096,128]{1,0:T(8,128)(2,1)S(1)}, bf16[256,128]{1,0:T(8,128)(2,1)S(1)}, bf16[256,128]{1,0:T(8,128)(2,1)S(1)}, bf16[256,128]{1,0:T(8,128)(2,1)S(1)}, bf16[256,128]{1,0:T(8,128)(2,1)S(1)}) custom-call(s32[4]{0:T(128)S(1)} %fusion.2.order_ref, s32[1024]{0:T(1024)S(1)} %bitcast.10, f32[2]{0:T(128)S(1)} %copy-done.4, ...), custom_call_target="tpu_custom_call" | custom-call | tf_op jit(solution)/shard_map/pallas_call | solution.py:287
  51.9 2.2 %collective-permute-start.8 = (bf16[256,128]{1,0:T(8,128)(2,1)S(1)}, bf16[256,128]{1,0:T(8,128)(2,1)S(1)}, u32[]{:S(2)}, u32[]{:S(2)}) collective-permute-start(bf16[256,128]{1,0:T(8,128)(2,1)S(1)} %get-tuple-element.36), channel_id=1, source_target_pairs={{0,2},{2,0},{4,6},{6,4},{8,10},{10,8},{12,14},{14,12},{1,5},{5,1},... | collective-permute-start | bytes 196616 | tf_op jit(solution)/shard_map/ppermute | solution.py:552
  54.7 4.0 %collective-permute-start.10 = (bf16[256,128]{1,0:T(8,128)(2,1)S(1)}, bf16[256,128]{1,0:T(8,128)(2,1)S(1)}, u32[]{:S(2)}, u32[]{:S(2)}) collective-permute-start(bf16[256,128]{1,0:T(8,128)(2,1)S(1)} %get-tuple-element.38), channel_id=1, source_target_pairs={{0,4},{4,0},{2,6},{6,2},{8,12},{12,8},{10,14},{14,10},{1,3},{3,1},... | collective-permute-start | bytes 196616 | tf_op jit(solution)/shard_map/ppermute | solution.py:552
  59.5 2.9 %collective-permute-done.10.h2 = bf16[256,128]{1,0:T(8,128)(2,1)S(1)} collective-permute-done((bf16[256,128]{1,0:T(8,128)(2,1)S(1)}, bf16[256,128]{1,0:T(8,128)(2,1)S(1)}, u32[]{:S(2)}, u32[]{:S(2)}) %collective-permute-start.10) | collective-permute-done | bytes 65568 | tf_op jit(solution)/shard_map/ppermute | solution.py:552
  62.3 18.5 %shard_map.77 = (f32[4096,128]{1,0:T(8,128)S(1)}, f32[256,128]{1,0:T(8,128)S(1)}, f32[256,128]{1,0:T(8,128)S(1)}, f32[256,128]{1,0:T(8,128)S(1)}, f32[256,128]{1,0:T(8,128)S(1)}) custom-call(s32[4]{0:T(128)S(1)} %fusion.2.order_ref, s32[8192]{0:T(1024)S(1)} %bitcast.8, f32[16]{0:T(128)} %scales_ref.3, bf16[512,512]{1,0:T(8,128)(2,1)} %whole_ref.3, ...), custom_call_target="tpu_custom_call" | custom-call | tf_op jit(solution)/shard_map/pallas_call | solution.py:172
  80.8 2.2 %collective-permute-start.12 = (f32[256,128]{1,0:T(8,128)S(1)}, f32[256,128]{1,0:T(8,128)S(1)}, u32[]{:S(2)}, u32[]{:S(2)}) collective-permute-start(f32[256,128]{1,0:T(8,128)S(1)} %get-tuple-element.41), channel_id=1, source_target_pairs={{0,2},{2,0},{4,6},{6,4},{8,10},{10,8},{12,14},{14,12},{1,5},{5,1},... | collective-permute-start | bytes 393224 | tf_op jit(solution)/shard_map/ppermute | solution.py:552
  83.7 5.2 %collective-permute-start.14 = (f32[256,128]{1,0:T(8,128)S(1)}, f32[256,128]{1,0:T(8,128)S(1)}, u32[]{:S(2)}, u32[]{:S(2)}) collective-permute-start(f32[256,128]{1,0:T(8,128)S(1)} %get-tuple-element.43), channel_id=1, source_target_pairs={{0,4},{4,0},{2,6},{6,2},{8,12},{12,8},{10,14},{14,10},{1,3},{3,1},... | collective-permute-start | bytes 393224 | tf_op jit(solution)/shard_map/ppermute | solution.py:552
  89.6 2.7 %shard_map.78.own_ref = f32[4096,128]{1,0:T(8,128)S(1)} custom-call(s32[4]{0:T(128)S(1)} %fusion.2.order_ref, s32[1024]{0:T(1024)S(1)} %bitcast.11, f32[4096,128]{1,0:T(8,128)S(1)} %get-tuple-element.40.own_ref, f32[256,128]{1,0:T(8,128)S(1)} %collective-permute-done.12.r0, f32[256,128]{1,0:T(8,128)S(1)} %collective-permute-done.13.r1), custom_call_target="tpu_custom_call" | custom-call | flops 1000000 | bytes 4000000 | tf_op jit(solution)/shard_map/pallas_call | solution.py:226
  93.3 3.4 %shard_map.79.own_ref = bf16[4096,128]{1,0:T(8,128)(2,1)S(1)} custom-call(s32[4]{0:T(128)S(1)} %fusion.2.order_ref, s32[1024]{0:T(1024)S(1)} %bitcast.12, f32[2]{0:T(128)S(1)} %copy-done.4, f32[4096,128]{1,0:T(8,128)S(1)} %shard_map.78.own_ref, f32[32,128]{1,0:T(8,128)S(1)} %bitcast.14, bf16[4096,128]{1,0:T(8,128)(2,1)S(1)} %get-tuple-element.35.vec_ref, ...), custom_call_target="tpu_custom_call" | custom-call | tf_op jit(solution)/shard_map/pallas_call | solution.py:305
  96.8 2.6 %collective-permute-done.16.other_ref = bf16[4096,128]{1,0:T(8,128)(2,1)S(1)} collective-permute-done((bf16[4096,128]{1,0:T(8,128)(2,1)S(1)}, bf16[4096,128]{1,0:T(8,128)(2,1)S(1)}, u32[]{:S(2)}, u32[]{:S(2)}) %collective-permute-start.16) | collective-permute-done | bytes 1048608 | tf_op jit(solution)/shard_map/ppermute | solution.py:533
  100.3 5.6 %collective-permute-start.19 = (f32[136,128]{1,0:T(8,128)S(1)}, f32[136,128]{1,0:T(8,128)S(1)}, u32[]{:S(2)}, u32[]{:S(2)}) collective-permute-start(f32[136,128]{1,0:T(8,128)S(1)} %shard_map.80), channel_id=1, source_target_pairs={{0,6},{2,4},{4,2},{6,0},{8,14},{10,12},{12,10},{14,8},{1,7},{3,5},... | collective-permute-start | bytes 208904 | tf_op jit(solution)/shard_map/ppermute | solution.py:524
  106.6 2.4 %collective-permute-done.19 = f32[136,128]{1,0:T(8,128)S(1)} collective-permute-done((f32[136,128]{1,0:T(8,128)S(1)}, f32[136,128]{1,0:T(8,128)S(1)}, u32[]{:S(2)}, u32[]{:S(2)}) %collective-permute-start.19) | collective-permute-done | bytes 69664 | tf_op jit(solution)/shard_map/ppermute | solution.py:524
  110.4 2.7 %collective-permute-start.20 = (f32[136,128]{1,0:T(8,128)S(1)}, f32[136,128]{1,0:T(8,128)S(1)}, u32[]{:S(2)}, u32[]{:S(2)}) collective-permute-start(f32[136,128]{1,0:T(8,128)S(1)} %add_add_fusion), channel_id=1, source_target_pairs={{0,8},{2,10},{4,12},{6,14},{8,0},{10,2},{12,4},{14,6},{1,9},{3,11}... | collective-permute-start | bytes 208904 | tf_op jit(solution)/shard_map/ppermute | solution.py:524
  113.1 4.0 %collective-permute-done.20 = f32[136,128]{1,0:T(8,128)S(1)} collective-permute-done((f32[136,128]{1,0:T(8,128)S(1)}, f32[136,128]{1,0:T(8,128)S(1)}, u32[]{:S(2)}, u32[]{:S(2)}) %collective-permute-start.20) | collective-permute-done | bytes 69664 | tf_op jit(solution)/shard_map/ppermute | solution.py:524
  118.5 10.9 %shard_map.81 = f32[4096,128]{1,0:T(8,128)} custom-call(s32[1]{0:T(128)} %bitcast.band_ref, f32[1]{0:T(128)} %constant.52.clone.1.count_ref, f32[136,128]{1,0:T(8,128)S(1)} %add.37.mine_ref, f32[136,128]{1,0:T(8,128)S(1)} %collective-permute-done.21.theirs_ref, bf16[4096,128]{1,0:T(8,128)(2,1)S(1)} %shard_map.79.own_ref, ...), custom_call_target="tpu_custom_call" | custom-call | tf_op jit(solution)/shard_map/pallas_call | solution.py:498
  (45 shorter events, 12.2 us)
Async XLA Ops:
  0.0 42.5 %copy-start.3 = (s32[4,256]{1,0:T(4,128)S(1)}, s32[4,256]{1,0:T(4,128)}, u32[]{:S(2)}) copy-start(s32[4,256]{1,0:T(4,128)} %faces_ref.1) | copy-start | bytes 12292
  5.2 8.0 %collective-permute-start = (bf16[256,128]{1,0:T(8,128)(2,1)S(1)}, bf16[256,128]{1,0:T(8,128)(2,1)S(1)}, u32[]{:S(2)}, u32[]{:S(2)}) collective-permute-start(bf16[256,128]{1,0:T(8,128)(2,1)S(1)} %get-tuple-element.26), channel_id=1, source_target_pairs={{0,2},{2,0},{4,6},{6,4},{8,10},{10,8},{12,14},{14,12},{1,5},{5,1},... | collective-permute-start | bytes 196616 | tf_op jit(solution)/shard_map/ppermute | solution.py:552
  8.2 5.0 %collective-permute-start.1 = (bf16[256,128]{1,0:T(8,128)(2,1)S(1)}, bf16[256,128]{1,0:T(8,128)(2,1)S(1)}, u32[]{:S(2)}, u32[]{:S(2)}) collective-permute-start(bf16[256,128]{1,0:T(8,128)(2,1)S(1)} %get-tuple-element.27), channel_id=1, source_target_pairs={{2,4},{4,2},{6,8},{8,6},{10,12},{12,10},{5,9},{9,5},{7,11},{11,7},... | collective-permute-start | bytes 196616 | tf_op jit(solution)/shard_map/ppermute | solution.py:552
  8.8 5.8 %collective-permute-start.2 = (bf16[256,128]{1,0:T(8,128)(2,1)S(1)}, bf16[256,128]{1,0:T(8,128)(2,1)S(1)}, u32[]{:S(2)}, u32[]{:S(2)}) collective-permute-start(bf16[256,128]{1,0:T(8,128)(2,1)S(1)} %get-tuple-element.28), channel_id=1, source_target_pairs={{0,4},{4,0},{2,6},{6,2},{8,12},{12,8},{10,14},{14,10},{1,3},{3,1},... | collective-permute-start | bytes 196616 | tf_op jit(solution)/shard_map/ppermute | solution.py:552
  11.7 2.9 %collective-permute-start.3 = (bf16[256,128]{1,0:T(8,128)(2,1)S(1)}, bf16[256,128]{1,0:T(8,128)(2,1)S(1)}, u32[]{:S(2)}, u32[]{:S(2)}) collective-permute-start(bf16[256,128]{1,0:T(8,128)(2,1)S(1)} %get-tuple-element.29), channel_id=1, source_target_pairs={{4,8},{8,4},{6,10},{10,6},{3,5},{5,3},{7,9},{9,7},{11,13},{13,11},... | collective-permute-start | bytes 196616 | tf_op jit(solution)/shard_map/ppermute | solution.py:552
  33.1 9.5 %collective-permute-start.4 = (f32[256,128]{1,0:T(8,128)S(1)}, f32[256,128]{1,0:T(8,128)S(1)}, u32[]{:S(2)}, u32[]{:S(2)}) collective-permute-start(f32[256,128]{1,0:T(8,128)S(1)} %get-tuple-element.31), channel_id=1, source_target_pairs={{0,2},{2,0},{4,6},{6,4},{8,10},{10,8},{12,14},{14,12},{1,5},{5,1},... | collective-permute-start | bytes 393224 | tf_op jit(solution)/shard_map/ppermute | solution.py:552
  36.0 6.6 %collective-permute-start.5 = (f32[256,128]{1,0:T(8,128)S(1)}, f32[256,128]{1,0:T(8,128)S(1)}, u32[]{:S(2)}, u32[]{:S(2)}) collective-permute-start(f32[256,128]{1,0:T(8,128)S(1)} %get-tuple-element.32), channel_id=1, source_target_pairs={{2,4},{4,2},{6,8},{8,6},{10,12},{12,10},{5,9},{9,5},{7,11},{11,7},... | collective-permute-start | bytes 393224 | tf_op jit(solution)/shard_map/ppermute | solution.py:552
  36.7 10.9 %collective-permute-start.6 = (f32[256,128]{1,0:T(8,128)S(1)}, f32[256,128]{1,0:T(8,128)S(1)}, u32[]{:S(2)}, u32[]{:S(2)}) collective-permute-start(f32[256,128]{1,0:T(8,128)S(1)} %get-tuple-element.33), channel_id=1, source_target_pairs={{0,4},{4,0},{2,6},{6,2},{8,12},{12,8},{10,14},{14,10},{1,3},{3,1},... | collective-permute-start | bytes 393224 | tf_op jit(solution)/shard_map/ppermute | solution.py:552
  41.9 5.7 %collective-permute-start.7 = (f32[256,128]{1,0:T(8,128)S(1)}, f32[256,128]{1,0:T(8,128)S(1)}, u32[]{:S(2)}, u32[]{:S(2)}) collective-permute-start(f32[256,128]{1,0:T(8,128)S(1)} %get-tuple-element.34), channel_id=1, source_target_pairs={{4,8},{8,4},{6,10},{10,6},{3,5},{5,3},{7,9},{9,7},{11,13},{13,11},... | collective-permute-start | bytes 393224 | tf_op jit(solution)/shard_map/ppermute | solution.py:552
  42.6 4.9 %copy-start.1 = (f32[4096]{0:T(1024)S(1)}, f32[4096]{0:T(1024)}, u32[]{:S(2)}) copy-start(f32[4096]{0:T(1024)} %param.11) | copy-start | bytes 49156
  51.9 7.6 %collective-permute-start.8 = (bf16[256,128]{1,0:T(8,128)(2,1)S(1)}, bf16[256,128]{1,0:T(8,128)(2,1)S(1)}, u32[]{:S(2)}, u32[]{:S(2)}) collective-permute-start(bf16[256,128]{1,0:T(8,128)(2,1)S(1)} %get-tuple-element.36), channel_id=1, source_target_pairs={{0,2},{2,0},{4,6},{6,4},{8,10},{10,8},{12,14},{14,12},{1,5},{5,1},... | collective-permute-start | bytes 196616 | tf_op jit(solution)/shard_map/ppermute | solution.py:552
  54.1 5.4 %collective-permute-start.9 = (bf16[256,128]{1,0:T(8,128)(2,1)S(1)}, bf16[256,128]{1,0:T(8,128)(2,1)S(1)}, u32[]{:S(2)}, u32[]{:S(2)}) collective-permute-start(bf16[256,128]{1,0:T(8,128)(2,1)S(1)} %get-tuple-element.37), channel_id=1, source_target_pairs={{2,4},{4,2},{6,8},{8,6},{10,12},{12,10},{5,9},{9,5},{7,11},{11,7},... | collective-permute-start | bytes 196616 | tf_op jit(solution)/shard_map/ppermute | solution.py:552
  54.7 7.6 %collective-permute-start.10 = (bf16[256,128]{1,0:T(8,128)(2,1)S(1)}, bf16[256,128]{1,0:T(8,128)(2,1)S(1)}, u32[]{:S(2)}, u32[]{:S(2)}) collective-permute-start(bf16[256,128]{1,0:T(8,128)(2,1)S(1)} %get-tuple-element.38), channel_id=1, source_target_pairs={{0,4},{4,0},{2,6},{6,2},{8,12},{12,8},{10,14},{14,10},{1,3},{3,1},... | collective-permute-start | bytes 196616 | tf_op jit(solution)/shard_map/ppermute | solution.py:552
  58.8 3.6 %collective-permute-start.11 = (bf16[256,128]{1,0:T(8,128)(2,1)S(1)}, bf16[256,128]{1,0:T(8,128)(2,1)S(1)}, u32[]{:S(2)}, u32[]{:S(2)}) collective-permute-start(bf16[256,128]{1,0:T(8,128)(2,1)S(1)} %get-tuple-element.39), channel_id=1, source_target_pairs={{4,8},{8,4},{6,10},{10,6},{3,5},{5,3},{7,9},{9,7},{11,13},{13,11},... | collective-permute-start | bytes 196616 | tf_op jit(solution)/shard_map/ppermute | solution.py:552
  80.8 8.8 %collective-permute-start.12 = (f32[256,128]{1,0:T(8,128)S(1)}, f32[256,128]{1,0:T(8,128)S(1)}, u32[]{:S(2)}, u32[]{:S(2)}) collective-permute-start(f32[256,128]{1,0:T(8,128)S(1)} %get-tuple-element.41), channel_id=1, source_target_pairs={{0,2},{2,0},{4,6},{6,4},{8,10},{10,8},{12,14},{14,12},{1,5},{5,1},... | collective-permute-start | bytes 393224 | tf_op jit(solution)/shard_map/ppermute | solution.py:552
  83.0 6.6 %collective-permute-start.13 = (f32[256,128]{1,0:T(8,128)S(1)}, f32[256,128]{1,0:T(8,128)S(1)}, u32[]{:S(2)}, u32[]{:S(2)}) collective-permute-start(f32[256,128]{1,0:T(8,128)S(1)} %get-tuple-element.42), channel_id=1, source_target_pairs={{2,4},{4,2},{6,8},{8,6},{10,12},{12,10},{5,9},{9,5},{7,11},{11,7},... | collective-permute-start | bytes 393224 | tf_op jit(solution)/shard_map/ppermute | solution.py:552
  83.7 9.6 %collective-permute-start.14 = (f32[256,128]{1,0:T(8,128)S(1)}, f32[256,128]{1,0:T(8,128)S(1)}, u32[]{:S(2)}, u32[]{:S(2)}) collective-permute-start(f32[256,128]{1,0:T(8,128)S(1)} %get-tuple-element.43), channel_id=1, source_target_pairs={{0,4},{4,0},{2,6},{6,2},{8,12},{12,8},{10,14},{14,10},{1,3},{3,1},... | collective-permute-start | bytes 393224 | tf_op jit(solution)/shard_map/ppermute | solution.py:552
  88.9 4.4 %collective-permute-start.15 = (f32[256,128]{1,0:T(8,128)S(1)}, f32[256,128]{1,0:T(8,128)S(1)}, u32[]{:S(2)}, u32[]{:S(2)}) collective-permute-start(f32[256,128]{1,0:T(8,128)S(1)} %get-tuple-element.44), channel_id=1, source_target_pairs={{4,8},{8,4},{6,10},{10,6},{3,5},{5,3},{7,9},{9,7},{11,13},{13,11},... | collective-permute-start | bytes 393224 | tf_op jit(solution)/shard_map/ppermute | solution.py:552
  96.7 2.7 %collective-permute-start.16 = (bf16[4096,128]{1,0:T(8,128)(2,1)S(1)}, bf16[4096,128]{1,0:T(8,128)(2,1)S(1)}, u32[]{:S(2)}, u32[]{:S(2)}) collective-permute-start(bf16[4096,128]{1,0:T(8,128)(2,1)S(1)} %shard_map.79.own_ref), channel_id=1, source_target_pairs={{0,1},{1,0},{2,3},{3,2},{4,5},{5,4},{6,7},{7,6},{8,9},{9,8},{10,11... | collective-permute-start | bytes 3145736 | tf_op jit(solution)/shard_map/ppermute | solution.py:533
  100.3 8.7 %collective-permute-start.19 = (f32[136,128]{1,0:T(8,128)S(1)}, f32[136,128]{1,0:T(8,128)S(1)}, u32[]{:S(2)}, u32[]{:S(2)}) collective-permute-start(f32[136,128]{1,0:T(8,128)S(1)} %shard_map.80), channel_id=1, source_target_pairs={{0,6},{2,4},{4,2},{6,0},{8,14},{10,12},{12,10},{14,8},{1,7},{3,5},... | collective-permute-start | bytes 208904 | tf_op jit(solution)/shard_map/ppermute | solution.py:524
  105.9 4.4 %collective-permute-start.18 = (f32[136,128]{1,0:T(8,128)S(1)}, f32[136,128]{1,0:T(8,128)S(1)}, u32[]{:S(2)}, u32[]{:S(2)}) collective-permute-start(f32[136,128]{1,0:T(8,128)S(1)} %shard_map.80), channel_id=1, source_target_pairs={{0,4},{2,6},{4,0},{6,2},{8,12},{10,14},{12,8},{14,10},{1,5},{3,7},... | collective-permute-start | bytes 208904 | tf_op jit(solution)/shard_map/ppermute | solution.py:524
  105.9 4.5 %collective-permute-start.17 = (f32[136,128]{1,0:T(8,128)S(1)}, f32[136,128]{1,0:T(8,128)S(1)}, u32[]{:S(2)}, u32[]{:S(2)}) collective-permute-start(f32[136,128]{1,0:T(8,128)S(1)} %shard_map.80), channel_id=1, source_target_pairs={{0,2},{2,0},{4,6},{6,4},{8,10},{10,8},{12,14},{14,12},{1,3},{3,1},... | collective-permute-start | bytes 208904 | tf_op jit(solution)/shard_map/ppermute | solution.py:524
  110.4 6.7 %collective-permute-start.20 = (f32[136,128]{1,0:T(8,128)S(1)}, f32[136,128]{1,0:T(8,128)S(1)}, u32[]{:S(2)}, u32[]{:S(2)}) collective-permute-start(f32[136,128]{1,0:T(8,128)S(1)} %add_add_fusion), channel_id=1, source_target_pairs={{0,8},{2,10},{4,12},{6,14},{8,0},{10,2},{12,4},{14,6},{1,9},{3,11}... | collective-permute-start | bytes 208904 | tf_op jit(solution)/shard_map/ppermute | solution.py:524
  117.2 1.3 %collective-permute-start.21 = (f32[136,128]{1,0:T(8,128)S(1)}, f32[136,128]{1,0:T(8,128)S(1)}, u32[]{:S(2)}, u32[]{:S(2)}) collective-permute-start(f32[136,128]{1,0:T(8,128)S(1)} %add.37.mine_ref), channel_id=1, source_target_pairs={{0,1},{1,0},{2,3},{3,2},{4,5},{5,4},{6,7},{7,6},{8,9},{9,8},{10,11... | collective-permute-start | bytes 208904 | tf_op jit(solution)/shard_map/ppermute | solution.py:533
  (3 other events, 9.4 us)

commit v7 on v6

--- a/solution.py
+++ b/solution.py
@@ -30,15 +30,16 @@
     ]
 
 
-def gather_faces(named, table_ref, rows_ref, out_refs):
+def gather_faces(order_ref, faces_ref, table_ref, rows_ref, out_refs):
     slots = out_refs[0].shape[0]
     for q in range(4):
-        row_of = named(q)
+        offset = order_ref[q] * slots
 
         def body(step, _):
             base = step * 64
             for u in range(64):
-                rows_ref[pl.ds(base + u, 1), :] = table_ref[pl.ds(row_of(base + u), 1), :]
+                face = faces_ref[offset + base + u]
+                rows_ref[pl.ds(base + u, 1), :] = table_ref[pl.ds(face, 1), :]
             return 0
 
         lax.fori_loop(0, slots // 64, body, 0)
@@ -54,20 +55,16 @@
         rows = pl.ds(c * chunk, chunk)
         copies.append(pltpu.make_async_copy(given_ref.at[rows], vec_ref.at[rows], sems.at[c]))
         copies[-1].start()
-    table_ref[0:8, :] = jnp.zeros((8, LANES), f32)
+    table_ref[nodes : nodes + 8, :] = jnp.zeros((8, LANES), f32)
     for c, copy in enumerate(copies):
+        rows = pl.ds(c * chunk, chunk)
         copy.wait()
-        table_ref[pl.ds(8 + c * chunk, chunk), :] = vec_ref[pl.ds(c * chunk, chunk), :].astype(f32)
-
-    def named(q):
-        face = order_ref[q]
-        return lambda slot: faces_ref[face, slot] + 8
-
-    gather_faces(named, table_ref, rows_ref, (o0, o1, o2, o3))
-
-
-def send_faces(side, face_nodes, vectors):
-    nodes, slots = vectors.shape[0], face_nodes.shape[1]
+        table_ref[rows, :] = vec_ref[rows, :].astype(f32)
+    gather_faces(order_ref, faces_ref, table_ref, rows_ref, (o0, o1, o2, o3))
+
+
+def send_faces(side, faces, vectors):
+    nodes, slots = vectors.shape[0], faces.shape[0] // 4
     *blocks, vectors = pl.pallas_call(
         face_kernel,
         out_shape=[jax.ShapeDtypeStruct((slots, LANES), bf16)] * 4
@@ -80,7 +77,7 @@
             pltpu.SemaphoreType.DMA((4,)),
         ],
         compiler_params=grant(8),
-    )(side, face_nodes, vectors)
+    )(side, faces, vectors)
     return blocks, vectors
 
 
@@ -262,11 +259,7 @@
     filtered(interval_ref, own_ref, pot_ref, vec_ref, acc, write)
     table_ref[nodes : nodes + 8, :] = jnp.zeros((8, LANES), f32)
 
-    def named(q):
-        offset = order_ref[q] * rows_ref.shape[0]
-        return lambda slot: faces_ref[offset + slot]
-
-    gather_faces(named, table_ref, rows_ref, (o0, o1, o2, o3))
+    gather_faces(order_ref, faces_ref, table_ref, rows_ref, (o0, o1, o2, o3))
 
 
 def second_kernel(
@@ -558,7 +551,7 @@
         ]
 
     cells = functools.partial(apply_cells, side, cell_nodes.reshape(-1), cell_scale, cell_matrix)
-    blocks, vectors = send_faces(side, face_nodes, held)
+    blocks, vectors = send_faces(side, faces, held)
     own, *sums = cells(vectors, exchanged(blocks))
     degree_one, *blocks = finish_first(
         side, faces, bounds, own, potential, vectors, exchanged(sums)

time: 130 us -> 128 us (0.985)
  Pallas kernels: 66.2 us -> 64.4 us
    pallas_call x1, Pallas kernels: 4.41 us -> 2.76 us  [send_faces(): pl.pallas_call(face_kernel, out_shape=[jax.ShapeDtypeStruct((slots, LANES...]
where the time goes in v7:
time: 128 us; the launch traced here: 127 us
  Pallas kernels  64.4 us (50%)
  starting transfers between devices  41.4 us (32%)
  waiting for transfers between devices  19.4 us (15%)
    pallas_call x2, Pallas kernels, apply_cells(): pl.pallas_call(cells_kernel, out_shape=[jax.ShapeDtypeStruct((nodes, LANE...  36.9 us
    ppermute x16, starting transfers between devices, exchanged(): lax.ppermute(block, ('dom', 'band'), [(2 * i + b, 2 * j + b) for b in ran...  32.7 us
    pallas_call x1, Pallas kernels, rotate(): pl.pallas_call(rotate_kernel, out_shape=jax.ShapeDtypeStruct(own.shape, f...  10.9 us
    ppermute x4, starting transfers between devices, summed_over(): lax.ppermute(value, axis, [(i, i ^ k * stride) for i in range(size)])  8.63 us
    ppermute x4, waiting for transfers between devices, summed_over(): lax.ppermute(value, axis, [(i, i ^ k * stride) for i in range(size)])  7.8 us
    ppermute x16, waiting for transfers between devices, exchanged(): lax.ppermute(block, ('dom', 'band'), [(2 * i + b, 2 * j + b) for b in ran...  7.71 us
    pallas_call x2, Pallas kernels, add_early(): pl.pallas_call(early_kernel, out_shape=jax.ShapeDtypeStruct((nodes, LANES...  5.3 us
    pallas_call x1, Pallas kernels, finish_first(): pl.pallas_call(first_kernel, out_shape=[jax.ShapeDtypeStruct((nodes, LANE...  4.17 us
  transfers between devices with their start and end apart: 22, of which 10 were waited for; matrix products, arithmetic and copies ran while one was open for 1% of the time, Pallas kernels for 4%

profile of v7, /device:TPU:0, one launch (start us, length us, event | category | flops | bytes accessed | tf_op | source)
XLA Modules:
  0.0 127.2 jit_solution(9039325102390779043)
XLA Ops:
  0.7 2.8 %shard_map.73 = (bf16[256,128]{1,0:T(8,128)(2,1)S(1)}, bf16[256,128]{1,0:T(8,128)(2,1)S(1)}, bf16[256,128]{1,0:T(8,128)(2,1)S(1)}, bf16[256,128]{1,0:T(8,128)(2,1)S(1)}, bf16[4096,128]{1,0:T(8,128)(2,1)S(1)}) custom-call(s32[4]{0:T(128)S(1)} %fusion.2.order_ref, s32[1024]{0:T(1024)S(1)} %bitcast.9, bf16[4096,128]{1,0:T(8,128)(2,1)} %old_ref.1), custom_call_target="tpu_custom_call" | custom-call | tf_op jit(solution)/shard_map/pallas_call | solution.py:68
  3.5 3.0 %collective-permute-start = (bf16[256,128]{1,0:T(8,128)(2,1)S(1)}, bf16[256,128]{1,0:T(8,128)(2,1)S(1)}, u32[]{:S(2)}, u32[]{:S(2)}) collective-permute-start(bf16[256,128]{1,0:T(8,128)(2,1)S(1)} %get-tuple-element.26), channel_id=1, source_target_pairs={{0,2},{2,0},{4,6},{6,4},{8,10},{10,8},{12,14},{14,12},{1,5},{5,1},... | collective-permute-start | bytes 196616 | tf_op jit(solution)/shard_map/ppermute | solution.py:545
  7.1 2.9 %collective-permute-start.2 = (bf16[256,128]{1,0:T(8,128)(2,1)S(1)}, bf16[256,128]{1,0:T(8,128)(2,1)S(1)}, u32[]{:S(2)}, u32[]{:S(2)}) collective-permute-start(bf16[256,128]{1,0:T(8,128)(2,1)S(1)} %get-tuple-element.28), channel_id=1, source_target_pairs={{0,4},{4,0},{2,6},{6,2},{8,12},{12,8},{10,14},{14,10},{1,3},{3,1},... | collective-permute-start | bytes 196616 | tf_op jit(solution)/shard_map/ppermute | solution.py:545
  11.5 1.4 %collective-permute-done.2.h2 = bf16[256,128]{1,0:T(8,128)(2,1)S(1)} collective-permute-done((bf16[256,128]{1,0:T(8,128)(2,1)S(1)}, bf16[256,128]{1,0:T(8,128)(2,1)S(1)}, u32[]{:S(2)}, u32[]{:S(2)}) %collective-permute-start.2) | collective-permute-done | bytes 65568 | tf_op jit(solution)/shard_map/ppermute | solution.py:545
  12.9 18.5 %shard_map.74 = (f32[4096,128]{1,0:T(8,128)S(1)}, f32[256,128]{1,0:T(8,128)S(1)}, f32[256,128]{1,0:T(8,128)S(1)}, f32[256,128]{1,0:T(8,128)S(1)}, f32[256,128]{1,0:T(8,128)S(1)}) custom-call(s32[4]{0:T(128)S(1)} %fusion.2.order_ref, s32[8192]{0:T(1024)S(1)} %bitcast.7, f32[16]{0:T(128)} %scales_ref.3, bf16[512,512]{1,0:T(8,128)(2,1)} %whole_ref.3, ...), custom_call_target="tpu_custom_call" | custom-call | tf_op jit(solution)/shard_map/pallas_call | solution.py:169
  31.4 2.9 %collective-permute-start.4 = (f32[256,128]{1,0:T(8,128)S(1)}, f32[256,128]{1,0:T(8,128)S(1)}, u32[]{:S(2)}, u32[]{:S(2)}) collective-permute-start(f32[256,128]{1,0:T(8,128)S(1)} %get-tuple-element.31), channel_id=1, source_target_pairs={{0,2},{2,0},{4,6},{6,4},{8,10},{10,8},{12,14},{14,12},{1,5},{5,1},... | collective-permute-start | bytes 393224 | tf_op jit(solution)/shard_map/ppermute | solution.py:545
  35.0 5.2 %collective-permute-start.6 = (f32[256,128]{1,0:T(8,128)S(1)}, f32[256,128]{1,0:T(8,128)S(1)}, u32[]{:S(2)}, u32[]{:S(2)}) collective-permute-start(f32[256,128]{1,0:T(8,128)S(1)} %get-tuple-element.33), channel_id=1, source_target_pairs={{0,4},{4,0},{2,6},{6,2},{8,12},{12,8},{10,14},{14,10},{1,3},{3,1},... | collective-permute-start | bytes 393224 | tf_op jit(solution)/shard_map/ppermute | solution.py:545
  40.9 2.6 %shard_map.75.own_ref = f32[4096,128]{1,0:T(8,128)S(1)} custom-call(s32[4]{0:T(128)S(1)} %fusion.2.order_ref, s32[1024]{0:T(1024)S(1)} %bitcast.10, f32[4096,128]{1,0:T(8,128)S(1)} %get-tuple-element.30.own_ref, f32[256,128]{1,0:T(8,128)S(1)} %collective-permute-done.4.r0, f32[256,128]{1,0:T(8,128)S(1)} %collective-permute-done.5.r1), custom_call_target="tpu_custom_call" | custom-call | flops 1000000 | bytes 4000000 | tf_op jit(solution)/shard_map/pallas_call | solution.py:223
  43.5 2.3 %collective-permute-done.6.r2 = f32[256,128]{1,0:T(8,128)S(1)} collective-permute-done((f32[256,128]{1,0:T(8,128)S(1)}, f32[256,128]{1,0:T(8,128)S(1)}, u32[]{:S(2)}, u32[]{:S(2)}) %collective-permute-start.6) | collective-permute-done | bytes 131104 | tf_op jit(solution)/shard_map/ppermute | solution.py:545
  45.9 4.2 %shard_map.76 = (bf16[4096,128]{1,0:T(8,128)(2,1)S(1)}, bf16[256,128]{1,0:T(8,128)(2,1)S(1)}, bf16[256,128]{1,0:T(8,128)(2,1)S(1)}, bf16[256,128]{1,0:T(8,128)(2,1)S(1)}, bf16[256,128]{1,0:T(8,128)(2,1)S(1)}) custom-call(s32[4]{0:T(128)S(1)} %fusion.2.order_ref, s32[1024]{0:T(1024)S(1)} %bitcast.11, f32[2]{0:T(128)S(1)} %copy-done.2, ...), custom_call_target="tpu_custom_call" | custom-call | tf_op jit(solution)/shard_map/pallas_call | solution.py:280
  50.0 2.4 %collective-permute-start.8 = (bf16[256,128]{1,0:T(8,128)(2,1)S(1)}, bf16[256,128]{1,0:T(8,128)(2,1)S(1)}, u32[]{:S(2)}, u32[]{:S(2)}) collective-permute-start(bf16[256,128]{1,0:T(8,128)(2,1)S(1)} %get-tuple-element.36), channel_id=1, source_target_pairs={{0,2},{2,0},{4,6},{6,4},{8,10},{10,8},{12,14},{14,12},{1,5},{5,1},... | collective-permute-start | bytes 196616 | tf_op jit(solution)/shard_map/ppermute | solution.py:545
  53.1 3.5 %collective-permute-start.10 = (bf16[256,128]{1,0:T(8,128)(2,1)S(1)}, bf16[256,128]{1,0:T(8,128)(2,1)S(1)}, u32[]{:S(2)}, u32[]{:S(2)}) collective-permute-start(bf16[256,128]{1,0:T(8,128)(2,1)S(1)} %get-tuple-element.38), channel_id=1, source_target_pairs={{0,4},{4,0},{2,6},{6,2},{8,12},{12,8},{10,14},{14,10},{1,3},{3,1},... | collective-permute-start | bytes 196616 | tf_op jit(solution)/shard_map/ppermute | solution.py:545
  57.3 2.9 %collective-permute-done.10.h2 = bf16[256,128]{1,0:T(8,128)(2,1)S(1)} collective-permute-done((bf16[256,128]{1,0:T(8,128)(2,1)S(1)}, bf16[256,128]{1,0:T(8,128)(2,1)S(1)}, u32[]{:S(2)}, u32[]{:S(2)}) %collective-permute-start.10) | collective-permute-done | bytes 65568 | tf_op jit(solution)/shard_map/ppermute | solution.py:545
  60.2 18.5 %shard_map.77 = (f32[4096,128]{1,0:T(8,128)S(1)}, f32[256,128]{1,0:T(8,128)S(1)}, f32[256,128]{1,0:T(8,128)S(1)}, f32[256,128]{1,0:T(8,128)S(1)}, f32[256,128]{1,0:T(8,128)S(1)}) custom-call(s32[4]{0:T(128)S(1)} %fusion.2.order_ref, s32[8192]{0:T(1024)S(1)} %bitcast.8, f32[16]{0:T(128)} %scales_ref.3, bf16[512,512]{1,0:T(8,128)(2,1)} %whole_ref.3, ...), custom_call_target="tpu_custom_call" | custom-call | tf_op jit(solution)/shard_map/pallas_call | solution.py:169
  78.6 2.2 %collective-permute-start.12 = (f32[256,128]{1,0:T(8,128)S(1)}, f32[256,128]{1,0:T(8,128)S(1)}, u32[]{:S(2)}, u32[]{:S(2)}) collective-permute-start(f32[256,128]{1,0:T(8,128)S(1)} %get-tuple-element.41), channel_id=1, source_target_pairs={{0,2},{2,0},{4,6},{6,4},{8,10},{10,8},{12,14},{14,12},{1,5},{5,1},... | collective-permute-start | bytes 393224 | tf_op jit(solution)/shard_map/ppermute | solution.py:545
  81.5 5.2 %collective-permute-start.14 = (f32[256,128]{1,0:T(8,128)S(1)}, f32[256,128]{1,0:T(8,128)S(1)}, u32[]{:S(2)}, u32[]{:S(2)}) collective-permute-start(f32[256,128]{1,0:T(8,128)S(1)} %get-tuple-element.43), channel_id=1, source_target_pairs={{0,4},{4,0},{2,6},{6,2},{8,12},{12,8},{10,14},{14,10},{1,3},{3,1},... | collective-permute-start | bytes 393224 | tf_op jit(solution)/shard_map/ppermute | solution.py:545
  87.4 2.6 %shard_map.78.own_ref = f32[4096,128]{1,0:T(8,128)S(1)} custom-call(s32[4]{0:T(128)S(1)} %fusion.2.order_ref, s32[1024]{0:T(1024)S(1)} %bitcast.12, f32[4096,128]{1,0:T(8,128)S(1)} %get-tuple-element.40.own_ref, f32[256,128]{1,0:T(8,128)S(1)} %collective-permute-done.12.r0, f32[256,128]{1,0:T(8,128)S(1)} %collective-permute-done.13.r1), custom_call_target="tpu_custom_call" | custom-call | flops 1000000 | bytes 4000000 | tf_op jit(solution)/shard_map/pallas_call | solution.py:223
  91.2 3.5 %shard_map.79.own_ref = bf16[4096,128]{1,0:T(8,128)(2,1)S(1)} custom-call(s32[4]{0:T(128)S(1)} %fusion.2.order_ref, s32[1024]{0:T(1024)S(1)} %bitcast.13, f32[2]{0:T(128)S(1)} %copy-done.2, f32[4096,128]{1,0:T(8,128)S(1)} %shard_map.78.own_ref, f32[32,128]{1,0:T(8,128)S(1)} %bitcast.15, bf16[4096,128]{1,0:T(8,128)(2,1)S(1)} %get-tuple-element.35.vec_ref, ...), custom_call_target="tpu_custom_call" | custom-call | tf_op jit(solution)/shard_map/pallas_call | solution.py:298
  94.8 2.6 %collective-permute-done.16.other_ref = bf16[4096,128]{1,0:T(8,128)(2,1)S(1)} collective-permute-done((bf16[4096,128]{1,0:T(8,128)(2,1)S(1)}, bf16[4096,128]{1,0:T(8,128)(2,1)S(1)}, u32[]{:S(2)}, u32[]{:S(2)}) %collective-permute-start.16) | collective-permute-done | bytes 1048608 | tf_op jit(solution)/shard_map/ppermute | solution.py:526
  98.4 5.2 %collective-permute-start.19 = (f32[136,128]{1,0:T(8,128)S(1)}, f32[136,128]{1,0:T(8,128)S(1)}, u32[]{:S(2)}, u32[]{:S(2)}) collective-permute-start(f32[136,128]{1,0:T(8,128)S(1)} %shard_map.80), channel_id=1, source_target_pairs={{0,6},{2,4},{4,2},{6,0},{8,14},{10,12},{12,10},{14,8},{1,7},{3,5},... | collective-permute-start | bytes 208904 | tf_op jit(solution)/shard_map/ppermute | solution.py:517
  104.2 2.4 %collective-permute-done.19 = f32[136,128]{1,0:T(8,128)S(1)} collective-permute-done((f32[136,128]{1,0:T(8,128)S(1)}, f32[136,128]{1,0:T(8,128)S(1)}, u32[]{:S(2)}, u32[]{:S(2)}) %collective-permute-start.19) | collective-permute-done | bytes 69664 | tf_op jit(solution)/shard_map/ppermute | solution.py:517
  108.1 2.7 %collective-permute-start.20 = (f32[136,128]{1,0:T(8,128)S(1)}, f32[136,128]{1,0:T(8,128)S(1)}, u32[]{:S(2)}, u32[]{:S(2)}) collective-permute-start(f32[136,128]{1,0:T(8,128)S(1)} %add_add_fusion), channel_id=1, source_target_pairs={{0,8},{2,10},{4,12},{6,14},{8,0},{10,2},{12,4},{14,6},{1,9},{3,11}... | collective-permute-start | bytes 208904 | tf_op jit(solution)/shard_map/ppermute | solution.py:517
  110.8 4.0 %collective-permute-done.20 = f32[136,128]{1,0:T(8,128)S(1)} collective-permute-done((f32[136,128]{1,0:T(8,128)S(1)}, f32[136,128]{1,0:T(8,128)S(1)}, u32[]{:S(2)}, u32[]{:S(2)}) %collective-permute-start.20) | collective-permute-done | bytes 69664 | tf_op jit(solution)/shard_map/ppermute | solution.py:517
  116.2 10.9 %shard_map.81 = f32[4096,128]{1,0:T(8,128)} custom-call(s32[1]{0:T(128)} %bitcast.band_ref, f32[1]{0:T(128)} %constant.52.clone.1.count_ref, f32[136,128]{1,0:T(8,128)S(1)} %add.37.mine_ref, f32[136,128]{1,0:T(8,128)S(1)} %collective-permute-done.21.theirs_ref, bf16[4096,128]{1,0:T(8,128)(2,1)S(1)} %shard_map.79.own_ref, ...), custom_call_target="tpu_custom_call" | custom-call | tf_op jit(solution)/shard_map/pallas_call | solution.py:491
  (41 shorter events, 12.3 us)
Async XLA Ops:
  3.5 8.0 %collective-permute-start = (bf16[256,128]{1,0:T(8,128)(2,1)S(1)}, bf16[256,128]{1,0:T(8,128)(2,1)S(1)}, u32[]{:S(2)}, u32[]{:S(2)}) collective-permute-start(bf16[256,128]{1,0:T(8,128)(2,1)S(1)} %get-tuple-element.26), channel_id=1, source_target_pairs={{0,2},{2,0},{4,6},{6,4},{8,10},{10,8},{12,14},{14,12},{1,5},{5,1},... | collective-permute-start | bytes 196616 | tf_op jit(solution)/shard_map/ppermute | solution.py:545
  6.5 5.0 %collective-permute-start.1 = (bf16[256,128]{1,0:T(8,128)(2,1)S(1)}, bf16[256,128]{1,0:T(8,128)(2,1)S(1)}, u32[]{:S(2)}, u32[]{:S(2)}) collective-permute-start(bf16[256,128]{1,0:T(8,128)(2,1)S(1)} %get-tuple-element.27), channel_id=1, source_target_pairs={{2,4},{4,2},{6,8},{8,6},{10,12},{12,10},{5,9},{9,5},{7,11},{11,7},... | collective-permute-start | bytes 196616 | tf_op jit(solution)/shard_map/ppermute | solution.py:545
  7.1 5.8 %collective-permute-start.2 = (bf16[256,128]{1,0:T(8,128)(2,1)S(1)}, bf16[256,128]{1,0:T(8,128)(2,1)S(1)}, u32[]{:S(2)}, u32[]{:S(2)}) collective-permute-start(bf16[256,128]{1,0:T(8,128)(2,1)S(1)} %get-tuple-element.28), channel_id=1, source_target_pairs={{0,4},{4,0},{2,6},{6,2},{8,12},{12,8},{10,14},{14,10},{1,3},{3,1},... | collective-permute-start | bytes 196616 | tf_op jit(solution)/shard_map/ppermute | solution.py:545
  10.0 2.9 %collective-permute-start.3 = (bf16[256,128]{1,0:T(8,128)(2,1)S(1)}, bf16[256,128]{1,0:T(8,128)(2,1)S(1)}, u32[]{:S(2)}, u32[]{:S(2)}) collective-permute-start(bf16[256,128]{1,0:T(8,128)(2,1)S(1)} %get-tuple-element.29), channel_id=1, source_target_pairs={{4,8},{8,4},{6,10},{10,6},{3,5},{5,3},{7,9},{9,7},{11,13},{13,11},... | collective-permute-start | bytes 196616 | tf_op jit(solution)/shard_map/ppermute | solution.py:545
  31.4 9.5 %collective-permute-start.4 = (f32[256,128]{1,0:T(8,128)S(1)}, f32[256,128]{1,0:T(8,128)S(1)}, u32[]{:S(2)}, u32[]{:S(2)}) collective-permute-start(f32[256,128]{1,0:T(8,128)S(1)} %get-tuple-element.31), channel_id=1, source_target_pairs={{0,2},{2,0},{4,6},{6,4},{8,10},{10,8},{12,14},{14,12},{1,5},{5,1},... | collective-permute-start | bytes 393224 | tf_op jit(solution)/shard_map/ppermute | solution.py:545
  34.3 6.6 %collective-permute-start.5 = (f32[256,128]{1,0:T(8,128)S(1)}, f32[256,128]{1,0:T(8,128)S(1)}, u32[]{:S(2)}, u32[]{:S(2)}) collective-permute-start(f32[256,128]{1,0:T(8,128)S(1)} %get-tuple-element.32), channel_id=1, source_target_pairs={{2,4},{4,2},{6,8},{8,6},{10,12},{12,10},{5,9},{9,5},{7,11},{11,7},... | collective-permute-start | bytes 393224 | tf_op jit(solution)/shard_map/ppermute | solution.py:545
  35.0 10.9 %collective-permute-start.6 = (f32[256,128]{1,0:T(8,128)S(1)}, f32[256,128]{1,0:T(8,128)S(1)}, u32[]{:S(2)}, u32[]{:S(2)}) collective-permute-start(f32[256,128]{1,0:T(8,128)S(1)} %get-tuple-element.33), channel_id=1, source_target_pairs={{0,4},{4,0},{2,6},{6,2},{8,12},{12,8},{10,14},{14,10},{1,3},{3,1},... | collective-permute-start | bytes 393224 | tf_op jit(solution)/shard_map/ppermute | solution.py:545
  40.2 5.7 %collective-permute-start.7 = (f32[256,128]{1,0:T(8,128)S(1)}, f32[256,128]{1,0:T(8,128)S(1)}, u32[]{:S(2)}, u32[]{:S(2)}) collective-permute-start(f32[256,128]{1,0:T(8,128)S(1)} %get-tuple-element.34), channel_id=1, source_target_pairs={{4,8},{8,4},{6,10},{10,6},{3,5},{5,3},{7,9},{9,7},{11,13},{13,11},... | collective-permute-start | bytes 393224 | tf_op jit(solution)/shard_map/ppermute | solution.py:545
  40.9 5.0 %copy-start.1 = (f32[4096]{0:T(1024)S(1)}, f32[4096]{0:T(1024)}, u32[]{:S(2)}) copy-start(f32[4096]{0:T(1024)} %param.11) | copy-start | bytes 49156
  40.9 5.0 %copy-start.2 = (f32[2]{0:T(128)S(1)}, f32[2]{0:T(128)}, u32[]{:S(2)}) copy-start(f32[2]{0:T(128)} %interval_ref.3) | copy-start | bytes 28
  50.0 7.2 %collective-permute-start.8 = (bf16[256,128]{1,0:T(8,128)(2,1)S(1)}, bf16[256,128]{1,0:T(8,128)(2,1)S(1)}, u32[]{:S(2)}, u32[]{:S(2)}) collective-permute-start(bf16[256,128]{1,0:T(8,128)(2,1)S(1)} %get-tuple-element.36), channel_id=1, source_target_pairs={{0,2},{2,0},{4,6},{6,4},{8,10},{10,8},{12,14},{14,12},{1,5},{5,1},... | collective-permute-start | bytes 196616 | tf_op jit(solution)/shard_map/ppermute | solution.py:545
  52.5 4.8 %collective-permute-start.9 = (bf16[256,128]{1,0:T(8,128)(2,1)S(1)}, bf16[256,128]{1,0:T(8,128)(2,1)S(1)}, u32[]{:S(2)}, u32[]{:S(2)}) collective-permute-start(bf16[256,128]{1,0:T(8,128)(2,1)S(1)} %get-tuple-element.37), channel_id=1, source_target_pairs={{2,4},{4,2},{6,8},{8,6},{10,12},{12,10},{5,9},{9,5},{7,11},{11,7},... | collective-permute-start | bytes 196616 | tf_op jit(solution)/shard_map/ppermute | solution.py:545
  53.1 7.0 %collective-permute-start.10 = (bf16[256,128]{1,0:T(8,128)(2,1)S(1)}, bf16[256,128]{1,0:T(8,128)(2,1)S(1)}, u32[]{:S(2)}, u32[]{:S(2)}) collective-permute-start(bf16[256,128]{1,0:T(8,128)(2,1)S(1)} %get-tuple-element.38), channel_id=1, source_target_pairs={{0,4},{4,0},{2,6},{6,2},{8,12},{12,8},{10,14},{14,10},{1,3},{3,1},... | collective-permute-start | bytes 196616 | tf_op jit(solution)/shard_map/ppermute | solution.py:545
  56.6 3.6 %collective-permute-start.11 = (bf16[256,128]{1,0:T(8,128)(2,1)S(1)}, bf16[256,128]{1,0:T(8,128)(2,1)S(1)}, u32[]{:S(2)}, u32[]{:S(2)}) collective-permute-start(bf16[256,128]{1,0:T(8,128)(2,1)S(1)} %get-tuple-element.39), channel_id=1, source_target_pairs={{4,8},{8,4},{6,10},{10,6},{3,5},{5,3},{7,9},{9,7},{11,13},{13,11},... | collective-permute-start | bytes 196616 | tf_op jit(solution)/shard_map/ppermute | solution.py:545
  78.6 8.8 %collective-permute-start.12 = (f32[256,128]{1,0:T(8,128)S(1)}, f32[256,128]{1,0:T(8,128)S(1)}, u32[]{:S(2)}, u32[]{:S(2)}) collective-permute-start(f32[256,128]{1,0:T(8,128)S(1)} %get-tuple-element.41), channel_id=1, source_target_pairs={{0,2},{2,0},{4,6},{6,4},{8,10},{10,8},{12,14},{14,12},{1,5},{5,1},... | collective-permute-start | bytes 393224 | tf_op jit(solution)/shard_map/ppermute | solution.py:545
  80.9 6.6 %collective-permute-start.13 = (f32[256,128]{1,0:T(8,128)S(1)}, f32[256,128]{1,0:T(8,128)S(1)}, u32[]{:S(2)}, u32[]{:S(2)}) collective-permute-start(f32[256,128]{1,0:T(8,128)S(1)} %get-tuple-element.42), channel_id=1, source_target_pairs={{2,4},{4,2},{6,8},{8,6},{10,12},{12,10},{5,9},{9,5},{7,11},{11,7},... | collective-permute-start | bytes 393224 | tf_op jit(solution)/shard_map/ppermute | solution.py:545
  81.5 9.7 %collective-permute-start.14 = (f32[256,128]{1,0:T(8,128)S(1)}, f32[256,128]{1,0:T(8,128)S(1)}, u32[]{:S(2)}, u32[]{:S(2)}) collective-permute-start(f32[256,128]{1,0:T(8,128)S(1)} %get-tuple-element.43), channel_id=1, source_target_pairs={{0,4},{4,0},{2,6},{6,2},{8,12},{12,8},{10,14},{14,10},{1,3},{3,1},... | collective-permute-start | bytes 393224 | tf_op jit(solution)/shard_map/ppermute | solution.py:545
  86.7 4.5 %collective-permute-start.15 = (f32[256,128]{1,0:T(8,128)S(1)}, f32[256,128]{1,0:T(8,128)S(1)}, u32[]{:S(2)}, u32[]{:S(2)}) collective-permute-start(f32[256,128]{1,0:T(8,128)S(1)} %get-tuple-element.44), channel_id=1, source_target_pairs={{4,8},{8,4},{6,10},{10,6},{3,5},{5,3},{7,9},{9,7},{11,13},{13,11},... | collective-permute-start | bytes 393224 | tf_op jit(solution)/shard_map/ppermute | solution.py:545
  94.7 2.7 %collective-permute-start.16 = (bf16[4096,128]{1,0:T(8,128)(2,1)S(1)}, bf16[4096,128]{1,0:T(8,128)(2,1)S(1)}, u32[]{:S(2)}, u32[]{:S(2)}) collective-permute-start(bf16[4096,128]{1,0:T(8,128)(2,1)S(1)} %shard_map.79.own_ref), channel_id=1, source_target_pairs={{0,1},{1,0},{2,3},{3,2},{4,5},{5,4},{6,7},{7,6},{8,9},{9,8},{10,11... | collective-permute-start | bytes 3145736 | tf_op jit(solution)/shard_map/ppermute | solution.py:526
  98.4 8.3 %collective-permute-start.19 = (f32[136,128]{1,0:T(8,128)S(1)}, f32[136,128]{1,0:T(8,128)S(1)}, u32[]{:S(2)}, u32[]{:S(2)}) collective-permute-start(f32[136,128]{1,0:T(8,128)S(1)} %shard_map.80), channel_id=1, source_target_pairs={{0,6},{2,4},{4,2},{6,0},{8,14},{10,12},{12,10},{14,8},{1,7},{3,5},... | collective-permute-start | bytes 208904 | tf_op jit(solution)/shard_map/ppermute | solution.py:517
  103.6 4.4 %collective-permute-start.18 = (f32[136,128]{1,0:T(8,128)S(1)}, f32[136,128]{1,0:T(8,128)S(1)}, u32[]{:S(2)}, u32[]{:S(2)}) collective-permute-start(f32[136,128]{1,0:T(8,128)S(1)} %shard_map.80), channel_id=1, source_target_pairs={{0,4},{2,6},{4,0},{6,2},{8,12},{10,14},{12,8},{14,10},{1,5},{3,7},... | collective-permute-start | bytes 208904 | tf_op jit(solution)/shard_map/ppermute | solution.py:517
  103.6 4.5 %collective-permute-start.17 = (f32[136,128]{1,0:T(8,128)S(1)}, f32[136,128]{1,0:T(8,128)S(1)}, u32[]{:S(2)}, u32[]{:S(2)}) collective-permute-start(f32[136,128]{1,0:T(8,128)S(1)} %shard_map.80), channel_id=1, source_target_pairs={{0,2},{2,0},{4,6},{6,4},{8,10},{10,8},{12,14},{14,12},{1,3},{3,1},... | collective-permute-start | bytes 208904 | tf_op jit(solution)/shard_map/ppermute | solution.py:517
  108.1 6.7 %collective-permute-start.20 = (f32[136,128]{1,0:T(8,128)S(1)}, f32[136,128]{1,0:T(8,128)S(1)}, u32[]{:S(2)}, u32[]{:S(2)}) collective-permute-start(f32[136,128]{1,0:T(8,128)S(1)} %add_add_fusion), channel_id=1, source_target_pairs={{0,8},{2,10},{4,12},{6,14},{8,0},{10,2},{12,4},{14,6},{1,9},{3,11}... | collective-permute-start | bytes 208904 | tf_op jit(solution)/shard_map/ppermute | solution.py:517
  114.8 1.3 %collective-permute-start.21 = (f32[136,128]{1,0:T(8,128)S(1)}, f32[136,128]{1,0:T(8,128)S(1)}, u32[]{:S(2)}, u32[]{:S(2)}) collective-permute-start(f32[136,128]{1,0:T(8,128)S(1)} %add.37.mine_ref), channel_id=1, source_target_pairs={{0,1},{1,0},{2,3},{3,2},{4,5},{5,4},{6,7},{7,6},{8,9},{9,8},{10,11... | collective-permute-start | bytes 208904 | tf_op jit(solution)/shard_map/ppermute | solution.py:526
  (1 other events, 3.8 us)

commit v8 on v7

--- a/solution.py
+++ b/solution.py
@@ -186,29 +186,29 @@
     )(side, maps, scale, matrix, vectors, *ghosts)
 
 
-def add_returned(order_ref, faces_ref, at, returned, acc):
-    slots = returned[0].shape[0]
+def add_returned(order_ref, faces_ref, pieces, count, acc):
     for a in acc:
         a[...] = jnp.zeros(a.shape, f32)
-    offsets = [order_ref[at + q] * slots for q in range(2)]
+    lists = [order_ref[q] * block.shape[0] + first for q, first, block in pieces]
 
     def body(step, _):
-        base = step * 32
-        for u in range(32):
-            rows = [faces_ref[offsets[q] + base + u] for q in range(2)]
+        base = step * 16
+        for u in range(16):
+            rows = [faces_ref[start + base + u] for start in lists]
             sums = [
-                acc[q][pl.ds(rows[q], 1), :] + returned[q][pl.ds(base + u, 1), :]
-                for q in range(2)
+                a[pl.ds(row, 1), :] + block[pl.ds(first + base + u, 1), :]
+                for a, row, (_, first, block) in zip(acc, rows, pieces)
             ]
-            for q in range(2):
-                acc[q][pl.ds(rows[q], 1), :] = sums[q]
+            for a, row, value in zip(acc, rows, sums):
+                a[pl.ds(row, 1), :] = value
         return 0
 
-    lax.fori_loop(0, slots // 32, body, 0)
-
-
-def early_kernel(order_ref, faces_ref, own_ref, r0, r1, out_ref, *acc):
-    add_returned(order_ref, faces_ref, 0, (r0, r1), acc)
+    lax.fori_loop(0, count // 16, body, 0)
+
+
+def early_kernel(order_ref, faces_ref, own_ref, r0, out_ref, *acc):
+    half = r0.shape[0] // 2
+    add_returned(order_ref, faces_ref, [(0, 0, r0), (0, half, r0)], half, acc)
 
     def combine(step, _):
         rows = pl.ds(pl.multiple_of(step * 64, 64), 64)
@@ -223,12 +223,12 @@
     return pl.pallas_call(
         early_kernel,
         out_shape=jax.ShapeDtypeStruct((nodes, LANES), f32),
-        in_specs=[smem] * 2 + [vmem] * 3,
+        in_specs=[smem] * 2 + [vmem] * 2,
         out_specs=vmem,
         scratch_shapes=[pltpu.VMEM((nodes + 8, LANES), f32)] * 2,
         compiler_params=grant(12),
         cost_estimate=pl.CostEstimate(flops=10**6, bytes_accessed=4 * 10**6, transcendentals=0),
-    )(side, faces, own, *returned)
+    )(side, faces, own, returned)
 
 
 def filtered(interval_ref, own_ref, pot_ref, vec_ref, acc, write):
@@ -239,17 +239,18 @@
     shifts = ((pot_ref[...] - center) * inverse).T
     for step in range(shifts.shape[1]):
         rows = slice(step * LANES, (step + 1) * LANES)
-        image = own_ref[rows, :] + (acc[0][rows, :] + acc[1][rows, :])
+        image = (own_ref[rows, :] + acc[0][rows, :]) + (acc[1][rows, :] + acc[2][rows, :])
         shift = jnp.broadcast_to(shifts[:, step : step + 1], (LANES, LANES))
         write(rows, image * inverse + shift * vec_ref[rows, :].astype(f32))
 
 
 def first_kernel(
-    order_ref, faces_ref, interval_ref, own_ref, pot_ref, vec_ref, r2, r3,
+    order_ref, faces_ref, interval_ref, own_ref, pot_ref, vec_ref, r1, r2, r3,
     out_ref, o0, o1, o2, o3, table_ref, rows_ref, *acc
 ):
     nodes = vec_ref.shape[0]
-    add_returned(order_ref, faces_ref, 2, (r2, r3), acc)
+    late = [(1, 0, r1), (2, 0, r2), (3, 0, r3)]
+    add_returned(order_ref, faces_ref, late, r1.shape[0], acc)
 
     def write(rows, value):
         value = value.astype(bf16)
@@ -263,10 +264,11 @@
 
 
 def second_kernel(
-    order_ref, faces_ref, interval_ref, own_ref, pot_ref, vec_ref, r2, r3, old_ref,
+    order_ref, faces_ref, interval_ref, own_ref, pot_ref, vec_ref, r1, r2, r3, old_ref,
     out_ref, *acc
 ):
-    add_returned(order_ref, faces_ref, 2, (r2, r3), acc)
+    late = [(1, 0, r1), (2, 0, r2), (3, 0, r3)]
+    add_returned(order_ref, faces_ref, late, r1.shape[0], acc)
 
     def write(rows, value):
         out_ref[rows, :] = (2.0 * value - old_ref[rows, :].astype(f32)).astype(bf16)
@@ -276,33 +278,33 @@
 
 def finish_first(side, faces, interval, own, potential, vectors, returned):
     nodes, slots = vectors.shape[0], returned[0].shape[0]
-    own = add_early(side, faces, own, returned[:2])
+    own = add_early(side, faces, own, returned[0])
     return pl.pallas_call(
         first_kernel,
         out_shape=[jax.ShapeDtypeStruct((nodes, LANES), bf16)]
         + [jax.ShapeDtypeStruct((slots, LANES), bf16)] * 4,
-        in_specs=[smem] * 3 + [vmem] * 5,
+        in_specs=[smem] * 3 + [vmem] * 6,
         out_specs=[vmem] * 5,
         scratch_shapes=[
             pltpu.VMEM((nodes + 8, LANES), f32),
             pltpu.VMEM((slots, LANES), f32),
         ]
-        + [pltpu.VMEM((nodes + 8, LANES), f32)] * 2,
+        + [pltpu.VMEM((nodes + 8, LANES), f32)] * 3,
         compiler_params=grant(20),
-    )(side, faces, interval, own, potential, vectors, *returned[2:])
+    )(side, faces, interval, own, potential, vectors, *returned[1:])
 
 
 def finish_second(side, faces, interval, own, potential, vectors, returned, old):
     nodes = vectors.shape[0]
-    own = add_early(side, faces, own, returned[:2])
+    own = add_early(side, faces, own, returned[0])
     return pl.pallas_call(
         second_kernel,
         out_shape=jax.ShapeDtypeStruct((nodes, LANES), bf16),
-        in_specs=[smem] * 3 + [vmem] * 6,
+        in_specs=[smem] * 3 + [vmem] * 7,
         out_specs=vmem,
-        scratch_shapes=[pltpu.VMEM((nodes + 8, LANES), f32)] * 2,
+        scratch_shapes=[pltpu.VMEM((nodes + 8, LANES), f32)] * 3,
         compiler_params=grant(20),
-    )(side, faces, interval, own, potential, vectors, *returned[2:], old)
+    )(side, faces, interval, own, potential, vectors, *returned[1:], old)
 
 
 def margin_kernel(band_ref, own_ref, other_ref, out_ref):

time: 128 us -> 128 us (level)
  transfers between devices with their start and end apart: 22 -> 22, of which waited for: 10 -> 10; matrix products, arithmetic and copies ran while one was open for 1% -> 1% of each run, Pallas kernels for 4% -> 3%
where the time goes in v8:
time: 128 us
  Pallas kernels  63.8 us (50%)
  starting transfers between devices  41.8 us (33%)
  waiting for transfers between devices  20.4 us (16%)
    pallas_call x2, Pallas kernels, apply_cells(): pl.pallas_call(cells_kernel, out_shape=[jax.ShapeDtypeStruct((nodes, LANE...  36.9 us
    ppermute x16, starting transfers between devices, exchanged(): lax.ppermute(block, ('dom', 'band'), [(2 * i + b, 2 * j + b) for b in ran...  32.7 us
    pallas_call x1, Pallas kernels, rotate(): pl.pallas_call(rotate_kernel, out_shape=jax.ShapeDtypeStruct(own.shape, f...  10.9 us
    ppermute x4, starting transfers between devices, summed_over(): lax.ppermute(value, axis, [(i, i ^ k * stride) for i in range(size)])  8.88 us
    ppermute x16, waiting for transfers between devices, exchanged(): lax.ppermute(block, ('dom', 'band'), [(2 * i + b, 2 * j + b) for b in ran...  8.77 us
    ppermute x4, waiting for transfers between devices, summed_over(): lax.ppermute(value, axis, [(i, i ^ k * stride) for i in range(size)])  7.7 us
    pallas_call x1, Pallas kernels, finish_first(): pl.pallas_call(first_kernel, out_shape=[jax.ShapeDtypeStruct((nodes, LANE...  4.34 us
    pallas_call x2, Pallas kernels, add_early(): pl.pallas_call(early_kernel, out_shape=jax.ShapeDtypeStruct((nodes, LANES...  4.29 us
  transfers between devices with their start and end apart: 22, of which 10 were waited for; matrix products, arithmetic and copies ran while one was open for 1% of the time, Pallas kernels for 3%

profile of v8, /device:TPU:0, one launch (start us, length us, event | category | flops | bytes accessed | tf_op | source)
XLA Modules:
  0.0 127.9 jit_solution(7984010215041674971)
XLA Ops:
  0.7 2.8 %shard_map.73 = (bf16[256,128]{1,0:T(8,128)(2,1)S(1)}, bf16[256,128]{1,0:T(8,128)(2,1)S(1)}, bf16[256,128]{1,0:T(8,128)(2,1)S(1)}, bf16[256,128]{1,0:T(8,128)(2,1)S(1)}, bf16[4096,128]{1,0:T(8,128)(2,1)S(1)}) custom-call(s32[4]{0:T(128)S(1)} %fusion.2.order_ref, s32[1024]{0:T(1024)S(1)} %bitcast.9, bf16[4096,128]{1,0:T(8,128)(2,1)} %old_ref.1), custom_call_target="tpu_custom_call" | custom-call | tf_op jit(solution)/shard_map/pallas_call | solution.py:68
  3.5 3.0 %collective-permute-start = (bf16[256,128]{1,0:T(8,128)(2,1)S(1)}, bf16[256,128]{1,0:T(8,128)(2,1)S(1)}, u32[]{:S(2)}, u32[]{:S(2)}) collective-permute-start(bf16[256,128]{1,0:T(8,128)(2,1)S(1)} %get-tuple-element.26), channel_id=1, source_target_pairs={{0,2},{2,0},{4,6},{6,4},{8,10},{10,8},{12,14},{14,12},{1,5},{5,1},... | collective-permute-start | bytes 196616 | tf_op jit(solution)/shard_map/ppermute | solution.py:547
  7.1 2.9 %collective-permute-start.2 = (bf16[256,128]{1,0:T(8,128)(2,1)S(1)}, bf16[256,128]{1,0:T(8,128)(2,1)S(1)}, u32[]{:S(2)}, u32[]{:S(2)}) collective-permute-start(bf16[256,128]{1,0:T(8,128)(2,1)S(1)} %get-tuple-element.28), channel_id=1, source_target_pairs={{0,4},{4,0},{2,6},{6,2},{8,12},{12,8},{10,14},{14,10},{1,3},{3,1},... | collective-permute-start | bytes 196616 | tf_op jit(solution)/shard_map/ppermute | solution.py:547
  11.5 1.4 %collective-permute-done.2.h2 = bf16[256,128]{1,0:T(8,128)(2,1)S(1)} collective-permute-done((bf16[256,128]{1,0:T(8,128)(2,1)S(1)}, bf16[256,128]{1,0:T(8,128)(2,1)S(1)}, u32[]{:S(2)}, u32[]{:S(2)}) %collective-permute-start.2) | collective-permute-done | bytes 65568 | tf_op jit(solution)/shard_map/ppermute | solution.py:547
  12.9 18.5 %shard_map.74 = (f32[4096,128]{1,0:T(8,128)S(1)}, f32[256,128]{1,0:T(8,128)S(1)}, f32[256,128]{1,0:T(8,128)S(1)}, f32[256,128]{1,0:T(8,128)S(1)}, f32[256,128]{1,0:T(8,128)S(1)}) custom-call(s32[4]{0:T(128)S(1)} %fusion.2.order_ref, s32[8192]{0:T(1024)S(1)} %bitcast.7, f32[16]{0:T(128)} %scales_ref.3, bf16[512,512]{1,0:T(8,128)(2,1)} %whole_ref.3, ...), custom_call_target="tpu_custom_call" | custom-call | tf_op jit(solution)/shard_map/pallas_call | solution.py:169
  31.4 2.9 %collective-permute-start.4 = (f32[256,128]{1,0:T(8,128)S(1)}, f32[256,128]{1,0:T(8,128)S(1)}, u32[]{:S(2)}, u32[]{:S(2)}) collective-permute-start(f32[256,128]{1,0:T(8,128)S(1)} %get-tuple-element.31), channel_id=1, source_target_pairs={{0,2},{2,0},{4,6},{6,4},{8,10},{10,8},{12,14},{14,12},{1,5},{5,1},... | collective-permute-start | bytes 393224 | tf_op jit(solution)/shard_map/ppermute | solution.py:547
  35.0 5.2 %collective-permute-start.6 = (f32[256,128]{1,0:T(8,128)S(1)}, f32[256,128]{1,0:T(8,128)S(1)}, u32[]{:S(2)}, u32[]{:S(2)}) collective-permute-start(f32[256,128]{1,0:T(8,128)S(1)} %get-tuple-element.33), channel_id=1, source_target_pairs={{0,4},{4,0},{2,6},{6,2},{8,12},{12,8},{10,14},{14,10},{1,3},{3,1},... | collective-permute-start | bytes 393224 | tf_op jit(solution)/shard_map/ppermute | solution.py:547
  40.9 2.1 %shard_map.75.own_ref = f32[4096,128]{1,0:T(8,128)S(1)} custom-call(s32[4]{0:T(128)S(1)} %fusion.2.order_ref, s32[1024]{0:T(1024)S(1)} %bitcast.10, f32[4096,128]{1,0:T(8,128)S(1)} %get-tuple-element.30.own_ref, f32[256,128]{1,0:T(8,128)S(1)} %collective-permute-done.4.r0), custom_call_target="tpu_custom_call" | custom-call | flops 1000000 | bytes 4000000 | tf_op jit(solution)/shard_map/pallas_call | solution.py:223
  43.0 2.8 %collective-permute-done.6.r2 = f32[256,128]{1,0:T(8,128)S(1)} collective-permute-done((f32[256,128]{1,0:T(8,128)S(1)}, f32[256,128]{1,0:T(8,128)S(1)}, u32[]{:S(2)}, u32[]{:S(2)}) %collective-permute-start.6) | collective-permute-done | bytes 131104 | tf_op jit(solution)/shard_map/ppermute | solution.py:547
  45.9 4.3 %shard_map.76 = (bf16[4096,128]{1,0:T(8,128)(2,1)S(1)}, bf16[256,128]{1,0:T(8,128)(2,1)S(1)}, bf16[256,128]{1,0:T(8,128)(2,1)S(1)}, bf16[256,128]{1,0:T(8,128)(2,1)S(1)}, bf16[256,128]{1,0:T(8,128)(2,1)S(1)}) custom-call(s32[4]{0:T(128)S(1)} %fusion.2.order_ref, s32[1024]{0:T(1024)S(1)} %bitcast.11, f32[2]{0:T(128)S(1)} %copy-done.2, ...), custom_call_target="tpu_custom_call" | custom-call | tf_op jit(solution)/shard_map/pallas_call | solution.py:282
  51.9 5.0 %collective-permute-start.10 = (bf16[256,128]{1,0:T(8,128)(2,1)S(1)}, bf16[256,128]{1,0:T(8,128)(2,1)S(1)}, u32[]{:S(2)}, u32[]{:S(2)}) collective-permute-start(bf16[256,128]{1,0:T(8,128)(2,1)S(1)} %get-tuple-element.38), channel_id=1, source_target_pairs={{0,4},{4,0},{2,6},{6,2},{8,12},{12,8},{10,14},{14,10},{1,3},{3,1},... | collective-permute-start | bytes 196616 | tf_op jit(solution)/shard_map/ppermute | solution.py:547
  57.6 2.9 %collective-permute-done.10.h2 = bf16[256,128]{1,0:T(8,128)(2,1)S(1)} collective-permute-done((bf16[256,128]{1,0:T(8,128)(2,1)S(1)}, bf16[256,128]{1,0:T(8,128)(2,1)S(1)}, u32[]{:S(2)}, u32[]{:S(2)}) %collective-permute-start.10) | collective-permute-done | bytes 65568 | tf_op jit(solution)/shard_map/ppermute | solution.py:547
  60.4 18.5 %shard_map.77 = (f32[4096,128]{1,0:T(8,128)S(1)}, f32[256,128]{1,0:T(8,128)S(1)}, f32[256,128]{1,0:T(8,128)S(1)}, f32[256,128]{1,0:T(8,128)S(1)}, f32[256,128]{1,0:T(8,128)S(1)}) custom-call(s32[4]{0:T(128)S(1)} %fusion.2.order_ref, s32[8192]{0:T(1024)S(1)} %bitcast.8, f32[16]{0:T(128)} %scales_ref.3, bf16[512,512]{1,0:T(8,128)(2,1)} %whole_ref.3, ...), custom_call_target="tpu_custom_call" | custom-call | tf_op jit(solution)/shard_map/pallas_call | solution.py:169
  78.9 2.2 %collective-permute-start.12 = (f32[256,128]{1,0:T(8,128)S(1)}, f32[256,128]{1,0:T(8,128)S(1)}, u32[]{:S(2)}, u32[]{:S(2)}) collective-permute-start(f32[256,128]{1,0:T(8,128)S(1)} %get-tuple-element.41), channel_id=1, source_target_pairs={{0,2},{2,0},{4,6},{6,4},{8,10},{10,8},{12,14},{14,12},{1,5},{5,1},... | collective-permute-start | bytes 393224 | tf_op jit(solution)/shard_map/ppermute | solution.py:547
  81.8 5.2 %collective-permute-start.14 = (f32[256,128]{1,0:T(8,128)S(1)}, f32[256,128]{1,0:T(8,128)S(1)}, u32[]{:S(2)}, u32[]{:S(2)}) collective-permute-start(f32[256,128]{1,0:T(8,128)S(1)} %get-tuple-element.43), channel_id=1, source_target_pairs={{0,4},{4,0},{2,6},{6,2},{8,12},{12,8},{10,14},{14,10},{1,3},{3,1},... | collective-permute-start | bytes 393224 | tf_op jit(solution)/shard_map/ppermute | solution.py:547
  87.7 2.1 %shard_map.78.own_ref = f32[4096,128]{1,0:T(8,128)S(1)} custom-call(s32[4]{0:T(128)S(1)} %fusion.2.order_ref, s32[1024]{0:T(1024)S(1)} %bitcast.12, f32[4096,128]{1,0:T(8,128)S(1)} %get-tuple-element.40.own_ref, f32[256,128]{1,0:T(8,128)S(1)} %collective-permute-done.12.r0), custom_call_target="tpu_custom_call" | custom-call | flops 1000000 | bytes 4000000 | tf_op jit(solution)/shard_map/pallas_call | solution.py:223
  89.9 1.7 %collective-permute-done.14.r2 = f32[256,128]{1,0:T(8,128)S(1)} collective-permute-done((f32[256,128]{1,0:T(8,128)S(1)}, f32[256,128]{1,0:T(8,128)S(1)}, u32[]{:S(2)}, u32[]{:S(2)}) %collective-permute-start.14) | collective-permute-done | bytes 131104 | tf_op jit(solution)/shard_map/ppermute | solution.py:547
  91.5 3.7 %shard_map.79.own_ref = bf16[4096,128]{1,0:T(8,128)(2,1)S(1)} custom-call(s32[4]{0:T(128)S(1)} %fusion.2.order_ref, s32[1024]{0:T(1024)S(1)} %bitcast.13, f32[2]{0:T(128)S(1)} %copy-done.2, f32[4096,128]{1,0:T(8,128)S(1)} %shard_map.78.own_ref, f32[32,128]{1,0:T(8,128)S(1)} %bitcast.15, bf16[4096,128]{1,0:T(8,128)(2,1)S(1)} %get-tuple-element.35.vec_ref, ...), custom_call_target="tpu_custom_call" | custom-call | tf_op jit(solution)/shard_map/pallas_call | solution.py:300
  95.3 2.6 %collective-permute-done.16.other_ref = bf16[4096,128]{1,0:T(8,128)(2,1)S(1)} collective-permute-done((bf16[4096,128]{1,0:T(8,128)(2,1)S(1)}, bf16[4096,128]{1,0:T(8,128)(2,1)S(1)}, u32[]{:S(2)}, u32[]{:S(2)}) %collective-permute-start.16) | collective-permute-done | bytes 1048608 | tf_op jit(solution)/shard_map/ppermute | solution.py:528
  98.9 5.3 %collective-permute-start.19 = (f32[136,128]{1,0:T(8,128)S(1)}, f32[136,128]{1,0:T(8,128)S(1)}, u32[]{:S(2)}, u32[]{:S(2)}) collective-permute-start(f32[136,128]{1,0:T(8,128)S(1)} %shard_map.80), channel_id=1, source_target_pairs={{0,6},{2,4},{4,2},{6,0},{8,14},{10,12},{12,10},{14,8},{1,7},{3,5},... | collective-permute-start | bytes 208904 | tf_op jit(solution)/shard_map/ppermute | solution.py:519
  104.8 2.4 %collective-permute-done.19 = f32[136,128]{1,0:T(8,128)S(1)} collective-permute-done((f32[136,128]{1,0:T(8,128)S(1)}, f32[136,128]{1,0:T(8,128)S(1)}, u32[]{:S(2)}, u32[]{:S(2)}) %collective-permute-start.19) | collective-permute-done | bytes 69664 | tf_op jit(solution)/shard_map/ppermute | solution.py:519
  108.7 3.0 %collective-permute-start.20 = (f32[136,128]{1,0:T(8,128)S(1)}, f32[136,128]{1,0:T(8,128)S(1)}, u32[]{:S(2)}, u32[]{:S(2)}) collective-permute-start(f32[136,128]{1,0:T(8,128)S(1)} %add_add_fusion), channel_id=1, source_target_pairs={{0,8},{2,10},{4,12},{6,14},{8,0},{10,2},{12,4},{14,6},{1,9},{3,11}... | collective-permute-start | bytes 208904 | tf_op jit(solution)/shard_map/ppermute | solution.py:519
  111.6 3.9 %collective-permute-done.20 = f32[136,128]{1,0:T(8,128)S(1)} collective-permute-done((f32[136,128]{1,0:T(8,128)S(1)}, f32[136,128]{1,0:T(8,128)S(1)}, u32[]{:S(2)}, u32[]{:S(2)}) %collective-permute-start.20) | collective-permute-done | bytes 69664 | tf_op jit(solution)/shard_map/ppermute | solution.py:519
  116.8 10.9 %shard_map.81 = f32[4096,128]{1,0:T(8,128)} custom-call(s32[1]{0:T(128)} %bitcast.band_ref, f32[1]{0:T(128)} %constant.52.clone.1.count_ref, f32[136,128]{1,0:T(8,128)S(1)} %add.37.mine_ref, f32[136,128]{1,0:T(8,128)S(1)} %collective-permute-done.21.theirs_ref, bf16[4096,128]{1,0:T(8,128)(2,1)S(1)} %shard_map.79.own_ref, ...), custom_call_target="tpu_custom_call" | custom-call | tf_op jit(solution)/shard_map/pallas_call | solution.py:493
  (41 shorter events, 12.2 us)
Async XLA Ops:
  3.5 8.0 %collective-permute-start = (bf16[256,128]{1,0:T(8,128)(2,1)S(1)}, bf16[256,128]{1,0:T(8,128)(2,1)S(1)}, u32[]{:S(2)}, u32[]{:S(2)}) collective-permute-start(bf16[256,128]{1,0:T(8,128)(2,1)S(1)} %get-tuple-element.26), channel_id=1, source_target_pairs={{0,2},{2,0},{4,6},{6,4},{8,10},{10,8},{12,14},{14,12},{1,5},{5,1},... | collective-permute-start | bytes 196616 | tf_op jit(solution)/shard_map/ppermute | solution.py:547
  6.5 5.0 %collective-permute-start.1 = (bf16[256,128]{1,0:T(8,128)(2,1)S(1)}, bf16[256,128]{1,0:T(8,128)(2,1)S(1)}, u32[]{:S(2)}, u32[]{:S(2)}) collective-permute-start(bf16[256,128]{1,0:T(8,128)(2,1)S(1)} %get-tuple-element.27), channel_id=1, source_target_pairs={{2,4},{4,2},{6,8},{8,6},{10,12},{12,10},{5,9},{9,5},{7,11},{11,7},... | collective-permute-start | bytes 196616 | tf_op jit(solution)/shard_map/ppermute | solution.py:547
  7.1 5.8 %collective-permute-start.2 = (bf16[256,128]{1,0:T(8,128)(2,1)S(1)}, bf16[256,128]{1,0:T(8,128)(2,1)S(1)}, u32[]{:S(2)}, u32[]{:S(2)}) collective-permute-start(bf16[256,128]{1,0:T(8,128)(2,1)S(1)} %get-tuple-element.28), channel_id=1, source_target_pairs={{0,4},{4,0},{2,6},{6,2},{8,12},{12,8},{10,14},{14,10},{1,3},{3,1},... | collective-permute-start | bytes 196616 | tf_op jit(solution)/shard_map/ppermute | solution.py:547
  10.0 2.9 %collective-permute-start.3 = (bf16[256,128]{1,0:T(8,128)(2,1)S(1)}, bf16[256,128]{1,0:T(8,128)(2,1)S(1)}, u32[]{:S(2)}, u32[]{:S(2)}) collective-permute-start(bf16[256,128]{1,0:T(8,128)(2,1)S(1)} %get-tuple-element.29), channel_id=1, source_target_pairs={{4,8},{8,4},{6,10},{10,6},{3,5},{5,3},{7,9},{9,7},{11,13},{13,11},... | collective-permute-start | bytes 196616 | tf_op jit(solution)/shard_map/ppermute | solution.py:547
  31.4 9.5 %collective-permute-start.4 = (f32[256,128]{1,0:T(8,128)S(1)}, f32[256,128]{1,0:T(8,128)S(1)}, u32[]{:S(2)}, u32[]{:S(2)}) collective-permute-start(f32[256,128]{1,0:T(8,128)S(1)} %get-tuple-element.31), channel_id=1, source_target_pairs={{0,2},{2,0},{4,6},{6,4},{8,10},{10,8},{12,14},{14,12},{1,5},{5,1},... | collective-permute-start | bytes 393224 | tf_op jit(solution)/shard_map/ppermute | solution.py:547
  34.3 8.7 %collective-permute-start.5 = (f32[256,128]{1,0:T(8,128)S(1)}, f32[256,128]{1,0:T(8,128)S(1)}, u32[]{:S(2)}, u32[]{:S(2)}) collective-permute-start(f32[256,128]{1,0:T(8,128)S(1)} %get-tuple-element.32), channel_id=1, source_target_pairs={{2,4},{4,2},{6,8},{8,6},{10,12},{12,10},{5,9},{9,5},{7,11},{11,7},... | collective-permute-start | bytes 393224 | tf_op jit(solution)/shard_map/ppermute | solution.py:547
  35.0 10.9 %collective-permute-start.6 = (f32[256,128]{1,0:T(8,128)S(1)}, f32[256,128]{1,0:T(8,128)S(1)}, u32[]{:S(2)}, u32[]{:S(2)}) collective-permute-start(f32[256,128]{1,0:T(8,128)S(1)} %get-tuple-element.33), channel_id=1, source_target_pairs={{0,4},{4,0},{2,6},{6,2},{8,12},{12,8},{10,14},{14,10},{1,3},{3,1},... | collective-permute-start | bytes 393224 | tf_op jit(solution)/shard_map/ppermute | solution.py:547
  40.2 5.7 %collective-permute-start.7 = (f32[256,128]{1,0:T(8,128)S(1)}, f32[256,128]{1,0:T(8,128)S(1)}, u32[]{:S(2)}, u32[]{:S(2)}) collective-permute-start(f32[256,128]{1,0:T(8,128)S(1)} %get-tuple-element.34), channel_id=1, source_target_pairs={{4,8},{8,4},{6,10},{10,6},{3,5},{5,3},{7,9},{9,7},{11,13},{13,11},... | collective-permute-start | bytes 393224 | tf_op jit(solution)/shard_map/ppermute | solution.py:547
  40.9 5.0 %copy-start.1 = (f32[4096]{0:T(1024)S(1)}, f32[4096]{0:T(1024)}, u32[]{:S(2)}) copy-start(f32[4096]{0:T(1024)} %param.11) | copy-start | bytes 49156
  40.9 5.0 %copy-start.2 = (f32[2]{0:T(128)S(1)}, f32[2]{0:T(128)}, u32[]{:S(2)}) copy-start(f32[2]{0:T(128)} %interval_ref.3) | copy-start | bytes 28
  50.2 7.3 %collective-permute-start.8 = (bf16[256,128]{1,0:T(8,128)(2,1)S(1)}, bf16[256,128]{1,0:T(8,128)(2,1)S(1)}, u32[]{:S(2)}, u32[]{:S(2)}) collective-permute-start(bf16[256,128]{1,0:T(8,128)(2,1)S(1)} %get-tuple-element.36), channel_id=1, source_target_pairs={{0,2},{2,0},{4,6},{6,4},{8,10},{10,8},{12,14},{14,12},{1,5},{5,1},... | collective-permute-start | bytes 196616 | tf_op jit(solution)/shard_map/ppermute | solution.py:547
  51.3 6.3 %collective-permute-start.9 = (bf16[256,128]{1,0:T(8,128)(2,1)S(1)}, bf16[256,128]{1,0:T(8,128)(2,1)S(1)}, u32[]{:S(2)}, u32[]{:S(2)}) collective-permute-start(bf16[256,128]{1,0:T(8,128)(2,1)S(1)} %get-tuple-element.37), channel_id=1, source_target_pairs={{2,4},{4,2},{6,8},{8,6},{10,12},{12,10},{5,9},{9,5},{7,11},{11,7},... | collective-permute-start | bytes 196616 | tf_op jit(solution)/shard_map/ppermute | solution.py:547
  51.9 8.5 %collective-permute-start.10 = (bf16[256,128]{1,0:T(8,128)(2,1)S(1)}, bf16[256,128]{1,0:T(8,128)(2,1)S(1)}, u32[]{:S(2)}, u32[]{:S(2)}) collective-permute-start(bf16[256,128]{1,0:T(8,128)(2,1)S(1)} %get-tuple-element.38), channel_id=1, source_target_pairs={{0,4},{4,0},{2,6},{6,2},{8,12},{12,8},{10,14},{14,10},{1,3},{3,1},... | collective-permute-start | bytes 196616 | tf_op jit(solution)/shard_map/ppermute | solution.py:547
  56.9 3.6 %collective-permute-start.11 = (bf16[256,128]{1,0:T(8,128)(2,1)S(1)}, bf16[256,128]{1,0:T(8,128)(2,1)S(1)}, u32[]{:S(2)}, u32[]{:S(2)}) collective-permute-start(bf16[256,128]{1,0:T(8,128)(2,1)S(1)} %get-tuple-element.39), channel_id=1, source_target_pairs={{4,8},{8,4},{6,10},{10,6},{3,5},{5,3},{7,9},{9,7},{11,13},{13,11},... | collective-permute-start | bytes 196616 | tf_op jit(solution)/shard_map/ppermute | solution.py:547
  78.9 8.8 %collective-permute-start.12 = (f32[256,128]{1,0:T(8,128)S(1)}, f32[256,128]{1,0:T(8,128)S(1)}, u32[]{:S(2)}, u32[]{:S(2)}) collective-permute-start(f32[256,128]{1,0:T(8,128)S(1)} %get-tuple-element.41), channel_id=1, source_target_pairs={{0,2},{2,0},{4,6},{6,4},{8,10},{10,8},{12,14},{14,12},{1,5},{5,1},... | collective-permute-start | bytes 393224 | tf_op jit(solution)/shard_map/ppermute | solution.py:547
  81.1 8.7 %collective-permute-start.13 = (f32[256,128]{1,0:T(8,128)S(1)}, f32[256,128]{1,0:T(8,128)S(1)}, u32[]{:S(2)}, u32[]{:S(2)}) collective-permute-start(f32[256,128]{1,0:T(8,128)S(1)} %get-tuple-element.42), channel_id=1, source_target_pairs={{2,4},{4,2},{6,8},{8,6},{10,12},{12,10},{5,9},{9,5},{7,11},{11,7},... | collective-permute-start | bytes 393224 | tf_op jit(solution)/shard_map/ppermute | solution.py:547
  81.8 9.7 %collective-permute-start.14 = (f32[256,128]{1,0:T(8,128)S(1)}, f32[256,128]{1,0:T(8,128)S(1)}, u32[]{:S(2)}, u32[]{:S(2)}) collective-permute-start(f32[256,128]{1,0:T(8,128)S(1)} %get-tuple-element.43), channel_id=1, source_target_pairs={{0,4},{4,0},{2,6},{6,2},{8,12},{12,8},{10,14},{14,10},{1,3},{3,1},... | collective-permute-start | bytes 393224 | tf_op jit(solution)/shard_map/ppermute | solution.py:547
  87.0 4.5 %collective-permute-start.15 = (f32[256,128]{1,0:T(8,128)S(1)}, f32[256,128]{1,0:T(8,128)S(1)}, u32[]{:S(2)}, u32[]{:S(2)}) collective-permute-start(f32[256,128]{1,0:T(8,128)S(1)} %get-tuple-element.44), channel_id=1, source_target_pairs={{4,8},{8,4},{6,10},{10,6},{3,5},{5,3},{7,9},{9,7},{11,13},{13,11},... | collective-permute-start | bytes 393224 | tf_op jit(solution)/shard_map/ppermute | solution.py:547
  95.2 2.7 %collective-permute-start.16 = (bf16[4096,128]{1,0:T(8,128)(2,1)S(1)}, bf16[4096,128]{1,0:T(8,128)(2,1)S(1)}, u32[]{:S(2)}, u32[]{:S(2)}) collective-permute-start(bf16[4096,128]{1,0:T(8,128)(2,1)S(1)} %shard_map.79.own_ref), channel_id=1, source_target_pairs={{0,1},{1,0},{2,3},{3,2},{4,5},{5,4},{6,7},{7,6},{8,9},{9,8},{10,11... | collective-permute-start | bytes 3145736 | tf_op jit(solution)/shard_map/ppermute | solution.py:528
  98.9 8.3 %collective-permute-start.19 = (f32[136,128]{1,0:T(8,128)S(1)}, f32[136,128]{1,0:T(8,128)S(1)}, u32[]{:S(2)}, u32[]{:S(2)}) collective-permute-start(f32[136,128]{1,0:T(8,128)S(1)} %shard_map.80), channel_id=1, source_target_pairs={{0,6},{2,4},{4,2},{6,0},{8,14},{10,12},{12,10},{14,8},{1,7},{3,5},... | collective-permute-start | bytes 208904 | tf_op jit(solution)/shard_map/ppermute | solution.py:519
  104.2 4.4 %collective-permute-start.18 = (f32[136,128]{1,0:T(8,128)S(1)}, f32[136,128]{1,0:T(8,128)S(1)}, u32[]{:S(2)}, u32[]{:S(2)}) collective-permute-start(f32[136,128]{1,0:T(8,128)S(1)} %shard_map.80), channel_id=1, source_target_pairs={{0,4},{2,6},{4,0},{6,2},{8,12},{10,14},{12,8},{14,10},{1,5},{3,7},... | collective-permute-start | bytes 208904 | tf_op jit(solution)/shard_map/ppermute | solution.py:519
  104.2 4.5 %collective-permute-start.17 = (f32[136,128]{1,0:T(8,128)S(1)}, f32[136,128]{1,0:T(8,128)S(1)}, u32[]{:S(2)}, u32[]{:S(2)}) collective-permute-start(f32[136,128]{1,0:T(8,128)S(1)} %shard_map.80), channel_id=1, source_target_pairs={{0,2},{2,0},{4,6},{6,4},{8,10},{10,8},{12,14},{14,12},{1,3},{3,1},... | collective-permute-start | bytes 208904 | tf_op jit(solution)/shard_map/ppermute | solution.py:519
  108.7 6.8 %collective-permute-start.20 = (f32[136,128]{1,0:T(8,128)S(1)}, f32[136,128]{1,0:T(8,128)S(1)}, u32[]{:S(2)}, u32[]{:S(2)}) collective-permute-start(f32[136,128]{1,0:T(8,128)S(1)} %add_add_fusion), channel_id=1, source_target_pairs={{0,8},{2,10},{4,12},{6,14},{8,0},{10,2},{12,4},{14,6},{1,9},{3,11}... | collective-permute-start | bytes 208904 | tf_op jit(solution)/shard_map/ppermute | solution.py:519
  115.5 1.3 %collective-permute-start.21 = (f32[136,128]{1,0:T(8,128)S(1)}, f32[136,128]{1,0:T(8,128)S(1)}, u32[]{:S(2)}, u32[]{:S(2)}) collective-permute-start(f32[136,128]{1,0:T(8,128)S(1)} %add.37.mine_ref), channel_id=1, source_target_pairs={{0,1},{1,0},{2,3},{3,2},{4,5},{5,4},{6,7},{7,6},{8,9},{9,8},{10,11... | collective-permute-start | bytes 208904 | tf_op jit(solution)/shard_map/ppermute | solution.py:528
  (1 other events, 3.8 us)

commit v9 on v8

--- a/solution.py
+++ b/solution.py
@@ -47,37 +47,47 @@
 
 
 def face_kernel(
-    order_ref, faces_ref, given_ref, o0, o1, o2, o3, vec_ref, table_ref, rows_ref, sems
+    order_ref, lists_ref, given_ref, o0, o1, o2, o3, vec_ref, faces_ref, table_ref, rows_ref, sems
 ):
-    nodes, chunk = vec_ref.shape[0], vec_ref.shape[0] // sems.shape[0]
+    nodes, chunks = vec_ref.shape[0], sems.shape[0] - 1
+    chunk = nodes // chunks
+    names = pltpu.make_async_copy(lists_ref, faces_ref, sems.at[chunks])
+    names.start()
     copies = []
-    for c in range(sems.shape[0]):
+    for c in range(chunks):
         rows = pl.ds(c * chunk, chunk)
         copies.append(pltpu.make_async_copy(given_ref.at[rows], vec_ref.at[rows], sems.at[c]))
         copies[-1].start()
-    table_ref[nodes : nodes + 8, :] = jnp.zeros((8, LANES), f32)
+    table_ref[0:8, :] = jnp.zeros((8, LANES), f32)
     for c, copy in enumerate(copies):
+        copy.wait()
         rows = pl.ds(c * chunk, chunk)
-        copy.wait()
-        table_ref[rows, :] = vec_ref[rows, :].astype(f32)
-    gather_faces(order_ref, faces_ref, table_ref, rows_ref, (o0, o1, o2, o3))
-
-
-def send_faces(side, faces, vectors):
-    nodes, slots = vectors.shape[0], faces.shape[0] // 4
+        table_ref[pl.ds(8 + c * chunk, chunk), :] = vec_ref[rows, :].astype(f32)
+    names.wait()
+    for q, out_ref in enumerate((o0, o1, o2, o3)):
+        face = order_ref[q]
+        for slot in range(rows_ref.shape[0]):
+            row = faces_ref[face, slot] + 8
+            rows_ref[slot : slot + 1, :] = table_ref[pl.ds(row, 1), :]
+        out_ref[...] = rows_ref[...].astype(bf16)
+
+
+def send_faces(side, face_nodes, vectors):
+    nodes, slots = vectors.shape[0], face_nodes.shape[1]
     *blocks, vectors = pl.pallas_call(
         face_kernel,
         out_shape=[jax.ShapeDtypeStruct((slots, LANES), bf16)] * 4
         + [jax.ShapeDtypeStruct((nodes, LANES), bf16)],
-        in_specs=[smem, smem, hbm],
+        in_specs=[smem, hbm, hbm],
         out_specs=[vmem] * 5,
         scratch_shapes=[
+            pltpu.SMEM(face_nodes.shape, jnp.int32),
             pltpu.VMEM((nodes + 8, LANES), f32),
             pltpu.VMEM((slots, LANES), f32),
-            pltpu.SemaphoreType.DMA((4,)),
+            pltpu.SemaphoreType.DMA((5,)),
         ],
         compiler_params=grant(8),
-    )(side, faces, vectors)
+    )(side, face_nodes, vectors)
     return blocks, vectors
 
 
@@ -532,6 +542,7 @@
     nodes = wavefunctions.shape[0]
     cell_matrix = pltpu.with_memory_space_constraint(cell_matrix, pltpu.HBM)
     cell_scale = pltpu.with_memory_space_constraint(cell_scale, pltpu.HBM)
+    lists = pltpu.with_memory_space_constraint(face_nodes, pltpu.HBM)
     held = pltpu.with_memory_space_constraint(wavefunctions, pltpu.HBM)
     faces = jnp.where(face_nodes < 0, nodes, face_nodes).reshape(-1)
     potential = potential.reshape(-1, LANES)
@@ -553,7 +564,7 @@
         ]
 
     cells = functools.partial(apply_cells, side, cell_nodes.reshape(-1), cell_scale, cell_matrix)
-    blocks, vectors = send_faces(side, faces, held)
+    blocks, vectors = send_faces(side, lists, held)
     own, *sums = cells(vectors, exchanged(blocks))
     degree_one, *blocks = finish_first(
         side, faces, bounds, own, potential, vectors, exchanged(sums)

time: 128 us -> 128 us (level)
  transfers between devices with their start and end apart: 22 -> 22, of which waited for: 10 -> 9; matrix products, arithmetic and copies ran while one was open for 1% -> 1% of each run, Pallas kernels for 3% -> 4%
where the time goes in v9:
time: 128 us; the launch traced here: 127 us
  Pallas kernels  64 us (50%)
  starting transfers between devices  41.7 us (33%)
  waiting for transfers between devices  20.3 us (16%)
    pallas_call x2, Pallas kernels, apply_cells(): pl.pallas_call(cells_kernel, out_shape=[jax.ShapeDtypeStruct((nodes, LANE...  36.9 us
    ppermute x16, starting transfers between devices, exchanged(): lax.ppermute(block, ('dom', 'band'), [(2 * i + b, 2 * j + b) for b in ran...  32.6 us
    pallas_call x1, Pallas kernels, rotate(): pl.pallas_call(rotate_kernel, out_shape=jax.ShapeDtypeStruct(own.shape, f...  10.9 us
    ppermute x4, starting transfers between devices, summed_over(): lax.ppermute(value, axis, [(i, i ^ k * stride) for i in range(size)])  9.03 us
    ppermute x16, waiting for transfers between devices, exchanged(): lax.ppermute(block, ('dom', 'band'), [(2 * i + b, 2 * j + b) for b in ran...  8.61 us
    ppermute x4, waiting for transfers between devices, summed_over(): lax.ppermute(value, axis, [(i, i ^ k * stride) for i in range(size)])  7.82 us
    pallas_call x2, Pallas kernels, add_early(): pl.pallas_call(early_kernel, out_shape=jax.ShapeDtypeStruct((nodes, LANES...  4.47 us
    pallas_call x1, Pallas kernels, finish_first(): pl.pallas_call(first_kernel, out_shape=[jax.ShapeDtypeStruct((nodes, LANE...  4.38 us
  transfers between devices with their start and end apart: 22, of which 9 were waited for; matrix products, arithmetic and copies ran while one was open for 1% of the time, Pallas kernels for 4%

profile of v9, /device:TPU:0, one launch (start us, length us, event | category | flops | bytes accessed | tf_op | source)
XLA Modules:
  0.0 127.3 jit_solution(13375669419733825436)
XLA Ops:
  0.0 2.9 %shard_map.73 = (bf16[256,128]{1,0:T(8,128)(2,1)S(1)}, bf16[256,128]{1,0:T(8,128)(2,1)S(1)}, bf16[256,128]{1,0:T(8,128)(2,1)S(1)}, bf16[256,128]{1,0:T(8,128)(2,1)S(1)}, bf16[4096,128]{1,0:T(8,128)(2,1)S(1)}) custom-call(s32[4]{0:T(128)S(1)} %fusion.2.order_ref, s32[4,256]{1,0:T(4,128)} %lists_ref.1, bf16[4096,128]{1,0:T(8,128)(2,1)} %old_ref.1), custom_call_target="tpu_custom_call" | custom-call | tf_op jit(solution)/shard_map/pallas_call | solution.py:77
  3.0 3.0 %collective-permute-start = (bf16[256,128]{1,0:T(8,128)(2,1)S(1)}, bf16[256,128]{1,0:T(8,128)(2,1)S(1)}, u32[]{:S(2)}, u32[]{:S(2)}) collective-permute-start(bf16[256,128]{1,0:T(8,128)(2,1)S(1)} %get-tuple-element.26), channel_id=1, source_target_pairs={{0,2},{2,0},{4,6},{6,4},{8,10},{10,8},{12,14},{14,12},{1,5},{5,1},... | collective-permute-start | bytes 196616 | tf_op jit(solution)/shard_map/ppermute | solution.py:558
  6.6 2.9 %collective-permute-start.2 = (bf16[256,128]{1,0:T(8,128)(2,1)S(1)}, bf16[256,128]{1,0:T(8,128)(2,1)S(1)}, u32[]{:S(2)}, u32[]{:S(2)}) collective-permute-start(bf16[256,128]{1,0:T(8,128)(2,1)S(1)} %get-tuple-element.28), channel_id=1, source_target_pairs={{0,4},{4,0},{2,6},{6,2},{8,12},{12,8},{10,14},{14,10},{1,3},{3,1},... | collective-permute-start | bytes 196616 | tf_op jit(solution)/shard_map/ppermute | solution.py:558
  12.4 18.5 %shard_map.74 = (f32[4096,128]{1,0:T(8,128)S(1)}, f32[256,128]{1,0:T(8,128)S(1)}, f32[256,128]{1,0:T(8,128)S(1)}, f32[256,128]{1,0:T(8,128)S(1)}, f32[256,128]{1,0:T(8,128)S(1)}) custom-call(s32[4]{0:T(128)S(1)} %fusion.2.order_ref, s32[8192]{0:T(1024)S(1)} %bitcast.7, f32[16]{0:T(128)} %scales_ref.3, bf16[512,512]{1,0:T(8,128)(2,1)} %whole_ref.3, ...), custom_call_target="tpu_custom_call" | custom-call | tf_op jit(solution)/shard_map/pallas_call | solution.py:179
  30.8 2.9 %collective-permute-start.4 = (f32[256,128]{1,0:T(8,128)S(1)}, f32[256,128]{1,0:T(8,128)S(1)}, u32[]{:S(2)}, u32[]{:S(2)}) collective-permute-start(f32[256,128]{1,0:T(8,128)S(1)} %get-tuple-element.31), channel_id=1, source_target_pairs={{0,2},{2,0},{4,6},{6,4},{8,10},{10,8},{12,14},{14,12},{1,5},{5,1},... | collective-permute-start | bytes 393224 | tf_op jit(solution)/shard_map/ppermute | solution.py:558
  34.4 5.2 %collective-permute-start.6 = (f32[256,128]{1,0:T(8,128)S(1)}, f32[256,128]{1,0:T(8,128)S(1)}, u32[]{:S(2)}, u32[]{:S(2)}) collective-permute-start(f32[256,128]{1,0:T(8,128)S(1)} %get-tuple-element.33), channel_id=1, source_target_pairs={{0,4},{4,0},{2,6},{6,2},{8,12},{12,8},{10,14},{14,10},{1,3},{3,1},... | collective-permute-start | bytes 393224 | tf_op jit(solution)/shard_map/ppermute | solution.py:558
  40.4 2.2 %shard_map.75.own_ref = f32[4096,128]{1,0:T(8,128)S(1)} custom-call(s32[4]{0:T(128)S(1)} %fusion.2.order_ref, s32[1024]{0:T(1024)S(1)} %bitcast.9, f32[4096,128]{1,0:T(8,128)S(1)} %get-tuple-element.30.own_ref, f32[256,128]{1,0:T(8,128)S(1)} %collective-permute-done.4.r0), custom_call_target="tpu_custom_call" | custom-call | flops 1000000 | bytes 4000000 | tf_op jit(solution)/shard_map/pallas_call | solution.py:233
  42.6 2.7 %collective-permute-done.6.r2 = f32[256,128]{1,0:T(8,128)S(1)} collective-permute-done((f32[256,128]{1,0:T(8,128)S(1)}, f32[256,128]{1,0:T(8,128)S(1)}, u32[]{:S(2)}, u32[]{:S(2)}) %collective-permute-start.6) | collective-permute-done | bytes 131104 | tf_op jit(solution)/shard_map/ppermute | solution.py:558
  45.3 4.4 %shard_map.76 = (bf16[4096,128]{1,0:T(8,128)(2,1)S(1)}, bf16[256,128]{1,0:T(8,128)(2,1)S(1)}, bf16[256,128]{1,0:T(8,128)(2,1)S(1)}, bf16[256,128]{1,0:T(8,128)(2,1)S(1)}, bf16[256,128]{1,0:T(8,128)(2,1)S(1)}) custom-call(s32[4]{0:T(128)S(1)} %fusion.2.order_ref, s32[1024]{0:T(1024)S(1)} %bitcast.10, f32[2]{0:T(128)S(1)} %copy-done.2, ...), custom_call_target="tpu_custom_call" | custom-call | tf_op jit(solution)/shard_map/pallas_call | solution.py:292
  51.3 4.9 %collective-permute-start.10 = (bf16[256,128]{1,0:T(8,128)(2,1)S(1)}, bf16[256,128]{1,0:T(8,128)(2,1)S(1)}, u32[]{:S(2)}, u32[]{:S(2)}) collective-permute-start(bf16[256,128]{1,0:T(8,128)(2,1)S(1)} %get-tuple-element.38), channel_id=1, source_target_pairs={{0,4},{4,0},{2,6},{6,2},{8,12},{12,8},{10,14},{14,10},{1,3},{3,1},... | collective-permute-start | bytes 196616 | tf_op jit(solution)/shard_map/ppermute | solution.py:558
  56.9 2.9 %collective-permute-done.10.h2 = bf16[256,128]{1,0:T(8,128)(2,1)S(1)} collective-permute-done((bf16[256,128]{1,0:T(8,128)(2,1)S(1)}, bf16[256,128]{1,0:T(8,128)(2,1)S(1)}, u32[]{:S(2)}, u32[]{:S(2)}) %collective-permute-start.10) | collective-permute-done | bytes 65568 | tf_op jit(solution)/shard_map/ppermute | solution.py:558
  59.8 18.5 %shard_map.77 = (f32[4096,128]{1,0:T(8,128)S(1)}, f32[256,128]{1,0:T(8,128)S(1)}, f32[256,128]{1,0:T(8,128)S(1)}, f32[256,128]{1,0:T(8,128)S(1)}, f32[256,128]{1,0:T(8,128)S(1)}) custom-call(s32[4]{0:T(128)S(1)} %fusion.2.order_ref, s32[8192]{0:T(1024)S(1)} %bitcast.8, f32[16]{0:T(128)} %scales_ref.3, bf16[512,512]{1,0:T(8,128)(2,1)} %whole_ref.3, ...), custom_call_target="tpu_custom_call" | custom-call | tf_op jit(solution)/shard_map/pallas_call | solution.py:179
  78.2 2.2 %collective-permute-start.12 = (f32[256,128]{1,0:T(8,128)S(1)}, f32[256,128]{1,0:T(8,128)S(1)}, u32[]{:S(2)}, u32[]{:S(2)}) collective-permute-start(f32[256,128]{1,0:T(8,128)S(1)} %get-tuple-element.41), channel_id=1, source_target_pairs={{0,2},{2,0},{4,6},{6,4},{8,10},{10,8},{12,14},{14,12},{1,5},{5,1},... | collective-permute-start | bytes 393224 | tf_op jit(solution)/shard_map/ppermute | solution.py:558
  81.1 5.2 %collective-permute-start.14 = (f32[256,128]{1,0:T(8,128)S(1)}, f32[256,128]{1,0:T(8,128)S(1)}, u32[]{:S(2)}, u32[]{:S(2)}) collective-permute-start(f32[256,128]{1,0:T(8,128)S(1)} %get-tuple-element.43), channel_id=1, source_target_pairs={{0,4},{4,0},{2,6},{6,2},{8,12},{12,8},{10,14},{14,10},{1,3},{3,1},... | collective-permute-start | bytes 393224 | tf_op jit(solution)/shard_map/ppermute | solution.py:558
  87.0 2.2 %shard_map.78.own_ref = f32[4096,128]{1,0:T(8,128)S(1)} custom-call(s32[4]{0:T(128)S(1)} %fusion.2.order_ref, s32[1024]{0:T(1024)S(1)} %bitcast.11, f32[4096,128]{1,0:T(8,128)S(1)} %get-tuple-element.40.own_ref, f32[256,128]{1,0:T(8,128)S(1)} %collective-permute-done.12.r0), custom_call_target="tpu_custom_call" | custom-call | flops 1000000 | bytes 4000000 | tf_op jit(solution)/shard_map/pallas_call | solution.py:233
  89.3 1.6 %collective-permute-done.14.r2 = f32[256,128]{1,0:T(8,128)S(1)} collective-permute-done((f32[256,128]{1,0:T(8,128)S(1)}, f32[256,128]{1,0:T(8,128)S(1)}, u32[]{:S(2)}, u32[]{:S(2)}) %collective-permute-start.14) | collective-permute-done | bytes 131104 | tf_op jit(solution)/shard_map/ppermute | solution.py:558
  90.9 3.7 %shard_map.79.own_ref = bf16[4096,128]{1,0:T(8,128)(2,1)S(1)} custom-call(s32[4]{0:T(128)S(1)} %fusion.2.order_ref, s32[1024]{0:T(1024)S(1)} %bitcast.12, f32[2]{0:T(128)S(1)} %copy-done.2, f32[4096,128]{1,0:T(8,128)S(1)} %shard_map.78.own_ref, f32[32,128]{1,0:T(8,128)S(1)} %bitcast.14, bf16[4096,128]{1,0:T(8,128)(2,1)S(1)} %get-tuple-element.35.vec_ref, ...), custom_call_target="tpu_custom_call" | custom-call | tf_op jit(solution)/shard_map/pallas_call | solution.py:310
  94.7 2.6 %collective-permute-done.16.other_ref = bf16[4096,128]{1,0:T(8,128)(2,1)S(1)} collective-permute-done((bf16[4096,128]{1,0:T(8,128)(2,1)S(1)}, bf16[4096,128]{1,0:T(8,128)(2,1)S(1)}, u32[]{:S(2)}, u32[]{:S(2)}) %collective-permute-start.16) | collective-permute-done | bytes 1048608 | tf_op jit(solution)/shard_map/ppermute | solution.py:538
  98.1 5.1 %collective-permute-start.19 = (f32[136,128]{1,0:T(8,128)S(1)}, f32[136,128]{1,0:T(8,128)S(1)}, u32[]{:S(2)}, u32[]{:S(2)}) collective-permute-start(f32[136,128]{1,0:T(8,128)S(1)} %shard_map.80), channel_id=1, source_target_pairs={{0,6},{2,4},{4,2},{6,0},{8,14},{10,12},{12,10},{14,8},{1,7},{3,5},... | collective-permute-start | bytes 208904 | tf_op jit(solution)/shard_map/ppermute | solution.py:529
  103.8 2.3 %collective-permute-done.19 = f32[136,128]{1,0:T(8,128)S(1)} collective-permute-done((f32[136,128]{1,0:T(8,128)S(1)}, f32[136,128]{1,0:T(8,128)S(1)}, u32[]{:S(2)}, u32[]{:S(2)}) %collective-permute-start.19) | collective-permute-done | bytes 69664 | tf_op jit(solution)/shard_map/ppermute | solution.py:529
  106.1 1.6 %collective-permute-done.18 = f32[136,128]{1,0:T(8,128)S(1)} collective-permute-done((f32[136,128]{1,0:T(8,128)S(1)}, f32[136,128]{1,0:T(8,128)S(1)}, u32[]{:S(2)}, u32[]{:S(2)}) %collective-permute-start.18) | collective-permute-done | bytes 69664 | tf_op jit(solution)/shard_map/ppermute | solution.py:529
  107.8 3.3 %collective-permute-start.20 = (f32[136,128]{1,0:T(8,128)S(1)}, f32[136,128]{1,0:T(8,128)S(1)}, u32[]{:S(2)}, u32[]{:S(2)}) collective-permute-start(f32[136,128]{1,0:T(8,128)S(1)} %add_add_fusion), channel_id=1, source_target_pairs={{0,8},{2,10},{4,12},{6,14},{8,0},{10,2},{12,4},{14,6},{1,9},{3,11}... | collective-permute-start | bytes 208904 | tf_op jit(solution)/shard_map/ppermute | solution.py:529
  111.1 3.9 %collective-permute-done.20 = f32[136,128]{1,0:T(8,128)S(1)} collective-permute-done((f32[136,128]{1,0:T(8,128)S(1)}, f32[136,128]{1,0:T(8,128)S(1)}, u32[]{:S(2)}, u32[]{:S(2)}) %collective-permute-start.20) | collective-permute-done | bytes 69664 | tf_op jit(solution)/shard_map/ppermute | solution.py:529
  116.3 10.9 %shard_map.81 = f32[4096,128]{1,0:T(8,128)} custom-call(s32[1]{0:T(128)} %bitcast.band_ref, f32[1]{0:T(128)} %constant.52.clone.1.count_ref, f32[136,128]{1,0:T(8,128)S(1)} %add.37.mine_ref, f32[136,128]{1,0:T(8,128)S(1)} %collective-permute-done.21.theirs_ref, bf16[4096,128]{1,0:T(8,128)(2,1)S(1)} %shard_map.79.own_ref, ...), custom_call_target="tpu_custom_call" | custom-call | tf_op jit(solution)/shard_map/pallas_call | solution.py:503
  (43 shorter events, 11.2 us)
Async XLA Ops:
  0.0 40.3 %copy-start.3 = (s32[4,256]{1,0:T(4,128)S(1)}, s32[4,256]{1,0:T(4,128)}, u32[]{:S(2)}) copy-start(s32[4,256]{1,0:T(4,128)} %lists_ref.1) | copy-start | bytes 12292
  3.0 8.0 %collective-permute-start = (bf16[256,128]{1,0:T(8,128)(2,1)S(1)}, bf16[256,128]{1,0:T(8,128)(2,1)S(1)}, u32[]{:S(2)}, u32[]{:S(2)}) collective-permute-start(bf16[256,128]{1,0:T(8,128)(2,1)S(1)} %get-tuple-element.26), channel_id=1, source_target_pairs={{0,2},{2,0},{4,6},{6,4},{8,10},{10,8},{12,14},{14,12},{1,5},{5,1},... | collective-permute-start | bytes 196616 | tf_op jit(solution)/shard_map/ppermute | solution.py:558
  6.0 5.0 %collective-permute-start.1 = (bf16[256,128]{1,0:T(8,128)(2,1)S(1)}, bf16[256,128]{1,0:T(8,128)(2,1)S(1)}, u32[]{:S(2)}, u32[]{:S(2)}) collective-permute-start(bf16[256,128]{1,0:T(8,128)(2,1)S(1)} %get-tuple-element.27), channel_id=1, source_target_pairs={{2,4},{4,2},{6,8},{8,6},{10,12},{12,10},{5,9},{9,5},{7,11},{11,7},... | collective-permute-start | bytes 196616 | tf_op jit(solution)/shard_map/ppermute | solution.py:558
  6.6 5.8 %collective-permute-start.2 = (bf16[256,128]{1,0:T(8,128)(2,1)S(1)}, bf16[256,128]{1,0:T(8,128)(2,1)S(1)}, u32[]{:S(2)}, u32[]{:S(2)}) collective-permute-start(bf16[256,128]{1,0:T(8,128)(2,1)S(1)} %get-tuple-element.28), channel_id=1, source_target_pairs={{0,4},{4,0},{2,6},{6,2},{8,12},{12,8},{10,14},{14,10},{1,3},{3,1},... | collective-permute-start | bytes 196616 | tf_op jit(solution)/shard_map/ppermute | solution.py:558
  9.5 2.9 %collective-permute-start.3 = (bf16[256,128]{1,0:T(8,128)(2,1)S(1)}, bf16[256,128]{1,0:T(8,128)(2,1)S(1)}, u32[]{:S(2)}, u32[]{:S(2)}) collective-permute-start(bf16[256,128]{1,0:T(8,128)(2,1)S(1)} %get-tuple-element.29), channel_id=1, source_target_pairs={{4,8},{8,4},{6,10},{10,6},{3,5},{5,3},{7,9},{9,7},{11,13},{13,11},... | collective-permute-start | bytes 196616 | tf_op jit(solution)/shard_map/ppermute | solution.py:558
  30.8 9.5 %collective-permute-start.4 = (f32[256,128]{1,0:T(8,128)S(1)}, f32[256,128]{1,0:T(8,128)S(1)}, u32[]{:S(2)}, u32[]{:S(2)}) collective-permute-start(f32[256,128]{1,0:T(8,128)S(1)} %get-tuple-element.31), channel_id=1, source_target_pairs={{0,2},{2,0},{4,6},{6,4},{8,10},{10,8},{12,14},{14,12},{1,5},{5,1},... | collective-permute-start | bytes 393224 | tf_op jit(solution)/shard_map/ppermute | solution.py:558
  33.8 8.9 %collective-permute-start.5 = (f32[256,128]{1,0:T(8,128)S(1)}, f32[256,128]{1,0:T(8,128)S(1)}, u32[]{:S(2)}, u32[]{:S(2)}) collective-permute-start(f32[256,128]{1,0:T(8,128)S(1)} %get-tuple-element.32), channel_id=1, source_target_pairs={{2,4},{4,2},{6,8},{8,6},{10,12},{12,10},{5,9},{9,5},{7,11},{11,7},... | collective-permute-start | bytes 393224 | tf_op jit(solution)/shard_map/ppermute | solution.py:558
  34.4 10.9 %collective-permute-start.6 = (f32[256,128]{1,0:T(8,128)S(1)}, f32[256,128]{1,0:T(8,128)S(1)}, u32[]{:S(2)}, u32[]{:S(2)}) collective-permute-start(f32[256,128]{1,0:T(8,128)S(1)} %get-tuple-element.33), channel_id=1, source_target_pairs={{0,4},{4,0},{2,6},{6,2},{8,12},{12,8},{10,14},{14,10},{1,3},{3,1},... | collective-permute-start | bytes 393224 | tf_op jit(solution)/shard_map/ppermute | solution.py:558
  39.6 5.7 %collective-permute-start.7 = (f32[256,128]{1,0:T(8,128)S(1)}, f32[256,128]{1,0:T(8,128)S(1)}, u32[]{:S(2)}, u32[]{:S(2)}) collective-permute-start(f32[256,128]{1,0:T(8,128)S(1)} %get-tuple-element.34), channel_id=1, source_target_pairs={{4,8},{8,4},{6,10},{10,6},{3,5},{5,3},{7,9},{9,7},{11,13},{13,11},... | collective-permute-start | bytes 393224 | tf_op jit(solution)/shard_map/ppermute | solution.py:558
  40.4 5.0 %copy-start.1 = (f32[4096]{0:T(1024)S(1)}, f32[4096]{0:T(1024)}, u32[]{:S(2)}) copy-start(f32[4096]{0:T(1024)} %param.11) | copy-start | bytes 49156
  49.7 7.2 %collective-permute-start.8 = (bf16[256,128]{1,0:T(8,128)(2,1)S(1)}, bf16[256,128]{1,0:T(8,128)(2,1)S(1)}, u32[]{:S(2)}, u32[]{:S(2)}) collective-permute-start(bf16[256,128]{1,0:T(8,128)(2,1)S(1)} %get-tuple-element.36), channel_id=1, source_target_pairs={{0,2},{2,0},{4,6},{6,4},{8,10},{10,8},{12,14},{14,12},{1,5},{5,1},... | collective-permute-start | bytes 196616 | tf_op jit(solution)/shard_map/ppermute | solution.py:558
  50.7 6.2 %collective-permute-start.9 = (bf16[256,128]{1,0:T(8,128)(2,1)S(1)}, bf16[256,128]{1,0:T(8,128)(2,1)S(1)}, u32[]{:S(2)}, u32[]{:S(2)}) collective-permute-start(bf16[256,128]{1,0:T(8,128)(2,1)S(1)} %get-tuple-element.37), channel_id=1, source_target_pairs={{2,4},{4,2},{6,8},{8,6},{10,12},{12,10},{5,9},{9,5},{7,11},{11,7},... | collective-permute-start | bytes 196616 | tf_op jit(solution)/shard_map/ppermute | solution.py:558
  51.3 8.4 %collective-permute-start.10 = (bf16[256,128]{1,0:T(8,128)(2,1)S(1)}, bf16[256,128]{1,0:T(8,128)(2,1)S(1)}, u32[]{:S(2)}, u32[]{:S(2)}) collective-permute-start(bf16[256,128]{1,0:T(8,128)(2,1)S(1)} %get-tuple-element.38), channel_id=1, source_target_pairs={{0,4},{4,0},{2,6},{6,2},{8,12},{12,8},{10,14},{14,10},{1,3},{3,1},... | collective-permute-start | bytes 196616 | tf_op jit(solution)/shard_map/ppermute | solution.py:558
  56.2 3.6 %collective-permute-start.11 = (bf16[256,128]{1,0:T(8,128)(2,1)S(1)}, bf16[256,128]{1,0:T(8,128)(2,1)S(1)}, u32[]{:S(2)}, u32[]{:S(2)}) collective-permute-start(bf16[256,128]{1,0:T(8,128)(2,1)S(1)} %get-tuple-element.39), channel_id=1, source_target_pairs={{4,8},{8,4},{6,10},{10,6},{3,5},{5,3},{7,9},{9,7},{11,13},{13,11},... | collective-permute-start | bytes 196616 | tf_op jit(solution)/shard_map/ppermute | solution.py:558
  78.2 8.8 %collective-permute-start.12 = (f32[256,128]{1,0:T(8,128)S(1)}, f32[256,128]{1,0:T(8,128)S(1)}, u32[]{:S(2)}, u32[]{:S(2)}) collective-permute-start(f32[256,128]{1,0:T(8,128)S(1)} %get-tuple-element.41), channel_id=1, source_target_pairs={{0,2},{2,0},{4,6},{6,4},{8,10},{10,8},{12,14},{14,12},{1,5},{5,1},... | collective-permute-start | bytes 393224 | tf_op jit(solution)/shard_map/ppermute | solution.py:558
  80.5 8.8 %collective-permute-start.13 = (f32[256,128]{1,0:T(8,128)S(1)}, f32[256,128]{1,0:T(8,128)S(1)}, u32[]{:S(2)}, u32[]{:S(2)}) collective-permute-start(f32[256,128]{1,0:T(8,128)S(1)} %get-tuple-element.42), channel_id=1, source_target_pairs={{2,4},{4,2},{6,8},{8,6},{10,12},{12,10},{5,9},{9,5},{7,11},{11,7},... | collective-permute-start | bytes 393224 | tf_op jit(solution)/shard_map/ppermute | solution.py:558
  81.1 9.8 %collective-permute-start.14 = (f32[256,128]{1,0:T(8,128)S(1)}, f32[256,128]{1,0:T(8,128)S(1)}, u32[]{:S(2)}, u32[]{:S(2)}) collective-permute-start(f32[256,128]{1,0:T(8,128)S(1)} %get-tuple-element.43), channel_id=1, source_target_pairs={{0,4},{4,0},{2,6},{6,2},{8,12},{12,8},{10,14},{14,10},{1,3},{3,1},... | collective-permute-start | bytes 393224 | tf_op jit(solution)/shard_map/ppermute | solution.py:558
  86.3 4.6 %collective-permute-start.15 = (f32[256,128]{1,0:T(8,128)S(1)}, f32[256,128]{1,0:T(8,128)S(1)}, u32[]{:S(2)}, u32[]{:S(2)}) collective-permute-start(f32[256,128]{1,0:T(8,128)S(1)} %get-tuple-element.44), channel_id=1, source_target_pairs={{4,8},{8,4},{6,10},{10,6},{3,5},{5,3},{7,9},{9,7},{11,13},{13,11},... | collective-permute-start | bytes 393224 | tf_op jit(solution)/shard_map/ppermute | solution.py:558
  94.6 2.7 %collective-permute-start.16 = (bf16[4096,128]{1,0:T(8,128)(2,1)S(1)}, bf16[4096,128]{1,0:T(8,128)(2,1)S(1)}, u32[]{:S(2)}, u32[]{:S(2)}) collective-permute-start(bf16[4096,128]{1,0:T(8,128)(2,1)S(1)} %shard_map.79.own_ref), channel_id=1, source_target_pairs={{0,1},{1,0},{2,3},{3,2},{4,5},{5,4},{6,7},{7,6},{8,9},{9,8},{10,11... | collective-permute-start | bytes 3145736 | tf_op jit(solution)/shard_map/ppermute | solution.py:538
  98.1 8.1 %collective-permute-start.19 = (f32[136,128]{1,0:T(8,128)S(1)}, f32[136,128]{1,0:T(8,128)S(1)}, u32[]{:S(2)}, u32[]{:S(2)}) collective-permute-start(f32[136,128]{1,0:T(8,128)S(1)} %shard_map.80), channel_id=1, source_target_pairs={{0,6},{2,4},{4,2},{6,0},{8,14},{10,12},{12,10},{14,8},{1,7},{3,5},... | collective-permute-start | bytes 208904 | tf_op jit(solution)/shard_map/ppermute | solution.py:529
  103.2 4.6 %collective-permute-start.18 = (f32[136,128]{1,0:T(8,128)S(1)}, f32[136,128]{1,0:T(8,128)S(1)}, u32[]{:S(2)}, u32[]{:S(2)}) collective-permute-start(f32[136,128]{1,0:T(8,128)S(1)} %shard_map.80), channel_id=1, source_target_pairs={{0,4},{2,6},{4,0},{6,2},{8,12},{10,14},{12,8},{14,10},{1,5},{3,7},... | collective-permute-start | bytes 208904 | tf_op jit(solution)/shard_map/ppermute | solution.py:529
  103.2 4.6 %collective-permute-start.17 = (f32[136,128]{1,0:T(8,128)S(1)}, f32[136,128]{1,0:T(8,128)S(1)}, u32[]{:S(2)}, u32[]{:S(2)}) collective-permute-start(f32[136,128]{1,0:T(8,128)S(1)} %shard_map.80), channel_id=1, source_target_pairs={{0,2},{2,0},{4,6},{6,4},{8,10},{10,8},{12,14},{14,12},{1,3},{3,1},... | collective-permute-start | bytes 208904 | tf_op jit(solution)/shard_map/ppermute | solution.py:529
  107.8 7.2 %collective-permute-start.20 = (f32[136,128]{1,0:T(8,128)S(1)}, f32[136,128]{1,0:T(8,128)S(1)}, u32[]{:S(2)}, u32[]{:S(2)}) collective-permute-start(f32[136,128]{1,0:T(8,128)S(1)} %add_add_fusion), channel_id=1, source_target_pairs={{0,8},{2,10},{4,12},{6,14},{8,0},{10,2},{12,4},{14,6},{1,9},{3,11}... | collective-permute-start | bytes 208904 | tf_op jit(solution)/shard_map/ppermute | solution.py:529
  115.0 1.3 %collective-permute-start.21 = (f32[136,128]{1,0:T(8,128)S(1)}, f32[136,128]{1,0:T(8,128)S(1)}, u32[]{:S(2)}, u32[]{:S(2)}) collective-permute-start(f32[136,128]{1,0:T(8,128)S(1)} %add.37.mine_ref), channel_id=1, source_target_pairs={{0,1},{1,0},{2,3},{3,2},{4,5},{5,4},{6,7},{7,6},{8,9},{9,8},{10,11... | collective-permute-start | bytes 208904 | tf_op jit(solution)/shard_map/ppermute | solution.py:538
  (2 other events, 8.8 us)

commit v10 on v9

--- a/solution.py
+++ b/solution.py
@@ -376,11 +376,11 @@
         block = rows[:, start_row : start_row + LANES]
         block = pltpu.roll(block, lax.rem(total - first, LANES), 1)
         for k in range(PANEL):
-            block_ref[k] = jnp.broadcast_to(block[:, k : k + 1], (PANEL, LANES))
+            block_ref[k, 0:PANEL, :] = jnp.broadcast_to(block[:, k : k + 1], (PANEL, LANES))
         panel = jnp.where((col >= first) & (col < first + PANEL), 0.0, rows)
         panel = jnp.where(col == row + first, 1.0, panel)
         for h in range(halves):
-            panel_ref[h] = panel[:, h * LANES : (h + 1) * LANES]
+            panel_ref[h, 0:PANEL, :] = panel[:, h * LANES : (h + 1) * LANES]
 
         def repeated(ref, k, i):
             return ref[k, pl.ds(i, HALF, stride=0), :]
@@ -421,19 +421,19 @@
         scales = factor(entry, below)
         for k in range(HALF):
             write_lines(k, [entry[k, m] for m in range(k)], scales[k])
-            lower_ref[k] = below[k]
+            lower_ref[k, 0:HALF, :] = below[k]
         cross = {(m, k): repeated(lower_ref, k, m) for k in range(HALF) for m in range(HALF)}
         for m in range(HALF):
             column = block_ref[HALF + m, HALF:PANEL, :]
             for k in range(HALF):
                 column = column - below[k] * cross[m, k]
-            second_ref[m] = column
+            second_ref[m, 0:HALF, :] = column
         entry = corner(second_ref)
         scales = factor(entry, None)
         for k in range(HALF):
             weights = [cross[k, m] for m in range(HALF)] + [entry[k, m] for m in range(k)]
             write_lines(HALF + k, weights, scales[k])
-        panel = jnp.concatenate([panel_ref[h] for h in range(halves)], 1)
+        panel = jnp.concatenate([panel_ref[h, 0:PANEL, :] for h in range(halves)], 1)
         right = jnp.where(col >= first + PANEL, panel, 0.0)
         ah, am, al = split_three(right)
         bh, bm, bl = split_three(panel)
@@ -507,10 +507,10 @@
         out_specs=hbm,
         scratch_shapes=[
             pltpu.VMEM((2 * LANES, 2 * LANES), f32),
-            pltpu.VMEM((PANEL, PANEL, LANES), f32),
-            pltpu.VMEM((2, PANEL, LANES), f32),
-            pltpu.VMEM((HALF, HALF, LANES), f32),
-            pltpu.VMEM((HALF, HALF, LANES), f32),
+            pltpu.VMEM((PANEL, PANEL + HALF, LANES), f32),
+            pltpu.VMEM((2, PANEL + HALF, LANES), f32),
+            pltpu.VMEM((HALF, 2 * HALF, LANES), f32),
+            pltpu.VMEM((HALF, 2 * HALF, LANES), f32),
             pltpu.VMEM(own.shape, f32),
             pltpu.SemaphoreType.DMA((8,)),
         ],

time: 128 us -> 128 us (level)
  no operation moved by 1% of the time
where the time goes in v10:
time: 128 us; the launch traced here: 127 us
  Pallas kernels  64.1 us (50%)
  starting transfers between devices  41.9 us (33%)
  waiting for transfers between devices  20.1 us (16%)
    pallas_call x2, Pallas kernels, apply_cells(): pl.pallas_call(cells_kernel, out_shape=[jax.ShapeDtypeStruct((nodes, LANE...  36.9 us
    ppermute x16, starting transfers between devices, exchanged(): lax.ppermute(block, ('dom', 'band'), [(2 * i + b, 2 * j + b) for b in ran...  32.9 us
    pallas_call x1, Pallas kernels, rotate(): pl.pallas_call(rotate_kernel, out_shape=jax.ShapeDtypeStruct(own.shape, f...  10.9 us
    ppermute x4, starting transfers between devices, summed_over(): lax.ppermute(value, axis, [(i, i ^ k * stride) for i in range(size)])  8.94 us
    ppermute x16, waiting for transfers between devices, exchanged(): lax.ppermute(block, ('dom', 'band'), [(2 * i + b, 2 * j + b) for b in ran...  8.26 us
    ppermute x4, waiting for transfers between devices, summed_over(): lax.ppermute(value, axis, [(i, i ^ k * stride) for i in range(size)])  7.96 us
    pallas_call x2, Pallas kernels, add_early(): pl.pallas_call(early_kernel, out_shape=jax.ShapeDtypeStruct((nodes, LANES...  4.57 us
    pallas_call x1, Pallas kernels, finish_first(): pl.pallas_call(first_kernel, out_shape=[jax.ShapeDtypeStruct((nodes, LANE...  4.36 us
  transfers between devices with their start and end apart: 22, of which 9 were waited for; matrix products, arithmetic and copies ran while one was open for 1% of the time, Pallas kernels for 4%

profile of v10, /device:TPU:0, one launch (start us, length us, event | category | flops | bytes accessed | tf_op | source)
XLA Modules:
  0.0 127.4 jit_solution(464394633397200671)
XLA Ops:
  0.0 2.9 %shard_map.73 = (bf16[256,128]{1,0:T(8,128)(2,1)S(1)}, bf16[256,128]{1,0:T(8,128)(2,1)S(1)}, bf16[256,128]{1,0:T(8,128)(2,1)S(1)}, bf16[256,128]{1,0:T(8,128)(2,1)S(1)}, bf16[4096,128]{1,0:T(8,128)(2,1)S(1)}) custom-call(s32[4]{0:T(128)S(1)} %fusion.2.order_ref, s32[4,256]{1,0:T(4,128)} %lists_ref.1, bf16[4096,128]{1,0:T(8,128)(2,1)} %old_ref.1), custom_call_target="tpu_custom_call" | custom-call | tf_op jit(solution)/shard_map/pallas_call | solution.py:77
  3.0 3.0 %collective-permute-start = (bf16[256,128]{1,0:T(8,128)(2,1)S(1)}, bf16[256,128]{1,0:T(8,128)(2,1)S(1)}, u32[]{:S(2)}, u32[]{:S(2)}) collective-permute-start(bf16[256,128]{1,0:T(8,128)(2,1)S(1)} %get-tuple-element.26), channel_id=1, source_target_pairs={{0,2},{2,0},{4,6},{6,4},{8,10},{10,8},{12,14},{14,12},{1,5},{5,1},... | collective-permute-start | bytes 196616 | tf_op jit(solution)/shard_map/ppermute | solution.py:558
  6.6 2.9 %collective-permute-start.2 = (bf16[256,128]{1,0:T(8,128)(2,1)S(1)}, bf16[256,128]{1,0:T(8,128)(2,1)S(1)}, u32[]{:S(2)}, u32[]{:S(2)}) collective-permute-start(bf16[256,128]{1,0:T(8,128)(2,1)S(1)} %get-tuple-element.28), channel_id=1, source_target_pairs={{0,4},{4,0},{2,6},{6,2},{8,12},{12,8},{10,14},{14,10},{1,3},{3,1},... | collective-permute-start | bytes 196616 | tf_op jit(solution)/shard_map/ppermute | solution.py:558
  11.0 1.4 %collective-permute-done.2.h2 = bf16[256,128]{1,0:T(8,128)(2,1)S(1)} collective-permute-done((bf16[256,128]{1,0:T(8,128)(2,1)S(1)}, bf16[256,128]{1,0:T(8,128)(2,1)S(1)}, u32[]{:S(2)}, u32[]{:S(2)}) %collective-permute-start.2) | collective-permute-done | bytes 65568 | tf_op jit(solution)/shard_map/ppermute | solution.py:558
  12.4 18.5 %shard_map.74 = (f32[4096,128]{1,0:T(8,128)S(1)}, f32[256,128]{1,0:T(8,128)S(1)}, f32[256,128]{1,0:T(8,128)S(1)}, f32[256,128]{1,0:T(8,128)S(1)}, f32[256,128]{1,0:T(8,128)S(1)}) custom-call(s32[4]{0:T(128)S(1)} %fusion.2.order_ref, s32[8192]{0:T(1024)S(1)} %bitcast.7, f32[16]{0:T(128)} %scales_ref.3, bf16[512,512]{1,0:T(8,128)(2,1)} %whole_ref.3, ...), custom_call_target="tpu_custom_call" | custom-call | tf_op jit(solution)/shard_map/pallas_call | solution.py:179
  30.8 2.9 %collective-permute-start.4 = (f32[256,128]{1,0:T(8,128)S(1)}, f32[256,128]{1,0:T(8,128)S(1)}, u32[]{:S(2)}, u32[]{:S(2)}) collective-permute-start(f32[256,128]{1,0:T(8,128)S(1)} %get-tuple-element.31), channel_id=1, source_target_pairs={{0,2},{2,0},{4,6},{6,4},{8,10},{10,8},{12,14},{14,12},{1,5},{5,1},... | collective-permute-start | bytes 393224 | tf_op jit(solution)/shard_map/ppermute | solution.py:558
  34.4 5.2 %collective-permute-start.6 = (f32[256,128]{1,0:T(8,128)S(1)}, f32[256,128]{1,0:T(8,128)S(1)}, u32[]{:S(2)}, u32[]{:S(2)}) collective-permute-start(f32[256,128]{1,0:T(8,128)S(1)} %get-tuple-element.33), channel_id=1, source_target_pairs={{0,4},{4,0},{2,6},{6,2},{8,12},{12,8},{10,14},{14,10},{1,3},{3,1},... | collective-permute-start | bytes 393224 | tf_op jit(solution)/shard_map/ppermute | solution.py:558
  40.4 2.3 %shard_map.75.own_ref = f32[4096,128]{1,0:T(8,128)S(1)} custom-call(s32[4]{0:T(128)S(1)} %fusion.2.order_ref, s32[1024]{0:T(1024)S(1)} %bitcast.9, f32[4096,128]{1,0:T(8,128)S(1)} %get-tuple-element.30.own_ref, f32[256,128]{1,0:T(8,128)S(1)} %collective-permute-done.4.r0), custom_call_target="tpu_custom_call" | custom-call | flops 1000000 | bytes 4000000 | tf_op jit(solution)/shard_map/pallas_call | solution.py:233
  42.7 2.6 %collective-permute-done.6.r2 = f32[256,128]{1,0:T(8,128)S(1)} collective-permute-done((f32[256,128]{1,0:T(8,128)S(1)}, f32[256,128]{1,0:T(8,128)S(1)}, u32[]{:S(2)}, u32[]{:S(2)}) %collective-permute-start.6) | collective-permute-done | bytes 131104 | tf_op jit(solution)/shard_map/ppermute | solution.py:558
  45.3 4.4 %shard_map.76 = (bf16[4096,128]{1,0:T(8,128)(2,1)S(1)}, bf16[256,128]{1,0:T(8,128)(2,1)S(1)}, bf16[256,128]{1,0:T(8,128)(2,1)S(1)}, bf16[256,128]{1,0:T(8,128)(2,1)S(1)}, bf16[256,128]{1,0:T(8,128)(2,1)S(1)}) custom-call(s32[4]{0:T(128)S(1)} %fusion.2.order_ref, s32[1024]{0:T(1024)S(1)} %bitcast.10, f32[2]{0:T(128)S(1)} %copy-done.2, ...), custom_call_target="tpu_custom_call" | custom-call | tf_op jit(solution)/shard_map/pallas_call | solution.py:292
  51.5 5.0 %collective-permute-start.10 = (bf16[256,128]{1,0:T(8,128)(2,1)S(1)}, bf16[256,128]{1,0:T(8,128)(2,1)S(1)}, u32[]{:S(2)}, u32[]{:S(2)}) collective-permute-start(bf16[256,128]{1,0:T(8,128)(2,1)S(1)} %get-tuple-element.38), channel_id=1, source_target_pairs={{0,4},{4,0},{2,6},{6,2},{8,12},{12,8},{10,14},{14,10},{1,3},{3,1},... | collective-permute-start | bytes 196616 | tf_op jit(solution)/shard_map/ppermute | solution.py:558
  57.2 2.9 %collective-permute-done.10.h2 = bf16[256,128]{1,0:T(8,128)(2,1)S(1)} collective-permute-done((bf16[256,128]{1,0:T(8,128)(2,1)S(1)}, bf16[256,128]{1,0:T(8,128)(2,1)S(1)}, u32[]{:S(2)}, u32[]{:S(2)}) %collective-permute-start.10) | collective-permute-done | bytes 65568 | tf_op jit(solution)/shard_map/ppermute | solution.py:558
  60.0 18.5 %shard_map.77 = (f32[4096,128]{1,0:T(8,128)S(1)}, f32[256,128]{1,0:T(8,128)S(1)}, f32[256,128]{1,0:T(8,128)S(1)}, f32[256,128]{1,0:T(8,128)S(1)}, f32[256,128]{1,0:T(8,128)S(1)}) custom-call(s32[4]{0:T(128)S(1)} %fusion.2.order_ref, s32[8192]{0:T(1024)S(1)} %bitcast.8, f32[16]{0:T(128)} %scales_ref.3, bf16[512,512]{1,0:T(8,128)(2,1)} %whole_ref.3, ...), custom_call_target="tpu_custom_call" | custom-call | tf_op jit(solution)/shard_map/pallas_call | solution.py:179
  78.5 2.2 %collective-permute-start.12 = (f32[256,128]{1,0:T(8,128)S(1)}, f32[256,128]{1,0:T(8,128)S(1)}, u32[]{:S(2)}, u32[]{:S(2)}) collective-permute-start(f32[256,128]{1,0:T(8,128)S(1)} %get-tuple-element.41), channel_id=1, source_target_pairs={{0,2},{2,0},{4,6},{6,4},{8,10},{10,8},{12,14},{14,12},{1,5},{5,1},... | collective-permute-start | bytes 393224 | tf_op jit(solution)/shard_map/ppermute | solution.py:558
  81.4 5.2 %collective-permute-start.14 = (f32[256,128]{1,0:T(8,128)S(1)}, f32[256,128]{1,0:T(8,128)S(1)}, u32[]{:S(2)}, u32[]{:S(2)}) collective-permute-start(f32[256,128]{1,0:T(8,128)S(1)} %get-tuple-element.43), channel_id=1, source_target_pairs={{0,4},{4,0},{2,6},{6,2},{8,12},{12,8},{10,14},{14,10},{1,3},{3,1},... | collective-permute-start | bytes 393224 | tf_op jit(solution)/shard_map/ppermute | solution.py:558
  87.3 2.3 %shard_map.78.own_ref = f32[4096,128]{1,0:T(8,128)S(1)} custom-call(s32[4]{0:T(128)S(1)} %fusion.2.order_ref, s32[1024]{0:T(1024)S(1)} %bitcast.11, f32[4096,128]{1,0:T(8,128)S(1)} %get-tuple-element.40.own_ref, f32[256,128]{1,0:T(8,128)S(1)} %collective-permute-done.12.r0), custom_call_target="tpu_custom_call" | custom-call | flops 1000000 | bytes 4000000 | tf_op jit(solution)/shard_map/pallas_call | solution.py:233
  90.9 3.7 %shard_map.79.own_ref = bf16[4096,128]{1,0:T(8,128)(2,1)S(1)} custom-call(s32[4]{0:T(128)S(1)} %fusion.2.order_ref, s32[1024]{0:T(1024)S(1)} %bitcast.12, f32[2]{0:T(128)S(1)} %copy-done.2, f32[4096,128]{1,0:T(8,128)S(1)} %shard_map.78.own_ref, f32[32,128]{1,0:T(8,128)S(1)} %bitcast.14, bf16[4096,128]{1,0:T(8,128)(2,1)S(1)} %get-tuple-element.35.vec_ref, ...), custom_call_target="tpu_custom_call" | custom-call | tf_op jit(solution)/shard_map/pallas_call | solution.py:310
  94.7 2.6 %collective-permute-done.16.other_ref = bf16[4096,128]{1,0:T(8,128)(2,1)S(1)} collective-permute-done((bf16[4096,128]{1,0:T(8,128)(2,1)S(1)}, bf16[4096,128]{1,0:T(8,128)(2,1)S(1)}, u32[]{:S(2)}, u32[]{:S(2)}) %collective-permute-start.16) | collective-permute-done | bytes 1048608 | tf_op jit(solution)/shard_map/ppermute | solution.py:538
  98.1 5.6 %collective-permute-start.19 = (f32[136,128]{1,0:T(8,128)S(1)}, f32[136,128]{1,0:T(8,128)S(1)}, u32[]{:S(2)}, u32[]{:S(2)}) collective-permute-start(f32[136,128]{1,0:T(8,128)S(1)} %shard_map.80), channel_id=1, source_target_pairs={{0,6},{2,4},{4,2},{6,0},{8,14},{10,12},{12,10},{14,8},{1,7},{3,5},... | collective-permute-start | bytes 208904 | tf_op jit(solution)/shard_map/ppermute | solution.py:529
  104.3 2.3 %collective-permute-done.19 = f32[136,128]{1,0:T(8,128)S(1)} collective-permute-done((f32[136,128]{1,0:T(8,128)S(1)}, f32[136,128]{1,0:T(8,128)S(1)}, u32[]{:S(2)}, u32[]{:S(2)}) %collective-permute-start.19) | collective-permute-done | bytes 69664 | tf_op jit(solution)/shard_map/ppermute | solution.py:529
  106.6 1.6 %collective-permute-done.18 = f32[136,128]{1,0:T(8,128)S(1)} collective-permute-done((f32[136,128]{1,0:T(8,128)S(1)}, f32[136,128]{1,0:T(8,128)S(1)}, u32[]{:S(2)}, u32[]{:S(2)}) %collective-permute-start.18) | collective-permute-done | bytes 69664 | tf_op jit(solution)/shard_map/ppermute | solution.py:529
  108.3 2.7 %collective-permute-start.20 = (f32[136,128]{1,0:T(8,128)S(1)}, f32[136,128]{1,0:T(8,128)S(1)}, u32[]{:S(2)}, u32[]{:S(2)}) collective-permute-start(f32[136,128]{1,0:T(8,128)S(1)} %add_add_fusion), channel_id=1, source_target_pairs={{0,8},{2,10},{4,12},{6,14},{8,0},{10,2},{12,4},{14,6},{1,9},{3,11}... | collective-permute-start | bytes 208904 | tf_op jit(solution)/shard_map/ppermute | solution.py:529
  111.0 4.0 %collective-permute-done.20 = f32[136,128]{1,0:T(8,128)S(1)} collective-permute-done((f32[136,128]{1,0:T(8,128)S(1)}, f32[136,128]{1,0:T(8,128)S(1)}, u32[]{:S(2)}, u32[]{:S(2)}) %collective-permute-start.20) | collective-permute-done | bytes 69664 | tf_op jit(solution)/shard_map/ppermute | solution.py:529
  116.4 10.9 %shard_map.81 = f32[4096,128]{1,0:T(8,128)} custom-call(s32[1]{0:T(128)} %bitcast.band_ref, f32[1]{0:T(128)} %constant.52.clone.1.count_ref, f32[136,128]{1,0:T(8,128)S(1)} %add.37.mine_ref, f32[136,128]{1,0:T(8,128)S(1)} %collective-permute-done.21.theirs_ref, bf16[4096,128]{1,0:T(8,128)(2,1)S(1)} %shard_map.79.own_ref, ...), custom_call_target="tpu_custom_call" | custom-call | tf_op jit(solution)/shard_map/pallas_call | solution.py:503
  (43 shorter events, 11.3 us)
Async XLA Ops:
  0.0 40.3 %copy-start.3 = (s32[4,256]{1,0:T(4,128)S(1)}, s32[4,256]{1,0:T(4,128)}, u32[]{:S(2)}) copy-start(s32[4,256]{1,0:T(4,128)} %lists_ref.1) | copy-start | bytes 12292
  3.0 8.0 %collective-permute-start = (bf16[256,128]{1,0:T(8,128)(2,1)S(1)}, bf16[256,128]{1,0:T(8,128)(2,1)S(1)}, u32[]{:S(2)}, u32[]{:S(2)}) collective-permute-start(bf16[256,128]{1,0:T(8,128)(2,1)S(1)} %get-tuple-element.26), channel_id=1, source_target_pairs={{0,2},{2,0},{4,6},{6,4},{8,10},{10,8},{12,14},{14,12},{1,5},{5,1},... | collective-permute-start | bytes 196616 | tf_op jit(solution)/shard_map/ppermute | solution.py:558
  6.0 5.0 %collective-permute-start.1 = (bf16[256,128]{1,0:T(8,128)(2,1)S(1)}, bf16[256,128]{1,0:T(8,128)(2,1)S(1)}, u32[]{:S(2)}, u32[]{:S(2)}) collective-permute-start(bf16[256,128]{1,0:T(8,128)(2,1)S(1)} %get-tuple-element.27), channel_id=1, source_target_pairs={{2,4},{4,2},{6,8},{8,6},{10,12},{12,10},{5,9},{9,5},{7,11},{11,7},... | collective-permute-start | bytes 196616 | tf_op jit(solution)/shard_map/ppermute | solution.py:558
  6.6 5.8 %collective-permute-start.2 = (bf16[256,128]{1,0:T(8,128)(2,1)S(1)}, bf16[256,128]{1,0:T(8,128)(2,1)S(1)}, u32[]{:S(2)}, u32[]{:S(2)}) collective-permute-start(bf16[256,128]{1,0:T(8,128)(2,1)S(1)} %get-tuple-element.28), channel_id=1, source_target_pairs={{0,4},{4,0},{2,6},{6,2},{8,12},{12,8},{10,14},{14,10},{1,3},{3,1},... | collective-permute-start | bytes 196616 | tf_op jit(solution)/shard_map/ppermute | solution.py:558
  9.5 2.9 %collective-permute-start.3 = (bf16[256,128]{1,0:T(8,128)(2,1)S(1)}, bf16[256,128]{1,0:T(8,128)(2,1)S(1)}, u32[]{:S(2)}, u32[]{:S(2)}) collective-permute-start(bf16[256,128]{1,0:T(8,128)(2,1)S(1)} %get-tuple-element.29), channel_id=1, source_target_pairs={{4,8},{8,4},{6,10},{10,6},{3,5},{5,3},{7,9},{9,7},{11,13},{13,11},... | collective-permute-start | bytes 196616 | tf_op jit(solution)/shard_map/ppermute | solution.py:558
  30.8 9.5 %collective-permute-start.4 = (f32[256,128]{1,0:T(8,128)S(1)}, f32[256,128]{1,0:T(8,128)S(1)}, u32[]{:S(2)}, u32[]{:S(2)}) collective-permute-start(f32[256,128]{1,0:T(8,128)S(1)} %get-tuple-element.31), channel_id=1, source_target_pairs={{0,2},{2,0},{4,6},{6,4},{8,10},{10,8},{12,14},{14,12},{1,5},{5,1},... | collective-permute-start | bytes 393224 | tf_op jit(solution)/shard_map/ppermute | solution.py:558
  33.8 8.9 %collective-permute-start.5 = (f32[256,128]{1,0:T(8,128)S(1)}, f32[256,128]{1,0:T(8,128)S(1)}, u32[]{:S(2)}, u32[]{:S(2)}) collective-permute-start(f32[256,128]{1,0:T(8,128)S(1)} %get-tuple-element.32), channel_id=1, source_target_pairs={{2,4},{4,2},{6,8},{8,6},{10,12},{12,10},{5,9},{9,5},{7,11},{11,7},... | collective-permute-start | bytes 393224 | tf_op jit(solution)/shard_map/ppermute | solution.py:558
  34.4 10.9 %collective-permute-start.6 = (f32[256,128]{1,0:T(8,128)S(1)}, f32[256,128]{1,0:T(8,128)S(1)}, u32[]{:S(2)}, u32[]{:S(2)}) collective-permute-start(f32[256,128]{1,0:T(8,128)S(1)} %get-tuple-element.33), channel_id=1, source_target_pairs={{0,4},{4,0},{2,6},{6,2},{8,12},{12,8},{10,14},{14,10},{1,3},{3,1},... | collective-permute-start | bytes 393224 | tf_op jit(solution)/shard_map/ppermute | solution.py:558
  39.6 5.7 %collective-permute-start.7 = (f32[256,128]{1,0:T(8,128)S(1)}, f32[256,128]{1,0:T(8,128)S(1)}, u32[]{:S(2)}, u32[]{:S(2)}) collective-permute-start(f32[256,128]{1,0:T(8,128)S(1)} %get-tuple-element.34), channel_id=1, source_target_pairs={{4,8},{8,4},{6,10},{10,6},{3,5},{5,3},{7,9},{9,7},{11,13},{13,11},... | collective-permute-start | bytes 393224 | tf_op jit(solution)/shard_map/ppermute | solution.py:558
  40.4 5.0 %copy-start.1 = (f32[4096]{0:T(1024)S(1)}, f32[4096]{0:T(1024)}, u32[]{:S(2)}) copy-start(f32[4096]{0:T(1024)} %param.11) | copy-start | bytes 49156
  49.7 7.4 %collective-permute-start.8 = (bf16[256,128]{1,0:T(8,128)(2,1)S(1)}, bf16[256,128]{1,0:T(8,128)(2,1)S(1)}, u32[]{:S(2)}, u32[]{:S(2)}) collective-permute-start(bf16[256,128]{1,0:T(8,128)(2,1)S(1)} %get-tuple-element.36), channel_id=1, source_target_pairs={{0,2},{2,0},{4,6},{6,4},{8,10},{10,8},{12,14},{14,12},{1,5},{5,1},... | collective-permute-start | bytes 196616 | tf_op jit(solution)/shard_map/ppermute | solution.py:558
  50.8 6.4 %collective-permute-start.9 = (bf16[256,128]{1,0:T(8,128)(2,1)S(1)}, bf16[256,128]{1,0:T(8,128)(2,1)S(1)}, u32[]{:S(2)}, u32[]{:S(2)}) collective-permute-start(bf16[256,128]{1,0:T(8,128)(2,1)S(1)} %get-tuple-element.37), channel_id=1, source_target_pairs={{2,4},{4,2},{6,8},{8,6},{10,12},{12,10},{5,9},{9,5},{7,11},{11,7},... | collective-permute-start | bytes 196616 | tf_op jit(solution)/shard_map/ppermute | solution.py:558
  51.5 8.6 %collective-permute-start.10 = (bf16[256,128]{1,0:T(8,128)(2,1)S(1)}, bf16[256,128]{1,0:T(8,128)(2,1)S(1)}, u32[]{:S(2)}, u32[]{:S(2)}) collective-permute-start(bf16[256,128]{1,0:T(8,128)(2,1)S(1)} %get-tuple-element.38), channel_id=1, source_target_pairs={{0,4},{4,0},{2,6},{6,2},{8,12},{12,8},{10,14},{14,10},{1,3},{3,1},... | collective-permute-start | bytes 196616 | tf_op jit(solution)/shard_map/ppermute | solution.py:558
  56.5 3.6 %collective-permute-start.11 = (bf16[256,128]{1,0:T(8,128)(2,1)S(1)}, bf16[256,128]{1,0:T(8,128)(2,1)S(1)}, u32[]{:S(2)}, u32[]{:S(2)}) collective-permute-start(bf16[256,128]{1,0:T(8,128)(2,1)S(1)} %get-tuple-element.39), channel_id=1, source_target_pairs={{4,8},{8,4},{6,10},{10,6},{3,5},{5,3},{7,9},{9,7},{11,13},{13,11},... | collective-permute-start | bytes 196616 | tf_op jit(solution)/shard_map/ppermute | solution.py:558
  78.5 8.8 %collective-permute-start.12 = (f32[256,128]{1,0:T(8,128)S(1)}, f32[256,128]{1,0:T(8,128)S(1)}, u32[]{:S(2)}, u32[]{:S(2)}) collective-permute-start(f32[256,128]{1,0:T(8,128)S(1)} %get-tuple-element.41), channel_id=1, source_target_pairs={{0,2},{2,0},{4,6},{6,4},{8,10},{10,8},{12,14},{14,12},{1,5},{5,1},... | collective-permute-start | bytes 393224 | tf_op jit(solution)/shard_map/ppermute | solution.py:558
  80.7 8.9 %collective-permute-start.13 = (f32[256,128]{1,0:T(8,128)S(1)}, f32[256,128]{1,0:T(8,128)S(1)}, u32[]{:S(2)}, u32[]{:S(2)}) collective-permute-start(f32[256,128]{1,0:T(8,128)S(1)} %get-tuple-element.42), channel_id=1, source_target_pairs={{2,4},{4,2},{6,8},{8,6},{10,12},{12,10},{5,9},{9,5},{7,11},{11,7},... | collective-permute-start | bytes 393224 | tf_op jit(solution)/shard_map/ppermute | solution.py:558
  81.4 9.5 %collective-permute-start.14 = (f32[256,128]{1,0:T(8,128)S(1)}, f32[256,128]{1,0:T(8,128)S(1)}, u32[]{:S(2)}, u32[]{:S(2)}) collective-permute-start(f32[256,128]{1,0:T(8,128)S(1)} %get-tuple-element.43), channel_id=1, source_target_pairs={{0,4},{4,0},{2,6},{6,2},{8,12},{12,8},{10,14},{14,10},{1,3},{3,1},... | collective-permute-start | bytes 393224 | tf_op jit(solution)/shard_map/ppermute | solution.py:558
  86.6 4.3 %collective-permute-start.15 = (f32[256,128]{1,0:T(8,128)S(1)}, f32[256,128]{1,0:T(8,128)S(1)}, u32[]{:S(2)}, u32[]{:S(2)}) collective-permute-start(f32[256,128]{1,0:T(8,128)S(1)} %get-tuple-element.44), channel_id=1, source_target_pairs={{4,8},{8,4},{6,10},{10,6},{3,5},{5,3},{7,9},{9,7},{11,13},{13,11},... | collective-permute-start | bytes 393224 | tf_op jit(solution)/shard_map/ppermute | solution.py:558
  94.6 2.7 %collective-permute-start.16 = (bf16[4096,128]{1,0:T(8,128)(2,1)S(1)}, bf16[4096,128]{1,0:T(8,128)(2,1)S(1)}, u32[]{:S(2)}, u32[]{:S(2)}) collective-permute-start(bf16[4096,128]{1,0:T(8,128)(2,1)S(1)} %shard_map.79.own_ref), channel_id=1, source_target_pairs={{0,1},{1,0},{2,3},{3,2},{4,5},{5,4},{6,7},{7,6},{8,9},{9,8},{10,11... | collective-permute-start | bytes 3145736 | tf_op jit(solution)/shard_map/ppermute | solution.py:538
  98.1 8.5 %collective-permute-start.19 = (f32[136,128]{1,0:T(8,128)S(1)}, f32[136,128]{1,0:T(8,128)S(1)}, u32[]{:S(2)}, u32[]{:S(2)}) collective-permute-start(f32[136,128]{1,0:T(8,128)S(1)} %shard_map.80), channel_id=1, source_target_pairs={{0,6},{2,4},{4,2},{6,0},{8,14},{10,12},{12,10},{14,8},{1,7},{3,5},... | collective-permute-start | bytes 208904 | tf_op jit(solution)/shard_map/ppermute | solution.py:529
  103.7 4.6 %collective-permute-start.18 = (f32[136,128]{1,0:T(8,128)S(1)}, f32[136,128]{1,0:T(8,128)S(1)}, u32[]{:S(2)}, u32[]{:S(2)}) collective-permute-start(f32[136,128]{1,0:T(8,128)S(1)} %shard_map.80), channel_id=1, source_target_pairs={{0,4},{2,6},{4,0},{6,2},{8,12},{10,14},{12,8},{14,10},{1,5},{3,7},... | collective-permute-start | bytes 208904 | tf_op jit(solution)/shard_map/ppermute | solution.py:529
  103.7 4.6 %collective-permute-start.17 = (f32[136,128]{1,0:T(8,128)S(1)}, f32[136,128]{1,0:T(8,128)S(1)}, u32[]{:S(2)}, u32[]{:S(2)}) collective-permute-start(f32[136,128]{1,0:T(8,128)S(1)} %shard_map.80), channel_id=1, source_target_pairs={{0,2},{2,0},{4,6},{6,4},{8,10},{10,8},{12,14},{14,12},{1,3},{3,1},... | collective-permute-start | bytes 208904 | tf_op jit(solution)/shard_map/ppermute | solution.py:529
  108.3 6.8 %collective-permute-start.20 = (f32[136,128]{1,0:T(8,128)S(1)}, f32[136,128]{1,0:T(8,128)S(1)}, u32[]{:S(2)}, u32[]{:S(2)}) collective-permute-start(f32[136,128]{1,0:T(8,128)S(1)} %add_add_fusion), channel_id=1, source_target_pairs={{0,8},{2,10},{4,12},{6,14},{8,0},{10,2},{12,4},{14,6},{1,9},{3,11}... | collective-permute-start | bytes 208904 | tf_op jit(solution)/shard_map/ppermute | solution.py:529
  115.0 1.3 %collective-permute-start.21 = (f32[136,128]{1,0:T(8,128)S(1)}, f32[136,128]{1,0:T(8,128)S(1)}, u32[]{:S(2)}, u32[]{:S(2)}) collective-permute-start(f32[136,128]{1,0:T(8,128)S(1)} %add.37.mine_ref), channel_id=1, source_target_pairs={{0,1},{1,0},{2,3},{3,2},{4,5},{5,4},{6,7},{7,6},{8,9},{9,8},{10,11... | collective-permute-start | bytes 208904 | tf_op jit(solution)/shard_map/ppermute | solution.py:538
  (2 other events, 8.6 us)

commit v11 on v10

--- a/solution.py
+++ b/solution.py
@@ -84,7 +84,7 @@
             pltpu.SMEM(face_nodes.shape, jnp.int32),
             pltpu.VMEM((nodes + 8, LANES), f32),
             pltpu.VMEM((slots, LANES), f32),
-            pltpu.SemaphoreType.DMA((5,)),
+            pltpu.SemaphoreType.DMA((9,)),
         ],
         compiler_params=grant(8),
     )(side, face_nodes, vectors)

time: 128 us -> 128 us (level)
  no operation moved by 1% of the time
where the time goes in v11:
time: 128 us; the launch traced here: 127 us
  Pallas kernels  64.1 us (50%)
  starting transfers between devices  41.8 us (33%)
  waiting for transfers between devices  20.2 us (16%)
    pallas_call x2, Pallas kernels, apply_cells(): pl.pallas_call(cells_kernel, out_shape=[jax.ShapeDtypeStruct((nodes, LANE...  36.9 us
    ppermute x16, starting transfers between devices, exchanged(): lax.ppermute(block, ('dom', 'band'), [(2 * i + b, 2 * j + b) for b in ran...  32.7 us
    pallas_call x1, Pallas kernels, rotate(): pl.pallas_call(rotate_kernel, out_shape=jax.ShapeDtypeStruct(own.shape, f...  10.9 us
    ppermute x4, starting transfers between devices, summed_over(): lax.ppermute(value, axis, [(i, i ^ k * stride) for i in range(size)])  8.97 us
    ppermute x16, waiting for transfers between devices, exchanged(): lax.ppermute(block, ('dom', 'band'), [(2 * i + b, 2 * j + b) for b in ran...  8.52 us
    ppermute x4, waiting for transfers between devices, summed_over(): lax.ppermute(value, axis, [(i, i ^ k * stride) for i in range(size)])  7.82 us
    pallas_call x2, Pallas kernels, add_early(): pl.pallas_call(early_kernel, out_shape=jax.ShapeDtypeStruct((nodes, LANES...  4.55 us
    pallas_call x1, Pallas kernels, finish_first(): pl.pallas_call(first_kernel, out_shape=[jax.ShapeDtypeStruct((nodes, LANE...  4.34 us
  transfers between devices with their start and end apart: 22, of which 9 were waited for; matrix products, arithmetic and copies ran while one was open for 1% of the time, Pallas kernels for 4%

profile of v11, /device:TPU:0, one launch (start us, length us, event | category | flops | bytes accessed | tf_op | source)
XLA Modules:
  0.0 127.4 jit_solution(13828575968075554767)
XLA Ops:
  0.0 3.0 %shard_map.73 = (bf16[256,128]{1,0:T(8,128)(2,1)S(1)}, bf16[256,128]{1,0:T(8,128)(2,1)S(1)}, bf16[256,128]{1,0:T(8,128)(2,1)S(1)}, bf16[256,128]{1,0:T(8,128)(2,1)S(1)}, bf16[4096,128]{1,0:T(8,128)(2,1)S(1)}) custom-call(s32[4]{0:T(128)S(1)} %fusion.2.order_ref, s32[4,256]{1,0:T(4,128)} %lists_ref.1, bf16[4096,128]{1,0:T(8,128)(2,1)} %old_ref.1), custom_call_target="tpu_custom_call" | custom-call | tf_op jit(solution)/shard_map/pallas_call | solution.py:77
  3.1 3.0 %collective-permute-start = (bf16[256,128]{1,0:T(8,128)(2,1)S(1)}, bf16[256,128]{1,0:T(8,128)(2,1)S(1)}, u32[]{:S(2)}, u32[]{:S(2)}) collective-permute-start(bf16[256,128]{1,0:T(8,128)(2,1)S(1)} %get-tuple-element.26), channel_id=1, source_target_pairs={{0,2},{2,0},{4,6},{6,4},{8,10},{10,8},{12,14},{14,12},{1,5},{5,1},... | collective-permute-start | bytes 196616 | tf_op jit(solution)/shard_map/ppermute | solution.py:558
  6.7 2.9 %collective-permute-start.2 = (bf16[256,128]{1,0:T(8,128)(2,1)S(1)}, bf16[256,128]{1,0:T(8,128)(2,1)S(1)}, u32[]{:S(2)}, u32[]{:S(2)}) collective-permute-start(bf16[256,128]{1,0:T(8,128)(2,1)S(1)} %get-tuple-element.28), channel_id=1, source_target_pairs={{0,4},{4,0},{2,6},{6,2},{8,12},{12,8},{10,14},{14,10},{1,3},{3,1},... | collective-permute-start | bytes 196616 | tf_op jit(solution)/shard_map/ppermute | solution.py:558
  12.5 18.5 %shard_map.74 = (f32[4096,128]{1,0:T(8,128)S(1)}, f32[256,128]{1,0:T(8,128)S(1)}, f32[256,128]{1,0:T(8,128)S(1)}, f32[256,128]{1,0:T(8,128)S(1)}, f32[256,128]{1,0:T(8,128)S(1)}) custom-call(s32[4]{0:T(128)S(1)} %fusion.2.order_ref, s32[8192]{0:T(1024)S(1)} %bitcast.7, f32[16]{0:T(128)} %scales_ref.3, bf16[512,512]{1,0:T(8,128)(2,1)} %whole_ref.3, ...), custom_call_target="tpu_custom_call" | custom-call | tf_op jit(solution)/shard_map/pallas_call | solution.py:179
  30.9 2.9 %collective-permute-start.4 = (f32[256,128]{1,0:T(8,128)S(1)}, f32[256,128]{1,0:T(8,128)S(1)}, u32[]{:S(2)}, u32[]{:S(2)}) collective-permute-start(f32[256,128]{1,0:T(8,128)S(1)} %get-tuple-element.31), channel_id=1, source_target_pairs={{0,2},{2,0},{4,6},{6,4},{8,10},{10,8},{12,14},{14,12},{1,5},{5,1},... | collective-permute-start | bytes 393224 | tf_op jit(solution)/shard_map/ppermute | solution.py:558
  34.5 5.2 %collective-permute-start.6 = (f32[256,128]{1,0:T(8,128)S(1)}, f32[256,128]{1,0:T(8,128)S(1)}, u32[]{:S(2)}, u32[]{:S(2)}) collective-permute-start(f32[256,128]{1,0:T(8,128)S(1)} %get-tuple-element.33), channel_id=1, source_target_pairs={{0,4},{4,0},{2,6},{6,2},{8,12},{12,8},{10,14},{14,10},{1,3},{3,1},... | collective-permute-start | bytes 393224 | tf_op jit(solution)/shard_map/ppermute | solution.py:558
  40.5 2.3 %shard_map.75.own_ref = f32[4096,128]{1,0:T(8,128)S(1)} custom-call(s32[4]{0:T(128)S(1)} %fusion.2.order_ref, s32[1024]{0:T(1024)S(1)} %bitcast.9, f32[4096,128]{1,0:T(8,128)S(1)} %get-tuple-element.30.own_ref, f32[256,128]{1,0:T(8,128)S(1)} %collective-permute-done.4.r0), custom_call_target="tpu_custom_call" | custom-call | flops 1000000 | bytes 4000000 | tf_op jit(solution)/shard_map/pallas_call | solution.py:233
  42.8 2.6 %collective-permute-done.6.r2 = f32[256,128]{1,0:T(8,128)S(1)} collective-permute-done((f32[256,128]{1,0:T(8,128)S(1)}, f32[256,128]{1,0:T(8,128)S(1)}, u32[]{:S(2)}, u32[]{:S(2)}) %collective-permute-start.6) | collective-permute-done | bytes 131104 | tf_op jit(solution)/shard_map/ppermute | solution.py:558
  45.4 4.3 %shard_map.76 = (bf16[4096,128]{1,0:T(8,128)(2,1)S(1)}, bf16[256,128]{1,0:T(8,128)(2,1)S(1)}, bf16[256,128]{1,0:T(8,128)(2,1)S(1)}, bf16[256,128]{1,0:T(8,128)(2,1)S(1)}, bf16[256,128]{1,0:T(8,128)(2,1)S(1)}) custom-call(s32[4]{0:T(128)S(1)} %fusion.2.order_ref, s32[1024]{0:T(1024)S(1)} %bitcast.10, f32[2]{0:T(128)S(1)} %copy-done.2, ...), custom_call_target="tpu_custom_call" | custom-call | tf_op jit(solution)/shard_map/pallas_call | solution.py:292
  51.6 4.8 %collective-permute-start.10 = (bf16[256,128]{1,0:T(8,128)(2,1)S(1)}, bf16[256,128]{1,0:T(8,128)(2,1)S(1)}, u32[]{:S(2)}, u32[]{:S(2)}) collective-permute-start(bf16[256,128]{1,0:T(8,128)(2,1)S(1)} %get-tuple-element.38), channel_id=1, source_target_pairs={{0,4},{4,0},{2,6},{6,2},{8,12},{12,8},{10,14},{14,10},{1,3},{3,1},... | collective-permute-start | bytes 196616 | tf_op jit(solution)/shard_map/ppermute | solution.py:558
  57.1 2.9 %collective-permute-done.10.h2 = bf16[256,128]{1,0:T(8,128)(2,1)S(1)} collective-permute-done((bf16[256,128]{1,0:T(8,128)(2,1)S(1)}, bf16[256,128]{1,0:T(8,128)(2,1)S(1)}, u32[]{:S(2)}, u32[]{:S(2)}) %collective-permute-start.10) | collective-permute-done | bytes 65568 | tf_op jit(solution)/shard_map/ppermute | solution.py:558
  59.9 18.5 %shard_map.77 = (f32[4096,128]{1,0:T(8,128)S(1)}, f32[256,128]{1,0:T(8,128)S(1)}, f32[256,128]{1,0:T(8,128)S(1)}, f32[256,128]{1,0:T(8,128)S(1)}, f32[256,128]{1,0:T(8,128)S(1)}) custom-call(s32[4]{0:T(128)S(1)} %fusion.2.order_ref, s32[8192]{0:T(1024)S(1)} %bitcast.8, f32[16]{0:T(128)} %scales_ref.3, bf16[512,512]{1,0:T(8,128)(2,1)} %whole_ref.3, ...), custom_call_target="tpu_custom_call" | custom-call | tf_op jit(solution)/shard_map/pallas_call | solution.py:179
  78.4 2.2 %collective-permute-start.12 = (f32[256,128]{1,0:T(8,128)S(1)}, f32[256,128]{1,0:T(8,128)S(1)}, u32[]{:S(2)}, u32[]{:S(2)}) collective-permute-start(f32[256,128]{1,0:T(8,128)S(1)} %get-tuple-element.41), channel_id=1, source_target_pairs={{0,2},{2,0},{4,6},{6,4},{8,10},{10,8},{12,14},{14,12},{1,5},{5,1},... | collective-permute-start | bytes 393224 | tf_op jit(solution)/shard_map/ppermute | solution.py:558
  81.3 5.2 %collective-permute-start.14 = (f32[256,128]{1,0:T(8,128)S(1)}, f32[256,128]{1,0:T(8,128)S(1)}, u32[]{:S(2)}, u32[]{:S(2)}) collective-permute-start(f32[256,128]{1,0:T(8,128)S(1)} %get-tuple-element.43), channel_id=1, source_target_pairs={{0,4},{4,0},{2,6},{6,2},{8,12},{12,8},{10,14},{14,10},{1,3},{3,1},... | collective-permute-start | bytes 393224 | tf_op jit(solution)/shard_map/ppermute | solution.py:558
  87.2 2.3 %shard_map.78.own_ref = f32[4096,128]{1,0:T(8,128)S(1)} custom-call(s32[4]{0:T(128)S(1)} %fusion.2.order_ref, s32[1024]{0:T(1024)S(1)} %bitcast.11, f32[4096,128]{1,0:T(8,128)S(1)} %get-tuple-element.40.own_ref, f32[256,128]{1,0:T(8,128)S(1)} %collective-permute-done.12.r0), custom_call_target="tpu_custom_call" | custom-call | flops 1000000 | bytes 4000000 | tf_op jit(solution)/shard_map/pallas_call | solution.py:233
  89.5 1.6 %collective-permute-done.14.r2 = f32[256,128]{1,0:T(8,128)S(1)} collective-permute-done((f32[256,128]{1,0:T(8,128)S(1)}, f32[256,128]{1,0:T(8,128)S(1)}, u32[]{:S(2)}, u32[]{:S(2)}) %collective-permute-start.14) | collective-permute-done | bytes 131104 | tf_op jit(solution)/shard_map/ppermute | solution.py:558
  91.1 3.7 %shard_map.79.own_ref = bf16[4096,128]{1,0:T(8,128)(2,1)S(1)} custom-call(s32[4]{0:T(128)S(1)} %fusion.2.order_ref, s32[1024]{0:T(1024)S(1)} %bitcast.12, f32[2]{0:T(128)S(1)} %copy-done.2, f32[4096,128]{1,0:T(8,128)S(1)} %shard_map.78.own_ref, f32[32,128]{1,0:T(8,128)S(1)} %bitcast.14, bf16[4096,128]{1,0:T(8,128)(2,1)S(1)} %get-tuple-element.35.vec_ref, ...), custom_call_target="tpu_custom_call" | custom-call | tf_op jit(solution)/shard_map/pallas_call | solution.py:310
  94.8 2.6 %collective-permute-done.16.other_ref = bf16[4096,128]{1,0:T(8,128)(2,1)S(1)} collective-permute-done((bf16[4096,128]{1,0:T(8,128)(2,1)S(1)}, bf16[4096,128]{1,0:T(8,128)(2,1)S(1)}, u32[]{:S(2)}, u32[]{:S(2)}) %collective-permute-start.16) | collective-permute-done | bytes 1048608 | tf_op jit(solution)/shard_map/ppermute | solution.py:538
  98.2 5.2 %collective-permute-start.19 = (f32[136,128]{1,0:T(8,128)S(1)}, f32[136,128]{1,0:T(8,128)S(1)}, u32[]{:S(2)}, u32[]{:S(2)}) collective-permute-start(f32[136,128]{1,0:T(8,128)S(1)} %shard_map.80), channel_id=1, source_target_pairs={{0,6},{2,4},{4,2},{6,0},{8,14},{10,12},{12,10},{14,8},{1,7},{3,5},... | collective-permute-start | bytes 208904 | tf_op jit(solution)/shard_map/ppermute | solution.py:529
  104.1 2.3 %collective-permute-done.19 = f32[136,128]{1,0:T(8,128)S(1)} collective-permute-done((f32[136,128]{1,0:T(8,128)S(1)}, f32[136,128]{1,0:T(8,128)S(1)}, u32[]{:S(2)}, u32[]{:S(2)}) %collective-permute-start.19) | collective-permute-done | bytes 69664 | tf_op jit(solution)/shard_map/ppermute | solution.py:529
  106.4 1.6 %collective-permute-done.18 = f32[136,128]{1,0:T(8,128)S(1)} collective-permute-done((f32[136,128]{1,0:T(8,128)S(1)}, f32[136,128]{1,0:T(8,128)S(1)}, u32[]{:S(2)}, u32[]{:S(2)}) %collective-permute-start.18) | collective-permute-done | bytes 69664 | tf_op jit(solution)/shard_map/ppermute | solution.py:529
  108.0 3.1 %collective-permute-start.20 = (f32[136,128]{1,0:T(8,128)S(1)}, f32[136,128]{1,0:T(8,128)S(1)}, u32[]{:S(2)}, u32[]{:S(2)}) collective-permute-start(f32[136,128]{1,0:T(8,128)S(1)} %add_add_fusion), channel_id=1, source_target_pairs={{0,8},{2,10},{4,12},{6,14},{8,0},{10,2},{12,4},{14,6},{1,9},{3,11}... | collective-permute-start | bytes 208904 | tf_op jit(solution)/shard_map/ppermute | solution.py:529
  111.1 3.9 %collective-permute-done.20 = f32[136,128]{1,0:T(8,128)S(1)} collective-permute-done((f32[136,128]{1,0:T(8,128)S(1)}, f32[136,128]{1,0:T(8,128)S(1)}, u32[]{:S(2)}, u32[]{:S(2)}) %collective-permute-start.20) | collective-permute-done | bytes 69664 | tf_op jit(solution)/shard_map/ppermute | solution.py:529
  116.4 10.9 %shard_map.81 = f32[4096,128]{1,0:T(8,128)} custom-call(s32[1]{0:T(128)} %bitcast.band_ref, f32[1]{0:T(128)} %constant.52.clone.1.count_ref, f32[136,128]{1,0:T(8,128)S(1)} %add.37.mine_ref, f32[136,128]{1,0:T(8,128)S(1)} %collective-permute-done.21.theirs_ref, bf16[4096,128]{1,0:T(8,128)(2,1)S(1)} %shard_map.79.own_ref, ...), custom_call_target="tpu_custom_call" | custom-call | tf_op jit(solution)/shard_map/pallas_call | solution.py:503
  (43 shorter events, 11.5 us)
Async XLA Ops:
  0.0 40.4 %copy-start.3 = (s32[4,256]{1,0:T(4,128)S(1)}, s32[4,256]{1,0:T(4,128)}, u32[]{:S(2)}) copy-start(s32[4,256]{1,0:T(4,128)} %lists_ref.1) | copy-start | bytes 12292
  3.1 8.0 %collective-permute-start = (bf16[256,128]{1,0:T(8,128)(2,1)S(1)}, bf16[256,128]{1,0:T(8,128)(2,1)S(1)}, u32[]{:S(2)}, u32[]{:S(2)}) collective-permute-start(bf16[256,128]{1,0:T(8,128)(2,1)S(1)} %get-tuple-element.26), channel_id=1, source_target_pairs={{0,2},{2,0},{4,6},{6,4},{8,10},{10,8},{12,14},{14,12},{1,5},{5,1},... | collective-permute-start | bytes 196616 | tf_op jit(solution)/shard_map/ppermute | solution.py:558
  6.1 5.0 %collective-permute-start.1 = (bf16[256,128]{1,0:T(8,128)(2,1)S(1)}, bf16[256,128]{1,0:T(8,128)(2,1)S(1)}, u32[]{:S(2)}, u32[]{:S(2)}) collective-permute-start(bf16[256,128]{1,0:T(8,128)(2,1)S(1)} %get-tuple-element.27), channel_id=1, source_target_pairs={{2,4},{4,2},{6,8},{8,6},{10,12},{12,10},{5,9},{9,5},{7,11},{11,7},... | collective-permute-start | bytes 196616 | tf_op jit(solution)/shard_map/ppermute | solution.py:558
  6.7 5.8 %collective-permute-start.2 = (bf16[256,128]{1,0:T(8,128)(2,1)S(1)}, bf16[256,128]{1,0:T(8,128)(2,1)S(1)}, u32[]{:S(2)}, u32[]{:S(2)}) collective-permute-start(bf16[256,128]{1,0:T(8,128)(2,1)S(1)} %get-tuple-element.28), channel_id=1, source_target_pairs={{0,4},{4,0},{2,6},{6,2},{8,12},{12,8},{10,14},{14,10},{1,3},{3,1},... | collective-permute-start | bytes 196616 | tf_op jit(solution)/shard_map/ppermute | solution.py:558
  9.6 2.9 %collective-permute-start.3 = (bf16[256,128]{1,0:T(8,128)(2,1)S(1)}, bf16[256,128]{1,0:T(8,128)(2,1)S(1)}, u32[]{:S(2)}, u32[]{:S(2)}) collective-permute-start(bf16[256,128]{1,0:T(8,128)(2,1)S(1)} %get-tuple-element.29), channel_id=1, source_target_pairs={{4,8},{8,4},{6,10},{10,6},{3,5},{5,3},{7,9},{9,7},{11,13},{13,11},... | collective-permute-start | bytes 196616 | tf_op jit(solution)/shard_map/ppermute | solution.py:558
  30.9 9.5 %collective-permute-start.4 = (f32[256,128]{1,0:T(8,128)S(1)}, f32[256,128]{1,0:T(8,128)S(1)}, u32[]{:S(2)}, u32[]{:S(2)}) collective-permute-start(f32[256,128]{1,0:T(8,128)S(1)} %get-tuple-element.31), channel_id=1, source_target_pairs={{0,2},{2,0},{4,6},{6,4},{8,10},{10,8},{12,14},{14,12},{1,5},{5,1},... | collective-permute-start | bytes 393224 | tf_op jit(solution)/shard_map/ppermute | solution.py:558
  33.9 8.9 %collective-permute-start.5 = (f32[256,128]{1,0:T(8,128)S(1)}, f32[256,128]{1,0:T(8,128)S(1)}, u32[]{:S(2)}, u32[]{:S(2)}) collective-permute-start(f32[256,128]{1,0:T(8,128)S(1)} %get-tuple-element.32), channel_id=1, source_target_pairs={{2,4},{4,2},{6,8},{8,6},{10,12},{12,10},{5,9},{9,5},{7,11},{11,7},... | collective-permute-start | bytes 393224 | tf_op jit(solution)/shard_map/ppermute | solution.py:558
  34.5 10.9 %collective-permute-start.6 = (f32[256,128]{1,0:T(8,128)S(1)}, f32[256,128]{1,0:T(8,128)S(1)}, u32[]{:S(2)}, u32[]{:S(2)}) collective-permute-start(f32[256,128]{1,0:T(8,128)S(1)} %get-tuple-element.33), channel_id=1, source_target_pairs={{0,4},{4,0},{2,6},{6,2},{8,12},{12,8},{10,14},{14,10},{1,3},{3,1},... | collective-permute-start | bytes 393224 | tf_op jit(solution)/shard_map/ppermute | solution.py:558
  39.8 5.7 %collective-permute-start.7 = (f32[256,128]{1,0:T(8,128)S(1)}, f32[256,128]{1,0:T(8,128)S(1)}, u32[]{:S(2)}, u32[]{:S(2)}) collective-permute-start(f32[256,128]{1,0:T(8,128)S(1)} %get-tuple-element.34), channel_id=1, source_target_pairs={{4,8},{8,4},{6,10},{10,6},{3,5},{5,3},{7,9},{9,7},{11,13},{13,11},... | collective-permute-start | bytes 393224 | tf_op jit(solution)/shard_map/ppermute | solution.py:558
  40.5 5.0 %copy-start.1 = (f32[4096]{0:T(1024)S(1)}, f32[4096]{0:T(1024)}, u32[]{:S(2)}) copy-start(f32[4096]{0:T(1024)} %param.11) | copy-start | bytes 49156
  49.8 7.3 %collective-permute-start.8 = (bf16[256,128]{1,0:T(8,128)(2,1)S(1)}, bf16[256,128]{1,0:T(8,128)(2,1)S(1)}, u32[]{:S(2)}, u32[]{:S(2)}) collective-permute-start(bf16[256,128]{1,0:T(8,128)(2,1)S(1)} %get-tuple-element.36), channel_id=1, source_target_pairs={{0,2},{2,0},{4,6},{6,4},{8,10},{10,8},{12,14},{14,12},{1,5},{5,1},... | collective-permute-start | bytes 196616 | tf_op jit(solution)/shard_map/ppermute | solution.py:558
  51.0 6.1 %collective-permute-start.9 = (bf16[256,128]{1,0:T(8,128)(2,1)S(1)}, bf16[256,128]{1,0:T(8,128)(2,1)S(1)}, u32[]{:S(2)}, u32[]{:S(2)}) collective-permute-start(bf16[256,128]{1,0:T(8,128)(2,1)S(1)} %get-tuple-element.37), channel_id=1, source_target_pairs={{2,4},{4,2},{6,8},{8,6},{10,12},{12,10},{5,9},{9,5},{7,11},{11,7},... | collective-permute-start | bytes 196616 | tf_op jit(solution)/shard_map/ppermute | solution.py:558
  51.6 8.3 %collective-permute-start.10 = (bf16[256,128]{1,0:T(8,128)(2,1)S(1)}, bf16[256,128]{1,0:T(8,128)(2,1)S(1)}, u32[]{:S(2)}, u32[]{:S(2)}) collective-permute-start(bf16[256,128]{1,0:T(8,128)(2,1)S(1)} %get-tuple-element.38), channel_id=1, source_target_pairs={{0,4},{4,0},{2,6},{6,2},{8,12},{12,8},{10,14},{14,10},{1,3},{3,1},... | collective-permute-start | bytes 196616 | tf_op jit(solution)/shard_map/ppermute | solution.py:558
  56.4 3.6 %collective-permute-start.11 = (bf16[256,128]{1,0:T(8,128)(2,1)S(1)}, bf16[256,128]{1,0:T(8,128)(2,1)S(1)}, u32[]{:S(2)}, u32[]{:S(2)}) collective-permute-start(bf16[256,128]{1,0:T(8,128)(2,1)S(1)} %get-tuple-element.39), channel_id=1, source_target_pairs={{4,8},{8,4},{6,10},{10,6},{3,5},{5,3},{7,9},{9,7},{11,13},{13,11},... | collective-permute-start | bytes 196616 | tf_op jit(solution)/shard_map/ppermute | solution.py:558
  78.4 8.8 %collective-permute-start.12 = (f32[256,128]{1,0:T(8,128)S(1)}, f32[256,128]{1,0:T(8,128)S(1)}, u32[]{:S(2)}, u32[]{:S(2)}) collective-permute-start(f32[256,128]{1,0:T(8,128)S(1)} %get-tuple-element.41), channel_id=1, source_target_pairs={{0,2},{2,0},{4,6},{6,4},{8,10},{10,8},{12,14},{14,12},{1,5},{5,1},... | collective-permute-start | bytes 393224 | tf_op jit(solution)/shard_map/ppermute | solution.py:558
  80.6 8.9 %collective-permute-start.13 = (f32[256,128]{1,0:T(8,128)S(1)}, f32[256,128]{1,0:T(8,128)S(1)}, u32[]{:S(2)}, u32[]{:S(2)}) collective-permute-start(f32[256,128]{1,0:T(8,128)S(1)} %get-tuple-element.42), channel_id=1, source_target_pairs={{2,4},{4,2},{6,8},{8,6},{10,12},{12,10},{5,9},{9,5},{7,11},{11,7},... | collective-permute-start | bytes 393224 | tf_op jit(solution)/shard_map/ppermute | solution.py:558
  81.3 9.8 %collective-permute-start.14 = (f32[256,128]{1,0:T(8,128)S(1)}, f32[256,128]{1,0:T(8,128)S(1)}, u32[]{:S(2)}, u32[]{:S(2)}) collective-permute-start(f32[256,128]{1,0:T(8,128)S(1)} %get-tuple-element.43), channel_id=1, source_target_pairs={{0,4},{4,0},{2,6},{6,2},{8,12},{12,8},{10,14},{14,10},{1,3},{3,1},... | collective-permute-start | bytes 393224 | tf_op jit(solution)/shard_map/ppermute | solution.py:558
  86.5 4.6 %collective-permute-start.15 = (f32[256,128]{1,0:T(8,128)S(1)}, f32[256,128]{1,0:T(8,128)S(1)}, u32[]{:S(2)}, u32[]{:S(2)}) collective-permute-start(f32[256,128]{1,0:T(8,128)S(1)} %get-tuple-element.44), channel_id=1, source_target_pairs={{4,8},{8,4},{6,10},{10,6},{3,5},{5,3},{7,9},{9,7},{11,13},{13,11},... | collective-permute-start | bytes 393224 | tf_op jit(solution)/shard_map/ppermute | solution.py:558
  94.8 2.7 %collective-permute-start.16 = (bf16[4096,128]{1,0:T(8,128)(2,1)S(1)}, bf16[4096,128]{1,0:T(8,128)(2,1)S(1)}, u32[]{:S(2)}, u32[]{:S(2)}) collective-permute-start(bf16[4096,128]{1,0:T(8,128)(2,1)S(1)} %shard_map.79.own_ref), channel_id=1, source_target_pairs={{0,1},{1,0},{2,3},{3,2},{4,5},{5,4},{6,7},{7,6},{8,9},{9,8},{10,11... | collective-permute-start | bytes 3145736 | tf_op jit(solution)/shard_map/ppermute | solution.py:538
  98.2 8.2 %collective-permute-start.19 = (f32[136,128]{1,0:T(8,128)S(1)}, f32[136,128]{1,0:T(8,128)S(1)}, u32[]{:S(2)}, u32[]{:S(2)}) collective-permute-start(f32[136,128]{1,0:T(8,128)S(1)} %shard_map.80), channel_id=1, source_target_pairs={{0,6},{2,4},{4,2},{6,0},{8,14},{10,12},{12,10},{14,8},{1,7},{3,5},... | collective-permute-start | bytes 208904 | tf_op jit(solution)/shard_map/ppermute | solution.py:529
  103.4 4.6 %collective-permute-start.18 = (f32[136,128]{1,0:T(8,128)S(1)}, f32[136,128]{1,0:T(8,128)S(1)}, u32[]{:S(2)}, u32[]{:S(2)}) collective-permute-start(f32[136,128]{1,0:T(8,128)S(1)} %shard_map.80), channel_id=1, source_target_pairs={{0,4},{2,6},{4,0},{6,2},{8,12},{10,14},{12,8},{14,10},{1,5},{3,7},... | collective-permute-start | bytes 208904 | tf_op jit(solution)/shard_map/ppermute | solution.py:529
  103.4 4.6 %collective-permute-start.17 = (f32[136,128]{1,0:T(8,128)S(1)}, f32[136,128]{1,0:T(8,128)S(1)}, u32[]{:S(2)}, u32[]{:S(2)}) collective-permute-start(f32[136,128]{1,0:T(8,128)S(1)} %shard_map.80), channel_id=1, source_target_pairs={{0,2},{2,0},{4,6},{6,4},{8,10},{10,8},{12,14},{14,12},{1,3},{3,1},... | collective-permute-start | bytes 208904 | tf_op jit(solution)/shard_map/ppermute | solution.py:529
  108.0 7.0 %collective-permute-start.20 = (f32[136,128]{1,0:T(8,128)S(1)}, f32[136,128]{1,0:T(8,128)S(1)}, u32[]{:S(2)}, u32[]{:S(2)}) collective-permute-start(f32[136,128]{1,0:T(8,128)S(1)} %add_add_fusion), channel_id=1, source_target_pairs={{0,8},{2,10},{4,12},{6,14},{8,0},{10,2},{12,4},{14,6},{1,9},{3,11}... | collective-permute-start | bytes 208904 | tf_op jit(solution)/shard_map/ppermute | solution.py:529
  115.1 1.3 %collective-permute-start.21 = (f32[136,128]{1,0:T(8,128)S(1)}, f32[136,128]{1,0:T(8,128)S(1)}, u32[]{:S(2)}, u32[]{:S(2)}) collective-permute-start(f32[136,128]{1,0:T(8,128)S(1)} %add.37.mine_ref), channel_id=1, source_target_pairs={{0,1},{1,0},{2,3},{3,2},{4,5},{5,4},{6,7},{7,6},{8,9},{9,8},{10,11... | collective-permute-start | bytes 208904 | tf_op jit(solution)/shard_map/ppermute | solution.py:538
  (2 other events, 8.8 us)
